TPU v7x, 32 devices: a whole 2x2x4 slice. The times are simulated.
32 devices in a mesh: dp: 8 (over y, x, core), sp: 4 (over z).
Axes of the slice: x: 2, y: 2, z: 4, core: 2. Of those that a mesh axis runs over, the one named last changes fastest.
Arguments:
- tokens: bfloat16 [2, 8192, 1408], P(None, ('dp', 'sp')), may hold values from -6 to 6
- skip_tokens: bfloat16 [2, 8192, 1408], P(None, ('dp', 'sp')), may hold values from -6 to 6
- text: bfloat16 [2, 2688, 1024], P(None, ('dp', 'sp')), may hold values from -6 to 6
- timestep: int32 [2, 8], P(None, 'dp'), may hold values from 0 to 999
- grid: int32 [2, 8, 2], P(None, 'dp'), may hold values from 19 to 32, as said below
- text_len: int32 [2, 8, 2], P(None, 'dp'), may hold values from 1 to 256, as said below
- w_skip: bfloat16 [2816, 1408], P('sp', 'dp'), may hold values from -0.109375 to 0.109375
- w_mod: bfloat16 [1408, 1408], P('sp', 'dp'), may hold values from -0.15625 to 0.15625
- w_qkv: bfloat16 [1408, 3, 1408], P('dp', None, 'sp'), may hold values from -0.15625 to 0.15625
- w_out1: bfloat16 [1408, 1408], P('sp', 'dp'), may hold values from -6 to 6
- w_query2: bfloat16 [1408, 1408], P('dp', 'sp'), may hold values from -0.15625 to 0.15625
- w_text_kv: bfloat16 [1024, 2, 1408], P('dp', None, 'sp'), may hold values from -0.1875 to 0.1875
- w_out2: bfloat16 [1408, 1408], P('sp', 'dp'), may hold values from -2 to 2
- w_fc1: bfloat16 [1408, 6144], P('dp', 'sp'), may hold values from -0.15625 to 0.15625
- w_fc2: bfloat16 [6144, 1408], P('sp', 'dp'), may hold values from -0.078125 to 0.078125
- gain_skip: float32 [1408], replicated, may hold values from 0.5 to 1.5
- gain_attn: float32 [1408], replicated, may hold values from 0.5 to 1.5
- gain_cross: float32 [1408], replicated, may hold values from 0.5 to 1.5
- gain_mlp: float32 [1408], replicated, may hold values from 0.5 to 1.5
- gain_query: float32 [88], replicated, may hold values from 0.5 to 1.5
- gain_key: float32 [88], replicated, may hold values from 0.5 to 1.5
- cotangent: bfloat16 [2, 8192, 1408], P(None, ('dp', 'sp')), may hold values from -6 to 6
Outputs:
- out: bfloat16 [2, 8192, 1408], P(None, ('dp', 'sp'))
- d_tokens: float32 [2, 8192, 1408], P(None, ('dp', 'sp'))
- d_skip: float32 [2, 8192, 1408], P(None, ('dp', 'sp'))
- d_text: float32 [2, 2688, 1024], P(None, ('dp', 'sp'))
- d_w_skip: float32 [2816, 1408], P('sp', 'dp')
- d_w_mod: float32 [1408, 1408], P('sp', 'dp')
- d_w_qkv: float32 [1408, 3, 1408], P('dp', None, 'sp')
- d_w_out1: float32 [1408, 1408], P('sp', 'dp')
- d_w_query2: float32 [1408, 1408], P('dp', 'sp')
- d_w_text_kv: float32 [1024, 2, 1408], P('dp', None, 'sp')
- d_w_out2: float32 [1408, 1408], P('sp', 'dp')
- d_w_fc1: float32 [1408, 6144], P('dp', 'sp')
- d_w_fc2: float32 [6144, 1408], P('sp', 'dp')
- d_gain_skip: float32 [1408], P(('dp', 'sp'))
- d_gain_attn: float32 [1408], P(('dp', 'sp'))
- d_gain_cross: float32 [1408], P(('dp', 'sp'))
- d_gain_mlp: float32 [1408], P(('dp', 'sp'))
- d_gain_query: float32 [88], replicated
- d_gain_key: float32 [88], replicated
Inputs may be any that keep to these rules, and one draw needn't show every extreme that they name: grid[m, r] holds (rows, columns) of patches of that image, rows from 19 to 32, columns from 21 to 32; its tokens fill the first rows * columns of its 1024 slots in row-major order. In micro-batch 0 the image on the last dp rank has 32 x 32 patches and the one on rank 0 the fewest rows and columns. text_len[m, r] holds (CLIP tokens, mT5 tokens) of that image's caption: the first from 1 to 77, the second from 1 to 256. In micro-batch 0 rank 0's caption is full in both and the last rank's has one token in each.
All inputs are finite; a program needn't handle non-finite values.
Results may differ from a plain program's by a relative error of at most 0.024.
Values may be sent and summed in bfloat16 or wider, within the bound.
No kernel may reach another device: no remote copies, remote signals or barrier semaphores. Data moves between devices by JAX's collectives and lax.ppermute only.
A program may use at most 512 MiB of HBM per device.

v0:
```python
import math

import jax
import jax.numpy as jnp
from jax import lax
from jax.sharding import PartitionSpec as P

H = 16
HD = 88
CLIP_LEN = 77
QB = 512


EPS = 1e-06
MASKED = -1e30


def norm_rows(value, gain):
    mean = jnp.mean(value, -1, keepdims=True)
    centre = value - mean
    spread = jnp.mean(centre * centre, -1, keepdims=True)
    return centre * lax.rsqrt(spread + EPS) * gain


def gelu_tanh(value):
    return jax.nn.gelu(value, approximate=True)


def time_embed(step, width):
    half = width // 2
    rate = jnp.exp(-math.log(10000.0) * jnp.arange(half, dtype=jnp.float32) / half)
    angle = step.astype(jnp.float32) * rate
    return jnp.concatenate([jnp.cos(angle), jnp.sin(angle)])


def rope_tables(place, wide, head):
    row = (place // wide).astype(jnp.float32)
    column = (place % wide).astype(jnp.float32)
    quarter = head // 4
    pair = jnp.arange(head // 2, dtype=jnp.int32)
    upper = pair < quarter
    rank = jnp.where(upper, pair, pair - quarter).astype(jnp.float32)
    rate = jnp.exp(-math.log(10000.0) * rank / quarter)
    angle = jnp.where(upper[None, :], row[:, None], column[:, None]) * rate[None, :]
    return (jnp.cos(angle)[:, None, :], jnp.sin(angle)[:, None, :])


def rotate(value, cosine, sine):
    pairs = value.reshape(value.shape[:-1] + (value.shape[-1] // 2, 2))
    even = pairs[..., 0]
    odd = pairs[..., 1]
    return jnp.stack([even * cosine - odd * sine, even * sine + odd * cosine], -1).reshape(
        value.shape
    )


def outer_sum(left, right):
    return lax.dot_general(
        left, right, (((0,), (0,)), ((), ())), preferred_element_type=jnp.float32
    )


def back_dot(incoming, weight):
    return lax.dot_general(
        incoming, weight, (((1,), (1,)), ((), ())), preferred_element_type=jnp.float32
    )


def split_heads(packed, parts):
    slots, groups, heads, head = packed.shape
    grouped = packed.reshape(slots, groups, parts, heads // parts, head)
    return jnp.transpose(grouped, (2, 0, 1, 3, 4)).reshape(parts, -1)


def join_heads(received, parts, slots, groups, head):
    local = received.shape[1] // (slots * groups * head)
    grouped = received.reshape(parts, slots, groups, local, head)
    return jnp.transpose(grouped, (1, 2, 0, 3, 4)).reshape(slots, groups, parts * local, head)


def attend_forward(query, key, value, live_keys, blocks, size):
    scale = query.shape[-1] ** (-0.5)

    def one_block(index, carry):
        results, log_totals = carry
        start = index * size
        rows = lax.dynamic_slice_in_dim(query, start, size, 0)
        scores = jnp.einsum("qhd,khd->hqk", rows, key, preferred_element_type=jnp.float32) * scale
        scores = jnp.where(live_keys[None, None, :], scores, MASKED)
        top = jnp.max(scores, -1, keepdims=True)
        raised = jnp.exp(scores - top)
        total = jnp.sum(raised, -1, keepdims=True)
        probs = (raised / total).astype(jnp.bfloat16)
        result = jnp.einsum("hqk,khd->qhd", probs, value, preferred_element_type=jnp.float32)
        results = lax.dynamic_update_slice_in_dim(results, result.astype(jnp.bfloat16), start, 0)
        log_totals = lax.dynamic_update_slice_in_dim(
            log_totals, (top + jnp.log(total))[..., 0], start, 1
        )
        return (results, log_totals)

    start_state = (
        jnp.zeros(query.shape, jnp.bfloat16),
        jnp.zeros((query.shape[1], query.shape[0]), jnp.float32),
    )
    return lax.fori_loop(0, blocks, one_block, start_state)


def attend_backward(query, key, value, live_keys, log_totals, incoming, blocks, size):
    scale = query.shape[-1] ** (-0.5)

    def one_block(index, carry):
        d_query, d_key, d_value = carry
        start = index * size
        rows = lax.dynamic_slice_in_dim(query, start, size, 0)
        grads = lax.dynamic_slice_in_dim(incoming, start, size, 0)
        norms = lax.dynamic_slice_in_dim(log_totals, start, size, 1)
        scores = jnp.einsum("qhd,khd->hqk", rows, key, preferred_element_type=jnp.float32) * scale
        scores = jnp.where(live_keys[None, None, :], scores, MASKED)
        probs = jnp.exp(scores - norms[..., None])
        d_value = d_value + jnp.einsum(
            "hqk,qhd->khd", probs.astype(jnp.bfloat16), grads, preferred_element_type=jnp.float32
        )
        d_probs = jnp.einsum("qhd,khd->hqk", grads, value, preferred_element_type=jnp.float32)
        inner = jnp.sum(probs * d_probs, -1, keepdims=True)
        d_scores = (probs * (d_probs - inner)).astype(jnp.bfloat16)
        block_query = (
            jnp.einsum("hqk,khd->qhd", d_scores, key, preferred_element_type=jnp.float32) * scale
        )
        d_query = lax.dynamic_update_slice_in_dim(
            d_query, block_query.astype(jnp.bfloat16), start, 0
        )
        d_key = (
            d_key
            + jnp.einsum("hqk,qhd->khd", d_scores, rows, preferred_element_type=jnp.float32) * scale
        )
        return (d_query, d_key, d_value)

    start_state = (
        jnp.zeros(query.shape, jnp.bfloat16),
        jnp.zeros(key.shape, jnp.float32),
        jnp.zeros(value.shape, jnp.float32),
    )
    return lax.fori_loop(0, blocks, one_block, start_state)


def turn_norm(raw_query, raw_key, query_gain, key_gain, cosine, sine):
    return (
        rotate(norm_rows(raw_query, query_gain), cosine, sine),
        rotate(norm_rows(raw_key, key_gain), cosine, sine),
    )


def on_device(
    tokens,
    skip_tokens,
    text,
    timestep,
    grid,
    text_len,
    w_skip,
    w_mod,
    w_qkv,
    w_out1,
    w_query2,
    w_text_kv,
    w_out2,
    w_fc1,
    w_fc2,
    gain_skip,
    gain_attn,
    gain_cross,
    gain_mlp,
    gain_query,
    gain_key,
    cotangent,
):
    slots = tokens.shape[1]
    width = tokens.shape[2]
    parts = lax.axis_size("sp")
    sequence = slots * parts
    local = H // parts
    text_slots = text.shape[1]
    text_total = text_slots * parts
    place = lax.axis_index("sp") * slots + jnp.arange(slots, dtype=jnp.int32)
    every = jnp.arange(sequence, dtype=jnp.int32)
    text_place = jnp.arange(text_total, dtype=jnp.int32)
    shards = (
        lax.all_gather(w_skip, "dp", axis=1, tiled=True),
        lax.all_gather(w_mod, "dp", axis=1, tiled=True),
        lax.all_gather(w_qkv, "dp", axis=0, tiled=True),
        lax.all_gather(w_out1, "dp", axis=1, tiled=True),
        lax.all_gather(w_query2, "dp", axis=0, tiled=True),
        lax.all_gather(w_text_kv, "dp", axis=0, tiled=True),
        lax.all_gather(w_out2, "dp", axis=1, tiled=True),
        lax.all_gather(w_fc1, "dp", axis=0, tiled=True),
        lax.all_gather(w_fc2, "dp", axis=1, tiled=True),
    )
    (
        skip_part,
        mod_part,
        qkv_part,
        out1_part,
        query2_part,
        words_part,
        out2_part,
        fc1_part,
        fc2_part,
    ) = shards
    gathered = (
        lax.all_gather(skip_part, "sp", axis=0, tiled=True),
        lax.all_gather(mod_part, "sp", axis=0, tiled=True),
        lax.all_gather(qkv_part, "sp", axis=2, tiled=True),
        lax.all_gather(out1_part, "sp", axis=0, tiled=True),
        lax.all_gather(query2_part, "sp", axis=1, tiled=True),
        lax.all_gather(words_part, "sp", axis=2, tiled=True),
        lax.all_gather(out2_part, "sp", axis=0, tiled=True),
        lax.all_gather(fc1_part, "sp", axis=1, tiled=True),
        lax.all_gather(fc2_part, "sp", axis=0, tiled=True),
    )
    skip_full = gathered[0]
    mod_full = gathered[1]
    inner_weights = gathered[2:]
    start_terms = tuple(
        (
            jnp.zeros(weight.shape, jnp.float32)
            for weight in (skip_full, mod_full) + tuple(inner_weights)
        )
    ) + tuple((jnp.zeros((width,), jnp.float32) for index in range(4)))
    start_gains = (jnp.zeros((HD,), jnp.float32), jnp.zeros((HD,), jnp.float32))

    def whole_path(stream, pre_attn, grad3, words, wide, live_keys, text_live, blocks):
        full_qkv, full_out1, full_query2, full_words, full_out2, full_fc1, full_fc2 = inner_weights
        qkv_flat = full_qkv.reshape(width, 3 * width)
        words_flat = full_words.reshape(full_words.shape[0], 2 * width)
        projected = jnp.dot(pre_attn, qkv_flat, preferred_element_type=jnp.float32).reshape(
            slots, 3, H, HD
        )
        cosine, sine = rope_tables(place, wide, HD)

        def turned(raw_query, raw_key, query_gain, key_gain):
            return turn_norm(raw_query, raw_key, query_gain, key_gain, cosine, sine)

        query, key = turned(projected[:, 0], projected[:, 1], gain_query, gain_key)
        packed = jnp.stack([query, key, projected[:, 2]], 1).astype(jnp.bfloat16)
        head_qkv = lax.all_to_all(
            split_heads(packed, parts), "sp", split_axis=0, concat_axis=0, tiled=True
        ).reshape(sequence, 3, local, HD)
        attended, log_totals = attend_forward(
            head_qkv[:, 0], head_qkv[:, 1], head_qkv[:, 2], live_keys, blocks, QB
        )
        returned = lax.all_to_all(
            attended.reshape(parts, -1), "sp", split_axis=0, concat_axis=0, tiled=True
        )
        attn_tokens = join_heads(returned, parts, slots, 1, HD).reshape(slots, width)
        stream1 = stream + jnp.dot(attn_tokens, full_out1, preferred_element_type=jnp.float32)
        pre_cross = norm_rows(stream1, gain_cross).astype(jnp.bfloat16)
        query2 = (
            jnp.dot(pre_cross, full_query2, preferred_element_type=jnp.float32)
            .astype(jnp.bfloat16)
            .reshape(slots, H, HD)
        )
        text_kv = jnp.dot(words, words_flat, preferred_element_type=jnp.float32).astype(
            jnp.bfloat16
        )
        all_kv = lax.all_gather(text_kv, "sp", axis=0, tiled=True)
        key2 = all_kv[:, :width].reshape(text_total, H, HD)
        value2 = all_kv[:, width:].reshape(text_total, H, HD)
        crossed, cross_totals = attend_forward(query2, key2, value2, text_live, 1, slots)
        cross_tokens = crossed.reshape(slots, width)
        stream2 = stream1 + jnp.dot(cross_tokens, full_out2, preferred_element_type=jnp.float32)
        pre_mlp = norm_rows(stream2, gain_mlp).astype(jnp.bfloat16)
        hidden = jnp.dot(pre_mlp, full_fc1, preferred_element_type=jnp.float32)
        activ = gelu_tanh(hidden).astype(jnp.bfloat16)
        stream3 = stream2 + jnp.dot(activ, full_fc2, preferred_element_type=jnp.float32)
        d_mlp = grad3.astype(jnp.bfloat16)
        term_fc2 = outer_sum(activ, d_mlp)
        d_activ = back_dot(d_mlp, full_fc2)
        unused, gelu_pull = jax.vjp(gelu_tanh, hidden)
        d_hidden = gelu_pull(d_activ)[0].astype(jnp.bfloat16)
        term_fc1 = outer_sum(pre_mlp, d_hidden)
        unused, mlp_pull = jax.vjp(norm_rows, stream2, gain_mlp)
        d_stream2, d_gain_mlp = mlp_pull(back_dot(d_hidden, full_fc1))
        grad2 = grad3 + d_stream2
        d_cross = grad2.astype(jnp.bfloat16)
        term_out2 = outer_sum(cross_tokens, d_cross)
        d_crossed = back_dot(d_cross, full_out2).astype(jnp.bfloat16).reshape(slots, H, HD)
        d_query2, d_key2, d_value2 = attend_backward(
            query2, key2, value2, text_live, cross_totals, d_crossed, 1, slots
        )
        d_text_kv = jnp.concatenate(
            [d_key2.reshape(text_total, width), d_value2.reshape(text_total, width)], 1
        )
        own_kv = lax.psum_scatter(
            d_text_kv.astype(jnp.bfloat16), "sp", scatter_dimension=0, tiled=True
        )
        term_words = outer_sum(words, own_kv).reshape(full_words.shape)
        d_words = back_dot(own_kv, words_flat)
        d_query2 = d_query2.reshape(slots, width)
        term_query2 = outer_sum(pre_cross, d_query2)
        unused, cross_pull = jax.vjp(norm_rows, stream1, gain_cross)
        d_stream1, d_gain_cross = cross_pull(back_dot(d_query2, full_query2))
        grad1 = grad2 + d_stream1
        d_attn = grad1.astype(jnp.bfloat16)
        term_out1 = outer_sum(attn_tokens, d_attn)
        d_attended = back_dot(d_attn, full_out1).astype(jnp.bfloat16).reshape(slots, 1, H, HD)
        d_heads = lax.all_to_all(
            split_heads(d_attended, parts), "sp", split_axis=0, concat_axis=0, tiled=True
        ).reshape(sequence, local, HD)
        d_query, d_key, d_value = attend_backward(
            head_qkv[:, 0],
            head_qkv[:, 1],
            head_qkv[:, 2],
            live_keys,
            log_totals,
            d_heads,
            blocks,
            QB,
        )
        d_packed = jnp.stack([d_query, d_key.astype(jnp.bfloat16), d_value.astype(jnp.bfloat16)], 1)
        d_returned = lax.all_to_all(
            d_packed.reshape(parts, -1), "sp", split_axis=0, concat_axis=0, tiled=True
        )
        d_turned = join_heads(d_returned, parts, slots, 3, HD)
        unused, turn_pull = jax.vjp(turned, projected[:, 0], projected[:, 1], gain_query, gain_key)
        d_raw_query, d_raw_key, d_query_gain, d_key_gain = turn_pull(
            (d_turned[:, 0].astype(jnp.float32), d_turned[:, 1].astype(jnp.float32))
        )
        d_projected = (
            jnp.stack([d_raw_query, d_raw_key, d_turned[:, 2].astype(jnp.float32)], 1)
            .reshape(slots, 3 * width)
            .astype(jnp.bfloat16)
        )
        term_qkv = outer_sum(pre_attn, d_projected).reshape(full_qkv.shape)
        d_pre = back_dot(d_projected, qkv_flat)
        terms = (term_qkv, term_out1, term_query2, term_words, term_out2, term_fc1, term_fc2)
        return (
            stream3,
            grad1,
            d_pre,
            d_words,
            terms,
            d_gain_cross,
            d_gain_mlp,
            d_query_gain,
            d_key_gain,
        )

    def one_micro(carry, items):
        totals, gain_sums = carry
        image, skips, words, incoming, step, shape, lengths = items
        wide = shape[0, 1]
        count = shape[0, 0] * wide
        live_rows = (place < count).astype(jnp.float32)
        live_keys = every < count
        text_live = (text_place < lengths[0, 0]) | (text_place >= CLIP_LEN) & (
            text_place < CLIP_LEN + lengths[0, 1]
        )
        blocks = sequence // QB
        joined = jnp.concatenate([image, skips], 1)
        base = jnp.dot(joined, skip_full, preferred_element_type=jnp.float32)
        stream = norm_rows(base, gain_skip)
        time_act = jax.nn.silu(time_embed(step[0], width)).astype(jnp.bfloat16)
        shift = jnp.dot(time_act[None, :], mod_full, preferred_element_type=jnp.float32)
        pre_attn = (norm_rows(stream, gain_attn) + shift).astype(jnp.bfloat16)
        grad3 = incoming.astype(jnp.float32) * live_rows[:, None]
        path = whole_path(stream, pre_attn, grad3, words, wide, live_keys, text_live, blocks)
        (
            stream3,
            grad1,
            d_pre,
            d_words,
            terms,
            d_gain_cross,
            d_gain_mlp,
            d_query_gain,
            d_key_gain,
        ) = path
        result = (stream3 * live_rows[:, None]).astype(jnp.bfloat16)
        d_shift = jnp.sum(d_pre, 0)
        term_mod = time_act.astype(jnp.float32)[:, None] * d_shift[None, :]
        unused, attn_pull = jax.vjp(norm_rows, stream, gain_attn)
        d_stream0, d_gain_attn = attn_pull(d_pre)
        grad0 = grad1 + d_stream0
        unused, skip_pull = jax.vjp(norm_rows, base, gain_skip)
        d_base, d_gain_skip = skip_pull(grad0)
        d_base = d_base.astype(jnp.bfloat16)
        term_skip = outer_sum(joined, d_base)
        d_joined = back_dot(d_base, skip_full)
        fresh = (
            (term_skip, term_mod)
            + tuple(terms)
            + (d_gain_skip, d_gain_attn, d_gain_cross, d_gain_mlp)
        )
        totals = tuple((before + after for before, after in zip(totals, fresh)))
        gain_sums = (gain_sums[0] + d_query_gain, gain_sums[1] + d_key_gain)
        return ((totals, gain_sums), (result, d_joined[:, :width], d_joined[:, width:], d_words))

    (totals, gain_sums), (results, d_images, d_skips, d_texts) = lax.scan(
        one_micro,
        (start_terms, start_gains),
        (tokens, skip_tokens, text, cotangent, timestep, grid, text_len),
    )
    reduced = (
        lax.psum_scatter(
            totals[0].astype(jnp.bfloat16), "dp", scatter_dimension=1, tiled=True
        ).astype(jnp.float32),
        lax.psum_scatter(
            totals[1].astype(jnp.bfloat16), "dp", scatter_dimension=1, tiled=True
        ).astype(jnp.float32),
        lax.psum_scatter(
            totals[2].astype(jnp.bfloat16), "dp", scatter_dimension=0, tiled=True
        ).astype(jnp.float32),
        lax.psum_scatter(
            totals[3].astype(jnp.bfloat16), "dp", scatter_dimension=1, tiled=True
        ).astype(jnp.float32),
        lax.psum_scatter(
            totals[4].astype(jnp.bfloat16), "dp", scatter_dimension=0, tiled=True
        ).astype(jnp.float32),
        lax.psum_scatter(
            totals[5].astype(jnp.bfloat16), "dp", scatter_dimension=0, tiled=True
        ).astype(jnp.float32),
        lax.psum_scatter(
            totals[6].astype(jnp.bfloat16), "dp", scatter_dimension=1, tiled=True
        ).astype(jnp.float32),
        lax.psum_scatter(
            totals[7].astype(jnp.bfloat16), "dp", scatter_dimension=0, tiled=True
        ).astype(jnp.float32),
        lax.psum_scatter(
            totals[8].astype(jnp.bfloat16), "dp", scatter_dimension=1, tiled=True
        ).astype(jnp.float32),
        lax.psum_scatter(
            totals[9].astype(jnp.bfloat16), "dp", scatter_dimension=0, tiled=True
        ).astype(jnp.float32),
        lax.psum_scatter(
            totals[10].astype(jnp.bfloat16), "dp", scatter_dimension=0, tiled=True
        ).astype(jnp.float32),
        lax.psum_scatter(
            totals[11].astype(jnp.bfloat16), "dp", scatter_dimension=0, tiled=True
        ).astype(jnp.float32),
        lax.psum_scatter(
            totals[12].astype(jnp.bfloat16), "dp", scatter_dimension=0, tiled=True
        ).astype(jnp.float32),
    )
    sums = (
        lax.psum_scatter(
            reduced[0].astype(jnp.bfloat16), "sp", scatter_dimension=0, tiled=True
        ).astype(jnp.float32),
        lax.psum_scatter(
            reduced[1].astype(jnp.bfloat16), "sp", scatter_dimension=0, tiled=True
        ).astype(jnp.float32),
        lax.psum_scatter(
            reduced[2].astype(jnp.bfloat16), "sp", scatter_dimension=2, tiled=True
        ).astype(jnp.float32),
        lax.psum_scatter(
            reduced[3].astype(jnp.bfloat16), "sp", scatter_dimension=0, tiled=True
        ).astype(jnp.float32),
        lax.psum_scatter(
            reduced[4].astype(jnp.bfloat16), "sp", scatter_dimension=1, tiled=True
        ).astype(jnp.float32),
        lax.psum_scatter(
            reduced[5].astype(jnp.bfloat16), "sp", scatter_dimension=2, tiled=True
        ).astype(jnp.float32),
        lax.psum_scatter(
            reduced[6].astype(jnp.bfloat16), "sp", scatter_dimension=0, tiled=True
        ).astype(jnp.float32),
        lax.psum_scatter(
            reduced[7].astype(jnp.bfloat16), "sp", scatter_dimension=1, tiled=True
        ).astype(jnp.float32),
        lax.psum_scatter(
            reduced[8].astype(jnp.bfloat16), "sp", scatter_dimension=0, tiled=True
        ).astype(jnp.float32),
        lax.psum_scatter(
            reduced[9].astype(jnp.bfloat16), "sp", scatter_dimension=0, tiled=True
        ).astype(jnp.float32),
        lax.psum_scatter(
            reduced[10].astype(jnp.bfloat16), "sp", scatter_dimension=0, tiled=True
        ).astype(jnp.float32),
        lax.psum_scatter(
            reduced[11].astype(jnp.bfloat16), "sp", scatter_dimension=0, tiled=True
        ).astype(jnp.float32),
        lax.psum_scatter(
            reduced[12].astype(jnp.bfloat16), "sp", scatter_dimension=0, tiled=True
        ).astype(jnp.float32),
    )
    query_sum, key_sum = lax.psum((gain_sums[0], gain_sums[1]), ("dp", "sp"))
    return (
        results,
        d_images,
        d_skips,
        d_texts,
        sums[0],
        sums[1],
        sums[2],
        sums[3],
        sums[4],
        sums[5],
        sums[6],
        sums[7],
        sums[8],
        sums[9],
        sums[10],
        sums[11],
        sums[12],
        query_sum,
        key_sum,
    )


def solution(mesh):
    in_specs = (
        P(None, ("dp", "sp"), None),
        P(None, ("dp", "sp"), None),
        P(None, ("dp", "sp"), None),
        P(None, "dp"),
        P(None, "dp", None),
        P(None, "dp", None),
        P("sp", "dp"),
        P("sp", "dp"),
        P("dp", None, "sp"),
        P("sp", "dp"),
        P("dp", "sp"),
        P("dp", None, "sp"),
        P("sp", "dp"),
        P("dp", "sp"),
        P("sp", "dp"),
        P(),
        P(),
        P(),
        P(),
        P(),
        P(),
        P(None, ("dp", "sp"), None),
    )
    out_specs = (
        P(None, ("dp", "sp"), None),
        P(None, ("dp", "sp"), None),
        P(None, ("dp", "sp"), None),
        P(None, ("dp", "sp"), None),
        P("sp", "dp"),
        P("sp", "dp"),
        P("dp", None, "sp"),
        P("sp", "dp"),
        P("dp", "sp"),
        P("dp", None, "sp"),
        P("sp", "dp"),
        P("dp", "sp"),
        P("sp", "dp"),
        P(("dp", "sp")),
        P(("dp", "sp")),
        P(("dp", "sp")),
        P(("dp", "sp")),
        P(),
        P(),
    )
    return jax.shard_map(
        on_device, mesh=mesh, in_specs=in_specs, out_specs=out_specs, check_vma=False
    )
```

profile of v0, /device:TPU:0, one launch (start us, length us, event | category | flops | bytes accessed | tf_op | source)
XLA Modules:
  0.0 4108.9 jit_solution(3676784421690250103)
XLA Ops:
  42.0 35.2 all-gather.22.cloned.1.call-done
  148.8 33.0 all-gather.46.cloned.1.call-done
  183.0 77.4 %all-gather.42.cloned.1.call-done = bf16[1408,1408]{0,1:T(8,128)(2,1)} async-done(((bf16[1408,352]{0,1:T(8,128)(2,1)}), bf16[1408,1408]{0,1:T(8,128)(2,1)}) %all-gather.42.cloned.1.call-update) | async-done | bytes 3964944 | tf_op jit(solution)/shard_map/all_gather | solution.py:214
  266.6 100.7 %all-gather.40.cloned.1.call-done = bf16[1024,2,1408]{0,1,2:T(2,128)(2,1)} async-done(((bf16[1024,2,352]{0,1,2:T(2,128)(2,1)}), bf16[1024,2,1408]{0,1,2:T(2,128)(2,1)}) %all-gather.40.cloned.1.call-update) | async-done | bytes 5767184 | tf_op jit(solution)/shard_map/all_gather | solution.py:215
  388.7 275.4 %all-gather.24.cloned.1.call-done = bf16[6144,1408]{0,1:T(8,128)(2,1)} async-done(((bf16[1536,1408]{0,1:T(8,128)(2,1)}), bf16[6144,1408]{0,1:T(8,128)(2,1)}) %all-gather.24.cloned.1.call-update) | async-done | bytes 17301520 | tf_op jit(solution)/shard_map/all_gather | solution.py:218
  685.1 57.2 %all-gather.30.cloned.1.call-done = bf16[1408,1408]{1,0:T(8,128)(2,1)} async-done(((bf16[352,1408]{1,0:T(8,128)(2,1)}), bf16[1408,1408]{1,0:T(8,128)(2,1)}) %all-gather.30.cloned.1.call-update) | async-done | bytes 3964944 | tf_op jit(solution)/shard_map/all_gather | solution.py:211
  742.2 77.6 %all-gather.36.cloned.1.call-done = bf16[1408,1408]{1,0:T(8,128)(2,1)} async-done(((bf16[352,1408]{1,0:T(8,128)(2,1)}), bf16[1408,1408]{1,0:T(8,128)(2,1)}) %all-gather.36.cloned.1.call-update) | async-done | bytes 3964944 | tf_op jit(solution)/shard_map/all_gather | solution.py:213
  819.8 77.2 %all-gather.44.cloned.1.call-done = bf16[1408,1408]{1,0:T(8,128)(2,1)} async-done(((bf16[352,1408]{1,0:T(8,128)(2,1)}), bf16[1408,1408]{1,0:T(8,128)(2,1)}) %all-gather.44.cloned.1.call-update) | async-done | bytes 3964944 | tf_op jit(solution)/shard_map/all_gather | solution.py:216
  897.0 142.2 %all-gather.28.cloned.1.call-done = bf16[2816,1408]{1,0:T(8,128)(2,1)} async-done(((bf16[704,1408]{1,0:T(8,128)(2,1)}), bf16[2816,1408]{1,0:T(8,128)(2,1)}) %all-gather.28.cloned.1.call-update) | async-done | bytes 7929872 | tf_op jit(solution)/shard_map/all_gather | solution.py:210
  1039.1 206.8 %all-gather.34.cloned.1.call-done = bf16[1408,3,1408]{0,2,1:T(8,128)(2,1)} async-done(((bf16[1408,3,352]{0,2,1:T(8,128)(2,1)}), bf16[1408,3,1408]{0,2,1:T(8,128)(2,1)}) %all-gather.34.cloned.1.call-update) | async-done | bytes 11894800 | tf_op jit(solution)/shard_map/all_gather | solution.py:212
  1245.9 296.6 %all-gather.48.cloned.1.call-done = bf16[1408,6144]{1,0:T(8,128)(2,1)} async-done(((bf16[1408,1536]{1,0:T(8,128)(2,1)}), bf16[1408,6144]{1,0:T(8,128)(2,1)}) %all-gather.48.cloned.1.call-update) | async-done | bytes 17301520 | tf_op jit(solution)/shard_map/all_gather | solution.py:217
  1542.5 1567.6 %while.131 = (s32[]{:T(128)}, f32[2816,1408]{1,0:T(8,128)}, f32[1408,1408]{1,0:T(8,128)}, f32[1408,3,1408]{2,0,1:T(8,128)}, f32[1408,1408]{1,0:T(8,128)}, /*inde...) while((s32[]{:T(128)}, f32[2816,1408]{1,0:T(8,128)}, ...), condition=%wide.region_43.44_spmd.clone.clone.clone.clone, body=%wide.region_0.43_spmd.clone.clone.clone.clone.sunk | while | flops 56759726080 | bytes 1653463808 | solution.py:398
  1638.2 72.4 %all-to-all-done = bf16[4,2,135168]{2,1,0:T(2,128)(2,1)} async-done(((bf16[4,2,135168]{2,1,0:T(2,128)(2,1)}), bf16[4,2,135168]{2,1,0:T(2,128)(2,1)}, u32[]{:S(2)}, u32[]{:S(2)}) %all-to-all-start) | async-done | bytes 2162720 | tf_op jit(solution)/shard_map/while/body/eval_jaxpr/all_to_all | solution.py:245
  1938.5 43.8 %fusion.388 = bf16[88,2816]{1,0:T(8,128)(2,1)S(1)} fusion(bf16[336,2816]{1,0:T(8,128)(2,1)} %pad_maximum_fusion.17), kind=kCustom, calls=%all-reduce-scatter.clone.1 | all-reduce-scatter fusion | flops 991233 | bytes 2388480 | tf_op jit(solution)/shard_map/while
  2048.1 39.6 while.133
  2395.1 71.6 %all-to-all-done = bf16[4,2,135168]{2,1,0:T(2,128)(2,1)} async-done(((bf16[4,2,135168]{2,1,0:T(2,128)(2,1)}), bf16[4,2,135168]{2,1,0:T(2,128)(2,1)}, u32[]{:S(2)}, u32[]{:S(2)}) %all-to-all-start) | async-done | bytes 2162720 | tf_op jit(solution)/shard_map/while/body/eval_jaxpr/all_to_all | solution.py:245
  2693.8 43.8 %fusion.388 = bf16[88,2816]{1,0:T(8,128)(2,1)S(1)} fusion(bf16[336,2816]{1,0:T(8,128)(2,1)} %pad_maximum_fusion.17), kind=kCustom, calls=%all-reduce-scatter.clone.1 | all-reduce-scatter fusion | flops 991233 | bytes 2388480 | tf_op jit(solution)/shard_map/while
  2744.1 26.9 select_add_fusion.26
  2778.9 28.5 select_add_fusion.27
  2837.6 39.6 while.133
  3232.1 46.8 %reduce-scatter.43.cloned.1.call-done = bf16[176,1408]{1,0:T(8,128)(2,1)} async-done(((bf16[1408,1408]{1,0:T(8,128)(2,1)}), bf16[176,1408]{1,0:T(8,128)(2,1)}) %reduce-scatter.43.cloned.1.call-update) | async-done | bytes 495632 | tf_op jit(solution)/shard_map/reduce_scatter | solution.py:416
  3281.2 53.3 %reduce-scatter.47.cloned.1.call-done = bf16[1408,176]{0,1:T(8,128)(2,1)} async-done(((bf16[1408,1408]{0,1:T(8,128)(2,1)}), bf16[1408,176]{0,1:T(8,128)(2,1)}) %reduce-scatter.47.cloned.1.call-update) | async-done | bytes 495632 | tf_op jit(solution)/shard_map/reduce_scatter | solution.py:422
  3336.7 60.3 %reduce-scatter.67.cloned.1.call-done = bf16[128,2816]{1,0:T(8,128)(2,1)} async-done(((bf16[1024,2816]{1,0:T(8,128)(2,1)}), bf16[128,2816]{1,0:T(8,128)(2,1)}) %reduce-scatter.67.cloned.1.call-update) | async-done | bytes 720912
  3399.3 70.8 %reduce-scatter.35.cloned.1.call-done = bf16[2816,176]{0,1:T(8,128)(2,1)} async-done(((bf16[2816,1408]{0,1:T(8,128)(2,1)}), bf16[2816,176]{0,1:T(8,128)(2,1)}) %reduce-scatter.35.cloned.1.call-update) | async-done | bytes 991248 | tf_op jit(solution)/shard_map/reduce_scatter | solution.py:404
  3472.6 90.8 %reduce-scatter.39.cloned.1.call-done = bf16[176,3,1408]{2,0,1:T(8,128)(2,1)} async-done(((bf16[1408,3,1408]{2,0,1:T(8,128)(2,1)}), bf16[176,3,1408]{2,0,1:T(8,128)(2,1)}) %reduce-scatter.39.cloned.1.call-update) | async-done | bytes 1486864 | tf_op jit(solution)/shard_map/reduce_scatter | solution.py:410
  3570.6 115.3 %reduce-scatter.49.cloned.1.call-done = bf16[176,6144]{1,0:T(8,128)(2,1)} async-done(((bf16[1408,6144]{1,0:T(8,128)(2,1)}), bf16[176,6144]{1,0:T(8,128)(2,1)}) %reduce-scatter.49.cloned.1.call-update) | async-done | bytes 2162704 | tf_op jit(solution)/shard_map/reduce_scatter | solution.py:425
  3686.1 122.1 %reduce-scatter.53.cloned.1.call-done = bf16[6144,176]{0,1:T(8,128)(2,1)} async-done(((bf16[6144,1408]{0,1:T(8,128)(2,1)}), bf16[6144,176]{0,1:T(8,128)(2,1)}) %reduce-scatter.53.cloned.1.call-update) | async-done | bytes 2162704 | tf_op jit(solution)/shard_map/reduce_scatter | solution.py:428
  3834.8 39.4 all-reduce.14
  3933.5 33.0 reduce-scatter.57.cloned.1.call-done
  3968.4 38.3 reduce-scatter.61.cloned.1.call-done
  4010.6 42.4 %reduce-scatter.51.cloned.1.call-done = bf16[176,1536]{1,0:T(8,128)(2,1)} async-done(((bf16[176,6144]{1,0:T(8,128)(2,1)}), bf16[176,1536]{1,0:T(8,128)(2,1)}) %reduce-scatter.51.cloned.1.call-update) | async-done | bytes 540688 | tf_op jit(solution)/shard_map/reduce_scatter | solution.py:466
  4055.1 44.6 %reduce-scatter.55.cloned.1.call-done = bf16[1536,176]{0,1:T(8,128)(2,1)} async-done(((bf16[6144,176]{0,1:T(8,128)(2,1)}), bf16[1536,176]{0,1:T(8,128)(2,1)}) %reduce-scatter.55.cloned.1.call-update) | async-done | bytes 540688 | tf_op jit(solution)/shard_map/reduce_scatter | solution.py:469
  (1284 shorter events, 1673.9 us)
Async XLA Ops:
  9.4 133.4 %all-gather.32.cloned.1.call-start = ((), (), s32[]{:S(2)}) async-start(), calls=%async_computation.27 | async-start | bytes 3649536 | tf_op jit(solution)/shard_map/all_gather | solution.py:190
  10.0 171.9 %all-gather.46.cloned.1.call-start = ((), (), s32[]{:S(2)}) async-start(), calls=%async_computation.34 | async-start | bytes 4866048 | tf_op jit(solution)/shard_map/all_gather | solution.py:195
  10.6 249.7 %all-gather.42.cloned.1.call-start = ((), (), s32[]{:S(2)}) async-start(), calls=%async_computation.32 | async-start | bytes 4956160 | tf_op jit(solution)/shard_map/all_gather | solution.py:214
  25.3 341.9 %all-gather.40.cloned.1.call-start = ((), (), s32[]{:S(2)}) async-start(), calls=%async_computation.31 | async-start | bytes 7208960 | tf_op jit(solution)/shard_map/all_gather | solution.py:215
  41.9 622.1 %all-gather.24.cloned.1.call-start = ((), (), s32[]{:S(2)}) async-start(), calls=%async_computation.23 | async-start | bytes 21626880 | tf_op jit(solution)/shard_map/all_gather | solution.py:218
  77.2 665.1 %all-gather.30.cloned.1.call-start = ((), (), s32[]{:S(2)}) async-start(), calls=%async_computation.26 | async-start | bytes 4956160 | tf_op jit(solution)/shard_map/all_gather | solution.py:211
  91.2 728.6 %all-gather.36.cloned.1.call-start = ((), (), s32[]{:S(2)}) async-start(), calls=%async_computation.29 | async-start | bytes 4956160 | tf_op jit(solution)/shard_map/all_gather | solution.py:213
  106.1 790.8 %all-gather.44.cloned.1.call-start = ((), (), s32[]{:S(2)}) async-start(), calls=%async_computation.33 | async-start | bytes 4956160 | tf_op jit(solution)/shard_map/all_gather | solution.py:216
  120.3 918.8 %all-gather.28.cloned.1.call-start = ((), (), s32[]{:S(2)}) async-start(), calls=%async_computation.25 | async-start | bytes 9912320 | tf_op jit(solution)/shard_map/all_gather | solution.py:210
  124.5 1121.4 %all-gather.34.cloned.1.call-start = ((), (), s32[]{:S(2)}) async-start(), calls=%async_computation.28 | async-start | bytes 14868480 | tf_op jit(solution)/shard_map/all_gather | solution.py:212
  148.8 1393.7 %all-gather.48.cloned.1.call-start = ((), (), s32[]{:S(2)}) async-start(), calls=%async_computation.35 | async-start | bytes 21626880 | tf_op jit(solution)/shard_map/all_gather | solution.py:217
  1628.8 170.4 %all-gather.50.cloned.1.call-start = ((), (), s32[]{:S(2)}) async-start(), calls=%async_computation.54 | async-start | bytes 2478080 | tf_op jit(solution)/shard_map/while/body/eval_jaxpr/all_gather | solution.py:265
  1983.1 157.6 %collective-permute-start = (bf16[12,2816]{1,0:T(8,128)(2,1)}, bf16[12,2816]{1,0:T(8,128)(2,1)}, u32[]{:S(2)}, u32[]{:S(2)}) collective-permute-start(bf16[12,2816]{1,0:T(8,128)(2,1)} %slice.309), channel_id=1, source_target_pairs={{0,1},{1,2},{2,3},{4,5},{5,6},{6,7},{8,9},{9,10},{10,11},{12,13},{... | collective-permute-start | bytes 202760 | tf_op jit(solution)/shard_map/while
  2385.7 169.6 %all-gather.50.cloned.1.call-start = ((), (), s32[]{:S(2)}) async-start(), calls=%async_computation.54 | async-start | bytes 2478080 | tf_op jit(solution)/shard_map/while/body/eval_jaxpr/all_gather | solution.py:265
  2682.7 140.3 %all-to-all-start.2 = ((bf16[4,2,45056]{2,1,0:T(2,128)(2,1)}), bf16[4,2,45056]{2,1,0:T(2,128)(2,1)}, u32[]{:S(2)}, u32[]{:S(2)}) async-start(bf16[4,2,45056]{2,1,0:T(2,128)(2,1)} %reshape.924), calls=%async_computation.2 | async-start | bytes 1441792 | tf_op jit(solution)/shard_map/while/body/eval_jaxpr/all_to_all | solution.py:306
  2738.4 191.8 %collective-permute-start = (bf16[12,2816]{1,0:T(8,128)(2,1)}, bf16[12,2816]{1,0:T(8,128)(2,1)}, u32[]{:S(2)}, u32[]{:S(2)}) collective-permute-start(bf16[12,2816]{1,0:T(8,128)(2,1)} %slice.309), channel_id=1, source_target_pairs={{0,1},{1,2},{2,3},{4,5},{5,6},{6,7},{8,9},{9,10},{10,11},{12,13},{... | collective-permute-start | bytes 202760 | tf_op jit(solution)/shard_map/while
  3124.5 154.4 %reduce-scatter.43.cloned.1.call-start = ((), (), s32[]{:S(2)}) async-start(), calls=%async_computation.40 | async-start | bytes 4460544 | tf_op jit(solution)/shard_map/reduce_scatter | solution.py:416
  3130.6 203.8 %reduce-scatter.47.cloned.1.call-start = ((), (), s32[]{:S(2)}) async-start(), calls=%async_computation.42 | async-start | bytes 4460544 | tf_op jit(solution)/shard_map/reduce_scatter | solution.py:422
  3137.9 259.1 %reduce-scatter.67.cloned.1.call-start = ((), (), s32[]{:S(2)}) async-start(), calls=%async_computation.52 | async-start | bytes 6488064
  3155.8 314.2 %reduce-scatter.35.cloned.1.call-start = ((), (), s32[]{:S(2)}) async-start(), calls=%async_computation.36 | async-start | bytes 8921088 | tf_op jit(solution)/shard_map/reduce_scatter | solution.py:404
  3168.7 394.6 %reduce-scatter.39.cloned.1.call-start = ((), (), s32[]{:S(2)}) async-start(), calls=%async_computation.38 | async-start | bytes 13381632 | tf_op jit(solution)/shard_map/reduce_scatter | solution.py:410
  3181.5 504.4 %reduce-scatter.49.cloned.1.call-start = ((), (), s32[]{:S(2)}) async-start(), calls=%async_computation.43 | async-start | bytes 19464192 | tf_op jit(solution)/shard_map/reduce_scatter | solution.py:425
  3201.1 607.0 %reduce-scatter.53.cloned.1.call-start = ((), (), s32[]{:S(2)}) async-start(), calls=%async_computation.45 | async-start | bytes 19464192 | tf_op jit(solution)/shard_map/reduce_scatter | solution.py:428
  3227.6 658.8 %reduce-scatter.59.cloned.1.call-start = ((), (), s32[]{:S(2)}) async-start(), calls=%async_computation.48 | async-start | bytes 901120
  3229.8 658.3 %reduce-scatter.63.cloned.1.call-start = ((), (), s32[]{:S(2)}) async-start(), calls=%async_computation.50 | async-start | bytes 901120
  3232.1 657.9 %reduce-scatter.65.cloned.1.call-start = ((), (), s32[]{:S(2)}) async-start(), calls=%async_computation.51 | async-start | bytes 901120
  3281.1 626.6 %reduce-scatter.69.cloned.1.call-start = ((), (), s32[]{:S(2)}) async-start(), calls=%async_computation.53 | async-start | bytes 901120
  3336.6 595.1 %reduce-scatter.45.cloned.1.call-start = ((), (), s32[]{:S(2)}) async-start(), calls=%async_computation.41 | async-start | bytes 901120 | tf_op jit(solution)/shard_map/reduce_scatter | solution.py:460
  3399.2 567.2 %reduce-scatter.57.cloned.1.call-start = ((), (), s32[]{:S(2)}) async-start(), calls=%async_computation.47 | async-start | bytes 1802240
  3472.6 534.2 %reduce-scatter.61.cloned.1.call-start = ((), (), s32[]{:S(2)}) async-start(), calls=%async_computation.49 | async-start | bytes 2252800
  3570.5 482.4 %reduce-scatter.51.cloned.1.call-start = ((), (), s32[]{:S(2)}) async-start(), calls=%async_computation.44 | async-start | bytes 2703360 | tf_op jit(solution)/shard_map/reduce_scatter | solution.py:466
  3686.0 413.7 %reduce-scatter.55.cloned.1.call-start = ((), (), s32[]{:S(2)}) async-start(), calls=%async_computation.46 | async-start | bytes 2703360 | tf_op jit(solution)/shard_map/reduce_scatter | solution.py:469
  (343 other events, 13770.6 us)
Sparse Core Ops, SparseCore 0:
  9.9 27.9 all-gather.37
  39.8 37.2 all-gather.21
  79.0 29.2 all-gather.25
  110.1 32.7 all-gather.31
  144.6 37.2 all-gather.45
  183.3 76.9 all-gather.41
  261.9 105.2 all-gather.39
  368.8 295.1 all-gather.23
  666.2 75.9 all-gather.29
  744.2 75.5 all-gather.35
  821.4 75.5 all-gather.43
  898.4 140.6 all-gather.27
  1040.7 205.1 all-gather.33
  1247.4 295.0 all-gather.47
  1637.0 72.7 all-gather.49
  2393.9 72.3 all-gather.49
  3117.4 50.7 reduce-scatter.36
  3172.0 51.7 reduce-scatter.40
  3227.2 51.6 reduce-scatter.42
  3282.7 51.7 reduce-scatter.46
  3337.9 59.0 reduce-scatter.66
  3401.0 69.0 reduce-scatter.34
  3473.6 89.6 reduce-scatter.38
  3567.3 118.5 reduce-scatter.48
  3689.6 118.5 reduce-scatter.52
  3811.0 22.7 reduce-scatter.58
  3861.4 21.9 reduce-scatter.64
  3885.7 21.9 reduce-scatter.68
  3934.2 32.2 reduce-scatter.56
  3968.9 37.7 reduce-scatter.60
  4008.9 44.0 reduce-scatter.50
  4055.4 44.2 reduce-scatter.54
  (2 shorter events, 43.4 us)
where the time goes:
time: 4120 us; the launch traced here: 4110 us
  waiting for transfers between devices  2360 us (57%)
  local copies, waits for them, and re-layouts  587 us (14%)
  matrix products  487 us (12%)
  other arithmetic  379 us (9%)
  blocking collectives  211 us (5%)
  starting transfers between devices  48.3 us (1%)
    all_gather x1, waiting for transfers between devices, on_device(): lax.all_gather(fc1_part, 'sp', axis=1, tiled=True)  297 us
    all_gather x1, waiting for transfers between devices, on_device(): lax.all_gather(fc2_part, 'sp', axis=0, tiled=True)  275 us
    all_gather x1, waiting for transfers between devices, on_device(): lax.all_gather(qkv_part, 'sp', axis=2, tiled=True)  207 us
    dot_general x16, matrix products, outer_sum(): lax.dot_general(left, right, (((0,), (0,)), ((), ())), preferred_element_...  191 us
    unnamed x39, waiting for transfers between devices  151 us
    all_to_all x2, waiting for transfers between devices, whole_path(): lax.all_to_all(split_heads(packed, parts), 'sp', split_axis=0, concat_axi...  144 us
    all_gather x1, waiting for transfers between devices, on_device(): lax.all_gather(skip_part, 'sp', axis=0, tiled=True)  142 us
    while x654, local copies, waits for them, and re-layouts  130 us
  transfers between devices with their start and end apart: 44, of which 32 were waited for; matrix products, arithmetic and copies ran while one was open for 21% of the time, Pallas kernels for 0%

commit v1 on v0

v1 whole, which is shorter than its diff:
```python
import math

import jax
import jax.numpy as jnp
from jax import lax
from jax.experimental import pallas as pl
from jax.experimental.pallas import tpu as pltpu
from jax.sharding import PartitionSpec as P

H = 16
HD = 88
HP = 96
CLIP_LEN = 77
ROWS = 256

EPS = 1e-06
MASKED = -1e30
LOG2E = 1.4426950408889634
BF = jnp.bfloat16
F32 = jnp.float32


def norm_parts(value):
    mean = jnp.mean(value, -1, keepdims=True)
    centre = value - mean
    scale = lax.rsqrt(jnp.mean(centre * centre, -1, keepdims=True) + EPS)
    return centre * scale, scale


def norm_rows(value, gain):
    return norm_parts(value)[0] * gain


def norm_back(value, gain, incoming):
    unit, scale = norm_parts(value)
    leading = incoming * gain
    inner = jnp.mean(leading * unit, -1, keepdims=True)
    back = scale * (leading - jnp.mean(leading, -1, keepdims=True) - unit * inner)
    return back, jnp.sum(incoming * unit, 0)


def time_embed(step, width):
    half = width // 2
    rate = jnp.exp(-math.log(10000.0) * jnp.arange(half, dtype=F32) / half)
    angle = step.astype(F32)[..., None] * rate
    return jnp.concatenate([jnp.cos(angle), jnp.sin(angle)], -1)


def mix(spec, left, right):
    return jnp.einsum(spec, left, right, preferred_element_type=F32)


def rope_tables(sequence, wide, local):
    place = jnp.arange(sequence, dtype=jnp.int32)[None, :, None]
    wide = wide[:, None, None]
    lane = jnp.arange(local * HP, dtype=jnp.int32)[None, None, :] % HP
    pair = lane // 2
    quarter = HD // 4
    upper = pair < quarter
    rank = jnp.where(upper, pair, pair - quarter).astype(F32)
    rate = jnp.exp(-math.log(10000.0) * rank / quarter)
    angle = jnp.where(upper, place // wide, place % wide).astype(F32) * rate
    sine = jnp.sin(angle)
    return jnp.cos(angle), jnp.where(lane % 2 == 0, -sine, sine)


def pad_heads(packed):
    rows, lanes = packed.shape
    groups = packed.reshape(rows, lanes // HD, HD)
    return jnp.pad(groups, ((0, 0), (0, 0), (0, HP - HD))).reshape(rows, -1)


def cut_heads(padded):
    rows, lanes = padded.shape
    return padded.reshape(rows, lanes // HP, HP)[:, :, :HD].reshape(rows, -1)


def head_masks(shape, local):
    lane = lax.broadcasted_iota(jnp.int32, shape, len(shape) - 1)
    inside = lane % HP < HD
    return [((lane // HP == h) & inside).astype(F32) for h in range(local)]


def head_mean(value, masks):
    total = None
    for mask in masks:
        term = (jnp.sum(value * mask, -1, keepdims=True) * (1.0 / HD)) * mask
        total = term if total is None else total + term
    return total


def head_unit(value, masks):
    centre = value - head_mean(value, masks)
    spread = None
    square = centre * centre
    for mask in masks:
        mean = jnp.sum(square * mask, -1, keepdims=True) * (1.0 / HD)
        term = lax.rsqrt(mean + EPS) * mask
        spread = term if spread is None else spread + term
    return centre * spread, spread


def turn_pairs(value):
    lanes = value.shape[-1]
    after = pltpu.roll(value, lanes - 1, 1)
    before = pltpu.roll(value, 1, 1)
    lane = lax.broadcasted_iota(jnp.int32, value.shape, 1)
    return jnp.where(lane % 2 == 0, after, before)


def dot_nt(left, right):
    return lax.dot_general(left, right, (((1,), (1,)), ((), ())), preferred_element_type=F32)


def dot_nn(left, right):
    return lax.dot_general(left, right, (((1,), (0,)), ((), ())), preferred_element_type=F32)


def dot_tn(left, right):
    return lax.dot_general(left, right, (((0,), (0,)), ((), ())), preferred_element_type=F32)


def self_forward(raw, counts, cosine, sine, gain_q, gain_k):
    parts, micros, slots, packed = raw.shape
    lanes = packed // 3
    local = lanes // HP
    sequence = parts * slots
    factor = HD ** (-0.5) * LOG2E

    def kernel(count_ref, raw_ref, cos_ref, sin_ref, gq_ref, gk_ref, out_ref, q_ref, k_ref, lse_ref):
        count = count_ref[pl.program_id(0)]
        blocks = (count + slots - 1) // slots
        out_ref[...] = jnp.zeros_like(out_ref)
        masks = head_masks((1, lanes), local)

        def prepare(part, carry):
            spot = pl.ds(pl.multiple_of(part * slots, slots), slots)
            cosine, sine = cos_ref[0, spot, :], sin_ref[0, spot, :]
            for index, gain_ref, dest in ((0, gq_ref, q_ref), (1, gk_ref, k_ref)):
                value = raw_ref[part, 0, :, index * lanes : (index + 1) * lanes].astype(F32)
                scaled = head_unit(value, masks)[0] * gain_ref[...]
                dest[0, spot, :] = (scaled * cosine + turn_pairs(scaled) * sine).astype(BF)
            return carry

        lax.fori_loop(0, parts, prepare, 0)
        column = lax.broadcasted_iota(jnp.int32, (1, sequence), 1)
        bias = jnp.where(column < count, 0.0, MASKED)
        for h in range(local):
            cut = slice(h * HP, (h + 1) * HP)
            keys = k_ref[0, :, cut]
            values = raw_ref[:, 0, :, 2 * lanes + h * HP : 2 * lanes + (h + 1) * HP].reshape(sequence, HP)

            def one_block(part, carry):
                spot = pl.ds(pl.multiple_of(part * slots, slots), slots)
                scores = dot_nt(q_ref[0, spot, cut], keys) + bias
                top = jnp.max(scores, -1, keepdims=True)
                raised = jnp.exp2((scores - top) * factor)
                total = jnp.sum(raised, -1, keepdims=True)
                result = dot_nn(raised.astype(BF), values) / total
                out_ref[part, 0, :, cut] = result.astype(BF)
                norm = jnp.broadcast_to(top * factor + jnp.log2(total), (slots, 128))
                lse_ref[0, h : h + 1, spot] = jnp.transpose(norm)[0:1, :]
                return carry

            lax.fori_loop(0, blocks, one_block, 0)

    whole = lambda m, c: (0, m, 0, 0)
    table = lambda m, c: (m, 0, 0)
    fixed = lambda m, c: (0, 0)
    return pl.pallas_call(
        kernel,
        name="self_forward",
        grid_spec=pltpu.PrefetchScalarGridSpec(
            num_scalar_prefetch=1,
            grid=(micros,),
            in_specs=[
                pl.BlockSpec((parts, 1, slots, packed), whole),
                pl.BlockSpec((1, sequence, lanes), table),
                pl.BlockSpec((1, sequence, lanes), table),
                pl.BlockSpec((1, lanes), fixed),
                pl.BlockSpec((1, lanes), fixed),
            ],
            out_specs=[
                pl.BlockSpec((parts, 1, slots, lanes), whole),
                pl.BlockSpec((1, sequence, lanes), table),
                pl.BlockSpec((1, sequence, lanes), table),
                pl.BlockSpec((1, local, sequence), table),
            ],
        ),
        out_shape=[
            jax.ShapeDtypeStruct((parts, micros, slots, lanes), BF),
            jax.ShapeDtypeStruct((micros, sequence, lanes), BF),
            jax.ShapeDtypeStruct((micros, sequence, lanes), BF),
            jax.ShapeDtypeStruct((micros, local, sequence), F32),
        ],
        compiler_params=pltpu.CompilerParams(vmem_limit_bytes=48 << 20),
        cost_estimate=pl.CostEstimate(
            flops=4 * micros * local * sequence * sequence * HP,
            bytes_accessed=2 * micros * sequence * lanes * 10,
            transcendentals=micros * local * sequence * sequence,
        ),
    )(counts, raw, cosine, sine, gain_q, gain_k)


def self_backward(raw, counts, cosine, sine, gain_q, gain_k, turned_q, turned_k, norms, incoming):
    parts, micros, slots, packed = raw.shape
    lanes = packed // 3
    local = lanes // HP
    sequence = parts * slots
    scale = HD ** (-0.5)
    factor = scale * LOG2E

    def kernel(
        count_ref,
        raw_ref,
        cos_ref,
        sin_ref,
        gq_ref,
        gk_ref,
        q_ref,
        k_ref,
        lse_ref,
        in_ref,
        out_ref,
        dgq_ref,
        dgk_ref,
        dq_s,
        dk_s,
        dv_s,
    ):
        count = count_ref[pl.program_id(0)]
        blocks = (count + slots - 1) // slots
        dq_s[...] = jnp.zeros_like(dq_s)
        dk_s[...] = jnp.zeros_like(dk_s)
        dv_s[...] = jnp.zeros_like(dv_s)
        row = lax.broadcasted_iota(jnp.int32, (sequence, 1), 0)
        bias = jnp.where(row < count, 0.0, MASKED)
        for h in range(local):
            cut = slice(h * HP, (h + 1) * HP)
            keys = k_ref[0, :, cut]
            values = raw_ref[:, 0, :, 2 * lanes + h * HP : 2 * lanes + (h + 1) * HP].reshape(sequence, HP)

            def one_block(part, carry):
                spot = pl.ds(pl.multiple_of(part * slots, slots), slots)
                rows = q_ref[0, spot, cut]
                grads = in_ref[part, 0, :, cut]
                norm = lse_ref[0, h : h + 1, spot]
                probs = jnp.exp2(dot_nt(keys, rows) * factor + bias - norm)
                d_probs = dot_nt(values, grads)
                inner = jnp.sum(probs * d_probs, 0, keepdims=True)
                d_scores = (probs * (d_probs - inner)).astype(BF)
                dv_s[:, cut] += dot_nn(probs.astype(BF), grads)
                dk_s[:, cut] += dot_nn(d_scores, rows)
                dq_s[spot, cut] = dot_tn(d_scores, keys)
                return carry

            lax.fori_loop(0, blocks, one_block, 0)
        masks = head_masks((1, lanes), local)

        def finish(part, carry):
            spot = pl.ds(pl.multiple_of(part * slots, slots), slots)
            cosine, sine = cos_ref[0, spot, :], sin_ref[0, spot, :]
            sums = []
            for index, gain_ref, source in ((0, gq_ref, dq_s), (1, gk_ref, dk_s)):
                grad = source[spot, :] * scale
                grad = grad * cosine - turn_pairs(grad) * sine
                value = raw_ref[part, 0, :, index * lanes : (index + 1) * lanes].astype(F32)
                unit, spread = head_unit(value, masks)
                leading = grad * gain_ref[...]
                back = leading - head_mean(leading, masks) - unit * head_mean(leading * unit, masks)
                out_ref[part, 0, :, index * lanes : (index + 1) * lanes] = (spread * back).astype(BF)
                sums.append(carry[index] + jnp.sum(grad * unit, 0, keepdims=True))
            out_ref[part, 0, :, 2 * lanes : 3 * lanes] = dv_s[spot, :].astype(BF)
            return tuple(sums)

        zero = jnp.zeros((1, lanes), F32)
        d_gains = lax.fori_loop(0, parts, finish, (zero, zero))
        dgq_ref[0] = d_gains[0]
        dgk_ref[0] = d_gains[1]

    whole = lambda m, c: (0, m, 0, 0)
    table = lambda m, c: (m, 0, 0)
    fixed = lambda m, c: (0, 0)
    return pl.pallas_call(
        kernel,
        name="self_backward",
        grid_spec=pltpu.PrefetchScalarGridSpec(
            num_scalar_prefetch=1,
            grid=(micros,),
            in_specs=[
                pl.BlockSpec((parts, 1, slots, packed), whole),
                pl.BlockSpec((1, sequence, lanes), table),
                pl.BlockSpec((1, sequence, lanes), table),
                pl.BlockSpec((1, lanes), fixed),
                pl.BlockSpec((1, lanes), fixed),
                pl.BlockSpec((1, sequence, lanes), table),
                pl.BlockSpec((1, sequence, lanes), table),
                pl.BlockSpec((1, local, sequence), table),
                pl.BlockSpec((parts, 1, slots, lanes), whole),
            ],
            out_specs=[
                pl.BlockSpec((parts, 1, slots, packed), whole),
                pl.BlockSpec((1, 1, lanes), table),
                pl.BlockSpec((1, 1, lanes), table),
            ],
            scratch_shapes=[pltpu.VMEM((sequence, lanes), F32) for index in range(3)],
        ),
        out_shape=[
            jax.ShapeDtypeStruct((parts, micros, slots, packed), BF),
            jax.ShapeDtypeStruct((micros, 1, lanes), F32),
            jax.ShapeDtypeStruct((micros, 1, lanes), F32),
        ],
        compiler_params=pltpu.CompilerParams(vmem_limit_bytes=48 << 20),
        cost_estimate=pl.CostEstimate(
            flops=10 * micros * local * sequence * sequence * HP,
            bytes_accessed=2 * micros * sequence * lanes * 14,
            transcendentals=micros * local * sequence * sequence,
        ),
    )(counts, raw, cosine, sine, gain_q, gain_k, turned_q, turned_k, norms, incoming)


def text_bias(lengths_ref, micro, words, axis):
    place = lax.broadcasted_iota(jnp.int32, (1, words) if axis else (words, 1), axis)
    live = (place < lengths_ref[micro, 0]) | (
        (place >= CLIP_LEN) & (place < CLIP_LEN + lengths_ref[micro, 1])
    )
    return jnp.where(live, 0.0, MASKED)


def cross_forward(query, text_kv, lengths):
    parts, micros, slots, lanes = query.shape
    words = text_kv.shape[2]
    local = lanes // HP
    factor = HD ** (-0.5) * LOG2E

    def kernel(len_ref, q_ref, kv_ref, out_ref):
        bias = text_bias(len_ref, pl.program_id(1), words, 1)
        for h in range(local):
            cut = slice(h * HP, (h + 1) * HP)
            scores = dot_nt(q_ref[0, 0, :, cut], kv_ref[0, 0, :, cut]) + bias
            top = jnp.max(scores, -1, keepdims=True)
            raised = jnp.exp2((scores - top) * factor)
            total = jnp.sum(raised, -1, keepdims=True)
            values = kv_ref[0, 0, :, lanes + h * HP : lanes + (h + 1) * HP]
            out_ref[0, 0, :, cut] = (dot_nn(raised.astype(BF), values) / total).astype(BF)

    spot = lambda p, m, c: (p, m, 0, 0)
    return pl.pallas_call(
        kernel,
        name="cross_forward",
        grid_spec=pltpu.PrefetchScalarGridSpec(
            num_scalar_prefetch=1,
            grid=(parts, micros),
            in_specs=[
                pl.BlockSpec((1, 1, slots, lanes), spot),
                pl.BlockSpec((1, 1, words, 2 * lanes), spot),
            ],
            out_specs=pl.BlockSpec((1, 1, slots, lanes), spot),
        ),
        out_shape=jax.ShapeDtypeStruct(query.shape, BF),
        compiler_params=pltpu.CompilerParams(vmem_limit_bytes=32 << 20),
        cost_estimate=pl.CostEstimate(
            flops=4 * parts * micros * slots * words * lanes,
            bytes_accessed=4 * parts * micros * (slots + words) * lanes,
            transcendentals=parts * micros * local * slots * words,
        ),
    )(lengths, query, text_kv)


def cross_backward(query, text_kv, lengths, incoming):
    parts, micros, slots, lanes = query.shape
    words = text_kv.shape[2]
    local = lanes // HP
    scale = HD ** (-0.5)
    factor = scale * LOG2E

    def kernel(len_ref, q_ref, kv_ref, in_ref, dq_ref, dkv_ref):
        bias = text_bias(len_ref, pl.program_id(1), words, 0)
        for h in range(local):
            cut = slice(h * HP, (h + 1) * HP)
            far = slice(lanes + h * HP, lanes + (h + 1) * HP)
            rows = q_ref[0, 0, :, cut]
            keys = kv_ref[0, 0, :, cut]
            grads = in_ref[0, 0, :, cut]
            scores = dot_nt(keys, rows) + bias
            top = jnp.max(scores, 0, keepdims=True)
            raised = jnp.exp2((scores - top) * factor)
            probs = raised * (1.0 / jnp.sum(raised, 0, keepdims=True))
            d_probs = dot_nt(kv_ref[0, 0, :, far], grads)
            inner = jnp.sum(probs * d_probs, 0, keepdims=True)
            d_scores = (probs * (d_probs - inner)).astype(BF)
            dkv_ref[0, 0, :, far] = dot_nn(probs.astype(BF), grads).astype(BF)
            dkv_ref[0, 0, :, cut] = (dot_nn(d_scores, rows) * scale).astype(BF)
            dq_ref[0, 0, :, cut] = (dot_tn(d_scores, keys) * scale).astype(BF)

    spot = lambda p, m, c: (p, m, 0, 0)
    return pl.pallas_call(
        kernel,
        name="cross_backward",
        grid_spec=pltpu.PrefetchScalarGridSpec(
            num_scalar_prefetch=1,
            grid=(parts, micros),
            in_specs=[
                pl.BlockSpec((1, 1, slots, lanes), spot),
                pl.BlockSpec((1, 1, words, 2 * lanes), spot),
                pl.BlockSpec((1, 1, slots, lanes), spot),
            ],
            out_specs=[
                pl.BlockSpec((1, 1, slots, lanes), spot),
                pl.BlockSpec((1, 1, words, 2 * lanes), spot),
            ],
        ),
        out_shape=[
            jax.ShapeDtypeStruct(query.shape, BF),
            jax.ShapeDtypeStruct(text_kv.shape, BF),
        ],
        compiler_params=pltpu.CompilerParams(vmem_limit_bytes=32 << 20),
        cost_estimate=pl.CostEstimate(
            flops=10 * parts * micros * slots * words * lanes,
            bytes_accessed=8 * parts * micros * (slots + words) * lanes,
            transcendentals=parts * micros * local * slots * words,
        ),
    )(lengths, query, text_kv, incoming)


class Cube:
    def __init__(self):
        self.size = lax.axis_size("dp")
        self.bits = self.size.bit_length() - 1
        self.rank = lax.axis_index("dp")

    def swap(self, value, bit):
        pairs = [(i, i ^ (1 << bit)) for i in range(self.size)]
        return lax.ppermute(value, "dp", pairs)

    def order(self, flip):
        outer = list(range(1, self.bits))
        return outer[::-1] if flip else outer

    def position(self):
        places = []
        for place in range(self.size):
            mask = 0
            for bit in range(self.bits):
                weight = self.bits - 1 if bit == 0 else bit - 1
                mask |= ((place >> weight) & 1) << bit
            places.append(mask)
        return places

    def owners(self):
        return self.rank ^ jnp.array(self.position(), jnp.int32)

    def gather(self, shard, flip):
        held = [(0, shard)]
        for bit in self.order(flip):
            held = held + [(mask | (1 << bit), self.swap(piece, bit)) for mask, piece in held]
        held = sorted(held, key=lambda item: self.position().index(item[0]))
        near = jnp.concatenate([piece for mask, piece in held], 1)
        return jnp.concatenate([near, self.swap(near, 0)], 1)

    def scatter(self, near, far, flip):
        held = (near + self.swap(far, 0).astype(F32)).astype(BF)
        parts, rows, lanes = held.shape
        outer = self.bits - 1
        held = held.reshape((parts,) + (2,) * outer + (rows >> outer, lanes))
        axes = list(range(outer, 0, -1))
        for bit in self.order(flip)[::-1]:
            axis = 1 + axes.index(bit)
            keep = lax.index_in_dim(held, 0, axis, keepdims=False)
            send = lax.index_in_dim(held, 1, axis, keepdims=False)
            held = (keep.astype(F32) + self.swap(send, bit).astype(F32)).astype(BF)
            axes.remove(bit)
        return held


def on_device(
    tokens,
    skip_tokens,
    text,
    timestep,
    grid,
    text_len,
    w_skip,
    w_mod,
    w_qkv,
    w_out1,
    w_query2,
    w_text_kv,
    w_out2,
    w_fc1,
    w_fc2,
    gain_skip,
    gain_attn,
    gain_cross,
    gain_mlp,
    gain_query,
    gain_key,
    cotangent,
):
    micros, slots, width = tokens.shape
    parts = lax.axis_size("sp")
    zone = lax.axis_index("sp")
    cube = Cube()
    ranks = cube.size
    owners = cube.owners()
    rows = micros * slots
    sequence = slots * parts
    local = H // parts
    lanes = local * HP
    text_slots = text.shape[1]
    words = text_slots * parts
    features = text.shape[2]
    strip = width // ranks

    def spread(shard):
        return lax.all_gather(shard, "sp", axis=0, tiled=False)

    def weight(shard, flip):
        return cube.gather(spread(shard), flip)

    half = w_skip.shape[0]
    skip_w = weight(w_skip.T, 0)
    qkv_w = weight(pad_heads(w_qkv.reshape(strip, -1)), 1)
    out1_w = weight(pad_heads(w_out1.T), 0)
    query2_w = weight(pad_heads(w_query2), 1)
    text_w = weight(pad_heads(w_text_kv.reshape(w_text_kv.shape[0], -1)), 0)
    out2_w = weight(pad_heads(w_out2.T), 1)
    fc1_w = weight(w_fc1, 0)
    fc2_w = weight(w_fc2.T, 1)

    def own_order(vector):
        return vector.reshape(ranks, -1)[owners].reshape(-1)

    def shuffle(count):
        block = count // ranks
        place = jnp.arange(count, dtype=jnp.int32)
        source = owners[place // block] * block + place % block
        return (place[:, None] == source[None, :]).astype(BF)

    turn = shuffle(width)
    text_turn = shuffle(features)
    g_skip, g_attn, g_cross, g_mlp = (
        own_order(gain) for gain in (gain_skip, gain_attn, gain_cross, gain_mlp)
    )

    wide = grid[:, 0, 1]
    counts = grid[:, 0, 0] * wide
    lengths = text_len[:, 0, :]
    place = zone * slots + jnp.arange(slots, dtype=jnp.int32)
    live = (place[None, :] < counts[:, None]).astype(F32).reshape(rows, 1)
    cosine, sine = rope_tables(sequence, wide, local)
    gain_q = pad_heads(jnp.tile(gain_query, local)[None, :])
    gain_k = pad_heads(jnp.tile(gain_key, local)[None, :])

    steps = lax.all_gather(timestep[:, 0], "dp", axis=0, tiled=False)
    time_act = jax.nn.silu(time_embed(steps, width)).astype(BF).reshape(ranks * micros, parts, -1)
    time_part = lax.dynamic_index_in_dim(time_act, zone, 1, keepdims=False)
    shift_part = jnp.dot(time_part, w_mod, preferred_element_type=F32)
    shift_own = lax.all_to_all(
        shift_part.reshape(ranks, micros, strip), "dp", split_axis=0, concat_axis=0, tiled=True
    )
    shift_own = lax.psum(shift_own, "sp")
    shift = jnp.transpose(shift_own[owners], (1, 0, 2)).reshape(micros, width)

    text_own = jnp.dot(text.reshape(-1, features), text_turn, preferred_element_type=F32).astype(BF)
    text_all = lax.all_gather(text_own.reshape(micros, text_slots, features), "sp", axis=1, tiled=True)
    text_all = text_all.reshape(micros * words, features)

    joined = jnp.stack([tokens, skip_tokens]).reshape(2, rows, parts // 2, half)
    joined = jnp.transpose(joined, (0, 2, 1, 3)).reshape(parts, rows, half)
    base = mix("pmk,pnk->mn", joined, skip_w)
    stream = norm_rows(base, g_skip)
    pre_attn = norm_rows(stream, g_attn).reshape(micros, slots, width) + shift[:, None, :]
    pre_attn = pre_attn.reshape(rows, width).astype(BF)
    projected = mix("mk,pkn->pmn", pre_attn, qkv_w).astype(BF)

    def exchange(value):
        return lax.all_to_all(value, "sp", split_axis=0, concat_axis=0, tiled=True)

    raw = exchange(projected.reshape(parts, micros, slots, 3 * lanes))
    attended, turned_q, turned_k, norms = self_forward(raw, counts, cosine, sine, gain_q, gain_k)
    attended = exchange(attended).reshape(parts, rows, lanes)
    stream1 = stream + mix("pmk,pnk->mn", attended, out1_w)
    pre_cross = norm_rows(stream1, g_cross).astype(BF)
    query2 = mix("mk,pkn->pmn", pre_cross, query2_w).astype(BF)
    query2 = query2.reshape(parts, micros, slots, lanes)
    text_kv = mix("mk,pkn->pmn", text_all, text_w).astype(BF)
    text_kv = text_kv.reshape(parts, micros, words, 2 * lanes)
    crossed = cross_forward(query2, text_kv, lengths).reshape(parts, rows, lanes)
    stream2 = stream1 + mix("pmk,pnk->mn", crossed, out2_w)
    pre_mlp = norm_rows(stream2, g_mlp).astype(BF)
    hidden = mix("mk,pkn->pmn", pre_mlp, fc1_w)
    activ = jax.nn.gelu(hidden, approximate=True).astype(BF)
    stream3 = stream2 + mix("pmk,pnk->mn", activ, fc2_w)
    result = jnp.dot((stream3 * live).astype(BF), turn.T, preferred_element_type=F32).astype(BF)

    def term(left, right, flip):
        cut = left.shape[1] // 2
        near = mix("md,pmn->pdn", left[:, :cut], right)
        far = mix("md,pmn->pdn", left[:, cut:], right).astype(BF)
        held = cube.scatter(near, far, flip)
        return lax.psum_scatter(held, "sp", scatter_dimension=0, tiled=False).astype(F32)

    grad3 = jnp.dot(cotangent.reshape(rows, width), turn, preferred_element_type=F32) * live
    d_mlp = grad3.astype(BF)
    term_fc2 = term(d_mlp, activ, 1)
    d_activ = mix("mn,pnk->pmk", d_mlp, fc2_w)
    unused, gelu_pull = jax.vjp(lambda value: jax.nn.gelu(value, approximate=True), hidden)
    d_hidden = gelu_pull(d_activ)[0].astype(BF)
    term_fc1 = term(pre_mlp, d_hidden, 0)
    d_stream2, d_gain_mlp = norm_back(stream2, g_mlp, mix("pmn,pkn->mk", d_hidden, fc1_w))
    grad2 = grad3 + d_stream2
    d_cross = grad2.astype(BF)
    term_out2 = term(d_cross, crossed, 1)
    d_crossed = mix("mn,pnk->pmk", d_cross, out2_w).astype(BF)
    d_query2, d_text_kv = cross_backward(
        query2, text_kv, lengths, d_crossed.reshape(parts, micros, slots, lanes)
    )
    d_query2 = d_query2.reshape(parts, rows, lanes)
    d_text_kv = d_text_kv.reshape(parts, micros * words, 2 * lanes)
    term_text = term(text_all, d_text_kv, 0)
    d_words = mix("pmn,pkn->mk", d_text_kv, text_w).astype(BF)
    d_words = lax.psum_scatter(
        d_words.reshape(micros, words, features), "sp", scatter_dimension=1, tiled=True
    )
    d_words = jnp.dot(d_words.reshape(-1, features), text_turn.T, preferred_element_type=F32)
    term_query2 = term(pre_cross, d_query2, 1)
    d_stream1, d_gain_cross = norm_back(stream1, g_cross, mix("pmn,pkn->mk", d_query2, query2_w))
    grad1 = grad2 + d_stream1
    d_attn = grad1.astype(BF)
    term_out1 = term(d_attn, attended, 0)
    d_attended = mix("mn,pnk->pmk", d_attn, out1_w).astype(BF)
    d_heads = exchange(d_attended.reshape(parts, micros, slots, lanes))
    d_raw, d_gain_q, d_gain_k = self_backward(
        raw, counts, cosine, sine, gain_q, gain_k, turned_q, turned_k, norms, d_heads
    )
    d_projected = exchange(d_raw).reshape(parts, rows, 3 * lanes)
    term_qkv = term(pre_attn, d_projected, 1)
    d_pre = mix("pmn,pkn->mk", d_projected, qkv_w)
    d_shift = jnp.sum(d_pre.reshape(micros, slots, width), 1)
    d_stream0, d_gain_attn = norm_back(stream, g_attn, d_pre)
    d_base, d_gain_skip = norm_back(base, g_skip, grad1 + d_stream0)
    d_base = d_base.astype(BF)
    term_skip = term(d_base, joined, 0)
    d_joined = mix("mn,pnk->pmk", d_base, skip_w).reshape(2, parts // 2, rows, half)
    d_joined = jnp.transpose(d_joined, (0, 2, 1, 3)).reshape(2, micros, slots, width)

    back = jnp.argsort(owners)
    d_shift = jnp.transpose(d_shift.reshape(micros, ranks, strip), (1, 0, 2))[back]
    d_shift = lax.all_to_all(d_shift, "dp", split_axis=0, concat_axis=0, tiled=True)
    d_shift = lax.psum(d_shift, "sp").reshape(ranks * micros, strip)
    term_mod = lax.dot_general(
        time_part.astype(F32), d_shift, (((0,), (0,)), ((), ())), precision=lax.Precision.HIGHEST
    )

    gains = jnp.stack([d_gain_skip, d_gain_attn, d_gain_cross, d_gain_mlp])
    gains = gains.reshape(4, ranks, strip)[:, back].reshape(4, width)
    heads = jnp.stack([jnp.sum(d_gain_q, (0, 1)), jnp.sum(d_gain_k, (0, 1))])
    heads = jnp.sum(heads.reshape(2, local, HP)[:, :, :HD], 1)
    packed = jnp.concatenate([gains.reshape(-1), heads.reshape(-1)])
    packed = lax.psum(packed, ("dp", "sp"))
    gains = packed[: 4 * width].reshape(4, ranks * parts, -1)
    gains = lax.dynamic_index_in_dim(gains, cube.rank * parts + zone, 1, keepdims=False)
    heads = packed[4 * width :].reshape(2, HD)

    def whole(term, groups):
        return cut_heads(term).reshape(term.shape[0], groups, -1)

    return (
        result.reshape(tokens.shape),
        d_joined[0],
        d_joined[1],
        d_words.reshape(text.shape),
        term_skip.T,
        term_mod,
        whole(term_qkv, 3),
        cut_heads(term_out1).T,
        cut_heads(term_query2),
        whole(term_text, 2),
        cut_heads(term_out2).T,
        term_fc1,
        term_fc2.T,
        gains[0],
        gains[1],
        gains[2],
        gains[3],
        heads[0],
        heads[1],
    )


def solution(mesh):
    rows = P(None, ("dp", "sp"), None)
    column = P("sp", "dp")
    row = P("dp", "sp")
    grouped = P("dp", None, "sp")
    in_specs = (
        (rows, rows, rows, P(None, "dp"), P(None, "dp", None), P(None, "dp", None))
        + (column, column, grouped, column, row, grouped, column, row, column)
        + (P(),) * 6
        + (rows,)
    )
    out_specs = (
        (rows, rows, rows, rows)
        + (column, column, grouped, column, row, grouped, column, row, column)
        + (P(("dp", "sp")),) * 4
        + (P(), P())
    )
    return jax.shard_map(
        on_device, mesh=mesh, in_specs=in_specs, out_specs=out_specs, check_vma=False
    )
```

time: 4120 us -> 1810 us (0.44)
  waiting for transfers between devices: 2360 us -> 467 us
  local copies, waits for them, and re-layouts: 587 us -> 303 us
  other arithmetic: 379 us -> 133 us
  matrix products: 487 us -> 287 us
  blocking collectives: 211 us -> 341 us
  Pallas kernels: 0 us -> 120 us
  starting transfers between devices: 48.3 us -> 122 us
    all_gather x16 -> x4, waiting for transfers between devices: 1410 us -> 40.4 us  [the longest x3 40.4 us: spread(): return lax.all_gather(shard, 'sp', axis=0, tiled=False)]
    reduce_scatter x11 -> x8, waiting for transfers between devices: 608 us -> 0.01 us  [term(): lax.psum_scatter(held, 'sp', scatter_dimension=0, tiled=False).astype(F32)]
    ppermute x0 -> x56, waiting for transfers between devices: none -> 424 us  [swap(): return lax.ppermute(value, 'dp', pairs)]
    while x670 -> x0, local copies, waits for them, and re-layouts: 221 us -> none
    dot_general x90 -> x38, matrix products: 487 us -> 287 us  [the longest x32 275 us: mix(): return jnp.einsum(spec, left, right, preferred_element_type=F32)]
    all_to_all x8 -> x6, waiting for transfers between devices: 188 us -> 0.92 us  [the longest x4 0.92 us: exchange(): return lax.all_to_all(value, 'sp', split_axis=0, concat_axis=0, tiled=True)]
    all_to_all x16 -> x0, other arithmetic: 169 us -> none  [the longest x4 63.4 us: whole_path(): lax.all_to_all(split_heads(packed, parts), 'sp', split_axis=0, concat_axi...]
    unnamed x39 -> x14, waiting for transfers between devices: 151 us -> 1.58 us
  transfers between devices with their start and end apart: 44 -> 75, of which waited for: 32 -> 21; matrix products, arithmetic and copies ran while one was open for 21% -> 33% of each run, Pallas kernels for 0% -> 5%
where the time goes in v1:
time: 1810 us; the launch traced here: 1790 us
  waiting for transfers between devices  467 us (26%)
  blocking collectives  341 us (19%)
  local copies, waits for them, and re-layouts  303 us (17%)
  matrix products  287 us (16%)
  other arithmetic  133 us (7%)
  starting transfers between devices  122 us (7%)
  Pallas kernels  120 us (7%)
    ppermute x56, waiting for transfers between devices, swap(): return lax.ppermute(value, 'dp', pairs)  424 us
    dot_general x32, matrix products, mix(): return jnp.einsum(spec, left, right, preferred_element_type=F32)  275 us
    all_gather x5, blocking collectives, spread(): return lax.all_gather(shard, 'sp', axis=0, tiled=False)  197 us
    ppermute x56, starting transfers between devices, swap(): return lax.ppermute(value, 'dp', pairs)  92.2 us
    unnamed x274, local copies, waits for them, and re-layouts  84.4 us
    concatenate x8, local copies, waits for them, and re-layouts, gather(): return jnp.concatenate([near, self.swap(near, 0)], 1)  79.6 us
    unnamed x1, blocking collectives  65.1 us
    pallas_call x1, Pallas kernels, self_backward(): pl.pallas_call(kernel, name='self_backward', grid_spec=pltpu.PrefetchScal...  50.9 us
  transfers between devices with their start and end apart: 75, of which 21 were waited for; matrix products, arithmetic and copies ran while one was open for 33% of the time, Pallas kernels for 5%

profile of v1, /device:TPU:0, one launch (start us, length us, event | category | flops | bytes accessed | tf_op | source)
XLA Modules:
  0.0 1790.3 jit_solution(15476494145174557768)
XLA Ops:
  10.5 40.4 %all-gather.9.cloned.1.call-done = bf16[4,176,1152]{2,1,0:T(8,128)(2,1)} async-done(((bf16[1,176,1152]{2,1,0:T(8,128)(2,1)}), bf16[4,176,1152]{2,1,0:T(8,128)(2,1)}) %all-gather.9.cloned.1.call-update) | async-done | bytes 1622032 | tf_op jit(solution)/shard_map/all_gather | solution.py:516
  52.3 33.0 %all-gather = bf16[704,704]{1,0:T(8,128)(2,1)} all-gather(bf16[176,704]{1,0:T(8,128)(2,1)S(1)} %bitcast.533), channel_id=2, replica_groups=mesh['dp'=8,'sp'=4] {'sp'}, dimensions={0}, use_global_device_ids=true | all-gather | bytes 1239040 | tf_op jit(solution)/shard_map/all_gather | solution.py:516
  86.8 22.6 %collective-permute-done = bf16[4,176,704]{2,1,0:T(8,128)(2,1)} collective-permute-done((bf16[4,176,704]{2,1,0:T(8,128)(2,1)}, bf16[4,176,704]{2,1,0:T(8,128)(2,1)}, u32[]{:S(2)}, u32[]{:S(2)}) %collective-permute-start) | collective-permute-done | bytes 991264 | tf_op jit(solution)/shard_map/ppermute | solution.py:434
  112.8 65.1 %all-reduce.7 = s32[16]{0:T(128)S(1)} all-reduce(s32[16]{0:T(128)S(1)} %bitcast_dynamic-update-slice_fusion), channel_id=3, replica_groups=mesh['dp'=8,'sp'=4] {'dp'}, use_global_device_ids=true, to_apply=%add.7 | all-reduce | flops 16 | bytes 128
  210.7 23.8 %all_gather.43 = bf16[4,176,384]{2,1,0:T(8,128)(2,1)S(1)} all-gather(bf16[1,176,384]{2,1,0:T(8,128)(2,1)S(1)} %copy-done.71), channel_id=1, replica_groups=mesh['dp'=8,'sp'=4] {'sp'}, dimensions={0}, use_global_device_ids=true | all-gather | bytes 675840 | tf_op jit(solution)/shard_map/all_gather | solution.py:516
  265.2 16.4 all_gather.44
  287.7 19.9 %psum.21 = f32[8,2,176]{2,1,0:T(2,128)S(1)} all-reduce(f32[8,2,176]{2,1,0:T(2,128)S(1)} %all-to-all-done), channel_id=1, replica_groups=mesh['dp'=8,'sp'=4] {'sp'}, use_global_device_ids=true, to_apply=%region_4.5 | all-reduce | flops 2816 | bytes 22528 | tf_op jit(solution)/shard_map/psum | solution.py:562
  321.8 15.3 concatenate.68
  361.8 45.9 %collective-permute-done.24 = bf16[4,176,1536]{2,1,0:T(8,128)(2,1)} collective-permute-done((bf16[4,176,1536]{2,1,0:T(8,128)(2,1)}, bf16[4,176,1536]{2,1,0:T(8,128)(2,1)}, u32[]{:S(2)}, u32[]{:S(2)}) %collective-permute-start.24) | collective-permute-done | bytes 2162720 | tf_op jit(solution)/shard_map/ppermute | solution.py:434
  408.2 36.3 %collective-permute-done.30 = bf16[4,176,1536]{2,1,0:T(8,128)(2,1)} collective-permute-done((bf16[4,176,1536]{2,1,0:T(8,128)(2,1)}, bf16[4,176,1536]{2,1,0:T(8,128)(2,1)}, u32[]{:S(2)}, u32[]{:S(2)}) %collective-permute-start.30) | collective-permute-done | bytes 2162720 | tf_op jit(solution)/shard_map/ppermute | solution.py:434
  501.0 107.2 %all_gather.45 = bf16[4,128,768]{2,1,0:T(8,128)(2,1)S(1)} all-gather(bf16[1,128,768]{2,1,0:T(8,128)(2,1)S(1)} %copy.429), channel_id=1, replica_groups=mesh['dp'=8,'sp'=4] {'sp'}, dimensions={0}, use_global_device_ids=true | all-gather | bytes 983040 | tf_op jit(solution)/shard_map/all_gather | solution.py:516
  610.8 16.2 all_gather.47
  770.8 34.1 %self_forward.1 = (bf16[4,2,256,384]{3,2,1,0:T(8,128)(2,1)}, bf16[2,1024,384]{2,1,0:T(8,128)(2,1)S(1)}, bf16[2,1024,384]{2,1,0:T(8,128)(2,1)S(1)}, f32[2,4,1024]{2,1,0:T(4,128)S(1)}) custom-call(s32[2]{0:T(128)S(1)} %mul.338.count_ref, bf16[4,2,256,1152]{3,2,1,0:T(8,128)(2,1)} %all-to-all-done.1.raw_ref, f32[2,1024,384]{2,1,0:T(8,128)} %get-tuple-element.195.cos_ref, ...), custom_call_target="tpu_custom_call" | custom-call | flops 3221225472 | bytes 15728640 | tf_op jit(solution)/shard_map/self_forward/pallas_call | solution.py:170
  856.6 31.9 %concatenate.82 = bf16[4,1408,1536]{1,2,0:T(8,128)(2,1)} concatenate(bf16[4,176,1536]{1,2,0:T(8,128)(2,1)S(1)} %copy-done.35, bf16[4,176,1536]{1,2,0:T(8,128)(2,1)} %copy.434, bf16[4,176,1536]{1,2,0:T(8,128)(2,1)} %copy.435, bf16[4,176,1536]{1,2,0:T(8,128)(2,1)} %copy.436, bf16[4,704,1536]{1,2,0:T(8,128)(2,1)} %copy.437), dimensions={1} | concatenate | bytes 34603008 | tf_op jit(solution)/shard_map/concatenate | solution.py:459
  912.2 16.1 cross_forward.1
  934.9 16.9 fusion.63
  951.8 24.9 %fusion.9 = bf16[4,512,1536]{1,2,0:T(8,128)(2,1)} fusion(f32[4,1536,512]{2,1,0:T(8,128)} %fusion.63, bf16[4,1408,1536]{2,1,0:T(8,128)(2,1)} %constant_dynamic-update-slice_fusion.20, bf16[512,1408]{1,0:T(8,128)(2,1)S(1)} %copy-done.112), kind=kOutput, calls=%fused_computation.21 | convolution fusion | flops 8921284608 | bytes 37617664 | tf_op jit(solution)/shard_map/mn,pnk->pmk/dot_general | solution.py:50
  976.7 17.4 multiply_reduce_fusion
  1008.0 18.8 %cross_backward.1 = (bf16[4,2,256,384]{3,2,1,0:T(8,128)(2,1)S(1)}, bf16[4,2,336,768]{3,2,1,0:T(8,128)(2,1)S(1)}) custom-call(s32[2,2]{1,0:T(2,128)S(1)} %bitcast.492, bf16[4,2,256,384]{3,2,1,0:T(8,128)(2,1)S(1)} %bitcast.484, bf16[4,2,336,768]{3,2,1,0:T(8,128)(2,1)S(1)} %bitcast.486, bf16[4,2,256,384]{3,2,1,0:T(8,128)(2,1)S(1)} %bitcast.487), custom_call_target="tpu_custom_call" | custom-call | flops 2642411520 | bytes 14548992 | tf_op jit(solution)/shard_map/cross_backward/pallas_call | solution.py:397
  1107.5 50.9 %self_backward.1 = (bf16[4,2,256,1152]{3,2,1,0:T(8,128)(2,1)}, f32[2,1,384]{2,1,0:T(1,128)S(1)}, f32[2,1,384]{2,1,0:T(1,128)S(1)}) custom-call(s32[2]{0:T(128)S(1)} %copy-done.12, bf16[4,2,256,1152]{3,2,1,0:T(8,128)(2,1)} %all-to-all-done.1.raw_ref, f32[2,1024,384]{2,1,0:T(8,128)} %get-tuple-element.195.cos_ref, f32[2,1024,384]{2,1,0:T(8,128)} %get-tuple-element.194.sin_ref, ...), custom_call_target="tpu_custom_call" | custom-call | flops 8053063680 | bytes 22020096 | tf_op jit(solution)/shard_map/self_backward/pallas_call | solution.py:284
  1190.6 16.0 collective-permute-done.40
  1215.5 16.1 collective-permute-done.43
  1263.4 19.4 %collective-permute-done.46 = bf16[4,128,768]{1,2,0:T(8,128)(2,1)S(1)} collective-permute-done((bf16[4,128,768]{1,2,0:T(8,128)(2,1)S(1)}, bf16[4,128,768]{1,2,0:T(8,128)(2,1)S(1)}, u32[]{:S(2)}, u32[]{:S(2)}) %collective-permute-start.46) | collective-permute-done | bytes 786464 | tf_op jit(solution)/shard_map/ppermute | solution.py:434
  1377.8 47.4 %collective-permute-done.51 = bf16[4,2,176,1536]{3,2,0,1:T(8,128)(2,1)} collective-permute-done((bf16[4,2,176,1536]{3,2,0,1:T(8,128)(2,1)}, bf16[4,2,176,1536]{3,2,0,1:T(8,128)(2,1)}, u32[]{:S(2)}, u32[]{:S(2)}) %collective-permute-start.51) | collective-permute-done | bytes 4325408 | tf_op jit(solution)/shard_map/ppermute | solution.py:434
  1428.8 42.3 %collective-permute-done.33 = bf16[4,2,176,704]{3,2,0,1:T(8,128)(2,1)S(1)} collective-permute-done((bf16[4,2,176,704]{3,2,0,1:T(8,128)(2,1)S(1)}, bf16[4,2,176,704]{3,2,0,1:T(8,128)(2,1)S(1)}, u32[]{:S(2)}, u32[]{:S(2)}) %collective-permute-start.33) | collective-permute-done | bytes 1982496 | tf_op jit(solution)/shard_map/ppermute | solution.py:434
  1486.7 23.3 %collective-permute-done.34 = bf16[4,176,704]{2,1,0:T(8,128)(2,1)S(1)} collective-permute-done((bf16[4,176,704]{2,1,0:T(8,128)(2,1)S(1)}, bf16[4,176,704]{2,1,0:T(8,128)(2,1)S(1)}, u32[]{:S(2)}, u32[]{:S(2)}) %collective-permute-start.34) | collective-permute-done | bytes 991264 | tf_op jit(solution)/shard_map/ppermute | solution.py:434
  1511.3 43.4 %collective-permute-done.52 = bf16[4,176,1536]{2,1,0:T(8,128)(2,1)S(1)} collective-permute-done((bf16[4,176,1536]{2,1,0:T(8,128)(2,1)}, bf16[4,176,1536]{2,1,0:T(8,128)(2,1)S(1)}, u32[]{:S(2)}, u32[]{:S(2)}) %collective-permute-start.52) | collective-permute-done | bytes 2162720 | tf_op jit(solution)/shard_map/ppermute | solution.py:434
  1582.7 30.0 %collective-permute-done.55 = bf16[4,176,1536]{2,1,0:T(8,128)(2,1)} collective-permute-done((bf16[4,176,1536]{2,1,0:T(8,128)(2,1)}, bf16[4,176,1536]{2,1,0:T(8,128)(2,1)}, u32[]{:S(2)}, u32[]{:S(2)}) %collective-permute-start.55) | collective-permute-done | bytes 2162720 | tf_op jit(solution)/shard_map/ppermute | solution.py:434
  1616.9 15.9 fusion.44
  1632.8 16.9 collective-permute-done.36
  1680.7 41.3 %psum.23 = f32[5808]{0:T(1024)S(1)} all-reduce(f32[5808]{0:T(1024)S(1)} %pad_maximum_fusion.11), channel_id=1, replica_groups=mesh['dp'=8,'sp'=4] {'dp','sp'}, use_global_device_ids=true, to_apply=%region_36.37 | all-reduce | flops 5808 | bytes 46464 | tf_op jit(solution)/shard_map/psum | solution.py:661
  1752.5 17.8 psum.22
  (671 shorter events, 789.9 us)
Async XLA Ops:
  9.7 192.3 %all-gather.15.cloned.1.call-start = ((), (), s32[]{:S(2)}) async-start(), calls=%async_computation.25 | async-start | bytes 2703360 | tf_op jit(solution)/shard_map/all_gather | solution.py:516
  86.8 95.2 %collective-permute-start.1 = (bf16[4,176,704]{2,1,0:T(8,128)(2,1)}, bf16[4,176,704]{2,1,0:T(8,128)(2,1)}, u32[]{:S(2)}, u32[]{:S(2)}) collective-permute-start(bf16[4,176,704]{2,1,0:T(8,128)(2,1)} %bitcast.3), channel_id=1, source_target_pairs={{0,16},{4,20},{8,24},{12,28},{16,0},{20,4},{24,8},{28,12},{1,17},{... | collective-permute-start | bytes 2973704 | tf_op jit(solution)/shard_map/ppermute | solution.py:434
  193.3 127.9 %collective-permute-start.3 = (bf16[4,704,704]{1,2,0:T(8,128)(2,1)}, bf16[4,704,704]{1,2,0:T(8,128)(2,1)}, u32[]{:S(2)}, u32[]{:S(2)}) collective-permute-start(bf16[4,704,704]{1,2,0:T(8,128)(2,1)} %pad_maximum_fusion.3), channel_id=1, source_target_pairs={{0,4},{4,0},{8,12},{12,8},{16,20},{20,16},{24,28},{28,24},{1,5},{5... | collective-permute-start | bytes 11894792 | tf_op jit(solution)/shard_map/ppermute | solution.py:434
  200.2 119.5 %all-gather.13.cloned.1.call-start = ((), (), s32[]{:S(2)}) async-start(), calls=%async_computation.24 | async-start | bytes 2703360 | tf_op jit(solution)/shard_map/all_gather | solution.py:516
  202.0 117.7 %collective-permute-start.29 = (bf16[4,176,1536]{2,1,0:T(8,128)(2,1)}, bf16[4,176,1536]{2,1,0:T(8,128)(2,1)}, u32[]{:S(2)}, u32[]{:S(2)}) collective-permute-start(bf16[4,176,1536]{2,1,0:T(8,128)(2,1)} %bitcast.45), channel_id=1, source_target_pairs={{0,16},{4,20},{8,24},{12,28},{16,0},{20,4},{24,8},{28,12},{1,17},{... | collective-permute-start | bytes 6488072 | tf_op jit(solution)/shard_map/ppermute | solution.py:434
  210.7 241.4 %collective-permute-start.7 = (bf16[4,704,1152]{2,1,0:T(8,128)(2,1)}, bf16[4,704,1152]{2,1,0:T(8,128)(2,1)}, u32[]{:S(2)}, u32[]{:S(2)}) collective-permute-start(bf16[4,704,1152]{2,1,0:T(8,128)(2,1)} %pad_maximum_fusion.2), channel_id=1, source_target_pairs={{0,4},{4,0},{8,12},{12,8},{16,20},{20,16},{24,28},{28,24},{1,5},{5... | collective-permute-start | bytes 19464200 | tf_op jit(solution)/shard_map/ppermute | solution.py:434
  234.5 265.9 %collective-permute-start.8 = (bf16[4,176,384]{2,1,0:T(8,128)(2,1)S(1)}, bf16[4,176,384]{2,1,0:T(8,128)(2,1)}, u32[]{:S(2)}, u32[]{:S(2)}) collective-permute-start(bf16[4,176,384]{2,1,0:T(8,128)(2,1)S(1)} %all_gather.43), channel_id=1, source_target_pairs={{0,8},{4,12},{8,0},{12,4},{16,24},{20,28},{24,16},{28,20},{1,9},{5... | collective-permute-start | bytes 1622024 | tf_op jit(solution)/shard_map/ppermute | solution.py:434
  321.2 123.3 %collective-permute-start.30 = (bf16[4,176,1536]{2,1,0:T(8,128)(2,1)}, bf16[4,176,1536]{2,1,0:T(8,128)(2,1)}, u32[]{:S(2)}, u32[]{:S(2)}) collective-permute-start(bf16[4,176,1536]{2,1,0:T(8,128)(2,1)} %collective-permute-done.29), channel_id=1, source_target_pairs={{0,8},{4,12},{8,0},{12,4},{16,24},{20,28},{24,16},{28,20},{1,9},{5... | collective-permute-start | bytes 6488072 | tf_op jit(solution)/shard_map/ppermute | solution.py:434
  361.3 265.7 %collective-permute-start.9 = (bf16[4,176,384]{2,1,0:T(8,128)(2,1)S(1)}, bf16[4,176,384]{2,1,0:T(8,128)(2,1)}, u32[]{:S(2)}, u32[]{:S(2)}) collective-permute-start(bf16[4,176,384]{2,1,0:T(8,128)(2,1)S(1)} %all_gather.43), channel_id=1, source_target_pairs={{0,16},{4,20},{8,24},{12,28},{16,0},{20,4},{24,8},{28,12},{1,17},{... | collective-permute-start | bytes 1622024 | tf_op jit(solution)/shard_map/ppermute | solution.py:434
  452.1 157.3 %collective-permute-start.13 = (bf16[4,176,384]{2,1,0:T(8,128)(2,1)}, bf16[4,176,384]{2,1,0:T(8,128)(2,1)}, u32[]{:S(2)}, u32[]{:S(2)}) collective-permute-start(bf16[4,176,384]{2,1,0:T(8,128)(2,1)} %all_gather.44), channel_id=1, source_target_pairs={{0,16},{4,20},{8,24},{12,28},{16,0},{20,4},{24,8},{28,12},{1,17},{... | collective-permute-start | bytes 1622024 | tf_op jit(solution)/shard_map/ppermute | solution.py:434
  473.4 297.4 %all-to-all-start.1 = ((bf16[4,2,256,1152]{3,2,1,0:T(8,128)(2,1)}), bf16[4,2,256,1152]{3,2,1,0:T(8,128)(2,1)}, u32[]{:S(2)}, u32[]{:S(2)}) async-start(bf16[4,2,256,1152]{3,2,1,0:T(8,128)(2,1)} %bitcast.506), calls=%async_computation.1 | async-start | bytes 9437184 | tf_op jit(solution)/shard_map/all_to_all | solution.py:578
  478.4 258.8 %all-gather.11.cloned.1.call-start = ((), (), s32[]{:S(2)}) async-start(), calls=%async_computation.15 | async-start | bytes 1720320 | tf_op jit(solution)/shard_map/all_gather | solution.py:566
  478.9 409.6 %collective-permute-start.31 = (bf16[4,704,1536]{2,1,0:T(8,128)(2,1)}, bf16[4,704,1536]{2,1,0:T(8,128)(2,1)}, u32[]{:S(2)}, u32[]{:S(2)}) collective-permute-start(bf16[4,704,1536]{2,1,0:T(8,128)(2,1)} %pad_maximum_fusion.1), channel_id=1, source_target_pairs={{0,4},{4,0},{8,12},{12,8},{16,20},{20,16},{24,28},{28,24},{1,5},{5... | collective-permute-start | bytes 25952264 | tf_op jit(solution)/shard_map/ppermute | solution.py:434
  497.2 347.1 %collective-permute-start.27 = (bf16[4,704,1536]{2,1,0:T(8,128)(2,1)}, bf16[4,704,1536]{2,1,0:T(8,128)(2,1)}, u32[]{:S(2)}, u32[]{:S(2)}) collective-permute-start(bf16[4,704,1536]{2,1,0:T(8,128)(2,1)} %pad_maximum_fusion), channel_id=1, source_target_pairs={{0,4},{4,0},{8,12},{12,8},{16,20},{20,16},{24,28},{28,24},{1,5},{5... | collective-permute-start | bytes 25952264 | tf_op jit(solution)/shard_map/ppermute | solution.py:434
  500.4 128.9 %collective-permute-start.12 = (bf16[4,176,384]{2,1,0:T(8,128)(2,1)}, bf16[4,176,384]{2,1,0:T(8,128)(2,1)}, u32[]{:S(2)}, u32[]{:S(2)}) collective-permute-start(bf16[4,176,384]{2,1,0:T(8,128)(2,1)} %all_gather.44), channel_id=1, source_target_pairs={{0,8},{4,12},{8,0},{12,4},{16,24},{20,28},{24,16},{28,20},{1,9},{5... | collective-permute-start | bytes 1622024 | tf_op jit(solution)/shard_map/ppermute | solution.py:434
  1050.9 608.6 %all-reduce.11.cloned.1.call-start = ((), (), s32[]{:S(2)}) async-start(), calls=%async_computation.26 | async-start | bytes 2752512
  1077.3 106.7 %collective-permute-start.44 = (bf16[4,512,768]{2,1,0:T(8,128)(2,1)}, bf16[4,512,768]{2,1,0:T(8,128)(2,1)}, u32[]{:S(2)}, u32[]{:S(2)}) collective-permute-start(bf16[4,512,768]{2,1,0:T(8,128)(2,1)} %convert_bitcast_fusion.3), channel_id=1, source_target_pairs={{0,4},{4,0},{8,12},{12,8},{16,20},{20,16},{24,28},{28,24},{1,5},{5... | collective-permute-start | bytes 9437192 | tf_op jit(solution)/shard_map/ppermute | solution.py:434
  1088.1 221.0 %collective-permute-start.50 = (bf16[4,704,1536]{2,1,0:T(8,128)(2,1)}, bf16[4,704,1536]{2,1,0:T(8,128)(2,1)}, u32[]{:S(2)}, u32[]{:S(2)}) collective-permute-start(bf16[4,704,1536]{2,1,0:T(8,128)(2,1)} %convert_bitcast_fusion.1), channel_id=1, source_target_pairs={{0,4},{4,0},{8,12},{12,8},{16,20},{20,16},{24,28},{28,24},{1,5},{5... | collective-permute-start | bytes 25952264 | tf_op jit(solution)/shard_map/ppermute | solution.py:434
  1098.7 110.2 %collective-permute-start.42 = (bf16[4,2,176,384]{3,2,1,0:T(8,128)(2,1)}, bf16[4,2,176,384]{3,2,1,0:T(8,128)(2,1)}, u32[]{:S(2)}, u32[]{:S(2)}) collective-permute-start(bf16[4,2,176,384]{3,2,1,0:T(8,128)(2,1)} %slice_bitcast_fusion.8), channel_id=1, source_target_pairs={{0,8},{4,12},{8,0},{12,4},{16,24},{20,28},{24,16},{28,20},{1,9},{5... | collective-permute-start | bytes 3244040 | tf_op jit(solution)/shard_map/ppermute | solution.py:434
  1158.4 125.5 %all-to-all-start.4 = ((bf16[4,2,256,1152]{3,2,1,0:T(8,128)(2,1)}), bf16[4,2,256,1152]{3,2,1,0:T(8,128)(2,1)}, u32[]{:S(2)}, u32[]{:S(2)}) async-start(bf16[4,2,256,1152]{3,2,1,0:T(8,128)(2,1)} %get-tuple-element.34), calls=%async_computation.4 | async-start | bytes 9437184 | tf_op jit(solution)/shard_map/all_to_all | solution.py:578
  1163.5 500.0 %reduce-scatter.13.cloned.1.call-start = ((), (), s32[]{:S(2)}) async-start(), calls=%async_computation.18 | async-start | bytes 675840 | tf_op jit(solution)/shard_map/reduce_scatter | solution.py:602
  1208.8 456.7 %reduce-scatter.15.cloned.1.call-start = ((), (), s32[]{:S(2)}) async-start(), calls=%async_computation.19 | async-start | bytes 675840 | tf_op jit(solution)/shard_map/reduce_scatter | solution.py:602
  1232.6 435.0 %reduce-scatter.19.cloned.1.call-start = ((), (), s32[]{:S(2)}) async-start(), calls=%async_computation.21 | async-start | bytes 675840 | tf_op jit(solution)/shard_map/reduce_scatter | solution.py:602
  1261.2 410.2 %reduce-scatter.17.cloned.1.call-start = ((), (), s32[]{:S(2)}) async-start(), calls=%async_computation.20 | async-start | bytes 983040 | tf_op jit(solution)/shard_map/reduce_scatter | solution.py:602
  1283.9 487.4 %reduce-scatter.9.cloned.1.call-start = ((), (), s32[]{:S(2)}) async-start(), calls=%async_computation.16 | async-start | bytes 1351680 | tf_op jit(solution)/shard_map/reduce_scatter | solution.py:602
  1328.8 96.5 %collective-permute-start.51 = (bf16[4,2,176,1536]{3,2,0,1:T(8,128)(2,1)}, bf16[4,2,176,1536]{3,2,0,1:T(8,128)(2,1)}, u32[]{:S(2)}, u32[]{:S(2)}) collective-permute-start(bf16[4,2,176,1536]{3,2,0,1:T(8,128)(2,1)} %bitcast.475), channel_id=1, source_target_pairs={{0,16},{4,20},{8,24},{12,28},{16,0},{20,4},{24,8},{28,12},{1,17},{... | collective-permute-start | bytes 12976136 | tf_op jit(solution)/shard_map/ppermute | solution.py:434
  1347.8 123.3 %collective-permute-start.33 = (bf16[4,2,176,704]{3,2,0,1:T(8,128)(2,1)S(1)}, bf16[4,2,176,704]{3,2,0,1:T(8,128)(2,1)S(1)}, u32[]{:S(2)}, u32[]{:S(2)}) collective-permute-start(bf16[4,2,176,704]{3,2,0,1:T(8,128)(2,1)S(1)} %bitcast.521), channel_id=1, source_target_pairs={{0,16},{4,20},{8,24},{12,28},{16,0},{20,4},{24,8},{28,12},{1,17},{... | collective-permute-start | bytes 5947400 | tf_op jit(solution)/shard_map/ppermute | solution.py:434
  1359.4 206.1 %collective-permute-start.35 = (bf16[4,704,1152]{2,1,0:T(8,128)(2,1)}, bf16[4,704,1152]{2,1,0:T(8,128)(2,1)}, u32[]{:S(2)}, u32[]{:S(2)}) collective-permute-start(bf16[4,704,1152]{2,1,0:T(8,128)(2,1)} %fusion.21), channel_id=1, source_target_pairs={{0,4},{4,0},{8,12},{12,8},{16,20},{20,16},{24,28},{28,24},{1,5},{5... | collective-permute-start | bytes 19464200 | tf_op jit(solution)/shard_map/ppermute | solution.py:434
  1364.1 194.5 %collective-permute-start.54 = (bf16[4,2,176,1536]{3,2,0,1:T(8,128)(2,1)}, bf16[4,2,176,1536]{3,2,0,1:T(8,128)(2,1)}, u32[]{:S(2)}, u32[]{:S(2)}) collective-permute-start(bf16[4,2,176,1536]{3,2,0,1:T(8,128)(2,1)} %bitcast.474), channel_id=1, source_target_pairs={{0,8},{4,12},{8,0},{12,4},{16,24},{20,28},{24,16},{28,20},{1,9},{5... | collective-permute-start | bytes 12976136 | tf_op jit(solution)/shard_map/ppermute | solution.py:434
  1511.3 261.8 %reduce-scatter.21.cloned.1.call-start = ((), (), s32[]{:S(2)}) async-start(), calls=%async_computation.22 | async-start | bytes 2703360 | tf_op jit(solution)/shard_map/reduce_scatter | solution.py:602
  1558.4 216.8 %reduce-scatter.23.cloned.1.call-start = ((), (), s32[]{:S(2)}) async-start(), calls=%async_computation.23 | async-start | bytes 2703360 | tf_op jit(solution)/shard_map/reduce_scatter | solution.py:602
  1679.8 97.6 %reduce-scatter.11.cloned.1.call-start = ((), (), s32[]{:S(2)}) async-start(), calls=%async_computation.17 | async-start | bytes 2027520 | tf_op jit(solution)/shard_map/reduce_scatter | solution.py:602
  (161 other events, 7109.3 us)
Sparse Core Ops, SparseCore 0:
  10.2 40.5 all-gather.8
  52.4 55.1 all-gather.14
  202.6 57.8 all-gather.12
  500.3 50.0 all-gather.10
  1062.3 83.2 all-reduce.10
  1209.0 49.5 reduce-scatter.12
  1261.4 28.0 reduce-scatter.14
  1291.9 22.6 reduce-scatter.18
  1317.5 21.5 reduce-scatter.16
  1511.4 26.2 reduce-scatter.8
  1558.5 43.2 reduce-scatter.20
  1617.0 43.2 reduce-scatter.22
  1725.3 36.1 reduce-scatter.10

commit v2 on v1

--- a/solution.py
+++ b/solution.py
@@ -423,54 +423,218 @@
     )(lengths, query, text_kv, incoming)
 
 
+def mlp_forward(rows_in, near1, far1, near2, far2):
+    rows, width = rows_in.shape
+    parts, half, ff = near1.shape
+    step = 512 if ff % 512 == 0 else ff
+    steps = ff // step
+
+    def kernel(x_ref, n1_ref, f1_ref, n2_ref, f2_ref, hid_ref, act_ref, out_ref, xa, xb, ya, yb):
+        first = (pl.program_id(0) == 0) & (pl.program_id(1) == 0)
+        last = (pl.program_id(0) == parts - 1) & (pl.program_id(1) == steps - 1)
+
+        @pl.when(first)
+        def _():
+            xa[...] = x_ref[:, :half]
+            xb[...] = x_ref[:, half:]
+            ya[...] = jnp.zeros_like(ya)
+            yb[...] = jnp.zeros_like(yb)
+
+        hidden = dot_nn(xa[...], n1_ref[0]) + dot_nn(xb[...], f1_ref[0])
+        hid_ref[0] = hidden
+        activ = jax.nn.gelu(hidden, approximate=True).astype(BF)
+        act_ref[0] = activ
+        ya[...] += dot_nt(activ, n2_ref[0])
+        yb[...] += dot_nt(activ, f2_ref[0])
+
+        @pl.when(last)
+        def _():
+            out_ref[:, :half] = ya[...]
+            out_ref[:, half:] = yb[...]
+
+    weight = pl.BlockSpec((1, half, step), lambda p, n: (p, 0, n))
+    unit = pl.BlockSpec((1, rows, step), lambda p, n: (p, 0, n))
+    whole = pl.BlockSpec((rows, width), lambda p, n: (0, 0))
+    return pl.pallas_call(
+        kernel,
+        name="mlp_forward",
+        grid=(parts, steps),
+        in_specs=[whole, weight, weight, weight, weight],
+        out_specs=[unit, unit, whole],
+        out_shape=[
+            jax.ShapeDtypeStruct((parts, rows, ff), F32),
+            jax.ShapeDtypeStruct((parts, rows, ff), BF),
+            jax.ShapeDtypeStruct((rows, width), F32),
+        ],
+        scratch_shapes=[
+            pltpu.VMEM((rows, half), BF),
+            pltpu.VMEM((rows, half), BF),
+            pltpu.VMEM((rows, half), F32),
+            pltpu.VMEM((rows, half), F32),
+        ],
+        compiler_params=pltpu.CompilerParams(vmem_limit_bytes=48 << 20),
+        cost_estimate=pl.CostEstimate(
+            flops=4 * rows * width * parts * ff,
+            bytes_accessed=parts * ff * (4 * width + 6 * rows),
+            transcendentals=rows * parts * ff,
+        ),
+    )(rows_in, near1, far1, near2, far2)
+
+
+def gelu_slope(value):
+    root = math.sqrt(2.0 / math.pi)
+    square = value * value
+    curve = jnp.tanh(root * value * (1.0 + 0.044715 * square))
+    return 0.5 * (1.0 + curve) + 0.5 * value * (1.0 - curve * curve) * root * (
+        1.0 + 3.0 * 0.044715 * square
+    )
+
+
+def mlp_backward(grads, rows_in, hidden, activ, near1, far1, near2, far2):
+    rows, width = rows_in.shape
+    parts, half, ff = near1.shape
+    step = 512 if ff % 512 == 0 else ff
+    steps = ff // step
+
+    def kernel(
+        g_ref, x_ref, hid_ref, act_ref, n1_ref, f1_ref, n2_ref, f2_ref,
+        dn1_ref, df1_ref, dn2_ref, df2_ref, out_ref,
+        ga, gb, gta, gtb, xta, xtb, ya, yb,
+    ):
+        first = (pl.program_id(0) == 0) & (pl.program_id(1) == 0)
+        last = (pl.program_id(0) == parts - 1) & (pl.program_id(1) == steps - 1)
+
+        @pl.when(first)
+        def _():
+            ga[...] = g_ref[:, :half]
+            gb[...] = g_ref[:, half:]
+            gta[...] = jnp.transpose(g_ref[:, :half])
+            gtb[...] = jnp.transpose(g_ref[:, half:])
+            xta[...] = jnp.transpose(x_ref[:, :half])
+            xtb[...] = jnp.transpose(x_ref[:, half:])
+            ya[...] = jnp.zeros_like(ya)
+            yb[...] = jnp.zeros_like(yb)
+
+        d_activ = dot_nn(ga[...], n2_ref[0]) + dot_nn(gb[...], f2_ref[0])
+        activ = act_ref[0]
+        dn2_ref[0] = dot_nn(gta[...], activ).astype(BF)
+        df2_ref[0] = dot_nn(gtb[...], activ).astype(BF)
+        d_hidden = (d_activ * gelu_slope(hid_ref[0])).astype(BF)
+        dn1_ref[0] = dot_nn(xta[...], d_hidden).astype(BF)
+        df1_ref[0] = dot_nn(xtb[...], d_hidden).astype(BF)
+        ya[...] += dot_nt(d_hidden, n1_ref[0])
+        yb[...] += dot_nt(d_hidden, f1_ref[0])
+
+        @pl.when(last)
+        def _():
+            out_ref[:, :half] = ya[...]
+            out_ref[:, half:] = yb[...]
+
+    weight = pl.BlockSpec((1, half, step), lambda p, n: (p, 0, n))
+    unit = pl.BlockSpec((1, rows, step), lambda p, n: (p, 0, n))
+    whole = pl.BlockSpec((rows, width), lambda p, n: (0, 0))
+    grad = jax.ShapeDtypeStruct((parts, half, ff), BF)
+    return pl.pallas_call(
+        kernel,
+        name="mlp_backward",
+        grid=(parts, steps),
+        in_specs=[whole, whole, unit, unit, weight, weight, weight, weight],
+        out_specs=[weight, weight, weight, weight, whole],
+        out_shape=[grad, grad, grad, grad, jax.ShapeDtypeStruct((rows, width), F32)],
+        scratch_shapes=[
+            pltpu.VMEM((rows, half), BF),
+            pltpu.VMEM((rows, half), BF),
+            pltpu.VMEM((half, rows), BF),
+            pltpu.VMEM((half, rows), BF),
+            pltpu.VMEM((half, rows), BF),
+            pltpu.VMEM((half, rows), BF),
+            pltpu.VMEM((rows, half), F32),
+            pltpu.VMEM((rows, half), F32),
+        ],
+        compiler_params=pltpu.CompilerParams(vmem_limit_bytes=56 << 20),
+        cost_estimate=pl.CostEstimate(
+            flops=8 * rows * width * parts * ff,
+            bytes_accessed=parts * ff * (8 * width + 6 * rows),
+            transcendentals=rows * parts * ff,
+        ),
+    )(grads, rows_in, hidden, activ, near1, far1, near2, far2)
+
+
+def tie(*values):
+    return lax.optimization_barrier(values)
+
+
 class Cube:
     def __init__(self):
         self.size = lax.axis_size("dp")
         self.bits = self.size.bit_length() - 1
+        self.outer = list(range(1, self.bits))
         self.rank = lax.axis_index("dp")
-
-    def swap(self, value, bit):
-        pairs = [(i, i ^ (1 << bit)) for i in range(self.size)]
-        return lax.ppermute(value, "dp", pairs)
-
-    def order(self, flip):
-        outer = list(range(1, self.bits))
-        return outer[::-1] if flip else outer
-
-    def position(self):
-        places = []
+        self.masks = []
         for place in range(self.size):
-            mask = 0
-            for bit in range(self.bits):
-                weight = self.bits - 1 if bit == 0 else bit - 1
-                mask |= ((place >> weight) & 1) << bit
-            places.append(mask)
-        return places
-
-    def owners(self):
-        return self.rank ^ jnp.array(self.position(), jnp.int32)
+            mask = place >> (self.bits - 1)
+            for bit in self.outer:
+                mask |= ((place >> (bit - 1)) & 1) << bit
+            self.masks.append(mask)
+        self.owners = self.rank ^ jnp.array(self.masks, jnp.int32)
+
+    def swap(self, value, bit, axis="dp"):
+        pairs = [(i, i ^ (1 << bit)) for i in range(lax.axis_size(axis))]
+        return lax.ppermute(value, axis, pairs)
 
     def gather(self, shard, flip):
         held = [(0, shard)]
-        for bit in self.order(flip):
+        for bit in self.outer[::-1] if flip else self.outer:
             held = held + [(mask | (1 << bit), self.swap(piece, bit)) for mask, piece in held]
-        held = sorted(held, key=lambda item: self.position().index(item[0]))
+        held = sorted(held, key=lambda item: self.masks.index(item[0]))
         near = jnp.concatenate([piece for mask, piece in held], 1)
-        return jnp.concatenate([near, self.swap(near, 0)], 1)
+        return near, self.swap(near, 0)
 
     def scatter(self, near, far, flip):
-        held = (near + self.swap(far, 0).astype(F32)).astype(BF)
-        parts, rows, lanes = held.shape
-        outer = self.bits - 1
-        held = held.reshape((parts,) + (2,) * outer + (rows >> outer, lanes))
-        axes = list(range(outer, 0, -1))
-        for bit in self.order(flip)[::-1]:
-            axis = 1 + axes.index(bit)
-            keep = lax.index_in_dim(held, 0, axis, keepdims=False)
-            send = lax.index_in_dim(held, 1, axis, keepdims=False)
-            held = (keep.astype(F32) + self.swap(send, bit).astype(F32)).astype(BF)
-            axes.remove(bit)
+        rows = near.shape[1] // (self.size // 2)
+        order = self.outer if flip else self.outer[::-1]
+        other = self.swap(far, 0)
+        yield other
+        terms = {}
+        for place in range(self.size // 2):
+            cut = slice(place * rows, (place + 1) * rows)
+            terms[self.masks[place]] = [near[:, cut], other[:, cut]]
+
+        def total(mask):
+            value = terms[mask][0].astype(F32)
+            for term in terms[mask][1:]:
+                value = value + term.astype(F32)
+            return value.astype(BF)
+
+        for bit in order:
+            send = [mask for mask in terms if mask >> bit & 1]
+            keep = [mask for mask in terms if not mask >> bit & 1]
+            got = self.swap(jnp.concatenate([total(mask) for mask in send], 1), bit)
+            yield got
+            for place, mask in enumerate(send):
+                terms[mask ^ (1 << bit)].append(got[:, place * rows : (place + 1) * rows])
+            terms = {mask: terms[mask] for mask in keep}
+        yield total(0)
+
+    def trade(self, value):
+        blocks = {mask: value[mask] for mask in range(self.size)}
+        for bit in range(self.bits):
+            send = sorted(mask for mask in blocks if mask >> bit & 1)
+            got = self.swap(jnp.stack([blocks[mask] for mask in send]), bit)
+            for place, mask in enumerate(send):
+                blocks[mask] = got[place]
+        return jnp.stack([blocks[mask] for mask in range(self.size)])
+
+    def spread(self, value):
+        held = value[None]
+        for bit in range(self.bits):
+            held = jnp.concatenate([held, self.swap(held, bit)])
         return held
+
+    def add(self, value, axis):
+        for bit in range(lax.axis_size(axis).bit_length() - 1):
+            value = value + self.swap(value, bit, axis)
+        return value
 
 
 def on_device(
@@ -502,7 +666,6 @@
     zone = lax.axis_index("sp")
     cube = Cube()
     ranks = cube.size
-    owners = cube.owners()
     rows = micros * slots
     sequence = slots * parts
     local = H // parts
@@ -511,37 +674,55 @@
     words = text_slots * parts
     features = text.shape[2]
     strip = width // ranks
-
-    def spread(shard):
-        return lax.all_gather(shard, "sp", axis=0, tiled=False)
-
-    def weight(shard, flip):
-        return cube.gather(spread(shard), flip)
-
     half = w_skip.shape[0]
-    skip_w = weight(w_skip.T, 0)
-    qkv_w = weight(pad_heads(w_qkv.reshape(strip, -1)), 1)
-    out1_w = weight(pad_heads(w_out1.T), 0)
-    query2_w = weight(pad_heads(w_query2), 1)
-    text_w = weight(pad_heads(w_text_kv.reshape(w_text_kv.shape[0], -1)), 0)
-    out2_w = weight(pad_heads(w_out2.T), 1)
-    fc1_w = weight(w_fc1, 0)
-    fc2_w = weight(w_fc2.T, 1)
-
-    def own_order(vector):
-        return vector.reshape(ranks, -1)[owners].reshape(-1)
+    middle = width // 2
+
+    skip_pad = -(-half // 256) * 256 - half
+    text_rows = w_text_kv.shape[0]
+    shards = [
+        jnp.pad(w_skip.T, ((0, 0), (0, skip_pad))),
+        pad_heads(w_qkv.reshape(strip, -1)),
+        jnp.concatenate([pad_heads(w_out1.T), pad_heads(w_query2), pad_heads(w_out2.T)], 1),
+        jnp.pad(pad_heads(w_text_kv.reshape(text_rows, -1)), ((0, max(0, strip - text_rows)), (0, 0))),
+        w_fc1,
+        w_fc2.T,
+    ]
+    spread = []
+    for shard in shards:
+        if spread:
+            shard, spread[-1] = tie(shard, spread[-1])
+        spread.append(lax.all_gather(shard, "sp", axis=0, tiled=False))
+    skip_z, qkv_z, cross_z, text_z, fc1_z, fc2_z = spread
+
+    def join(near, far):
+        return jnp.concatenate([near, far], 1)
+
+    def split_weight(value, cut):
+        left = join(*cube.gather(value[:, :, :cut], 0))
+        right = join(*cube.gather(value[:, :, cut:], 1))
+        return jnp.concatenate([left, right], 2)
+
+    skip_w = split_weight(skip_z, (half + skip_pad) // 2)
+    qkv_w = split_weight(qkv_z, (3 * lanes) // 256 * 128 + 128)
+    out1_w = join(*cube.gather(cross_z[:, :, :lanes], 0))
+    query2_w = join(*cube.gather(cross_z[:, :, lanes : 2 * lanes], 1))
+    out2_w = join(*cube.gather(cross_z[:, :, 2 * lanes :], 0))
+    text_w = join(*cube.gather(text_z[:, :text_rows], 1))
+    fc1_n, fc1_f = cube.gather(fc1_z, 0)
+    fc2_n, fc2_f = cube.gather(fc2_z, 1)
+
+    gains = jnp.stack([gain_skip, gain_attn, gain_cross, gain_mlp])
+    gains = gains.reshape(4, ranks, strip)[:, cube.owners].reshape(4, width)
+    g_skip, g_attn, g_cross, g_mlp = gains
 
     def shuffle(count):
         block = count // ranks
         place = jnp.arange(count, dtype=jnp.int32)
-        source = owners[place // block] * block + place % block
+        source = cube.owners[place // block] * block + place % block
         return (place[:, None] == source[None, :]).astype(BF)
 
     turn = shuffle(width)
     text_turn = shuffle(features)
-    g_skip, g_attn, g_cross, g_mlp = (
-        own_order(gain) for gain in (gain_skip, gain_attn, gain_cross, gain_mlp)
-    )
 
     wide = grid[:, 0, 1]
     counts = grid[:, 0, 0] * wide
@@ -552,22 +733,24 @@
     gain_q = pad_heads(jnp.tile(gain_query, local)[None, :])
     gain_k = pad_heads(jnp.tile(gain_key, local)[None, :])
 
-    steps = lax.all_gather(timestep[:, 0], "dp", axis=0, tiled=False)
+    steps = cube.spread(timestep[:, 0])
     time_act = jax.nn.silu(time_embed(steps, width)).astype(BF).reshape(ranks * micros, parts, -1)
     time_part = lax.dynamic_index_in_dim(time_act, zone, 1, keepdims=False)
-    shift_part = jnp.dot(time_part, w_mod, preferred_element_type=F32)
-    shift_own = lax.all_to_all(
-        shift_part.reshape(ranks, micros, strip), "dp", split_axis=0, concat_axis=0, tiled=True
-    )
-    shift_own = lax.psum(shift_own, "sp")
-    shift = jnp.transpose(shift_own[owners], (1, 0, 2)).reshape(micros, width)
+    shift = jnp.dot(time_part, w_mod, preferred_element_type=F32)
+    shift = cube.trade(cube.add(shift, "sp").reshape(ranks, micros, strip))
+    shift = jnp.stack([shift[mask] for mask in cube.masks], 1).reshape(micros, width)
 
     text_own = jnp.dot(text.reshape(-1, features), text_turn, preferred_element_type=F32).astype(BF)
-    text_all = lax.all_gather(text_own.reshape(micros, text_slots, features), "sp", axis=1, tiled=True)
+    text_all = lax.all_gather(text_own, "sp", axis=0, tiled=False)
+    text_all = jnp.transpose(text_all.reshape(parts, micros, text_slots, features), (1, 0, 2, 3))
     text_all = text_all.reshape(micros * words, features)
+
+    grad3 = jnp.dot(cotangent.reshape(rows, width), turn, preferred_element_type=F32) * live
+    d_mlp = grad3.astype(BF)
 
     joined = jnp.stack([tokens, skip_tokens]).reshape(2, rows, parts // 2, half)
     joined = jnp.transpose(joined, (0, 2, 1, 3)).reshape(parts, rows, half)
+    joined = jnp.pad(joined, ((0, 0), (0, 0), (0, skip_pad)))
     base = mix("pmk,pnk->mn", joined, skip_w)
     stream = norm_rows(base, g_skip)
     pre_attn = norm_rows(stream, g_attn).reshape(micros, slots, width) + shift[:, None, :]
@@ -578,108 +761,136 @@
         return lax.all_to_all(value, "sp", split_axis=0, concat_axis=0, tiled=True)
 
     raw = exchange(projected.reshape(parts, micros, slots, 3 * lanes))
+    text_kv = mix("mk,pkn->pmn", text_all, text_w).astype(BF)
+    text_kv = text_kv.reshape(parts, micros, words, 2 * lanes)
     attended, turned_q, turned_k, norms = self_forward(raw, counts, cosine, sine, gain_q, gain_k)
     attended = exchange(attended).reshape(parts, rows, lanes)
     stream1 = stream + mix("pmk,pnk->mn", attended, out1_w)
     pre_cross = norm_rows(stream1, g_cross).astype(BF)
     query2 = mix("mk,pkn->pmn", pre_cross, query2_w).astype(BF)
     query2 = query2.reshape(parts, micros, slots, lanes)
-    text_kv = mix("mk,pkn->pmn", text_all, text_w).astype(BF)
-    text_kv = text_kv.reshape(parts, micros, words, 2 * lanes)
     crossed = cross_forward(query2, text_kv, lengths).reshape(parts, rows, lanes)
     stream2 = stream1 + mix("pmk,pnk->mn", crossed, out2_w)
     pre_mlp = norm_rows(stream2, g_mlp).astype(BF)
-    hidden = mix("mk,pkn->pmn", pre_mlp, fc1_w)
-    activ = jax.nn.gelu(hidden, approximate=True).astype(BF)
-    stream3 = stream2 + mix("pmk,pnk->mn", activ, fc2_w)
-    result = jnp.dot((stream3 * live).astype(BF), turn.T, preferred_element_type=F32).astype(BF)
-
-    def term(left, right, flip):
-        cut = left.shape[1] // 2
-        near = mix("md,pmn->pdn", left[:, :cut], right)
-        far = mix("md,pmn->pdn", left[:, cut:], right).astype(BF)
-        held = cube.scatter(near, far, flip)
-        return lax.psum_scatter(held, "sp", scatter_dimension=0, tiled=False).astype(F32)
-
-    grad3 = jnp.dot(cotangent.reshape(rows, width), turn, preferred_element_type=F32) * live
-    d_mlp = grad3.astype(BF)
-    term_fc2 = term(d_mlp, activ, 1)
-    d_activ = mix("mn,pnk->pmk", d_mlp, fc2_w)
-    unused, gelu_pull = jax.vjp(lambda value: jax.nn.gelu(value, approximate=True), hidden)
-    d_hidden = gelu_pull(d_activ)[0].astype(BF)
-    term_fc1 = term(pre_mlp, d_hidden, 0)
-    d_stream2, d_gain_mlp = norm_back(stream2, g_mlp, mix("pmn,pkn->mk", d_hidden, fc1_w))
+    hidden, activ, mlp_out = mlp_forward(pre_mlp, fc1_n, fc1_f, fc2_n, fc2_f)
+    result = ((stream2 + mlp_out) * live).astype(BF)
+
+    def halves(left, right):
+        near = mix("md,pmn->pdn", left[:, : left.shape[1] // 2], right)
+        far = mix("md,pmn->pdn", left[:, left.shape[1] // 2 :], right).astype(BF)
+        return near, far
+
+    def settle(value):
+        return lax.psum_scatter(value, "sp", scatter_dimension=0, tiled=False)
+
+    d_fc1_n, d_fc1_f, d_fc2_n, d_fc2_f, d_pre_mlp = mlp_backward(
+        d_mlp, pre_mlp, hidden, activ, fc1_n, fc1_f, fc2_n, fc2_f
+    )
+    sum_fc2 = cube.scatter(d_fc2_n, d_fc2_f, 1)
+    sum_fc1 = cube.scatter(d_fc1_n, d_fc1_f, 0)
+    fc2_1, fc1_1 = next(sum_fc2), next(sum_fc1)
+    d_stream2, d_gain_mlp = norm_back(stream2, g_mlp, d_pre_mlp)
     grad2 = grad3 + d_stream2
     d_cross = grad2.astype(BF)
-    term_out2 = term(d_cross, crossed, 1)
+    out2_n, out2_f = halves(d_cross, crossed)
     d_crossed = mix("mn,pnk->pmk", d_cross, out2_w).astype(BF)
     d_query2, d_text_kv = cross_backward(
         query2, text_kv, lengths, d_crossed.reshape(parts, micros, slots, lanes)
     )
     d_query2 = d_query2.reshape(parts, rows, lanes)
     d_text_kv = d_text_kv.reshape(parts, micros * words, 2 * lanes)
-    term_text = term(text_all, d_text_kv, 0)
-    d_words = mix("pmn,pkn->mk", d_text_kv, text_w).astype(BF)
-    d_words = lax.psum_scatter(
-        d_words.reshape(micros, words, features), "sp", scatter_dimension=1, tiled=True
-    )
-    d_words = jnp.dot(d_words.reshape(-1, features), text_turn.T, preferred_element_type=F32)
-    term_query2 = term(pre_cross, d_query2, 1)
+    fc2_2, fc1_2 = next(sum_fc2), next(sum_fc1)
+    sum_out2 = cube.scatter(out2_n, out2_f, 1)
+    out2_1 = next(sum_out2)
+    query2_n, query2_f = halves(pre_cross, d_query2)
+    sum_query2 = cube.scatter(query2_n, query2_f, 0)
+    query2_1 = next(sum_query2)
     d_stream1, d_gain_cross = norm_back(stream1, g_cross, mix("pmn,pkn->mk", d_query2, query2_w))
     grad1 = grad2 + d_stream1
     d_attn = grad1.astype(BF)
-    term_out1 = term(d_attn, attended, 0)
     d_attended = mix("mn,pnk->pmk", d_attn, out1_w).astype(BF)
     d_heads = exchange(d_attended.reshape(parts, micros, slots, lanes))
+    text_n, text_f = halves(text_all, d_text_kv)
+    sum_text = cube.scatter(text_n, text_f, 1)
+    text_1 = next(sum_text)
+    out1_n, out1_f = halves(d_attn, attended)
+    sum_out1 = cube.scatter(out1_n, out1_f, 0)
+    out1_1 = next(sum_out1)
+    d_words = mix("pmn,pkn->mk", d_text_kv, text_w).astype(BF).reshape(micros, parts, text_slots, features)
+    d_words = jnp.transpose(d_words, (1, 0, 2, 3)).reshape(parts, micros * text_slots, features)
+    d_words = settle(d_words)
     d_raw, d_gain_q, d_gain_k = self_backward(
         raw, counts, cosine, sine, gain_q, gain_k, turned_q, turned_k, norms, d_heads
     )
     d_projected = exchange(d_raw).reshape(parts, rows, 3 * lanes)
-    term_qkv = term(pre_attn, d_projected, 1)
+    fc2_3, fc1_3 = next(sum_fc2), next(sum_fc1)
+    fc2_4, fc1_4 = next(sum_fc2), next(sum_fc1)
+    term_fc2, term_fc1 = settle(fc2_4), settle(fc1_4)
+    for stage in range(len(cube.outer)):
+        out2_1, query2_1, text_1, out1_1 = (
+            next(value) for value in (sum_out2, sum_query2, sum_text, sum_out1)
+        )
+    cross_1 = [next(value) for value in (sum_out1, sum_query2, sum_out2)]
+    term_cross = settle(jnp.concatenate(cross_1, 2))
+    term_text = settle(next(sum_text))
+    d_words = jnp.dot(d_words, text_turn.T, preferred_element_type=F32)
+
     d_pre = mix("pmn,pkn->mk", d_projected, qkv_w)
     d_shift = jnp.sum(d_pre.reshape(micros, slots, width), 1)
     d_stream0, d_gain_attn = norm_back(stream, g_attn, d_pre)
     d_base, d_gain_skip = norm_back(base, g_skip, grad1 + d_stream0)
     d_base = d_base.astype(BF)
-    term_skip = term(d_base, joined, 0)
-    d_joined = mix("mn,pnk->pmk", d_base, skip_w).reshape(2, parts // 2, rows, half)
+
+    def split_term(left, right, cut):
+        for part, flip in ((right[:, :, :cut], 0), (right[:, :, cut:], 1)):
+            yield cube.scatter(*halves(left, part), flip)
+
+    def finish(sums):
+        values = [list(value)[-1] for value in sums]
+        return settle(jnp.concatenate(values, 2))
+
+    term_qkv = finish(split_term(pre_attn, d_projected, (3 * lanes) // 256 * 128 + 128))
+    term_skip = finish(split_term(d_base, joined, (half + skip_pad) // 2))
+    d_joined = mix("mn,pnk->pmk", d_base, skip_w)[:, :, :half].reshape(2, parts // 2, rows, half)
     d_joined = jnp.transpose(d_joined, (0, 2, 1, 3)).reshape(2, micros, slots, width)
-
-    back = jnp.argsort(owners)
-    d_shift = jnp.transpose(d_shift.reshape(micros, ranks, strip), (1, 0, 2))[back]
-    d_shift = lax.all_to_all(d_shift, "dp", split_axis=0, concat_axis=0, tiled=True)
-    d_shift = lax.psum(d_shift, "sp").reshape(ranks * micros, strip)
+    result = jnp.dot(result, turn.T, preferred_element_type=F32).astype(BF)
+
+    d_shift = d_shift.reshape(micros, ranks, strip)
+    d_shift = jnp.stack([d_shift[:, cube.masks.index(mask)] for mask in range(ranks)])
+    d_shift = cube.add(cube.trade(d_shift), "sp").reshape(ranks * micros, strip)
     term_mod = lax.dot_general(
         time_part.astype(F32), d_shift, (((0,), (0,)), ((), ())), precision=lax.Precision.HIGHEST
     )
 
+    places = jnp.array([cube.masks.index(mask) for mask in range(ranks)], jnp.int32)
+    places = places[jnp.arange(ranks, dtype=jnp.int32) ^ cube.rank]
     gains = jnp.stack([d_gain_skip, d_gain_attn, d_gain_cross, d_gain_mlp])
-    gains = gains.reshape(4, ranks, strip)[:, back].reshape(4, width)
+    gains = gains.reshape(4, ranks, strip)[:, places].reshape(-1)
     heads = jnp.stack([jnp.sum(d_gain_q, (0, 1)), jnp.sum(d_gain_k, (0, 1))])
     heads = jnp.sum(heads.reshape(2, local, HP)[:, :, :HD], 1)
-    packed = jnp.concatenate([gains.reshape(-1), heads.reshape(-1)])
-    packed = lax.psum(packed, ("dp", "sp"))
+    packed = jnp.concatenate([gains, heads.reshape(-1)])
+    packed = cube.add(cube.add(packed, "sp"), "dp")
     gains = packed[: 4 * width].reshape(4, ranks * parts, -1)
     gains = lax.dynamic_index_in_dim(gains, cube.rank * parts + zone, 1, keepdims=False)
     heads = packed[4 * width :].reshape(2, HD)
 
     def whole(term, groups):
-        return cut_heads(term).reshape(term.shape[0], groups, -1)
+        return cut_heads(term.astype(F32)).reshape(term.shape[0], groups, -1)
 
     return (
         result.reshape(tokens.shape),
         d_joined[0],
         d_joined[1],
         d_words.reshape(text.shape),
-        term_skip.T,
+        term_skip.astype(F32)[:, :half].T,
         term_mod,
         whole(term_qkv, 3),
-        cut_heads(term_out1).T,
-        cut_heads(term_query2),
+        cut_heads(term_cross[:, :lanes].astype(F32)).T,
+        cut_heads(term_cross[:, lanes : 2 * lanes].astype(F32)),
         whole(term_text, 2),
-        cut_heads(term_out2).T,
-        term_fc1,
-        term_fc2.T,
+        cut_heads(term_cross[:, 2 * lanes :].astype(F32)).T,
+        term_fc1.astype(F32),
+        term_fc2.astype(F32).T,
         gains[0],
         gains[1],
         gains[2],

time: 1810 us -> 1610 us (0.89)
  blocking collectives: 341 us -> 0 us
  waiting for transfers between devices: 467 us -> 712 us
  matrix products: 287 us -> 150 us
  local copies, waits for them, and re-layouts: 303 us -> 187 us
  Pallas kernels: 120 us -> 204 us
  other arithmetic: 133 us -> 177 us
  starting transfers between devices: 122 us -> 153 us
    all_gather x5 -> x0, blocking collectives: 197 us -> none  [spread(): return lax.all_gather(shard, 'sp', axis=0, tiled=False)]
    ppermute x56 -> x88, waiting for transfers between devices: 424 us -> 603 us  [swap(): return lax.ppermute(value, axis, pairs)]
    dot_general x32 -> x28, matrix products: 275 us -> 136 us  [mix(): return jnp.einsum(spec, left, right, preferred_element_type=F32)]
    pallas_call x0 -> x2, Pallas kernels: none -> 84 us  [the longest x1 54.2 us: mlp_backward(): pl.pallas_call(kernel, name='mlp_backward', grid=(parts, steps), in_specs...]
    psum x3 -> x0, blocking collectives: 79 us -> none  [the longest x1 41.3 us: on_device(): packed = lax.psum(packed, ('dp', 'sp'))]
    unnamed x1 -> x0, blocking collectives: 65.1 us -> none
    concatenate x8 -> x11, local copies, waits for them, and re-layouts: 79.6 us -> 28 us  [the longest x8 24.8 us: join(): return jnp.concatenate([near, far], 1)]
    ppermute x56 -> x88, starting transfers between devices: 92.2 us -> 135 us  [swap(): return lax.ppermute(value, axis, pairs)]
  transfers between devices with their start and end apart: 75 -> 106, of which waited for: 21 -> 47; matrix products, arithmetic and copies ran while one was open for 33% -> 28% of each run, Pallas kernels for 5% -> 6%
where the time goes in v2:
time: 1610 us; the launch traced here: 1600 us
  waiting for transfers between devices  712 us (44%)
  Pallas kernels  204 us (13%)
  local copies, waits for them, and re-layouts  187 us (12%)
  other arithmetic  177 us (11%)
  starting transfers between devices  153 us (10%)
  matrix products  150 us (9%)
  between operations  17 us (1%)
    ppermute x88, waiting for transfers between devices, swap(): return lax.ppermute(value, axis, pairs)  603 us
    dot_general x28, matrix products, mix(): return jnp.einsum(spec, left, right, preferred_element_type=F32)  136 us
    ppermute x88, starting transfers between devices, swap(): return lax.ppermute(value, axis, pairs)  135 us
    unnamed x352, local copies, waits for them, and re-layouts  79.2 us
    all_gather x6, waiting for transfers between devices, on_device(): spread.append(lax.all_gather(shard, 'sp', axis=0, tiled=False))  70.3 us
    convert_element_type x30, other arithmetic, total(): return value.astype(BF)  63.1 us
    pallas_call x1, Pallas kernels, mlp_backward(): pl.pallas_call(kernel, name='mlp_backward', grid=(parts, steps), in_specs...  54.2 us
    pallas_call x1, Pallas kernels, self_backward(): pl.pallas_call(kernel, name='self_backward', grid_spec=pltpu.PrefetchScal...  50.7 us
  transfers between devices with their start and end apart: 106, of which 47 were waited for; matrix products, arithmetic and copies ran while one was open for 28% of the time, Pallas kernels for 6%

profile of v2, /device:TPU:0, one launch (start us, length us, event | category | flops | bytes accessed | tf_op | source)
XLA Modules:
  0.0 1599.9 jit_solution(16446478715599644434)
XLA Ops:
  11.6 29.9 %all-gather.15.cloned.1.call-done = bf16[704,768]{1,0:T(8,128)(2,1)} async-done(((bf16[176,768]{1,0:T(8,128)(2,1)}), bf16[704,768]{1,0:T(8,128)(2,1)}) %all-gather.15.cloned.1.call-update) | async-done | bytes 1081360 | tf_op jit(solution)/shard_map/all_gather | solution.py:694
  100.7 10.4 collective-permute-done.5
  124.9 10.5 collective-permute-done.6
  151.7 9.7 collective-permute-done.13
  190.6 11.6 collective-permute-done.10
  243.2 11.3 fusion.6
  262.5 32.2 %all-gather.27.cloned.1.call-done = bf16[704,1536]{1,0:T(8,128)(2,1)} async-done(((bf16[176,1536]{1,0:T(8,128)(2,1)}), bf16[704,1536]{1,0:T(8,128)(2,1)}) %all-gather.27.cloned.1.call-update) | async-done | bytes 2162704 | tf_op jit(solution)/shard_map/all_gather | solution.py:694
  306.7 14.8 collective-permute-done.24
  324.6 32.2 %collective-permute-done.25 = bf16[4,176,384]{2,1,0:T(8,128)(2,1)S(1)} collective-permute-done((bf16[4,176,384]{2,1,0:T(8,128)(2,1)S(1)}, bf16[4,176,384]{2,1,0:T(8,128)(2,1)S(1)}, u32[]{:S(2)}, u32[]{:S(2)}) %collective-permute-start.25) | collective-permute-done | bytes 540704 | tf_op jit(solution)/shard_map/ppermute | solution.py:583
  370.5 13.9 negate_select_fusion
  415.0 73.1 %collective-permute-done.37 = bf16[4,176,384]{2,1,0:T(8,128)(2,1)S(1)} collective-permute-done((bf16[4,176,384]{2,1,0:T(8,128)(2,1)S(1)}, bf16[4,176,384]{2,1,0:T(8,128)(2,1)S(1)}, u32[]{:S(2)}, u32[]{:S(2)}) %collective-permute-start.37) | collective-permute-done | bytes 540704 | tf_op jit(solution)/shard_map/ppermute | solution.py:583
  521.8 10.1 collective-permute-done.30
  541.0 34.3 %self_forward.1 = (bf16[4,2,256,384]{3,2,1,0:T(8,128)(2,1)}, bf16[2,1024,384]{2,1,0:T(8,128)(2,1)S(1)}, bf16[2,1024,384]{2,1,0:T(8,128)(2,1)S(1)}, f32[2,4,1024]{2,1,0:T(4,128)S(1)}) custom-call(s32[2]{0:T(128)S(1)} %mul.291.count_ref, bf16[4,2,256,1152]{3,2,1,0:T(8,128)(2,1)} %all-to-all-done.raw_ref, f32[2,1024,384]{2,1,0:T(8,128)} %get-tuple-element.260.cos_ref, ...), custom_call_target="tpu_custom_call" | custom-call | flops 3221225472 | bytes 15728640 | tf_op jit(solution)/shard_map/self_forward/pallas_call | solution.py:170
  634.7 16.3 %cross_forward.1 = bf16[4,2,256,384]{3,2,1,0:T(8,128)(2,1)S(1)} custom-call(s32[2,2]{1,0:T(2,128)S(1)} %bitcast.342, bf16[4,2,256,384]{3,2,1,0:T(8,128)(2,1)S(1)} %bitcast.331, bf16[4,2,336,768]{3,2,1,0:T(8,128)(2,1)S(1)} %bitcast.336), custom_call_target="tpu_custom_call" | custom-call | flops 1056964608 | bytes 7274496 | tf_op jit(solution)/shard_map/cross_forward/pallas_call | solution.py:348
  657.7 29.8 %mlp_forward.1 = (f32[4,512,1536]{2,1,0:T(8,128)}, bf16[4,512,1536]{2,1,0:T(8,128)(2,1)}, f32[512,1408]{1,0:T(8,128)S(1)}) custom-call(bf16[512,1408]{1,0:T(8,128)(2,1)S(1)} %multiply_convert_fusion.2.x_ref, bf16[4,704,1536]{2,1,0:T(8,128)(2,1)} %constant_dynamic-update-slice_fusion.48.n1_ref, bf16[4,704,1536]{2,1,0:T(8,128)(2,1)} %collective-permute-done.43.f1_ref, ...), custom_call_target="tpu_custom_call" | custom-call | flops 17716740096 | bytes 53477376 | tf_op jit(solution)/shard_map/mlp_forward/pallas_call | solution.py:458
  687.5 54.2 %mlp_backward.1 = (bf16[4,704,1536]{2,1,0:T(8,128)(2,1)}, bf16[4,704,1536]{2,1,0:T(8,128)(2,1)}, bf16[4,704,1536]{2,1,0:T(8,128)(2,1)}, bf16[4,704,1536]{2,1,0:T(8,128)(2,1)}, f32[512,1408]{1,0:T(8,128)}) custom-call(bf16[512,1408]{1,0:T(8,128)(2,1)} %get-tuple-element.303.g_ref, bf16[512,1408]{1,0:T(8,128)(2,1)} %copy-done.7, ...), custom_call_target="tpu_custom_call" | custom-call | flops 35433480192 | bytes 88080384 | tf_op jit(solution)/shard_map/mlp_backward/pallas_call | solution.py:537
  763.6 18.7 %cross_backward.1 = (bf16[4,2,256,384]{3,2,1,0:T(8,128)(2,1)S(1)}, bf16[4,2,336,768]{3,2,1,0:T(8,128)(2,1)S(1)}) custom-call(s32[2,2]{1,0:T(2,128)S(1)} %bitcast.343, bf16[4,2,256,384]{3,2,1,0:T(8,128)(2,1)S(1)} %bitcast.332, bf16[4,2,336,768]{3,2,1,0:T(8,128)(2,1)S(1)} %bitcast.337, bf16[4,2,256,384]{3,2,1,0:T(8,128)(2,1)S(1)} %bitcast.338), custom_call_target="tpu_custom_call" | custom-call | flops 2642411520 | bytes 14548992 | tf_op jit(solution)/shard_map/cross_backward/pallas_call | solution.py:397
  849.0 21.0 %all-to-all-done.2.in_ref = bf16[4,2,256,384]{3,2,1,0:T(8,128)(2,1)S(1)} async-done(((bf16[4,2,256,384]{3,2,1,0:T(8,128)(2,1)}), bf16[4,2,256,384]{3,2,1,0:T(8,128)(2,1)S(1)}, u32[]{:S(2)}, u32[]{:S(2)}) %all-to-all-start.2) | async-done | bytes 1572896 | tf_op jit(solution)/shard_map/all_to_all | solution.py:761
  871.4 50.7 %self_backward.1 = (bf16[4,2,256,1152]{3,2,1,0:T(8,128)(2,1)}, f32[2,1,384]{2,1,0:T(1,128)S(1)}, f32[2,1,384]{2,1,0:T(1,128)S(1)}) custom-call(s32[2]{0:T(128)S(1)} %copy-done.14, bf16[4,2,256,1152]{3,2,1,0:T(8,128)(2,1)} %all-to-all-done.raw_ref, f32[2,1024,384]{2,1,0:T(8,128)} %get-tuple-element.260.cos_ref, f32[2,1024,384]{2,1,0:T(8,128)} %get-tuple-element.259.sin_ref, ...), custom_call_target="tpu_custom_call" | custom-call | flops 8053063680 | bytes 22020096 | tf_op jit(solution)/shard_map/self_backward/pallas_call | solution.py:284
  927.5 12.5 collective-permute-start.66
  962.5 9.3 collective-permute-start.67
  987.0 33.5 %collective-permute-done.75 = bf16[4,256,768]{2,1,0:T(8,128)(2,1)S(1)} collective-permute-done((bf16[4,256,768]{2,1,0:T(8,128)(2,1)S(1)}, bf16[4,256,768]{2,1,0:T(8,128)(2,1)S(1)}, u32[]{:S(2)}, u32[]{:S(2)}) %collective-permute-start.75) | collective-permute-done | bytes 1572896 | tf_op jit(solution)/shard_map/ppermute | solution.py:583
  1024.5 14.6 collective-permute-done.76
  1047.7 10.6 all-to-all-done.3
  1058.3 14.2 fusion.20
  1113.3 15.6 collective-permute-start.52
  1138.7 14.3 collective-permute-done.52
  1163.7 89.5 %collective-permute-done.49 = bf16[4,352,384]{2,1,0:T(8,128)(2,1)S(1)} collective-permute-done((bf16[4,352,384]{2,1,0:T(8,128)(2,1)S(1)}, bf16[4,352,384]{2,1,0:T(8,128)(2,1)S(1)}, u32[]{:S(2)}, u32[]{:S(2)}) %collective-permute-start.49) | collective-permute-done | bytes 1081376 | tf_op jit(solution)/shard_map/ppermute | solution.py:583
  1256.1 8.7 collective-permute-done.53
  1266.7 31.5 %collective-permute-done.50 = bf16[4,176,384]{2,1,0:T(8,128)(2,1)S(1)} collective-permute-done((bf16[4,176,384]{2,1,0:T(8,128)(2,1)S(1)}, bf16[4,176,384]{2,1,0:T(8,128)(2,1)S(1)}, u32[]{:S(2)}, u32[]{:S(2)}) %collective-permute-start.50) | collective-permute-done | bytes 540704 | tf_op jit(solution)/shard_map/ppermute | solution.py:583
  1339.2 127.1 %collective-permute-done.79 = bf16[4,176,1536]{2,1,0:T(8,128)(2,1)} collective-permute-done((bf16[4,176,1536]{2,1,0:T(8,128)(2,1)}, bf16[4,176,1536]{2,1,0:T(8,128)(2,1)}, u32[]{:S(2)}, u32[]{:S(2)}) %collective-permute-start.79) | collective-permute-done | bytes 2162720 | tf_op jit(solution)/shard_map/ppermute | solution.py:583
  1497.8 28.5 %collective-permute-done.82 = bf16[4,176,1536]{2,1,0:T(8,128)(2,1)} collective-permute-done((bf16[4,176,1536]{2,1,0:T(8,128)(2,1)}, bf16[4,176,1536]{2,1,0:T(8,128)(2,1)}, u32[]{:S(2)}, u32[]{:S(2)}) %collective-permute-start.82) | collective-permute-done | bytes 2162720 | tf_op jit(solution)/shard_map/ppermute | solution.py:583
  (848 shorter events, 688.3 us)
Async XLA Ops:
  121.0 101.1 %all-gather.25.cloned.1.call-start = ((), (), s32[]{:S(2)}) async-start(), calls=%async_computation.23 | async-start | bytes 2703360 | tf_op jit(solution)/shard_map/all_gather | solution.py:694
  149.5 145.2 %all-gather.27.cloned.1.call-start = ((), (), s32[]{:S(2)}) async-start(), calls=%async_computation.24 | async-start | bytes 2703360 | tf_op jit(solution)/shard_map/all_gather | solution.py:694
  254.5 286.5 %all-to-all-start = ((bf16[4,2,256,1152]{3,2,1,0:T(8,128)(2,1)}), bf16[4,2,256,1152]{3,2,1,0:T(8,128)(2,1)}, u32[]{:S(2)}, u32[]{:S(2)}) async-start(bf16[4,2,256,1152]{3,2,1,0:T(8,128)(2,1)} %bitcast.366), calls=%async_computation | async-start | bytes 9437184 | tf_op jit(solution)/shard_map/all_to_all | solution.py:761
  260.1 134.5 %all-gather.23.cloned.1.call-start = ((), (), s32[]{:S(2)}) async-start(), calls=%async_computation.22 | async-start | bytes 1720320 | tf_op jit(solution)/shard_map/all_gather | solution.py:744
  260.1 110.3 %collective-permute-start.40 = (bf16[4,176,1536]{2,1,0:T(8,128)(2,1)}, bf16[4,176,1536]{2,1,0:T(8,128)(2,1)}, u32[]{:S(2)}, u32[]{:S(2)}) collective-permute-start(bf16[4,176,1536]{2,1,0:T(8,128)(2,1)} %bitcast.57), channel_id=1, source_target_pairs={{0,8},{4,12},{8,0},{12,4},{16,24},{20,28},{24,16},{28,20},{1,9},{5... | collective-permute-start | bytes 6488072 | tf_op jit(solution)/shard_map/ppermute | solution.py:583
  294.7 92.7 %collective-permute-start.45 = (bf16[4,176,1536]{2,1,0:T(8,128)(2,1)}, bf16[4,176,1536]{2,1,0:T(8,128)(2,1)}, u32[]{:S(2)}, u32[]{:S(2)}) collective-permute-start(bf16[4,176,1536]{2,1,0:T(8,128)(2,1)} %bitcast.58), channel_id=1, source_target_pairs={{0,16},{4,20},{8,24},{12,28},{16,0},{20,4},{24,8},{28,12},{1,17},{... | collective-permute-start | bytes 6488072 | tf_op jit(solution)/shard_map/ppermute | solution.py:583
  368.3 122.9 %collective-permute-start.41 = (bf16[4,176,1536]{2,1,0:T(8,128)(2,1)}, bf16[4,176,1536]{2,1,0:T(8,128)(2,1)}, u32[]{:S(2)}, u32[]{:S(2)}) collective-permute-start(bf16[4,176,1536]{2,1,0:T(8,128)(2,1)} %bitcast.57), channel_id=1, source_target_pairs={{0,16},{4,20},{8,24},{12,28},{16,0},{20,4},{24,8},{28,12},{1,17},{... | collective-permute-start | bytes 6488072 | tf_op jit(solution)/shard_map/ppermute | solution.py:583
  370.4 122.6 %collective-permute-start.42 = (bf16[4,176,1536]{2,1,0:T(8,128)(2,1)}, bf16[4,176,1536]{2,1,0:T(8,128)(2,1)}, u32[]{:S(2)}, u32[]{:S(2)}) collective-permute-start(bf16[4,176,1536]{2,1,0:T(8,128)(2,1)} %collective-permute-done.40), channel_id=1, source_target_pairs={{0,16},{4,20},{8,24},{12,28},{16,0},{20,4},{24,8},{28,12},{1,17},{... | collective-permute-start | bytes 6488072 | tf_op jit(solution)/shard_map/ppermute | solution.py:583
  387.4 122.5 %collective-permute-start.44 = (bf16[4,176,1536]{2,1,0:T(8,128)(2,1)}, bf16[4,176,1536]{2,1,0:T(8,128)(2,1)}, u32[]{:S(2)}, u32[]{:S(2)}) collective-permute-start(bf16[4,176,1536]{2,1,0:T(8,128)(2,1)} %bitcast.58), channel_id=1, source_target_pairs={{0,8},{4,12},{8,0},{12,4},{16,24},{20,28},{24,16},{28,20},{1,9},{5... | collective-permute-start | bytes 6488072 | tf_op jit(solution)/shard_map/ppermute | solution.py:583
  387.4 122.7 %collective-permute-start.46 = (bf16[4,176,1536]{2,1,0:T(8,128)(2,1)}, bf16[4,176,1536]{2,1,0:T(8,128)(2,1)}, u32[]{:S(2)}, u32[]{:S(2)}) collective-permute-start(bf16[4,176,1536]{2,1,0:T(8,128)(2,1)} %collective-permute-done.45), channel_id=1, source_target_pairs={{0,8},{4,12},{8,0},{12,4},{16,24},{20,28},{24,16},{28,20},{1,9},{5... | collective-permute-start | bytes 6488072 | tf_op jit(solution)/shard_map/ppermute | solution.py:583
  510.1 89.2 %collective-permute-start.35 = (bf16[4,512,768]{2,1,0:T(8,128)(2,1)}, bf16[4,512,768]{2,1,0:T(8,128)(2,1)}, u32[]{:S(2)}, u32[]{:S(2)}) collective-permute-start(bf16[4,512,768]{2,1,0:T(8,128)(2,1)} %pad_maximum_fusion.14), channel_id=1, source_target_pairs={{0,4},{4,0},{8,12},{12,8},{16,20},{20,16},{24,28},{28,24},{1,5},{5... | collective-permute-start | bytes 9437192 | tf_op jit(solution)/shard_map/ppermute | solution.py:583
  521.8 135.2 %collective-permute-start.43 = (bf16[4,704,1536]{2,1,0:T(8,128)(2,1)}, bf16[4,704,1536]{2,1,0:T(8,128)(2,1)}, u32[]{:S(2)}, u32[]{:S(2)}) collective-permute-start(bf16[4,704,1536]{2,1,0:T(8,128)(2,1)} %constant_dynamic-update-slice_fusion.48.n1_ref), channel_id=1, source_target_pairs={{0,4},{4,0},{8,12},{12,8},{16,20},{20,16},{24,28},{28,24},{1,5},{5... | collective-permute-start | bytes 25952264 | tf_op jit(solution)/shard_map/ppermute | solution.py:583
  531.9 125.7 %collective-permute-start.47 = (bf16[4,704,1536]{2,1,0:T(8,128)(2,1)}, bf16[4,704,1536]{2,1,0:T(8,128)(2,1)}, u32[]{:S(2)}, u32[]{:S(2)}) collective-permute-start(bf16[4,704,1536]{2,1,0:T(8,128)(2,1)} %pad_maximum_fusion.2.n2_ref), channel_id=1, source_target_pairs={{0,4},{4,0},{8,12},{12,8},{16,20},{20,16},{24,28},{28,24},{1,5},{5... | collective-permute-start | bytes 25952264 | tf_op jit(solution)/shard_map/ppermute | solution.py:583
  812.8 672.5 %reduce-scatter.8.cloned.1.call-start = ((), (), s32[]{:S(2)}) async-start(), calls=%async_computation.11 | async-start | bytes 1720320 | tf_op jit(solution)/shard_map/reduce_scatter | solution.py:784
  828.4 155.4 %collective-permute-start.74 = (bf16[4,512,768]{2,1,0:T(8,128)(2,1)}, bf16[4,512,768]{2,1,0:T(8,128)(2,1)}, u32[]{:S(2)}, u32[]{:S(2)}) collective-permute-start(bf16[4,512,768]{2,1,0:T(8,128)(2,1)} %convert_bitcast_fusion.1), channel_id=1, source_target_pairs={{0,4},{4,0},{8,12},{12,8},{16,20},{20,16},{24,28},{28,24},{1,5},{5... | collective-permute-start | bytes 9437192 | tf_op jit(solution)/shard_map/ppermute | solution.py:583
  828.5 213.7 %collective-permute-start.77 = (bf16[4,704,1536]{2,1,0:T(8,128)(2,1)}, bf16[4,704,1536]{2,1,0:T(8,128)(2,1)}, u32[]{:S(2)}, u32[]{:S(2)}) collective-permute-start(bf16[4,704,1536]{2,1,0:T(8,128)(2,1)} %get-tuple-element.68), channel_id=1, source_target_pairs={{0,4},{4,0},{8,12},{12,8},{16,20},{20,16},{24,28},{28,24},{1,5},{5... | collective-permute-start | bytes 25952264 | tf_op jit(solution)/shard_map/ppermute | solution.py:583
  837.7 109.3 %collective-permute-start.72 = (bf16[4,352,384]{2,1,0:T(8,128)(2,1)}, bf16[4,352,384]{2,1,0:T(8,128)(2,1)}, u32[]{:S(2)}, u32[]{:S(2)}) collective-permute-start(bf16[4,352,384]{2,1,0:T(8,128)(2,1)} %pad_maximum_fusion.33), channel_id=1, source_target_pairs={{0,8},{4,12},{8,0},{12,4},{16,24},{20,28},{24,16},{28,20},{1,9},{5... | collective-permute-start | bytes 3244040 | tf_op jit(solution)/shard_map/ppermute | solution.py:583
  844.7 105.3 %collective-permute-start.69 = (bf16[4,352,384]{2,1,0:T(8,128)(2,1)}, bf16[4,352,384]{2,1,0:T(8,128)(2,1)}, u32[]{:S(2)}, u32[]{:S(2)}) collective-permute-start(bf16[4,352,384]{2,1,0:T(8,128)(2,1)} %pad_maximum_fusion.32), channel_id=1, source_target_pairs={{0,16},{4,20},{8,24},{12,28},{16,0},{20,4},{24,8},{28,12},{1,17},{... | collective-permute-start | bytes 3244040 | tf_op jit(solution)/shard_map/ppermute | solution.py:583
  922.1 136.2 %all-to-all-start.3 = ((bf16[4,2,256,1152]{3,2,1,0:T(8,128)(2,1)}), bf16[4,2,256,1152]{3,2,1,0:T(8,128)(2,1)}, u32[]{:S(2)}, u32[]{:S(2)}) async-start(bf16[4,2,256,1152]{3,2,1,0:T(8,128)(2,1)} %get-tuple-element.65), calls=%async_computation.3 | async-start | bytes 9437184 | tf_op jit(solution)/shard_map/all_to_all | solution.py:761
  927.3 561.5 %reduce-scatter.14.cloned.1.call-start = ((), (), s32[]{:S(2)}) async-start(), calls=%async_computation.14 | async-start | bytes 2027520 | tf_op jit(solution)/shard_map/reduce_scatter | solution.py:784
  983.6 512.1 %reduce-scatter.16.cloned.1.call-start = ((), (), s32[]{:S(2)}) async-start(), calls=%async_computation.15 | async-start | bytes 983040 | tf_op jit(solution)/shard_map/reduce_scatter | solution.py:784
  1024.5 283.1 %collective-permute-start.80 = (bf16[4,704,1536]{2,1,0:T(8,128)(2,1)}, bf16[4,704,1536]{2,1,0:T(8,128)(2,1)}, u32[]{:S(2)}, u32[]{:S(2)}) collective-permute-start(bf16[4,704,1536]{2,1,0:T(8,128)(2,1)} %get-tuple-element.70), channel_id=1, source_target_pairs={{0,4},{4,0},{8,12},{12,8},{16,20},{20,16},{24,28},{28,24},{1,5},{5... | collective-permute-start | bytes 25952264 | tf_op jit(solution)/shard_map/ppermute | solution.py:583
  1042.2 538.6 %reduce-scatter.10.cloned.1.call-start = ((), (), s32[]{:S(2)}) async-start(), calls=%async_computation.12 | async-start | bytes 1351680 | tf_op jit(solution)/shard_map/reduce_scatter | solution.py:784
  1130.3 202.5 %collective-permute-start.78 = (bf16[4,352,1536]{2,1,0:T(8,128)(2,1)}, bf16[4,352,1536]{2,1,0:T(8,128)(2,1)}, u32[]{:S(2)}, u32[]{:S(2)}) collective-permute-start(bf16[4,352,1536]{2,1,0:T(8,128)(2,1)} %pad_maximum_fusion.9), channel_id=1, source_target_pairs={{0,16},{4,20},{8,24},{12,28},{16,0},{20,4},{24,8},{28,12},{1,17},{... | collective-permute-start | bytes 12976136 | tf_op jit(solution)/shard_map/ppermute | solution.py:583
  1137.1 116.0 %collective-permute-start.49 = (bf16[4,352,384]{2,1,0:T(8,128)(2,1)S(1)}, bf16[4,352,384]{2,1,0:T(8,128)(2,1)S(1)}, u32[]{:S(2)}, u32[]{:S(2)}) collective-permute-start(bf16[4,352,384]{2,1,0:T(8,128)(2,1)S(1)} %pad_maximum_fusion.28), channel_id=1, source_target_pairs={{0,16},{4,20},{8,24},{12,28},{16,0},{20,4},{24,8},{28,12},{1,17},{... | collective-permute-start | bytes 3244040 | tf_op jit(solution)/shard_map/ppermute | solution.py:583
  1153.1 111.6 %collective-permute-start.53 = (bf16[4,176,384]{2,1,0:T(8,128)(2,1)S(1)}, bf16[4,176,384]{2,1,0:T(8,128)(2,1)S(1)}, u32[]{:S(2)}, u32[]{:S(2)}) collective-permute-start(bf16[4,176,384]{2,1,0:T(8,128)(2,1)S(1)} %fusion.87), channel_id=1, source_target_pairs={{0,16},{4,20},{8,24},{12,28},{16,0},{20,4},{24,8},{28,12},{1,17},{... | collective-permute-start | bytes 1622024 | tf_op jit(solution)/shard_map/ppermute | solution.py:583
  1162.3 141.9 %collective-permute-start.60 = (bf16[4,352,640]{2,1,0:T(8,128)(2,1)S(1)}, bf16[4,352,640]{2,1,0:T(8,128)(2,1)}, u32[]{:S(2)}, u32[]{:S(2)}) collective-permute-start(bf16[4,352,640]{2,1,0:T(8,128)(2,1)S(1)} %pad_maximum_fusion.23), channel_id=1, source_target_pairs={{0,16},{4,20},{8,24},{12,28},{16,0},{20,4},{24,8},{28,12},{1,17},{... | collective-permute-start | bytes 5406728 | tf_op jit(solution)/shard_map/ppermute | solution.py:583
  1300.5 282.0 %reduce-scatter.12.cloned.1.call-start = ((), (), s32[]{:S(2)}) async-start(), calls=%async_computation.13 | async-start | bytes 2027520 | tf_op jit(solution)/shard_map/reduce_scatter | solution.py:784
  1314.2 159.2 %collective-permute-start.81 = (bf16[4,352,1536]{2,1,0:T(8,128)(2,1)}, bf16[4,352,1536]{2,1,0:T(8,128)(2,1)}, u32[]{:S(2)}, u32[]{:S(2)}) collective-permute-start(bf16[4,352,1536]{2,1,0:T(8,128)(2,1)} %pad_maximum_fusion.10), channel_id=1, source_target_pairs={{0,8},{4,12},{8,0},{12,4},{16,24},{20,28},{24,16},{28,20},{1,9},{5... | collective-permute-start | bytes 12976136 | tf_op jit(solution)/shard_map/ppermute | solution.py:583
  1332.7 255.9 %reduce-scatter.18.cloned.1.call-start = ((), (), s32[]{:S(2)}) async-start(), calls=%async_computation.16 | async-start | bytes 2703360 | tf_op jit(solution)/shard_map/reduce_scatter | solution.py:784
  1337.9 128.4 %collective-permute-start.79 = (bf16[4,176,1536]{2,1,0:T(8,128)(2,1)}, bf16[4,176,1536]{2,1,0:T(8,128)(2,1)}, u32[]{:S(2)}, u32[]{:S(2)}) collective-permute-start(bf16[4,176,1536]{2,1,0:T(8,128)(2,1)} %add_convert_fusion.5), channel_id=1, source_target_pairs={{0,8},{4,12},{8,0},{12,4},{16,24},{20,28},{24,16},{28,20},{1,9},{5... | collective-permute-start | bytes 6488072 | tf_op jit(solution)/shard_map/ppermute | solution.py:583
  1472.4 118.4 %reduce-scatter.20.cloned.1.call-start = ((), (), s32[]{:S(2)}) async-start(), calls=%async_computation.17 | async-start | bytes 2703360 | tf_op jit(solution)/shard_map/reduce_scatter | solution.py:784
  (229 other events, 7130.4 us)
Sparse Core Ops, SparseCore 0:
  10.3 31.1 all-gather.14
  43.6 37.3 all-gather.16
  83.2 36.9 all-gather.18
  122.1 27.3 all-gather.20
  150.9 46.7 all-gather.24
  222.2 72.4 all-gather.26
  296.8 68.2 all-gather.22
  820.3 51.3 reduce-scatter.7
  983.7 60.6 reduce-scatter.13
  1047.1 35.2 reduce-scatter.15
  1300.7 25.5 reduce-scatter.9
  1332.8 34.2 reduce-scatter.11
  1472.5 42.8 reduce-scatter.17
  1532.5 43.8 reduce-scatter.19

commit v3 on v2

--- a/solution.py
+++ b/solution.py
@@ -423,13 +423,17 @@
     )(lengths, query, text_kv, incoming)
 
 
-def mlp_forward(rows_in, near1, far1, near2, far2):
+def mlp_forward(rows_in, grads, near1, far1, near2, far2):
     rows, width = rows_in.shape
     parts, half, ff = near1.shape
-    step = 512 if ff % 512 == 0 else ff
+    step = 384 if ff % 384 == 0 else ff
     steps = ff // step
 
-    def kernel(x_ref, n1_ref, f1_ref, n2_ref, f2_ref, hid_ref, act_ref, out_ref, xa, xb, ya, yb):
+    def kernel(
+        x_ref, g_ref, n1_ref, f1_ref, n2_ref, f2_ref,
+        hid_ref, act_ref, out_ref, dn2_ref, df2_ref,
+        xa, xb, gta, gtb, ya, yb,
+    ):
         first = (pl.program_id(0) == 0) & (pl.program_id(1) == 0)
         last = (pl.program_id(0) == parts - 1) & (pl.program_id(1) == steps - 1)
 
@@ -437,6 +441,8 @@
         def _():
             xa[...] = x_ref[:, :half]
             xb[...] = x_ref[:, half:]
+            gta[...] = jnp.transpose(g_ref[:, :half])
+            gtb[...] = jnp.transpose(g_ref[:, half:])
             ya[...] = jnp.zeros_like(ya)
             yb[...] = jnp.zeros_like(yb)
 
@@ -446,6 +452,8 @@
         act_ref[0] = activ
         ya[...] += dot_nt(activ, n2_ref[0])
         yb[...] += dot_nt(activ, f2_ref[0])
+        dn2_ref[0] = dot_nn(gta[...], activ).astype(BF)
+        df2_ref[0] = dot_nn(gtb[...], activ).astype(BF)
 
         @pl.when(last)
         def _():
@@ -455,30 +463,35 @@
     weight = pl.BlockSpec((1, half, step), lambda p, n: (p, 0, n))
     unit = pl.BlockSpec((1, rows, step), lambda p, n: (p, 0, n))
     whole = pl.BlockSpec((rows, width), lambda p, n: (0, 0))
+    grad = jax.ShapeDtypeStruct((parts, half, ff), BF)
     return pl.pallas_call(
         kernel,
         name="mlp_forward",
         grid=(parts, steps),
-        in_specs=[whole, weight, weight, weight, weight],
-        out_specs=[unit, unit, whole],
+        in_specs=[whole, whole, weight, weight, weight, weight],
+        out_specs=[unit, unit, whole, weight, weight],
         out_shape=[
             jax.ShapeDtypeStruct((parts, rows, ff), F32),
             jax.ShapeDtypeStruct((parts, rows, ff), BF),
             jax.ShapeDtypeStruct((rows, width), F32),
+            grad,
+            grad,
         ],
         scratch_shapes=[
             pltpu.VMEM((rows, half), BF),
             pltpu.VMEM((rows, half), BF),
+            pltpu.VMEM((half, rows), BF),
+            pltpu.VMEM((half, rows), BF),
             pltpu.VMEM((rows, half), F32),
             pltpu.VMEM((rows, half), F32),
         ],
         compiler_params=pltpu.CompilerParams(vmem_limit_bytes=48 << 20),
         cost_estimate=pl.CostEstimate(
-            flops=4 * rows * width * parts * ff,
-            bytes_accessed=parts * ff * (4 * width + 6 * rows),
+            flops=6 * rows * width * parts * ff,
+            bytes_accessed=parts * ff * (6 * width + 6 * rows),
             transcendentals=rows * parts * ff,
         ),
-    )(rows_in, near1, far1, near2, far2)
+    )(rows_in, grads, near1, far1, near2, far2)
 
 
 def gelu_slope(value):
@@ -490,16 +503,16 @@
     )
 
 
-def mlp_backward(grads, rows_in, hidden, activ, near1, far1, near2, far2):
+def mlp_backward(grads, rows_in, hidden, near1, far1, near2, far2):
     rows, width = rows_in.shape
     parts, half, ff = near1.shape
-    step = 512 if ff % 512 == 0 else ff
+    step = 384 if ff % 384 == 0 else ff
     steps = ff // step
 
     def kernel(
-        g_ref, x_ref, hid_ref, act_ref, n1_ref, f1_ref, n2_ref, f2_ref,
-        dn1_ref, df1_ref, dn2_ref, df2_ref, out_ref,
-        ga, gb, gta, gtb, xta, xtb, ya, yb,
+        g_ref, x_ref, hid_ref, n1_ref, f1_ref, n2_ref, f2_ref,
+        dn1_ref, df1_ref, out_ref,
+        ga, gb, xta, xtb, ya, yb,
     ):
         first = (pl.program_id(0) == 0) & (pl.program_id(1) == 0)
         last = (pl.program_id(0) == parts - 1) & (pl.program_id(1) == steps - 1)
@@ -508,17 +521,12 @@
         def _():
             ga[...] = g_ref[:, :half]
             gb[...] = g_ref[:, half:]
-            gta[...] = jnp.transpose(g_ref[:, :half])
-            gtb[...] = jnp.transpose(g_ref[:, half:])
             xta[...] = jnp.transpose(x_ref[:, :half])
             xtb[...] = jnp.transpose(x_ref[:, half:])
             ya[...] = jnp.zeros_like(ya)
             yb[...] = jnp.zeros_like(yb)
 
         d_activ = dot_nn(ga[...], n2_ref[0]) + dot_nn(gb[...], f2_ref[0])
-        activ = act_ref[0]
-        dn2_ref[0] = dot_nn(gta[...], activ).astype(BF)
-        df2_ref[0] = dot_nn(gtb[...], activ).astype(BF)
         d_hidden = (d_activ * gelu_slope(hid_ref[0])).astype(BF)
         dn1_ref[0] = dot_nn(xta[...], d_hidden).astype(BF)
         df1_ref[0] = dot_nn(xtb[...], d_hidden).astype(BF)
@@ -538,26 +546,24 @@
         kernel,
         name="mlp_backward",
         grid=(parts, steps),
-        in_specs=[whole, whole, unit, unit, weight, weight, weight, weight],
-        out_specs=[weight, weight, weight, weight, whole],
-        out_shape=[grad, grad, grad, grad, jax.ShapeDtypeStruct((rows, width), F32)],
+        in_specs=[whole, whole, unit, weight, weight, weight, weight],
+        out_specs=[weight, weight, whole],
+        out_shape=[grad, grad, jax.ShapeDtypeStruct((rows, width), F32)],
         scratch_shapes=[
             pltpu.VMEM((rows, half), BF),
             pltpu.VMEM((rows, half), BF),
             pltpu.VMEM((half, rows), BF),
             pltpu.VMEM((half, rows), BF),
-            pltpu.VMEM((half, rows), BF),
-            pltpu.VMEM((half, rows), BF),
             pltpu.VMEM((rows, half), F32),
             pltpu.VMEM((rows, half), F32),
         ],
-        compiler_params=pltpu.CompilerParams(vmem_limit_bytes=56 << 20),
+        compiler_params=pltpu.CompilerParams(vmem_limit_bytes=48 << 20),
         cost_estimate=pl.CostEstimate(
-            flops=8 * rows * width * parts * ff,
-            bytes_accessed=parts * ff * (8 * width + 6 * rows),
+            flops=6 * rows * width * parts * ff,
+            bytes_accessed=parts * ff * (6 * width + 4 * rows),
             transcendentals=rows * parts * ff,
         ),
-    )(grads, rows_in, hidden, activ, near1, far1, near2, far2)
+    )(grads, rows_in, hidden, near1, far1, near2, far2)
 
 
 def tie(*values):
@@ -582,40 +588,6 @@
         pairs = [(i, i ^ (1 << bit)) for i in range(lax.axis_size(axis))]
         return lax.ppermute(value, axis, pairs)
 
-    def gather(self, shard, flip):
-        held = [(0, shard)]
-        for bit in self.outer[::-1] if flip else self.outer:
-            held = held + [(mask | (1 << bit), self.swap(piece, bit)) for mask, piece in held]
-        held = sorted(held, key=lambda item: self.masks.index(item[0]))
-        near = jnp.concatenate([piece for mask, piece in held], 1)
-        return near, self.swap(near, 0)
-
-    def scatter(self, near, far, flip):
-        rows = near.shape[1] // (self.size // 2)
-        order = self.outer if flip else self.outer[::-1]
-        other = self.swap(far, 0)
-        yield other
-        terms = {}
-        for place in range(self.size // 2):
-            cut = slice(place * rows, (place + 1) * rows)
-            terms[self.masks[place]] = [near[:, cut], other[:, cut]]
-
-        def total(mask):
-            value = terms[mask][0].astype(F32)
-            for term in terms[mask][1:]:
-                value = value + term.astype(F32)
-            return value.astype(BF)
-
-        for bit in order:
-            send = [mask for mask in terms if mask >> bit & 1]
-            keep = [mask for mask in terms if not mask >> bit & 1]
-            got = self.swap(jnp.concatenate([total(mask) for mask in send], 1), bit)
-            yield got
-            for place, mask in enumerate(send):
-                terms[mask ^ (1 << bit)].append(got[:, place * rows : (place + 1) * rows])
-            terms = {mask: terms[mask] for mask in keep}
-        yield total(0)
-
     def trade(self, value):
         blocks = {mask: value[mask] for mask in range(self.size)}
         for bit in range(self.bits):
@@ -635,6 +607,84 @@
         for bit in range(lax.axis_size(axis).bit_length() - 1):
             value = value + self.swap(value, bit, axis)
         return value
+
+
+class Gather:
+    def __init__(self, cube, shard, flip):
+        self.cube = cube
+        self.masks = [0]
+        self.pieces = [shard]
+        self.todo = cube.outer[::-1] if flip else list(cube.outer)
+
+    def move(self):
+        bit = self.todo.pop(0)
+        self.masks = self.masks + [mask | (1 << bit) for mask in self.masks]
+        self.pieces = self.pieces + [self.cube.swap(piece, bit) for piece in self.pieces]
+
+    def join(self):
+        while self.todo:
+            self.move()
+        order = sorted(range(len(self.masks)), key=lambda i: self.cube.masks.index(self.masks[i]))
+        return jnp.concatenate([self.pieces[i] for i in order], 1)
+
+
+class Scatter:
+    def __init__(self, cube, near, far, flip):
+        self.cube = cube
+        self.todo = list(cube.outer) if flip else cube.outer[::-1]
+        self.near = near
+        self.rows = near.shape[1] // (cube.size // 2)
+        self.pieces = [cube.swap(far, 0)]
+        self.terms = None
+        self.packet = None
+
+    def absorb(self):
+        got = self.pieces[0]
+        if self.terms is None:
+            self.terms = {}
+            for place in range(self.cube.size // 2):
+                cut = slice(place * self.rows, (place + 1) * self.rows)
+                self.terms[self.cube.masks[place]] = [self.near[:, cut], got[:, cut]]
+            return
+        for place, mask in enumerate(self.sent):
+            self.terms[mask ^ self.bit].append(got[:, place * self.rows : (place + 1) * self.rows])
+            del self.terms[mask]
+
+    def total(self, mask):
+        value = self.terms[mask][0].astype(F32)
+        for term in self.terms[mask][1:]:
+            value = value + term.astype(F32)
+        return value.astype(BF)
+
+    def pack(self):
+        self.absorb()
+        self.bit = 1 << self.todo.pop(0)
+        self.sent = [mask for mask in self.terms if mask & self.bit]
+        self.pieces = [jnp.concatenate([self.total(mask) for mask in self.sent], 1)]
+        self.packet = True
+
+    def move(self):
+        if not self.packet:
+            self.pack()
+        self.pieces = [self.cube.swap(self.pieces[0], self.bit.bit_length() - 1)]
+        self.packet = None
+
+    def result(self):
+        while self.todo or self.packet:
+            self.move()
+        self.absorb()
+        return self.total(0)
+
+
+def bind(value, *movers):
+    flat = [piece for mover in movers for piece in mover.pieces]
+    held = tie(value, *flat)
+    spot = 1
+    for mover in movers:
+        count = len(mover.pieces)
+        mover.pieces = list(held[spot : spot + count])
+        spot += count
+    return held[0]
 
 
 def on_device(
@@ -678,38 +728,34 @@
     middle = width // 2
 
     skip_pad = -(-half // 256) * 256 - half
+    skip_cut = (half + skip_pad) // 2
+    qkv_cut = (3 * lanes) // 256 * 128 + 128
     text_rows = w_text_kv.shape[0]
-    shards = [
-        jnp.pad(w_skip.T, ((0, 0), (0, skip_pad))),
-        pad_heads(w_qkv.reshape(strip, -1)),
-        jnp.concatenate([pad_heads(w_out1.T), pad_heads(w_query2), pad_heads(w_out2.T)], 1),
-        jnp.pad(pad_heads(w_text_kv.reshape(text_rows, -1)), ((0, max(0, strip - text_rows)), (0, 0))),
-        w_fc1,
-        w_fc2.T,
-    ]
-    spread = []
-    for shard in shards:
-        if spread:
-            shard, spread[-1] = tie(shard, spread[-1])
-        spread.append(lax.all_gather(shard, "sp", axis=0, tiled=False))
-    skip_z, qkv_z, cross_z, text_z, fc1_z, fc2_z = spread
-
-    def join(near, far):
-        return jnp.concatenate([near, far], 1)
-
-    def split_weight(value, cut):
-        left = join(*cube.gather(value[:, :, :cut], 0))
-        right = join(*cube.gather(value[:, :, cut:], 1))
-        return jnp.concatenate([left, right], 2)
-
-    skip_w = split_weight(skip_z, (half + skip_pad) // 2)
-    qkv_w = split_weight(qkv_z, (3 * lanes) // 256 * 128 + 128)
-    out1_w = join(*cube.gather(cross_z[:, :, :lanes], 0))
-    query2_w = join(*cube.gather(cross_z[:, :, lanes : 2 * lanes], 1))
-    out2_w = join(*cube.gather(cross_z[:, :, 2 * lanes :], 0))
-    text_w = join(*cube.gather(text_z[:, :text_rows], 1))
-    fc1_n, fc1_f = cube.gather(fc1_z, 0)
-    fc2_n, fc2_f = cube.gather(fc2_z, 1)
+    hidden_cut = w_fc1.shape[1] // 2
+
+    def spread(shard, before=None):
+        if before is not None:
+            shard, before = tie(shard, before)
+        return lax.all_gather(shard, "sp", axis=0, tiled=False)
+
+    def fetch(value, cut):
+        return Gather(cube, value[:, :, :cut], 0), Gather(cube, value[:, :, cut:], 1)
+
+    def rows_of(mover):
+        near = mover.join()
+        return jnp.concatenate([near, cube.swap(near, 0)], 1)
+
+    skip_z = spread(jnp.pad(w_skip.T, ((0, 0), (0, skip_pad))))
+    skip_m = fetch(skip_z, skip_cut)
+    for mover in skip_m:
+        mover.move()
+    qkv_z = spread(pad_heads(w_qkv.reshape(strip, -1)), skip_z)
+    fc1_z = spread(w_fc1, qkv_z)
+    fc2_z = spread(w_fc2.T, fc1_z)
+    qkv_m = fetch(qkv_z, qkv_cut)
+    skip_w = jnp.concatenate([rows_of(mover) for mover in skip_m], 2)
+    for mover in qkv_m:
+        mover.move()
 
     gains = jnp.stack([gain_skip, gain_attn, gain_cross, gain_mlp])
     gains = gains.reshape(4, ranks, strip)[:, cube.owners].reshape(4, width)
@@ -740,11 +786,6 @@
     shift = cube.trade(cube.add(shift, "sp").reshape(ranks, micros, strip))
     shift = jnp.stack([shift[mask] for mask in cube.masks], 1).reshape(micros, width)
 
-    text_own = jnp.dot(text.reshape(-1, features), text_turn, preferred_element_type=F32).astype(BF)
-    text_all = lax.all_gather(text_own, "sp", axis=0, tiled=False)
-    text_all = jnp.transpose(text_all.reshape(parts, micros, text_slots, features), (1, 0, 2, 3))
-    text_all = text_all.reshape(micros * words, features)
-
     grad3 = jnp.dot(cotangent.reshape(rows, width), turn, preferred_element_type=F32) * live
     d_mlp = grad3.astype(BF)
 
@@ -755,102 +796,151 @@
     stream = norm_rows(base, g_skip)
     pre_attn = norm_rows(stream, g_attn).reshape(micros, slots, width) + shift[:, None, :]
     pre_attn = pre_attn.reshape(rows, width).astype(BF)
+    pre_attn = bind(pre_attn, *qkv_m)
+    qkv_w = jnp.concatenate([rows_of(mover) for mover in qkv_m], 2)
+    fc_m = fetch(fc1_z, hidden_cut) + fetch(fc2_z, hidden_cut)[::-1]
     projected = mix("mk,pkn->pmn", pre_attn, qkv_w).astype(BF)
+    projected = bind(projected, *fc_m)
+    for mover in fc_m:
+        mover.move()
 
     def exchange(value):
         return lax.all_to_all(value, "sp", split_axis=0, concat_axis=0, tiled=True)
 
     raw = exchange(projected.reshape(parts, micros, slots, 3 * lanes))
-    text_kv = mix("mk,pkn->pmn", text_all, text_w).astype(BF)
-    text_kv = text_kv.reshape(parts, micros, words, 2 * lanes)
+    raw = bind(raw, *fc_m)
+    cross_z = jnp.concatenate([pad_heads(w_out1.T), pad_heads(w_query2), pad_heads(w_out2.T)], 1)
+    cross_z = spread(cross_z, raw)
+    text_z = jnp.pad(pad_heads(w_text_kv.reshape(text_rows, -1)), ((0, max(0, strip - text_rows)), (0, 0)))
+    text_z = spread(text_z, cross_z)
+    text_own = jnp.dot(text.reshape(-1, features), text_turn, preferred_element_type=F32).astype(BF)
+    text_all = spread(text_own, text_z)
+    text_all = jnp.transpose(text_all.reshape(parts, micros, text_slots, features), (1, 0, 2, 3))
+    text_all = text_all.reshape(micros * words, features)
+    while fc_m[0].todo:
+        for mover in fc_m:
+            mover.move()
     attended, turned_q, turned_k, norms = self_forward(raw, counts, cosine, sine, gain_q, gain_k)
+    attended = bind(attended, *fc_m)
     attended = exchange(attended).reshape(parts, rows, lanes)
+    fc1_n, fc2_n = [mover.join() for mover in fc_m[:2]], [mover.join() for mover in fc_m[:1:-1]]
+    fc1_f, fc2_f = ([cube.swap(near, 0) for near in value] for value in (fc1_n, fc2_n))
+    out1_w = rows_of(Gather(cube, cross_z[:, :, :lanes], 0))
+    query2_w = rows_of(Gather(cube, cross_z[:, :, lanes : 2 * lanes], 1))
+    out2_w = rows_of(Gather(cube, cross_z[:, :, 2 * lanes :], 0))
+    text_w = rows_of(Gather(cube, text_z[:, :text_rows], 1))
     stream1 = stream + mix("pmk,pnk->mn", attended, out1_w)
     pre_cross = norm_rows(stream1, g_cross).astype(BF)
     query2 = mix("mk,pkn->pmn", pre_cross, query2_w).astype(BF)
     query2 = query2.reshape(parts, micros, slots, lanes)
+    text_kv = mix("mk,pkn->pmn", text_all, text_w).astype(BF)
+    text_kv = text_kv.reshape(parts, micros, words, 2 * lanes)
     crossed = cross_forward(query2, text_kv, lengths).reshape(parts, rows, lanes)
     stream2 = stream1 + mix("pmk,pnk->mn", crossed, out2_w)
     pre_mlp = norm_rows(stream2, g_mlp).astype(BF)
-    hidden, activ, mlp_out = mlp_forward(pre_mlp, fc1_n, fc1_f, fc2_n, fc2_f)
-    result = ((stream2 + mlp_out) * live).astype(BF)
+    forward = [
+        mlp_forward(pre_mlp, d_mlp, n1, f1, n2, f2)
+        for n1, f1, n2, f2 in zip(fc1_n, fc1_f, fc2_n, fc2_f)
+    ]
+    result = ((stream2 + forward[0][2] + forward[1][2]) * live).astype(BF)
+    fc2_s = [Scatter(cube, item[3], item[4], flip) for flip, item in enumerate(forward)]
 
     def halves(left, right):
         near = mix("md,pmn->pdn", left[:, : left.shape[1] // 2], right)
         far = mix("md,pmn->pdn", left[:, left.shape[1] // 2 :], right).astype(BF)
         return near, far
 
-    def settle(value):
+    def settle(values, before=None):
+        value = values[0] if len(values) == 1 else jnp.concatenate(values, 2)
+        if before is not None:
+            value, before = tie(value, before)
         return lax.psum_scatter(value, "sp", scatter_dimension=0, tiled=False)
 
-    d_fc1_n, d_fc1_f, d_fc2_n, d_fc2_f, d_pre_mlp = mlp_backward(
-        d_mlp, pre_mlp, hidden, activ, fc1_n, fc1_f, fc2_n, fc2_f
-    )
-    sum_fc2 = cube.scatter(d_fc2_n, d_fc2_f, 1)
-    sum_fc1 = cube.scatter(d_fc1_n, d_fc1_f, 0)
-    fc2_1, fc1_1 = next(sum_fc2), next(sum_fc1)
+    backward = []
+    for index in range(2):
+        item = mlp_backward(
+            d_mlp, pre_mlp, forward[index][0], fc1_n[index], fc1_f[index], fc2_n[index], fc2_f[index]
+        )
+        backward.append(item)
+    fc1_s = [Scatter(cube, item[0], item[1], flip) for flip, item in enumerate(backward)]
+    d_pre_mlp = bind(backward[0][2] + backward[1][2], *fc2_s)
+    for mover in fc2_s:
+        mover.pack()
+    d_pre_mlp = bind(d_pre_mlp, *fc2_s)
+    for mover in fc2_s:
+        mover.move()
     d_stream2, d_gain_mlp = norm_back(stream2, g_mlp, d_pre_mlp)
     grad2 = grad3 + d_stream2
     d_cross = grad2.astype(BF)
-    out2_n, out2_f = halves(d_cross, crossed)
     d_crossed = mix("mn,pnk->pmk", d_cross, out2_w).astype(BF)
     d_query2, d_text_kv = cross_backward(
         query2, text_kv, lengths, d_crossed.reshape(parts, micros, slots, lanes)
     )
+    d_query2 = bind(d_query2, *fc1_s, *fc2_s)
+    for mover in fc1_s + fc2_s:
+        mover.pack()
+    d_query2 = bind(d_query2, *fc1_s, *fc2_s)
+    for mover in fc2_s + fc1_s:
+        mover.move()
     d_query2 = d_query2.reshape(parts, rows, lanes)
     d_text_kv = d_text_kv.reshape(parts, micros * words, 2 * lanes)
-    fc2_2, fc1_2 = next(sum_fc2), next(sum_fc1)
-    sum_out2 = cube.scatter(out2_n, out2_f, 1)
-    out2_1 = next(sum_out2)
-    query2_n, query2_f = halves(pre_cross, d_query2)
-    sum_query2 = cube.scatter(query2_n, query2_f, 0)
-    query2_1 = next(sum_query2)
     d_stream1, d_gain_cross = norm_back(stream1, g_cross, mix("pmn,pkn->mk", d_query2, query2_w))
     grad1 = grad2 + d_stream1
     d_attn = grad1.astype(BF)
     d_attended = mix("mn,pnk->pmk", d_attn, out1_w).astype(BF)
     d_heads = exchange(d_attended.reshape(parts, micros, slots, lanes))
-    text_n, text_f = halves(text_all, d_text_kv)
-    sum_text = cube.scatter(text_n, text_f, 1)
-    text_1 = next(sum_text)
-    out1_n, out1_f = halves(d_attn, attended)
-    sum_out1 = cube.scatter(out1_n, out1_f, 0)
-    out1_1 = next(sum_out1)
     d_words = mix("pmn,pkn->mk", d_text_kv, text_w).astype(BF).reshape(micros, parts, text_slots, features)
     d_words = jnp.transpose(d_words, (1, 0, 2, 3)).reshape(parts, micros * text_slots, features)
-    d_words = settle(d_words)
+    out2_s = Scatter(cube, *halves(d_cross, crossed), 1)
+    query2_s = Scatter(cube, *halves(pre_cross, d_query2), 0)
+    text_s = Scatter(cube, *halves(text_all, d_text_kv), 1)
+    out1_s = Scatter(cube, *halves(d_attn, attended), 0)
+    cross_s = [out2_s, query2_s, text_s, out1_s]
+    d_heads = bind(d_heads, *fc2_s, *cross_s)
+    total_fc2 = [mover.result() for mover in fc2_s]
+    term_fc2 = settle(total_fc2)
     d_raw, d_gain_q, d_gain_k = self_backward(
         raw, counts, cosine, sine, gain_q, gain_k, turned_q, turned_k, norms, d_heads
     )
+    d_words = settle([d_words])
+    d_raw = bind(d_raw, *fc1_s)
     d_projected = exchange(d_raw).reshape(parts, rows, 3 * lanes)
-    fc2_3, fc1_3 = next(sum_fc2), next(sum_fc1)
-    fc2_4, fc1_4 = next(sum_fc2), next(sum_fc1)
-    term_fc2, term_fc1 = settle(fc2_4), settle(fc1_4)
-    for stage in range(len(cube.outer)):
-        out2_1, query2_1, text_1, out1_1 = (
-            next(value) for value in (sum_out2, sum_query2, sum_text, sum_out1)
-        )
-    cross_1 = [next(value) for value in (sum_out1, sum_query2, sum_out2)]
-    term_cross = settle(jnp.concatenate(cross_1, 2))
-    term_text = settle(next(sum_text))
-    d_words = jnp.dot(d_words, text_turn.T, preferred_element_type=F32)
-
+    for mover in fc1_s:
+        mover.pack()
+    for mover in cross_s:
+        mover.pack()
+    for mover in fc1_s + cross_s:
+        mover.move()
+    d_projected = bind(d_projected, *fc1_s, *cross_s)
+    total_fc1 = [mover.result() for mover in fc1_s]
+    term_fc1 = settle(total_fc1)
+    d_words = jnp.dot(d_words.reshape(-1, features), text_turn.T, preferred_element_type=F32)
+
+    def split_term(left, right, cut):
+        return [
+            Scatter(cube, *halves(left, part), flip)
+            for part, flip in ((right[:, :, :cut], 0), (right[:, :, cut:], 1))
+        ]
+
+    qkv_s = split_term(pre_attn, d_projected, qkv_cut)
     d_pre = mix("pmn,pkn->mk", d_projected, qkv_w)
+    d_pre = bind(d_pre, *qkv_s)
+    for mover in qkv_s:
+        mover.pack()
+    d_pre = bind(d_pre, *qkv_s)
+    for mover in qkv_s:
+        mover.move()
     d_shift = jnp.sum(d_pre.reshape(micros, slots, width), 1)
     d_stream0, d_gain_attn = norm_back(stream, g_attn, d_pre)
     d_base, d_gain_skip = norm_back(base, g_skip, grad1 + d_stream0)
     d_base = d_base.astype(BF)
-
-    def split_term(left, right, cut):
-        for part, flip in ((right[:, :, :cut], 0), (right[:, :, cut:], 1)):
-            yield cube.scatter(*halves(left, part), flip)
-
-    def finish(sums):
-        values = [list(value)[-1] for value in sums]
-        return settle(jnp.concatenate(values, 2))
-
-    term_qkv = finish(split_term(pre_attn, d_projected, (3 * lanes) // 256 * 128 + 128))
-    term_skip = finish(split_term(d_base, joined, (half + skip_pad) // 2))
+    skip_s = split_term(d_base, joined, skip_cut)
+    for mover in skip_s:
+        mover.move()
+    term_cross = settle([out1_s.result(), query2_s.result(), out2_s.result()])
+    term_text = settle([text_s.result()])
+    term_qkv = settle([mover.result() for mover in qkv_s])
+    term_skip = settle([mover.result() for mover in skip_s])
     d_joined = mix("mn,pnk->pmk", d_base, skip_w)[:, :, :half].reshape(2, parts // 2, rows, half)
     d_joined = jnp.transpose(d_joined, (0, 2, 1, 3)).reshape(2, micros, slots, width)
     result = jnp.dot(result, turn.T, preferred_element_type=F32).astype(BF)

time: 1610 us -> 1480 us (0.919)
  waiting for transfers between devices: 712 us -> 457 us
  local copies, waits for them, and re-layouts: 187 us -> 278 us
  Pallas kernels: 204 us -> 227 us
  starting transfers between devices: 153 us -> 131 us
    ppermute x88 -> x102, waiting for transfers between devices: 603 us -> 396 us  [swap(): return lax.ppermute(value, axis, pairs)]
    all_gather x7, waiting for transfers between devices: 70.3 us -> 1.07 us  [spread(): return lax.all_gather(shard, 'sp', axis=0, tiled=False)]
    concatenate x9 -> x14, local copies, waits for them, and re-layouts: 27.9 us -> 65.2 us  [the longest x8 45.4 us: rows_of(): return jnp.concatenate([near, cube.swap(near, 0)], 1)]
    ppermute x88 -> x102, starting transfers between devices: 135 us -> 109 us  [swap(): return lax.ppermute(value, axis, pairs)]
    pallas_call x1 -> x2, Pallas kernels: 29.8 us -> 52.5 us  [mlp_forward(): pl.pallas_call(kernel, name='mlp_forward', grid=(parts, steps), in_specs=...]
    convert_element_type x30 -> x36, other arithmetic: 63.1 us -> 83.2 us  [total(): return value.astype(BF)]
    ppermute x3 -> x9, local copies, waits for them, and re-layouts: 0.28 us -> 19.4 us  [swap(): return lax.ppermute(value, axis, pairs)]
    optimization_barrier x1 -> x8, local copies, waits for them, and re-layouts: 0.86 us -> 18.8 us  [tie(): return lax.optimization_barrier(values)]
  transfers between devices with their start and end apart: 106 -> 120, of which waited for: 47 -> 40; matrix products, arithmetic and copies ran while one was open for 28% -> 40% of each run, Pallas kernels for 6% -> 16%
where the time goes in v3:
time: 1480 us; the launch traced here: 1460 us
  waiting for transfers between devices  457 us (31%)
  local copies, waits for them, and re-layouts  278 us (19%)
  Pallas kernels  227 us (15%)
  other arithmetic  185 us (12%)
  matrix products  165 us (11%)
  starting transfers between devices  131 us (9%)
  between operations  16.7 us (1%)
    ppermute x102, waiting for transfers between devices, swap(): return lax.ppermute(value, axis, pairs)  396 us
    dot_general x28, matrix products, mix(): return jnp.einsum(spec, left, right, preferred_element_type=F32)  149 us
    ppermute x102, starting transfers between devices, swap(): return lax.ppermute(value, axis, pairs)  109 us
    unnamed x335, local copies, waits for them, and re-layouts  87.7 us
    convert_element_type x36, other arithmetic, total(): return value.astype(BF)  83.2 us
    pallas_call x2, Pallas kernels, mlp_backward(): pl.pallas_call(kernel, name='mlp_backward', grid=(parts, steps), in_specs...  54.9 us
    pallas_call x2, Pallas kernels, mlp_forward(): pl.pallas_call(kernel, name='mlp_forward', grid=(parts, steps), in_specs=...  52.5 us
    pallas_call x1, Pallas kernels, self_backward(): pl.pallas_call(kernel, name='self_backward', grid_spec=pltpu.PrefetchScal...  50.4 us
  transfers between devices with their start and end apart: 120, of which 40 were waited for; matrix products, arithmetic and copies ran while one was open for 40% of the time, Pallas kernels for 16%

profile of v3, /device:TPU:0, one launch (start us, length us, event | category | flops | bytes accessed | tf_op | source)
XLA Modules:
  0.0 1458.5 jit_solution(17902770022854394729)
XLA Ops:
  66.2 10.9 collective-permute-done.4
  77.1 10.9 collective-permute-done.6
  145.1 14.6 %collective-permute-done.18 = bf16[4,176,640]{2,1,0:T(8,128)(2,1)} collective-permute-done((bf16[4,176,640]{2,1,0:T(8,128)(2,1)}, bf16[4,176,640]{2,1,0:T(8,128)(2,1)}, u32[]{:S(2)}, u32[]{:S(2)}) %collective-permute-start.18) | collective-permute-done | bytes 901152 | tf_op jit(solution)/shard_map/ppermute | solution.py:589
  162.1 15.1 %collective-permute-done.19 = bf16[4,176,640]{2,1,0:T(8,128)(2,1)} collective-permute-done((bf16[4,176,640]{2,1,0:T(8,128)(2,1)}, bf16[4,176,640]{2,1,0:T(8,128)(2,1)}, u32[]{:S(2)}, u32[]{:S(2)}) %collective-permute-start.19) | collective-permute-done | bytes 901152 | tf_op jit(solution)/shard_map/ppermute | solution.py:589
  217.5 11.7 concatenate.171
  235.5 13.9 concatenate.169
  249.3 12.4 fusion.7
  294.3 16.2 %collective-permute-done.24 = bf16[4,176,768]{2,1,0:T(8,128)(2,1)S(1)} collective-permute-done((bf16[4,176,768]{2,1,0:T(8,128)(2,1)}, bf16[4,176,768]{2,1,0:T(8,128)(2,1)S(1)}, u32[]{:S(2)}, u32[]{:S(2)}) %collective-permute-start.24) | collective-permute-done | bytes 1081376 | tf_op jit(solution)/shard_map/ppermute | solution.py:589
  311.9 21.4 %collective-permute-done.26 = bf16[4,176,768]{2,1,0:T(8,128)(2,1)} collective-permute-done((bf16[4,176,768]{2,1,0:T(8,128)(2,1)}, bf16[4,176,768]{2,1,0:T(8,128)(2,1)}, u32[]{:S(2)}, u32[]{:S(2)}) %collective-permute-start.26) | collective-permute-done | bytes 1081376 | tf_op jit(solution)/shard_map/ppermute | solution.py:589
  333.3 48.5 %all-to-all-done.raw_ref = bf16[4,2,256,1152]{3,2,1,0:T(8,128)(2,1)} async-done(((bf16[4,2,256,1152]{3,2,1,0:T(8,128)(2,1)}), bf16[4,2,256,1152]{3,2,1,0:T(8,128)(2,1)}, u32[]{:S(2)}, u32[]{:S(2)}) %all-to-all-start) | async-done | bytes 4718624 | tf_op jit(solution)/shard_map/all_to_all | solution.py:808
  385.9 13.9 negate_select_fusion
  409.5 21.2 %collective-permute-done.29 = bf16[4,176,768]{2,1,0:T(8,128)(2,1)} collective-permute-done((bf16[4,176,768]{2,1,0:T(8,128)(2,1)}, bf16[4,176,768]{2,1,0:T(8,128)(2,1)}, u32[]{:S(2)}, u32[]{:S(2)}) %collective-permute-start.29) | collective-permute-done | bytes 1081376 | tf_op jit(solution)/shard_map/ppermute | solution.py:589
  442.5 34.2 %self_forward.1 = (bf16[4,2,256,384]{3,2,1,0:T(8,128)(2,1)}, bf16[2,1024,384]{2,1,0:T(8,128)(2,1)S(1)}, bf16[2,1024,384]{2,1,0:T(8,128)(2,1)S(1)}, f32[2,4,1024]{2,1,0:T(4,128)S(1)}) custom-call(s32[2]{0:T(128)S(1)} %mul.291.count_ref, bf16[4,2,256,1152]{3,2,1,0:T(8,128)(2,1)} %all-to-all-done.raw_ref, f32[2,1024,384]{2,1,0:T(8,128)} %get-tuple-element.418.cos_ref, ...), custom_call_target="tpu_custom_call" | custom-call | flops 3221225472 | bytes 15728640 | tf_op jit(solution)/shard_map/self_forward/pallas_call | solution.py:170
  550.8 14.7 %collective-permute-done.41 = bf16[4,176,384]{2,1,0:T(8,128)(2,1)} collective-permute-done((bf16[4,176,384]{2,1,0:T(8,128)(2,1)S(1)}, bf16[4,176,384]{2,1,0:T(8,128)(2,1)}, u32[]{:S(2)}, u32[]{:S(2)}) %collective-permute-start.41) | collective-permute-done | bytes 540704 | tf_op jit(solution)/shard_map/ppermute | solution.py:589
  577.9 12.9 collective-permute-done.50
  654.1 16.3 %cross_forward.1 = bf16[4,2,256,384]{3,2,1,0:T(8,128)(2,1)S(1)} custom-call(s32[2,2]{1,0:T(2,128)S(1)} %bitcast.334, bf16[4,2,256,384]{3,2,1,0:T(8,128)(2,1)S(1)} %bitcast.323, bf16[4,2,336,768]{3,2,1,0:T(8,128)(2,1)S(1)} %bitcast.328), custom_call_target="tpu_custom_call" | custom-call | flops 1056964608 | bytes 7274496 | tf_op jit(solution)/shard_map/cross_forward/pallas_call | solution.py:348
  676.1 26.2 %mlp_forward.3 = (f32[4,512,768]{2,1,0:T(8,128)}, bf16[4,512,768]{2,1,0:T(8,128)(2,1)}, f32[512,1408]{1,0:T(8,128)S(1)}, bf16[4,704,768]{2,1,0:T(8,128)(2,1)}, bf16[4,704,768]{2,1,0:T(8,128)(2,1)}) custom-call(bf16[512,1408]{1,0:T(8,128)(2,1)S(1)} %multiply_convert_fusion.2.x_ref, bf16[512,1408]{1,0:T(8,128)(2,1)S(1)} %copy-done.26, ...), custom_call_target="tpu_custom_call" | custom-call | flops 13287555072 | bytes 35389440 | tf_op jit(solution)/shard_map/mlp_forward/pallas_call | solution.py:467
  704.3 26.3 %mlp_forward.2 = (f32[4,512,768]{2,1,0:T(8,128)}, bf16[4,512,768]{2,1,0:T(8,128)(2,1)}, f32[512,1408]{1,0:T(8,128)S(1)}, bf16[4,704,768]{2,1,0:T(8,128)(2,1)}, bf16[4,704,768]{2,1,0:T(8,128)(2,1)}) custom-call(bf16[512,1408]{1,0:T(8,128)(2,1)S(1)} %multiply_convert_fusion.2.x_ref, bf16[512,1408]{1,0:T(8,128)(2,1)S(1)} %copy-done.26, ...), custom_call_target="tpu_custom_call" | custom-call | flops 13287555072 | bytes 35389440 | tf_op jit(solution)/shard_map/mlp_forward/pallas_call | solution.py:467
  737.3 27.5 %mlp_backward.3 = (bf16[4,704,768]{2,1,0:T(8,128)(2,1)}, bf16[4,704,768]{2,1,0:T(8,128)(2,1)}, f32[512,1408]{1,0:T(8,128)S(1)}) custom-call(bf16[512,1408]{1,0:T(8,128)(2,1)S(1)} %copy-done.27, bf16[512,1408]{1,0:T(8,128)(2,1)S(1)} %copy-done.9, f32[4,512,768]{2,1,0:T(8,128)} %get-tuple-element.170.hid_ref, ...), custom_call_target="tpu_custom_call" | custom-call | flops 13287555072 | bytes 32243712 | tf_op jit(solution)/shard_map/mlp_backward/pallas_call | solution.py:545
  765.3 27.4 %mlp_backward.2 = (bf16[4,704,768]{2,1,0:T(8,128)(2,1)}, bf16[4,704,768]{2,1,0:T(8,128)(2,1)}, f32[512,1408]{1,0:T(8,128)S(1)}) custom-call(bf16[512,1408]{1,0:T(8,128)(2,1)S(1)} %copy-done.27, bf16[512,1408]{1,0:T(8,128)(2,1)S(1)} %copy-done.9, f32[4,512,768]{2,1,0:T(8,128)} %get-tuple-element.168.hid_ref, ...), custom_call_target="tpu_custom_call" | custom-call | flops 13287555072 | bytes 32243712 | tf_op jit(solution)/shard_map/mlp_backward/pallas_call | solution.py:545
  819.5 18.7 %cross_backward.1 = (bf16[4,2,256,384]{3,2,1,0:T(8,128)(2,1)S(1)}, bf16[4,2,336,768]{3,2,1,0:T(8,128)(2,1)S(1)}) custom-call(s32[2,2]{1,0:T(2,128)S(1)} %bitcast.335, bf16[4,2,256,384]{3,2,1,0:T(8,128)(2,1)S(1)} %bitcast.324, bf16[4,2,336,768]{3,2,1,0:T(8,128)(2,1)S(1)} %bitcast.329, bf16[4,2,256,384]{3,2,1,0:T(8,128)(2,1)S(1)} %bitcast.330), custom_call_target="tpu_custom_call" | custom-call | flops 2642411520 | bytes 14548992 | tf_op jit(solution)/shard_map/cross_backward/pallas_call | solution.py:397
  893.7 19.2 %collective-permute-done.62 = bf16[4,176,768]{2,1,0:T(8,128)(2,1)S(1)} collective-permute-done((bf16[4,176,768]{2,1,0:T(8,128)(2,1)}, bf16[4,176,768]{2,1,0:T(8,128)(2,1)S(1)}, u32[]{:S(2)}, u32[]{:S(2)}) %collective-permute-start.62) | collective-permute-done | bytes 1081376 | tf_op jit(solution)/shard_map/ppermute | solution.py:589
  913.2 51.4 %collective-permute-done.63 = bf16[4,176,768]{2,1,0:T(8,128)(2,1)S(1)} collective-permute-done((bf16[4,176,768]{2,1,0:T(8,128)(2,1)S(1)}, bf16[4,176,768]{2,1,0:T(8,128)(2,1)S(1)}, u32[]{:S(2)}, u32[]{:S(2)}) %collective-permute-start.63) | collective-permute-done | bytes 1081376 | tf_op jit(solution)/shard_map/ppermute | solution.py:589
  969.8 50.4 %self_backward.1 = (bf16[4,2,256,1152]{3,2,1,0:T(8,128)(2,1)}, f32[2,1,384]{2,1,0:T(1,128)S(1)}, f32[2,1,384]{2,1,0:T(1,128)S(1)}) custom-call(s32[2]{0:T(128)S(1)} %copy-done.16, bf16[4,2,256,1152]{3,2,1,0:T(8,128)(2,1)} %all-to-all-done.raw_ref, f32[2,1024,384]{2,1,0:T(8,128)} %get-tuple-element.418.cos_ref, f32[2,1024,384]{2,1,0:T(8,128)} %get-tuple-element.417.sin_ref, ...), custom_call_target="tpu_custom_call" | custom-call | flops 8053063680 | bytes 22020096 | tf_op jit(solution)/shard_map/self_backward/pallas_call | solution.py:284
  1092.5 23.2 %collective-permute-done.73 = bf16[4,352,384]{2,1,0:T(8,128)(2,1)} collective-permute-done((bf16[4,352,384]{2,1,0:T(8,128)(2,1)S(1)}, bf16[4,352,384]{2,1,0:T(8,128)(2,1)}, u32[]{:S(2)}, u32[]{:S(2)}) %collective-permute-start.73) | collective-permute-done | bytes 1081376 | tf_op jit(solution)/shard_map/ppermute | solution.py:589
  1115.7 25.0 %collective-permute-done.72 = bf16[4,352,384]{2,1,0:T(8,128)(2,1)} collective-permute-done((bf16[4,352,384]{2,1,0:T(8,128)(2,1)S(1)}, bf16[4,352,384]{2,1,0:T(8,128)(2,1)}, u32[]{:S(2)}, u32[]{:S(2)}) %collective-permute-start.72) | collective-permute-done | bytes 1081376 | tf_op jit(solution)/shard_map/ppermute | solution.py:589
  1140.7 20.4 %collective-permute-done.70 = bf16[4,176,768]{2,1,0:T(8,128)(2,1)} collective-permute-done((bf16[4,176,768]{2,1,0:T(8,128)(2,1)S(1)}, bf16[4,176,768]{2,1,0:T(8,128)(2,1)}, u32[]{:S(2)}, u32[]{:S(2)}) %collective-permute-start.70) | collective-permute-done | bytes 1081376 | tf_op jit(solution)/shard_map/ppermute | solution.py:589
  1164.2 11.3 collective-permute-start.96
  1178.7 13.3 collective-permute-done.96
  1265.1 10.1 fusion.17
  1313.3 20.0 %collective-permute-done.85 = f32[4,2,176]{2,0,1:T(4,128)S(1)} collective-permute-done((f32[4,2,176]{2,0,1:T(4,128)S(1)}, f32[4,2,176]{2,0,1:T(4,128)S(1)}, u32[]{:S(2)}, u32[]{:S(2)}) %collective-permute-start.85) | collective-permute-done | bytes 5664 | tf_op jit(solution)/shard_map/ppermute | solution.py:589
  1439.2 10.8 reduce-scatter.10.cloned.1.call-done
  (894 shorter events, 772.0 us)
Async XLA Ops:
  9.5 96.3 %all-gather.17.cloned.1.call-start = ((), (), s32[]{:S(2)}) async-start(), calls=%async_computation.19 | async-start | bytes 2027520 | tf_op jit(solution)/shard_map/all_gather | solution.py:739
  66.1 141.4 %all-gather.19.cloned.1.call-start = ((), (), s32[]{:S(2)}) async-start(), calls=%async_computation.20 | async-start | bytes 2703360 | tf_op jit(solution)/shard_map/all_gather | solution.py:739
  115.0 146.8 %all-gather.21.cloned.1.call-start = ((), (), s32[]{:S(2)}) async-start(), calls=%async_computation.21 | async-start | bytes 2703360 | tf_op jit(solution)/shard_map/all_gather | solution.py:739
  271.5 110.3 %all-to-all-start = ((bf16[4,2,256,1152]{3,2,1,0:T(8,128)(2,1)}), bf16[4,2,256,1152]{3,2,1,0:T(8,128)(2,1)}, u32[]{:S(2)}, u32[]{:S(2)}) async-start(bf16[4,2,256,1152]{3,2,1,0:T(8,128)(2,1)} %bitcast.345), calls=%async_computation | async-start | bytes 9437184 | tf_op jit(solution)/shard_map/all_to_all | solution.py:808
  276.6 220.8 %all-gather.23.cloned.1.call-start = ((), (), s32[]{:S(2)}) async-start(), calls=%async_computation.22 | async-start | bytes 2027520 | tf_op jit(solution)/shard_map/all_gather | solution.py:739
  399.9 79.1 %collective-permute-start.31 = (bf16[4,176,768]{2,1,0:T(8,128)(2,1)}, bf16[4,176,768]{2,1,0:T(8,128)(2,1)}, u32[]{:S(2)}, u32[]{:S(2)}) collective-permute-start(bf16[4,176,768]{2,1,0:T(8,128)(2,1)} %copy-done.79), channel_id=1, source_target_pairs={{0,8},{4,12},{8,0},{12,4},{16,24},{20,28},{24,16},{28,20},{1,9},{5... | collective-permute-start | bytes 3244040 | tf_op jit(solution)/shard_map/ppermute | solution.py:589
  401.4 77.5 %collective-permute-start.32 = (bf16[4,176,768]{2,1,0:T(8,128)(2,1)}, bf16[4,176,768]{2,1,0:T(8,128)(2,1)}, u32[]{:S(2)}, u32[]{:S(2)}) collective-permute-start(bf16[4,176,768]{2,1,0:T(8,128)(2,1)} %get-tuple-element.163), channel_id=1, source_target_pairs={{0,8},{4,12},{8,0},{12,4},{16,24},{20,28},{24,16},{28,20},{1,9},{5... | collective-permute-start | bytes 3244040 | tf_op jit(solution)/shard_map/ppermute | solution.py:589
  408.9 70.1 %collective-permute-start.33 = (bf16[4,176,768]{2,1,0:T(8,128)(2,1)}, bf16[4,176,768]{2,1,0:T(8,128)(2,1)}, u32[]{:S(2)}, u32[]{:S(2)}) collective-permute-start(bf16[4,176,768]{2,1,0:T(8,128)(2,1)} %collective-permute-done.26), channel_id=1, source_target_pairs={{0,8},{4,12},{8,0},{12,4},{16,24},{20,28},{24,16},{28,20},{1,9},{5... | collective-permute-start | bytes 3244040 | tf_op jit(solution)/shard_map/ppermute | solution.py:589
  479.0 138.5 %all-to-all-start.1 = ((bf16[4,2,256,384]{3,2,1,0:T(8,128)(2,1)}), bf16[4,2,256,384]{3,2,1,0:T(8,128)(2,1)}, u32[]{:S(2)}, u32[]{:S(2)}) async-start(bf16[4,2,256,384]{3,2,1,0:T(8,128)(2,1)} %get-tuple-element.146), calls=%async_computation.1 | async-start | bytes 3145728 | tf_op jit(solution)/shard_map/all_to_all | solution.py:808
  498.3 139.1 %all-gather.27.cloned.1.call-start = ((), (), s32[]{:S(2)}) async-start(), calls=%async_computation.24 | async-start | bytes 1720320 | tf_op jit(solution)/shard_map/all_gather | solution.py:739
  543.8 69.8 %collective-permute-start.39 = (bf16[4,704,384]{2,1,0:T(8,128)(2,1)}, bf16[4,704,384]{2,1,0:T(8,128)(2,1)}, u32[]{:S(2)}, u32[]{:S(2)}) collective-permute-start(bf16[4,704,384]{2,1,0:T(8,128)(2,1)} %pad_maximum_fusion.21), channel_id=1, source_target_pairs={{0,4},{4,0},{8,12},{12,8},{16,20},{20,16},{24,28},{28,24},{1,5},{5... | collective-permute-start | bytes 6488072 | tf_op jit(solution)/shard_map/ppermute | solution.py:589
  590.8 83.3 %collective-permute-start.55 = (bf16[4,704,768]{2,1,0:T(8,128)(2,1)}, bf16[4,704,768]{2,1,0:T(8,128)(2,1)}, u32[]{:S(2)}, u32[]{:S(2)}) collective-permute-start(bf16[4,704,768]{2,1,0:T(8,128)(2,1)} %constant_dynamic-update-slice_fusion.50.n2_ref), channel_id=1, source_target_pairs={{0,4},{4,0},{8,12},{12,8},{16,20},{20,16},{24,28},{28,24},{1,5},{5... | collective-permute-start | bytes 12976136 | tf_op jit(solution)/shard_map/ppermute | solution.py:589
  592.4 81.7 %collective-permute-start.54 = (bf16[4,704,768]{2,1,0:T(8,128)(2,1)}, bf16[4,704,768]{2,1,0:T(8,128)(2,1)}, u32[]{:S(2)}, u32[]{:S(2)}) collective-permute-start(bf16[4,704,768]{2,1,0:T(8,128)(2,1)} %constant_dynamic-update-slice_fusion.46.n1_ref), channel_id=1, source_target_pairs={{0,4},{4,0},{8,12},{12,8},{16,20},{20,16},{24,28},{28,24},{1,5},{5... | collective-permute-start | bytes 12976136 | tf_op jit(solution)/shard_map/ppermute | solution.py:589
  624.7 79.6 %collective-permute-start.53 = (bf16[4,704,768]{2,1,0:T(8,128)(2,1)}, bf16[4,704,768]{2,1,0:T(8,128)(2,1)}, u32[]{:S(2)}, u32[]{:S(2)}) collective-permute-start(bf16[4,704,768]{2,1,0:T(8,128)(2,1)} %constant_dynamic-update-slice_fusion.42.n2_ref), channel_id=1, source_target_pairs={{0,4},{4,0},{8,12},{12,8},{16,20},{20,16},{24,28},{28,24},{1,5},{5... | collective-permute-start | bytes 12976136 | tf_op jit(solution)/shard_map/ppermute | solution.py:589
  634.2 70.1 %collective-permute-start.52 = (bf16[4,704,768]{2,1,0:T(8,128)(2,1)}, bf16[4,704,768]{2,1,0:T(8,128)(2,1)}, u32[]{:S(2)}, u32[]{:S(2)}) collective-permute-start(bf16[4,704,768]{2,1,0:T(8,128)(2,1)} %constant_dynamic-update-slice_fusion.38.n1_ref), channel_id=1, source_target_pairs={{0,4},{4,0},{8,12},{12,8},{16,20},{20,16},{24,28},{28,24},{1,5},{5... | collective-permute-start | bytes 12976136 | tf_op jit(solution)/shard_map/ppermute | solution.py:589
  703.8 89.2 %collective-permute-start.57 = (bf16[4,704,768]{2,1,0:T(8,128)(2,1)}, bf16[4,704,768]{2,1,0:T(8,128)(2,1)}, u32[]{:S(2)}, u32[]{:S(2)}) collective-permute-start(bf16[4,704,768]{2,1,0:T(8,128)(2,1)} %get-tuple-element.173), channel_id=1, source_target_pairs={{0,4},{4,0},{8,12},{12,8},{16,20},{20,16},{24,28},{28,24},{1,5},{5... | collective-permute-start | bytes 12976136 | tf_op jit(solution)/shard_map/ppermute | solution.py:589
  764.8 77.9 %collective-permute-start.59 = (bf16[4,704,768]{2,1,0:T(8,128)(2,1)}, bf16[4,704,768]{2,1,0:T(8,128)(2,1)}, u32[]{:S(2)}, u32[]{:S(2)}) collective-permute-start(bf16[4,704,768]{2,1,0:T(8,128)(2,1)} %get-tuple-element.182), channel_id=1, source_target_pairs={{0,4},{4,0},{8,12},{12,8},{16,20},{20,16},{24,28},{28,24},{1,5},{5... | collective-permute-start | bytes 12976136 | tf_op jit(solution)/shard_map/ppermute | solution.py:589
  819.4 72.7 %collective-permute-start.64 = (bf16[4,704,384]{2,1,0:T(8,128)(2,1)}, bf16[4,704,384]{2,1,0:T(8,128)(2,1)}, u32[]{:S(2)}, u32[]{:S(2)}) collective-permute-start(bf16[4,704,384]{2,1,0:T(8,128)(2,1)} %convert_bitcast_fusion.7), channel_id=1, source_target_pairs={{0,4},{4,0},{8,12},{12,8},{16,20},{20,16},{24,28},{28,24},{1,5},{5... | collective-permute-start | bytes 6488072 | tf_op jit(solution)/shard_map/ppermute | solution.py:589
  880.9 86.1 %all-to-all-start.2 = ((bf16[4,2,256,384]{3,2,1,0:T(8,128)(2,1)}), bf16[4,2,256,384]{3,2,1,0:T(8,128)(2,1)S(1)}, u32[]{:S(2)}, u32[]{:S(2)}) async-start(bf16[4,2,256,384]{3,2,1,0:T(8,128)(2,1)} %bitcast.352), calls=%async_computation.2 | async-start | bytes 3145728 | tf_op jit(solution)/shard_map/all_to_all | solution.py:808
  891.6 73.0 %collective-permute-start.65 = (bf16[4,704,384]{2,1,0:T(8,128)(2,1)S(1)}, bf16[4,704,384]{2,1,0:T(8,128)(2,1)S(1)}, u32[]{:S(2)}, u32[]{:S(2)}) collective-permute-start(bf16[4,704,384]{2,1,0:T(8,128)(2,1)S(1)} %convert_bitcast_fusion.6), channel_id=1, source_target_pairs={{0,4},{4,0},{8,12},{12,8},{16,20},{20,16},{24,28},{28,24},{1,5},{5... | collective-permute-start | bytes 6488072 | tf_op jit(solution)/shard_map/ppermute | solution.py:589
  891.7 75.2 %collective-permute-start.67 = (bf16[4,704,384]{2,1,0:T(8,128)(2,1)S(1)}, bf16[4,704,384]{2,1,0:T(8,128)(2,1)}, u32[]{:S(2)}, u32[]{:S(2)}) collective-permute-start(bf16[4,704,384]{2,1,0:T(8,128)(2,1)S(1)} %convert_bitcast_fusion.5), channel_id=1, source_target_pairs={{0,4},{4,0},{8,12},{12,8},{16,20},{20,16},{24,28},{28,24},{1,5},{5... | collective-permute-start | bytes 6488072 | tf_op jit(solution)/shard_map/ppermute | solution.py:589
  892.2 128.0 %collective-permute-start.68 = (bf16[4,352,768]{2,1,0:T(8,128)(2,1)}, bf16[4,352,768]{2,1,0:T(8,128)(2,1)}, u32[]{:S(2)}, u32[]{:S(2)}) collective-permute-start(bf16[4,352,768]{2,1,0:T(8,128)(2,1)} %pad_maximum_fusion.26), channel_id=1, source_target_pairs={{0,16},{4,20},{8,24},{12,28},{16,0},{20,4},{24,8},{28,12},{1,17},{... | collective-permute-start | bytes 6488072 | tf_op jit(solution)/shard_map/ppermute | solution.py:589
  892.5 127.7 %collective-permute-start.69 = (bf16[4,352,768]{2,1,0:T(8,128)(2,1)}, bf16[4,352,768]{2,1,0:T(8,128)(2,1)}, u32[]{:S(2)}, u32[]{:S(2)}) collective-permute-start(bf16[4,352,768]{2,1,0:T(8,128)(2,1)} %pad_maximum_fusion.27), channel_id=1, source_target_pairs={{0,8},{4,12},{8,0},{12,4},{16,24},{20,28},{24,16},{28,20},{1,9},{5... | collective-permute-start | bytes 6488072 | tf_op jit(solution)/shard_map/ppermute | solution.py:589
  1020.1 141.0 %all-to-all-start.3 = ((bf16[4,2,256,1152]{3,2,1,0:T(8,128)(2,1)}), bf16[4,2,256,1152]{3,2,1,0:T(8,128)(2,1)}, u32[]{:S(2)}, u32[]{:S(2)}) async-start(bf16[4,2,256,1152]{3,2,1,0:T(8,128)(2,1)} %get-tuple-element.203), calls=%async_computation.3 | async-start | bytes 9437184 | tf_op jit(solution)/shard_map/all_to_all | solution.py:808
  1025.2 201.8 %reduce-scatter.8.cloned.1.call-start = ((), (), s32[]{:S(2)}) async-start(), calls=%async_computation.11 | async-start | bytes 1720320 | tf_op jit(solution)/shard_map/reduce_scatter | solution.py:857
  1040.4 190.4 %reduce-scatter.20.cloned.1.call-start = ((), (), s32[]{:S(2)}) async-start(), calls=%async_computation.17 | async-start | bytes 2703360 | tf_op jit(solution)/shard_map/reduce_scatter | solution.py:857
  1073.9 201.2 %reduce-scatter.16.cloned.1.call-start = ((), (), s32[]{:S(2)}) async-start(), calls=%async_computation.15 | async-start | bytes 983040 | tf_op jit(solution)/shard_map/reduce_scatter | solution.py:857
  1080.0 81.1 %collective-permute-start.74 = (bf16[4,256,768]{1,2,0:T(8,128)(2,1)S(1)}, bf16[4,256,768]{1,2,0:T(8,128)(2,1)}, u32[]{:S(2)}, u32[]{:S(2)}) collective-permute-start(bf16[4,256,768]{1,2,0:T(8,128)(2,1)S(1)} %pad_maximum_fusion.33), channel_id=1, source_target_pairs={{0,8},{4,12},{8,0},{12,4},{16,24},{20,28},{24,16},{28,20},{1,9},{5... | collective-permute-start | bytes 4718600 | tf_op jit(solution)/shard_map/ppermute | solution.py:589
  1195.1 231.4 %reduce-scatter.14.cloned.1.call-start = ((), (), s32[]{:S(2)}) async-start(), calls=%async_computation.14 | async-start | bytes 2027520 | tf_op jit(solution)/shard_map/reduce_scatter | solution.py:857
  1219.2 211.7 %reduce-scatter.18.cloned.1.call-start = ((), (), s32[]{:S(2)}) async-start(), calls=%async_computation.16 | async-start | bytes 2703360 | tf_op jit(solution)/shard_map/reduce_scatter | solution.py:857
  1251.7 181.4 %reduce-scatter.12.cloned.1.call-start = ((), (), s32[]{:S(2)}) async-start(), calls=%async_computation.13 | async-start | bytes 2027520 | tf_op jit(solution)/shard_map/reduce_scatter | solution.py:857
  1372.6 77.4 %reduce-scatter.10.cloned.1.call-start = ((), (), s32[]{:S(2)}) async-start(), calls=%async_computation.12 | async-start | bytes 1351680 | tf_op jit(solution)/shard_map/reduce_scatter | solution.py:857
  (233 other events, 6519.3 us)
Sparse Core Ops, SparseCore 0:
  10.2 31.1 all-gather.14
  66.2 39.5 all-gather.16
  115.1 45.8 all-gather.18
  207.7 46.1 all-gather.20
  400.0 36.0 all-gather.22
  498.4 41.1 all-gather.24
  599.0 34.9 all-gather.26
  1040.5 93.7 reduce-scatter.7
  1136.8 52.2 reduce-scatter.19
  1195.2 25.1 reduce-scatter.15
  1222.7 35.5 reduce-scatter.13
  1260.5 43.9 reduce-scatter.17
  1372.7 32.8 reduce-scatter.11
  1424.3 25.6 reduce-scatter.9

commit v4 on v1

v4 whole, which is shorter than its diff:
```python
import math

import jax
import jax.numpy as jnp
from jax import lax
from jax.experimental import pallas as pl
from jax.experimental.pallas import tpu as pltpu
from jax.sharding import PartitionSpec as P

H = 16
HD = 88
HP = 96
CLIP_LEN = 77
ROWS = 256

EPS = 1e-06
MASKED = -1e30
LOG2E = 1.4426950408889634
BF = jnp.bfloat16
F32 = jnp.float32


def time_embed(step, width):
    half = width // 2
    rate = jnp.exp(-math.log(10000.0) * jnp.arange(half, dtype=F32) / half)
    angle = step.astype(F32)[..., None] * rate
    return jnp.concatenate([jnp.cos(angle), jnp.sin(angle)], -1)


def rope_tables(sequence, wide, lanes):
    place = jnp.arange(sequence, dtype=jnp.int32)[None, :, None]
    wide = wide[:, None, None]
    lane = jnp.arange(lanes, dtype=jnp.int32)[None, None, :] % HP
    pair = lane // 2
    quarter = HD // 4
    upper = pair < quarter
    rank = jnp.where(upper, pair, pair - quarter).astype(F32)
    rate = jnp.exp(-math.log(10000.0) * rank / quarter)
    angle = jnp.where(upper, place // wide, place % wide).astype(F32) * rate
    sine = jnp.sin(angle)
    return jnp.cos(angle), jnp.where(lane % 2 == 0, -sine, sine)


def pad_heads(packed, local):
    rows, lanes = packed.shape
    groups = packed.reshape(rows, lanes // (local * HD), local, HD)
    groups = jnp.pad(groups, ((0, 0), (0, 0), (0, 0), (0, HP - HD)))
    groups = groups.reshape(rows, -1, local * HP)
    return jnp.pad(groups, ((0, 0), (0, 0), (0, -local * HP % 128))).reshape(rows, -1)


def cut_heads(padded, local):
    rows = padded.shape[0]
    groups = padded.reshape(rows, -1, local * HP + -local * HP % 128)[:, :, : local * HP]
    return groups.reshape(rows, -1, local, HP)[..., :HD].reshape(rows, -1)


def head_masks(shape, local):
    lane = lax.broadcasted_iota(jnp.int32, shape, len(shape) - 1)
    inside = lane % HP < HD
    return [((lane // HP == h) & inside).astype(F32) for h in range(local)]


def head_mean(value, masks):
    total = None
    for mask in masks:
        term = (jnp.sum(value * mask, -1, keepdims=True) * (1.0 / HD)) * mask
        total = term if total is None else total + term
    return total


def head_unit(value, masks):
    centre = value - head_mean(value, masks)
    spread = None
    square = centre * centre
    for mask in masks:
        mean = jnp.sum(square * mask, -1, keepdims=True) * (1.0 / HD)
        term = lax.rsqrt(mean + EPS) * mask
        spread = term if spread is None else spread + term
    return centre * spread, spread


def turn_pairs(value):
    lanes = value.shape[-1]
    after = pltpu.roll(value, lanes - 1, 1)
    before = pltpu.roll(value, 1, 1)
    lane = lax.broadcasted_iota(jnp.int32, value.shape, 1)
    return jnp.where(lane % 2 == 0, after, before)


def dot_nt(left, right):
    return lax.dot_general(left, right, (((1,), (1,)), ((), ())), preferred_element_type=F32)


def dot_nn(left, right):
    return lax.dot_general(left, right, (((1,), (0,)), ((), ())), preferred_element_type=F32)


def dot_tn(left, right):
    return lax.dot_general(left, right, (((0,), (0,)), ((), ())), preferred_element_type=F32)


def self_forward(raw, counts, cosine, sine, gain_q, gain_k):
    parts, micros, slots, packed = raw.shape
    lanes = packed // 3
    local = lanes // HP
    sequence = parts * slots
    factor = HD ** (-0.5) * LOG2E

    def kernel(count_ref, raw_ref, cos_ref, sin_ref, gq_ref, gk_ref, out_ref, q_ref, k_ref, lse_ref):
        count = count_ref[pl.program_id(0)]
        blocks = (count + slots - 1) // slots
        out_ref[...] = jnp.zeros_like(out_ref)
        masks = head_masks((1, lanes), local)

        def prepare(part, carry):
            spot = pl.ds(pl.multiple_of(part * slots, slots), slots)
            cosine, sine = cos_ref[0, spot, :], sin_ref[0, spot, :]
            for index, gain_ref, dest in ((0, gq_ref, q_ref), (1, gk_ref, k_ref)):
                value = raw_ref[part, 0, :, index * lanes : (index + 1) * lanes].astype(F32)
                scaled = head_unit(value, masks)[0] * gain_ref[...]
                dest[0, spot, :] = (scaled * cosine + turn_pairs(scaled) * sine).astype(BF)
            return carry

        lax.fori_loop(0, parts, prepare, 0)
        column = lax.broadcasted_iota(jnp.int32, (1, sequence), 1)
        bias = jnp.where(column < count, 0.0, MASKED)
        for h in range(local):
            cut = slice(h * HP, (h + 1) * HP)
            keys = k_ref[0, :, cut]
            values = raw_ref[:, 0, :, 2 * lanes + h * HP : 2 * lanes + (h + 1) * HP].reshape(sequence, HP)

            def one_block(part, carry):
                spot = pl.ds(pl.multiple_of(part * slots, slots), slots)
                scores = dot_nt(q_ref[0, spot, cut], keys) + bias
                top = jnp.max(scores, -1, keepdims=True)
                raised = jnp.exp2((scores - top) * factor)
                total = jnp.sum(raised, -1, keepdims=True)
                result = dot_nn(raised.astype(BF), values) / total
                out_ref[part, 0, :, cut] = result.astype(BF)
                norm = jnp.broadcast_to(top * factor + jnp.log2(total), (slots, 128))
                lse_ref[0, h : h + 1, spot] = jnp.transpose(norm)[0:1, :]
                return carry

            lax.fori_loop(0, blocks, one_block, 0)

    whole = lambda m, c: (0, m, 0, 0)
    table = lambda m, c: (m, 0, 0)
    fixed = lambda m, c: (0, 0)
    return pl.pallas_call(
        kernel,
        name="self_forward",
        grid_spec=pltpu.PrefetchScalarGridSpec(
            num_scalar_prefetch=1,
            grid=(micros,),
            in_specs=[
                pl.BlockSpec((parts, 1, slots, packed), whole),
                pl.BlockSpec((1, sequence, lanes), table),
                pl.BlockSpec((1, sequence, lanes), table),
                pl.BlockSpec((1, lanes), fixed),
                pl.BlockSpec((1, lanes), fixed),
            ],
            out_specs=[
                pl.BlockSpec((parts, 1, slots, lanes), whole),
                pl.BlockSpec((1, sequence, lanes), table),
                pl.BlockSpec((1, sequence, lanes), table),
                pl.BlockSpec((1, local, sequence), table),
            ],
        ),
        out_shape=[
            jax.ShapeDtypeStruct((parts, micros, slots, lanes), BF),
            jax.ShapeDtypeStruct((micros, sequence, lanes), BF),
            jax.ShapeDtypeStruct((micros, sequence, lanes), BF),
            jax.ShapeDtypeStruct((micros, local, sequence), F32),
        ],
        compiler_params=pltpu.CompilerParams(vmem_limit_bytes=48 << 20),
        cost_estimate=cost(4 * micros * local * sequence * sequence * HP),
    )(counts, raw, cosine, sine, gain_q, gain_k)


def self_backward(raw, counts, cosine, sine, gain_q, gain_k, turned_q, turned_k, norms, incoming):
    parts, micros, slots, packed = raw.shape
    lanes = packed // 3
    local = lanes // HP
    sequence = parts * slots
    scale = HD ** (-0.5)
    factor = scale * LOG2E

    def kernel(
        count_ref,
        raw_ref,
        cos_ref,
        sin_ref,
        gq_ref,
        gk_ref,
        q_ref,
        k_ref,
        lse_ref,
        in_ref,
        out_ref,
        dgq_ref,
        dgk_ref,
        dq_s,
        dk_s,
        dv_s,
    ):
        count = count_ref[pl.program_id(0)]
        blocks = (count + slots - 1) // slots
        dq_s[...] = jnp.zeros_like(dq_s)
        dk_s[...] = jnp.zeros_like(dk_s)
        dv_s[...] = jnp.zeros_like(dv_s)
        row = lax.broadcasted_iota(jnp.int32, (sequence, 1), 0)
        bias = jnp.where(row < count, 0.0, MASKED)
        for h in range(local):
            cut = slice(h * HP, (h + 1) * HP)
            keys = k_ref[0, :, cut]
            values = raw_ref[:, 0, :, 2 * lanes + h * HP : 2 * lanes + (h + 1) * HP].reshape(sequence, HP)

            def one_block(part, carry):
                spot = pl.ds(pl.multiple_of(part * slots, slots), slots)
                rows = q_ref[0, spot, cut]
                grads = in_ref[part, 0, :, cut]
                norm = lse_ref[0, h : h + 1, spot]
                probs = jnp.exp2(dot_nt(keys, rows) * factor + bias - norm)
                d_probs = dot_nt(values, grads)
                inner = jnp.sum(probs * d_probs, 0, keepdims=True)
                d_scores = (probs * (d_probs - inner)).astype(BF)
                dv_s[:, cut] += dot_nn(probs.astype(BF), grads)
                dk_s[:, cut] += dot_nn(d_scores, rows)
                dq_s[spot, cut] = dot_tn(d_scores, keys)
                return carry

            lax.fori_loop(0, blocks, one_block, 0)
        masks = head_masks((1, lanes), local)

        def finish(part, carry):
            spot = pl.ds(pl.multiple_of(part * slots, slots), slots)
            cosine, sine = cos_ref[0, spot, :], sin_ref[0, spot, :]
            sums = []
            for index, gain_ref, source in ((0, gq_ref, dq_s), (1, gk_ref, dk_s)):
                grad = source[spot, :] * scale
                grad = grad * cosine - turn_pairs(grad) * sine
                value = raw_ref[part, 0, :, index * lanes : (index + 1) * lanes].astype(F32)
                unit, spread = head_unit(value, masks)
                leading = grad * gain_ref[...]
                back = leading - head_mean(leading, masks) - unit * head_mean(leading * unit, masks)
                out_ref[part, 0, :, index * lanes : (index + 1) * lanes] = (spread * back).astype(BF)
                sums.append(carry[index] + jnp.sum(grad * unit, 0, keepdims=True))
            out_ref[part, 0, :, 2 * lanes : 3 * lanes] = dv_s[spot, :].astype(BF)
            return tuple(sums)

        zero = jnp.zeros((1, lanes), F32)
        d_gains = lax.fori_loop(0, parts, finish, (zero, zero))
        dgq_ref[0] = d_gains[0]
        dgk_ref[0] = d_gains[1]

    whole = lambda m, c: (0, m, 0, 0)
    table = lambda m, c: (m, 0, 0)
    fixed = lambda m, c: (0, 0)
    return pl.pallas_call(
        kernel,
        name="self_backward",
        grid_spec=pltpu.PrefetchScalarGridSpec(
            num_scalar_prefetch=1,
            grid=(micros,),
            in_specs=[
                pl.BlockSpec((parts, 1, slots, packed), whole),
                pl.BlockSpec((1, sequence, lanes), table),
                pl.BlockSpec((1, sequence, lanes), table),
                pl.BlockSpec((1, lanes), fixed),
                pl.BlockSpec((1, lanes), fixed),
                pl.BlockSpec((1, sequence, lanes), table),
                pl.BlockSpec((1, sequence, lanes), table),
                pl.BlockSpec((1, local, sequence), table),
                pl.BlockSpec((parts, 1, slots, lanes), whole),
            ],
            out_specs=[
                pl.BlockSpec((parts, 1, slots, packed), whole),
                pl.BlockSpec((1, 1, lanes), table),
                pl.BlockSpec((1, 1, lanes), table),
            ],
            scratch_shapes=[pltpu.VMEM((sequence, lanes), F32) for index in range(3)],
        ),
        out_shape=[
            jax.ShapeDtypeStruct((parts, micros, slots, packed), BF),
            jax.ShapeDtypeStruct((micros, 1, lanes), F32),
            jax.ShapeDtypeStruct((micros, 1, lanes), F32),
        ],
        compiler_params=pltpu.CompilerParams(vmem_limit_bytes=48 << 20),
        cost_estimate=cost(10 * micros * local * sequence * sequence * HP),
    )(counts, raw, cosine, sine, gain_q, gain_k, turned_q, turned_k, norms, incoming)


def cost(flops):
    return pl.CostEstimate(flops=flops, bytes_accessed=flops // 1000, transcendentals=0)


def full(shape):
    return pl.BlockSpec(shape, lambda *index: (0,) * len(shape))


def params(megabytes=48):
    return pltpu.CompilerParams(vmem_limit_bytes=megabytes << 20)


class Lanes:
    def __init__(self, near, far, block=None, index=0):
        self.near, self.far = near, far
        self.block = block or near.shape[2]
        self.index = index

    def spec(self):
        index = self.index
        return pl.BlockSpec((1, self.near.shape[1], self.block), lambda p, *rest: (p, 0, index))


def to_lanes(value, weights, dtype=BF, name="to_lanes"):
    rows = value.shape[1]
    parts, half, _ = weights[0].near.shape
    total = sum(weight.block for weight in weights)

    def kernel(x_ref, *refs):
        out_ref = refs[-1]
        at = 0
        for index, weight in enumerate(weights):
            result = dot_nn(x_ref[0], refs[2 * index][0]) + dot_nn(x_ref[1], refs[2 * index + 1][0])
            out_ref[0, :, at : at + weight.block] = result.astype(dtype)
            at += weight.block

    return pl.pallas_call(
        kernel,
        name=name,
        grid=(parts,),
        in_specs=[full(value.shape)] + [weight.spec() for weight in weights for side in range(2)],
        out_specs=pl.BlockSpec((1, rows, total), lambda p: (p, 0, 0)),
        out_shape=jax.ShapeDtypeStruct((parts, rows, total), dtype),
        compiler_params=params(),
        cost_estimate=cost(4 * rows * half * parts * total),
    )(value, *[side for weight in weights for side in (weight.near, weight.far)])


def to_inputs(value, weights, kept):
    rows = value.shape[1]
    parts, half, _ = weights[0].near.shape
    sides = parts // 2

    def kernel(x_ref, *refs):
        out_ref = refs[-1]
        for side in range(sides):

            @pl.when(pl.program_id(0) % sides == side)
            def _():
                at = 0
                for index, weight in enumerate(weights):
                    result = dot_nn(x_ref[0], refs[2 * index][0]) + dot_nn(
                        x_ref[1], refs[2 * index + 1][0]
                    )
                    take = min(weight.block, kept - at)
                    start = side * kept + at
                    out_ref[0, :, start : start + take] = result[:, :take]
                    at += take

    return pl.pallas_call(
        kernel,
        name="to_inputs",
        grid=(parts,),
        in_specs=[full(value.shape)] + [weight.spec() for weight in weights for side in range(2)],
        out_specs=pl.BlockSpec((1, rows, sides * kept), lambda p: (p // sides, 0, 0)),
        out_shape=jax.ShapeDtypeStruct((2, rows, sides * kept), F32),
        compiler_params=params(),
        cost_estimate=cost(4 * rows * half * parts * kept),
    )(value, *[side for weight in weights for side in (weight.near, weight.far)])


def to_features(value, weights, extras, outs, finish, name="to_features"):
    parts, rows, total = value.shape
    half = weights[0].near.shape[1]
    count = 2 * len(weights)

    def kernel(*refs):
        y_ref, weight_refs = refs[0], refs[1 : 1 + count]
        extra_refs = refs[1 + count : 1 + count + len(extras)]
        out_refs = refs[1 + count + len(extras) : -1]
        sums = refs[-1]

        @pl.when(pl.program_id(0) == 0)
        def _():
            sums[...] = jnp.zeros_like(sums)

        at = 0
        for index, weight in enumerate(weights):
            left = y_ref[0, :, at : at + weight.block]
            for side in range(2):
                sums[side] += dot_nt(left, weight_refs[2 * index + side][0])
            at += weight.block

        @pl.when(pl.program_id(0) == parts - 1)
        def _():
            finish([sums[0], sums[1]], extra_refs, out_refs)

    return pl.pallas_call(
        kernel,
        name=name,
        grid=(parts,),
        in_specs=[pl.BlockSpec((1, rows, total), lambda p: (p, 0, 0))]
        + [weight.spec() for weight in weights for side in range(2)]
        + [full(extra.shape) for extra in extras],
        out_specs=[full(out.shape) for out in outs],
        out_shape=outs,
        scratch_shapes=[pltpu.VMEM((2, rows, half), F32)],
        compiler_params=params(56),
        cost_estimate=cost(4 * rows * half * parts * total),
    )(value, *[side for weight in weights for side in (weight.near, weight.far)], *extras)


def terms_of(pairs, name="terms_of"):
    half = pairs[0][0].shape[2]
    parts = pairs[0][1].shape[0]
    total = sum(pair[2] for pair in pairs)
    rows = [pair[0].shape[1] for pair in pairs]

    def kernel(*refs):
        count = len(pairs)
        lefts, rights = refs[:count], refs[count : 2 * count]
        near_ref, far_ref = refs[2 * count : 2 * count + 2]
        turned = refs[2 * count + 2 :]

        @pl.when(pl.program_id(0) == 0)
        def _():
            for left, flat in zip(lefts, turned):
                for side in range(2):
                    flat[side] = jnp.transpose(left[side])

        at = 0
        for pair, right, flat in zip(pairs, rights, turned):
            lanes = pair[2]
            near_ref[0, :, at : at + lanes] = dot_nn(flat[0], right[0]).astype(BF)
            far_ref[0, :, at : at + lanes] = dot_nn(flat[1], right[0]).astype(BF)
            at += lanes

    def right_spec(pair):
        return pl.BlockSpec((1, pair[1].shape[1], pair[2]), lambda p: (p, 0, pair[3]))

    out = jax.ShapeDtypeStruct((parts, half, total), BF)
    return pl.pallas_call(
        kernel,
        name=name,
        grid=(parts,),
        in_specs=[full(pair[0].shape) for pair in pairs] + [right_spec(pair) for pair in pairs],
        out_specs=[pl.BlockSpec((1, half, total), lambda p: (p, 0, 0))] * 2,
        out_shape=[out, out],
        scratch_shapes=[pltpu.VMEM((2, half, count), BF) for count in rows],
        compiler_params=params(),
        cost_estimate=cost(sum(4 * half * parts * pair[2] * count for pair, count in zip(pairs, rows))),
    )(*[pair[0] for pair in pairs], *[pair[1] for pair in pairs])


def norm_unit(halves):
    width = 2 * halves[0].shape[-1]
    mean = sum(jnp.sum(half, -1, keepdims=True) for half in halves) / width
    centre = [half - mean for half in halves]
    spread = sum(jnp.sum(half * half, -1, keepdims=True) for half in centre) / width
    scale = lax.rsqrt(spread + EPS)
    return [half * scale for half in centre], scale


def norm_back(halves, gain_ref, incoming):
    width = 2 * halves[0].shape[-1]
    unit, scale = norm_unit(halves)
    leading = [incoming[side] * gain_ref[side] for side in range(2)]
    mean = sum(jnp.sum(half, -1, keepdims=True) for half in leading) / width
    inner = sum(jnp.sum(leading[side] * unit[side], -1, keepdims=True) for side in range(2)) / width
    back = [scale * (leading[side] - mean - unit[side] * inner) for side in range(2)]
    gains = [jnp.sum(incoming[side] * unit[side], 0, keepdims=True) for side in range(2)]
    return back, gains


def join_rows(pieces, name="join_rows"):
    parts, rows, lanes = pieces[0].shape
    count = len(pieces)
    if rows % 16:
        return jnp.concatenate(pieces, 1)

    def kernel(*refs):
        for index in range(count):

            @pl.when(pl.program_id(1) == index)
            def _():
                refs[-1][...] = refs[index][...]

    return pl.pallas_call(
        kernel,
        name=name,
        grid=(parts, count),
        in_specs=[pl.BlockSpec((1, rows, lanes), lambda p, i: (p, 0, 0))] * count,
        out_specs=pl.BlockSpec((1, rows, lanes), lambda p, i: (p, i, 0)),
        out_shape=jax.ShapeDtypeStruct((parts, count * rows, lanes), BF),
        compiler_params=params(24),
        cost_estimate=cost(parts * count * rows * lanes),
    )(*pieces)


def sum_rows(terms, rows, count, name="sum_rows"):
    parts, _, lanes = terms[0][0].shape
    if rows % 16:
        value = 0.0
        for array, first, step in terms:
            blocks = array.reshape(parts, -1, rows, lanes)[:, first :: step][:, :count]
            value = value + blocks.astype(F32)
        return value.astype(BF).reshape(parts, count * rows, lanes)

    def kernel(*refs):
        value = refs[0][...].astype(F32)
        for ref in refs[1:-1]:
            value = value + ref[...].astype(F32)
        refs[-1][...] = value.astype(BF)

    def spec(first, step):
        return pl.BlockSpec((1, rows, lanes), lambda p, i: (p, first + step * i, 0))

    return pl.pallas_call(
        kernel,
        name=name,
        grid=(parts, count),
        in_specs=[spec(first, step) for _, first, step in terms],
        out_specs=spec(0, 1),
        out_shape=jax.ShapeDtypeStruct((parts, count * rows, lanes), BF),
        compiler_params=params(24),
        cost_estimate=cost(parts * count * rows * lanes),
    )(*[term[0] for term in terms])


def side_by_side(left, right, kept, lanes):
    rows, width = left.shape
    count = width // kept

    def kernel(left_ref, right_ref, out_ref):
        for index, ref in enumerate((left_ref, right_ref)):
            for side in range(count):
                spot = count * index + side
                out_ref[spot, :, :kept] = ref[:, side * kept : (side + 1) * kept]
                if lanes > kept:
                    out_ref[spot, :, kept:] = jnp.zeros((rows, lanes - kept), BF)

    return pl.pallas_call(
        kernel,
        name="side_by_side",
        out_shape=jax.ShapeDtypeStruct((2 * count, rows, lanes), BF),
        compiler_params=params(24),
        cost_estimate=cost(4 * rows * lanes),
    )(left, right)


def mlp_forward(rows_in, grads, start, weight1, weight2, part, live=None):
    _, rows, half = rows_in.shape
    parts, _, lanes = weight1.near.shape
    ff = lanes // 2
    step = 384 if ff % 384 == 0 else ff
    steps = ff // step
    extras = [] if live is None else [live]

    def kernel(x_ref, g_ref, s_ref, n1_ref, f1_ref, n2_ref, f2_ref, *refs):
        hid_ref, act_ref, out_ref, dn2_ref, df2_ref, turned, sums = refs[len(extras) :]
        first = (pl.program_id(0) == 0) & (pl.program_id(1) == 0)
        last = (pl.program_id(0) == parts - 1) & (pl.program_id(1) == steps - 1)

        @pl.when(first)
        def _():
            for side in range(2):
                turned[side] = jnp.transpose(g_ref[side])
            sums[...] = s_ref[...]

        hidden = dot_nn(x_ref[0], n1_ref[0]) + dot_nn(x_ref[1], f1_ref[0])
        hid_ref[0] = hidden
        activ = jax.nn.gelu(hidden, approximate=True).astype(BF)
        act_ref[0] = activ
        sums[0] += dot_nt(activ, n2_ref[0])
        sums[1] += dot_nt(activ, f2_ref[0])
        dn2_ref[0] = dot_nn(turned[0], activ).astype(BF)
        df2_ref[0] = dot_nn(turned[1], activ).astype(BF)

        @pl.when(last)
        def _():
            if live is None:
                out_ref[...] = sums[...]
            else:
                out_ref[...] = (sums[...] * refs[0][...]).astype(BF)

    weight = pl.BlockSpec((1, half, step), lambda p, n: (p, 0, part * steps + n))
    grad = pl.BlockSpec((1, half, step), lambda p, n: (p, 0, n))
    unit = pl.BlockSpec((1, rows, step), lambda p, n: (p, 0, n))
    whole = full((2, rows, half))
    grad_shape = jax.ShapeDtypeStruct((parts, half, ff), BF)
    return pl.pallas_call(
        kernel,
        name="mlp_forward",
        grid=(parts, steps),
        in_specs=[whole, whole, whole, weight, weight, weight, weight] + [full(extra.shape) for extra in extras],
        out_specs=[unit, unit, whole, grad, grad],
        out_shape=[
            jax.ShapeDtypeStruct((parts, rows, ff), F32),
            jax.ShapeDtypeStruct((parts, rows, ff), BF),
            jax.ShapeDtypeStruct((2, rows, half), F32 if live is None else BF),
            grad_shape,
            grad_shape,
        ],
        scratch_shapes=[pltpu.VMEM((2, half, rows), BF), pltpu.VMEM((2, rows, half), F32)],
        compiler_params=params(),
        cost_estimate=cost(12 * rows * half * parts * ff),
    )(rows_in, grads, start, weight1.near, weight1.far, weight2.near, weight2.far, *extras)


def gelu_slope(value):
    root = math.sqrt(2.0 / math.pi)
    square = value * value
    curve = jnp.tanh(root * value * (1.0 + 0.044715 * square))
    return 0.5 * (1.0 + curve) + 0.5 * value * (1.0 - curve * curve) * root * (
        1.0 + 3.0 * 0.044715 * square
    )


def mlp_backward(grads, rows_in, hidden, weight1, weight2, part, start, finish=None):
    _, rows, half = rows_in.shape
    parts, _, lanes = weight1.near.shape
    ff = lanes // 2
    step = 384 if ff % 384 == 0 else ff
    steps = ff // step
    extras = list(finish or []) + ([] if start is None else [start])

    def kernel(g_ref, x_ref, hid_ref, n1_ref, f1_ref, n2_ref, f2_ref, *refs):
        extra_refs, refs = refs[: len(extras)], refs[len(extras) :]
        dn1_ref, df1_ref = refs[:2]
        out_refs = refs[2:-2]
        turned, sums = refs[-2:]
        first = (pl.program_id(0) == 0) & (pl.program_id(1) == 0)
        last = (pl.program_id(0) == parts - 1) & (pl.program_id(1) == steps - 1)

        @pl.when(first)
        def _():
            for side in range(2):
                turned[side] = jnp.transpose(x_ref[side])
            sums[...] = jnp.zeros_like(sums) if start is None else extra_refs[-1][...]

        d_activ = dot_nn(g_ref[0], n2_ref[0]) + dot_nn(g_ref[1], f2_ref[0])
        d_hidden = (d_activ * gelu_slope(hid_ref[0])).astype(BF)
        dn1_ref[0] = dot_nn(turned[0], d_hidden).astype(BF)
        df1_ref[0] = dot_nn(turned[1], d_hidden).astype(BF)
        sums[0] += dot_nt(d_hidden, n1_ref[0])
        sums[1] += dot_nt(d_hidden, f1_ref[0])

        @pl.when(last)
        def _():
            if finish is None:
                out_refs[0][...] = sums[...]
            else:
                value_ref, gain_ref, add_ref = extra_refs[:3]
                add_norm_back([sums[0], sums[1]], value_ref, gain_ref, add_ref, *out_refs)

    weight = pl.BlockSpec((1, half, step), lambda p, n: (p, 0, part * steps + n))
    grad = pl.BlockSpec((1, half, step), lambda p, n: (p, 0, n))
    unit = pl.BlockSpec((1, rows, step), lambda p, n: (p, 0, n))
    whole = full((2, rows, half))
    grad_shape = jax.ShapeDtypeStruct((parts, half, ff), BF)
    wide = jax.ShapeDtypeStruct((2, rows, half), F32)
    outs = [wide] if finish is None else [wide, *back_shapes(rows, half)]
    return pl.pallas_call(
        kernel,
        name="mlp_backward",
        grid=(parts, steps),
        in_specs=[whole, whole, unit, weight, weight, weight, weight] + [full(extra.shape) for extra in extras],
        out_specs=[grad, grad] + [full(out.shape) for out in outs],
        out_shape=[grad_shape, grad_shape] + outs,
        scratch_shapes=[pltpu.VMEM((2, half, rows), BF), pltpu.VMEM((2, rows, half), F32)],
        compiler_params=params(56),
        cost_estimate=cost(12 * rows * half * parts * ff),
    )(grads, rows_in, hidden, weight1.near, weight1.far, weight2.near, weight2.far, *extras)


def back_shapes(rows, half):
    return [jax.ShapeDtypeStruct((2, rows, half), BF), jax.ShapeDtypeStruct((2, 1, half), F32)]


def add_norm_back(incoming, value_ref, gain_ref, add_ref, out_ref, low_ref, d_gain_ref):
    back, gains = norm_back([value_ref[0], value_ref[1]], gain_ref, incoming)
    for side in range(2):
        total = add_ref[side] + back[side]
        out_ref[side] = total
        low_ref[side] = total.astype(BF)
        d_gain_ref[side] = gains[side]


def text_bias(lengths_ref, micro, words, strip, text_slots, axis):
    spot = lax.broadcasted_iota(jnp.int32, (1, words) if axis else (words, 1), axis)
    inner = spot % strip
    place = spot // strip * text_slots + inner
    live = (place < lengths_ref[micro, 0]) | (
        (place >= CLIP_LEN) & (place < CLIP_LEN + lengths_ref[micro, 1])
    )
    return jnp.where(live & (inner < text_slots), 0.0, MASKED)


def cross_forward(query, text_kv, lengths, text_slots):
    parts, micros, slots, lanes = query.shape
    zones, strip = text_kv.shape[1], text_kv.shape[3]
    words = zones * strip
    local = lanes // HP
    factor = HD ** (-0.5) * LOG2E

    def kernel(len_ref, q_ref, kv_ref, out_ref):
        bias = text_bias(len_ref, pl.program_id(1), words, strip, text_slots, 1)
        for h in range(local):
            cut = slice(h * HP, (h + 1) * HP)
            keys = kv_ref[0, :, 0, :, cut].reshape(words, HP)
            scores = dot_nt(q_ref[0, 0, :, cut], keys) + bias
            top = jnp.max(scores, -1, keepdims=True)
            raised = jnp.exp2((scores - top) * factor)
            total = jnp.sum(raised, -1, keepdims=True)
            values = kv_ref[0, :, 0, :, lanes + h * HP : lanes + (h + 1) * HP].reshape(words, HP)
            out_ref[0, 0, :, cut] = (dot_nn(raised.astype(BF), values) / total).astype(BF)

    spot = lambda p, m, c: (p, m, 0, 0)
    far = lambda p, m, c: (p, 0, m, 0, 0)
    return pl.pallas_call(
        kernel,
        name="cross_forward",
        grid_spec=pltpu.PrefetchScalarGridSpec(
            num_scalar_prefetch=1,
            grid=(parts, micros),
            in_specs=[
                pl.BlockSpec((1, 1, slots, lanes), spot),
                pl.BlockSpec((1, zones, 1, strip, 2 * lanes), far),
            ],
            out_specs=pl.BlockSpec((1, 1, slots, lanes), spot),
        ),
        out_shape=jax.ShapeDtypeStruct(query.shape, BF),
        compiler_params=pltpu.CompilerParams(vmem_limit_bytes=32 << 20),
        cost_estimate=cost(4 * parts * micros * slots * words * lanes),
    )(lengths, query, text_kv)


def cross_backward(query, text_kv, lengths, incoming, text_slots):
    parts, micros, slots, lanes = query.shape
    zones, strip = text_kv.shape[1], text_kv.shape[3]
    words = zones * strip
    local = lanes // HP
    scale = HD ** (-0.5)
    factor = scale * LOG2E

    def kernel(len_ref, q_ref, kv_ref, in_ref, dq_ref, dkv_ref):
        bias = text_bias(len_ref, pl.program_id(1), words, strip, text_slots, 0)
        for h in range(local):
            cut = slice(h * HP, (h + 1) * HP)
            far = slice(lanes + h * HP, lanes + (h + 1) * HP)
            rows = q_ref[0, 0, :, cut]
            keys = kv_ref[0, :, 0, :, cut].reshape(words, HP)
            values = kv_ref[0, :, 0, :, far].reshape(words, HP)
            grads = in_ref[0, 0, :, cut]
            scores = dot_nt(keys, rows) + bias
            top = jnp.max(scores, 0, keepdims=True)
            raised = jnp.exp2((scores - top) * factor)
            probs = raised * (1.0 / jnp.sum(raised, 0, keepdims=True))
            d_probs = dot_nt(values, grads)
            inner = jnp.sum(probs * d_probs, 0, keepdims=True)
            d_scores = (probs * (d_probs - inner)).astype(BF)
            shape = (zones, strip, HP)
            dkv_ref[0, :, 0, :, far] = dot_nn(probs.astype(BF), grads).astype(BF).reshape(shape)
            dkv_ref[0, :, 0, :, cut] = (dot_nn(d_scores, rows) * scale).astype(BF).reshape(shape)
            dq_ref[0, 0, :, cut] = (dot_tn(d_scores, keys) * scale).astype(BF)

    spot = lambda p, m, c: (p, m, 0, 0)
    far = lambda p, m, c: (p, 0, m, 0, 0)
    return pl.pallas_call(
        kernel,
        name="cross_backward",
        grid_spec=pltpu.PrefetchScalarGridSpec(
            num_scalar_prefetch=1,
            grid=(parts, micros),
            in_specs=[
                pl.BlockSpec((1, 1, slots, lanes), spot),
                pl.BlockSpec((1, zones, 1, strip, 2 * lanes), far),
                pl.BlockSpec((1, 1, slots, lanes), spot),
            ],
            out_specs=[
                pl.BlockSpec((1, 1, slots, lanes), spot),
                pl.BlockSpec((1, zones, 1, strip, 2 * lanes), far),
            ],
        ),
        out_shape=[
            jax.ShapeDtypeStruct(query.shape, BF),
            jax.ShapeDtypeStruct(text_kv.shape, BF),
        ],
        compiler_params=pltpu.CompilerParams(vmem_limit_bytes=32 << 20),
        cost_estimate=cost(10 * parts * micros * slots * words * lanes),
    )(lengths, query, text_kv, incoming)


def tie(*values):
    return lax.optimization_barrier(values)


class Cube:
    def __init__(self):
        self.size = lax.axis_size("dp")
        self.bits = self.size.bit_length() - 1
        self.outer = list(range(1, self.bits))
        self.rank = lax.axis_index("dp")
        self.masks = []
        for place in range(self.size):
            mask = place >> (self.bits - 1)
            for bit in self.outer:
                mask |= ((place >> (bit - 1)) & 1) << bit
            self.masks.append(mask)
        self.owners = self.rank ^ jnp.array(self.masks, jnp.int32)

    def swap(self, value, bit, axis="dp"):
        pairs = [(i, i ^ (1 << bit)) for i in range(lax.axis_size(axis))]
        return lax.ppermute(value, axis, pairs)

    def trade(self, value):
        blocks = {mask: value[mask] for mask in range(self.size)}
        for bit in range(self.bits):
            send = sorted(mask for mask in blocks if mask >> bit & 1)
            got = self.swap(jnp.stack([blocks[mask] for mask in send]), bit)
            for place, mask in enumerate(send):
                blocks[mask] = got[place]
        return jnp.stack([blocks[mask] for mask in range(self.size)])

    def spread(self, value):
        held = value[None]
        for bit in range(self.bits):
            held = jnp.concatenate([held, self.swap(held, bit)])
        return held

    def add(self, value, axis):
        for bit in range(lax.axis_size(axis).bit_length() - 1):
            value = value + self.swap(value, bit, axis)
        return value


class Gather:
    def __init__(self, cube, shard, flip):
        self.cube = cube
        self.masks = [0]
        self.pieces = [shard]
        self.todo = cube.outer[::-1] if flip else list(cube.outer)

    def move(self):
        bit = self.todo.pop(0)
        self.masks = self.masks + [mask | (1 << bit) for mask in self.masks]
        self.pieces = self.pieces + [self.cube.swap(piece, bit) for piece in self.pieces]

    def join(self):
        while self.todo:
            self.move()
        order = sorted(range(len(self.masks)), key=lambda i: self.cube.masks.index(self.masks[i]))
        self.pieces = [join_rows([self.pieces[i] for i in order])]

    def weight(self):
        near = self.pieces[0]
        return Lanes(near, self.cube.swap(near, 0))


class Scatter:
    def __init__(self, cube, near, far, flip):
        self.cube = cube
        self.todo = list(cube.outer) if flip else cube.outer[::-1]
        self.rows = near.shape[1] // (cube.size // 2)
        self.places = list(range(cube.size // 2))
        self.near = near
        self.got = []
        self.pieces = [cube.swap(far, 0)]
        self.arriving = self.places
        self.packed = False

    def total(self, places):
        first = places[0]
        step = places[1] - first if len(places) > 1 else 1
        terms = [(self.near, first, step)]
        for value, held in self.got:
            spots = [held.index(place) for place in places]
            terms.append((value, spots[0], spots[1] - spots[0] if len(spots) > 1 else 1))
        return sum_rows(terms, self.rows, len(places))

    def absorb(self):
        self.got.append((self.pieces[0], self.arriving))

    def pack(self):
        self.absorb()
        self.bit = self.todo.pop(0)
        weight = 1 << (self.bit - 1)
        sent = [place for place in self.places if place & weight]
        self.places = [place for place in self.places if not place & weight]
        self.arriving = [place ^ weight for place in sent]
        self.pieces = [self.total(sent)]
        self.packed = True

    def move(self):
        if not self.packed:
            self.pack()
        self.pieces = [self.cube.swap(self.pieces[0], self.bit)]
        self.packed = False

    def result(self):
        while self.todo or self.packed:
            self.move()
        self.absorb()
        return self.total([0])


def bind(value, *movers):
    flat = [piece for mover in movers for piece in mover.pieces]
    held = tie(value, *flat)
    spot = 1
    for mover in movers:
        count = len(mover.pieces)
        mover.pieces = list(held[spot : spot + count])
        spot += count
    return held[0]


def on_device(
    tokens,
    skip_tokens,
    text,
    timestep,
    grid,
    text_len,
    w_skip,
    w_mod,
    w_qkv,
    w_out1,
    w_query2,
    w_text_kv,
    w_out2,
    w_fc1,
    w_fc2,
    gain_skip,
    gain_attn,
    gain_cross,
    gain_mlp,
    gain_query,
    gain_key,
    cotangent,
):
    micros, slots, width = tokens.shape
    parts = lax.axis_size("sp")
    zone = lax.axis_index("sp")
    cube = Cube()
    ranks = cube.size
    rows = micros * slots
    sequence = slots * parts
    local = H // parts
    lanes = local * HP + -local * HP % 128
    text_slots = text.shape[1]
    text_strip = -(-text_slots // 16) * 16
    features = text.shape[2]
    strip = width // ranks
    middle = width // 2
    kept = w_skip.shape[0]
    skip_lanes = -(-kept // 256) * 256
    skip_cut = skip_lanes // 2
    qkv_cut = (3 * lanes) // 256 * 128 + 128
    text_rows = w_text_kv.shape[0]

    def spread(shard, before=None):
        if before is not None:
            shard, before = tie(shard, before)
        return lax.all_gather(shard, "sp", axis=0, tiled=False)

    def fetch(value, cut):
        return [Gather(cube, value[:, :, :cut], 0), Gather(cube, value[:, :, cut:], 1)]

    def advance(movers):
        for mover in movers:
            mover.move()

    def join(movers):
        for mover in movers:
            mover.join()

    def exchange(value):
        return lax.all_to_all(value, "sp", split_axis=0, concat_axis=0, tiled=True)

    skip_z = spread(jnp.pad(w_skip.T, ((0, 0), (0, skip_lanes - kept))))
    skip_m = fetch(skip_z, skip_cut)
    qkv_z = spread(pad_heads(w_qkv.reshape(strip, -1), local), skip_z)
    while skip_m[0].todo:
        advance(skip_m)
    qkv_z = bind(qkv_z, *skip_m)
    fc1_z = spread(w_fc1, qkv_z)
    fc2_z = spread(w_fc2.T, fc1_z)
    join(skip_m)
    skip_w = [mover.weight() for mover in skip_m]
    qkv_m = fetch(qkv_z, qkv_cut)
    advance(qkv_m)

    def shuffle(count):
        block = count // ranks
        place = jnp.arange(count, dtype=jnp.int32)
        source = cube.owners[place // block] * block + place % block
        return (place[:, None] == source[None, :]).astype(BF)

    turn = shuffle(width)
    text_turn = shuffle(features)
    gains = jnp.stack([gain_skip, gain_attn, gain_cross, gain_mlp])
    gains = gains.reshape(4, ranks, strip)[:, cube.owners].reshape(4, 2, 1, middle)
    g_skip, g_attn, g_cross, g_mlp = gains

    wide = grid[:, 0, 1]
    counts = grid[:, 0, 0] * wide
    lengths = text_len[:, 0, :]
    place = zone * slots + jnp.arange(slots, dtype=jnp.int32)
    live = (place[None, :] < counts[:, None]).astype(F32).reshape(rows, 1)
    cosine, sine = rope_tables(sequence, wide, lanes)
    gain_q = pad_heads(jnp.tile(gain_query, local)[None, :], local)
    gain_k = pad_heads(jnp.tile(gain_key, local)[None, :], local)

    steps = cube.spread(timestep[:, 0])
    time_act = jax.nn.silu(time_embed(steps, width)).astype(BF).reshape(ranks * micros, parts, -1)
    time_part = lax.dynamic_index_in_dim(time_act, zone, 1, keepdims=False)
    shift = jnp.dot(time_part, w_mod, preferred_element_type=F32)
    shift = cube.trade(cube.add(shift, "sp").reshape(ranks, micros, strip))
    shift = jnp.stack([shift[mask] for mask in cube.masks]).reshape(2, ranks // 2, micros, strip)
    shift = jnp.transpose(shift, (0, 2, 1, 3)).reshape(2, micros, middle)

    grad3 = jnp.stack(
        [
            jnp.dot(cotangent.reshape(rows, width), side, preferred_element_type=F32) * live
            for side in (turn[:, :middle], turn[:, middle:])
        ]
    )
    d_mlp = grad3.astype(BF)

    wide_shape = jax.ShapeDtypeStruct((2, rows, middle), F32)
    low_shape = jax.ShapeDtypeStruct((2, rows, middle), BF)
    gain_shape = jax.ShapeDtypeStruct((2, 1, middle), F32)
    joined = side_by_side(tokens.reshape(rows, width), skip_tokens.reshape(rows, width), kept, skip_lanes)

    def first_norms(sums, extra, out):
        g0_ref, g1_ref, shift_ref = extra
        base_ref, stream_ref, pre_ref = out
        unit, _ = norm_unit(sums)
        stream = [unit[side] * g0_ref[side] for side in range(2)]
        unit, _ = norm_unit(stream)
        for side in range(2):
            base_ref[side] = sums[side]
            stream_ref[side] = stream[side]
            for micro in range(micros):
                cut = slice(micro * slots, (micro + 1) * slots)
                pre = unit[side][cut] * g1_ref[side] + shift_ref[side, micro : micro + 1]
                pre_ref[side, cut] = pre.astype(BF)

    def next_norm(sums, extra, out):
        before_ref, gain_ref = extra
        after_ref, pre_ref = out
        stream = [before_ref[side] + sums[side] for side in range(2)]
        unit, _ = norm_unit(stream)
        for side in range(2):
            after_ref[side] = stream[side]
            pre_ref[side] = (unit[side] * gain_ref[side]).astype(BF)

    base, stream, pre_attn = to_features(
        joined, skip_w, [g_skip, g_attn, shift], [wide_shape, wide_shape, low_shape], first_norms
    )
    while qkv_m[0].todo:
        advance(qkv_m)
    pre_attn = bind(pre_attn, *qkv_m)
    join(qkv_m)
    qkv_w = [mover.weight() for mover in qkv_m]
    fc_m = [Gather(cube, fc1_z, 0), Gather(cube, fc2_z, 1)]
    projected = to_lanes(pre_attn, qkv_w)
    projected = bind(projected, fc_m[0])
    advance(fc_m)
    raw = exchange(projected.reshape(parts, micros, slots, 3 * lanes))
    raw = bind(raw, *fc_m)
    cross_z = jnp.concatenate([pad_heads(side, local) for side in (w_out1.T, w_query2, w_out2.T)], 1)
    cross_z = spread(cross_z, raw)
    text_z = jnp.pad(pad_heads(w_text_kv.reshape(text_rows, -1), local), ((0, max(0, strip - text_rows)), (0, 0)))
    text_z = spread(text_z, cross_z)
    text_own = jnp.dot(text.reshape(-1, features), text_turn, preferred_element_type=F32).astype(BF)
    text_own = jnp.pad(
        text_own.reshape(micros, text_slots, features), ((0, 0), (0, text_strip - text_slots), (0, 0))
    ).reshape(micros * text_strip, features)
    text_all = spread(text_own, text_z).reshape(-1, features)
    text_all = jnp.stack([text_all[:, : features // 2], text_all[:, features // 2 :]])
    while fc_m[0].todo:
        advance(fc_m)
    attended, turned_q, turned_k, norms = self_forward(raw, counts, cosine, sine, gain_q, gain_k)
    attended = bind(attended, *fc_m)
    attended = exchange(attended).reshape(parts, rows, lanes)
    cross_m = fetch(cross_z, 2 * lanes)
    text_m = Gather(cube, text_z[:, :text_rows], 1)
    join(cross_m)
    first_w, out2_w = [mover.weight() for mover in cross_m]
    out1_w, query2_w = (Lanes(first_w.near, first_w.far, lanes, index) for index in range(2))
    join(fc_m)
    fc1_w, fc2_w = [mover.weight() for mover in fc_m]
    text_m.join()
    text_w = text_m.weight()
    stream1, pre_cross = to_features(
        attended, [out1_w], [stream, g_cross], [wide_shape, low_shape], next_norm
    )
    query2 = to_lanes(pre_cross, [query2_w]).reshape(parts, micros, slots, lanes)
    text_kv = to_lanes(text_all, [text_w]).reshape(parts, parts, micros, text_strip, 2 * lanes)
    crossed = cross_forward(query2, text_kv, lengths, text_slots).reshape(parts, rows, lanes)
    stream2, pre_mlp = to_features(
        crossed, [out2_w], [stream1, g_mlp], [wide_shape, low_shape], next_norm
    )
    hidden0, activ0, partial, fc2_n0, fc2_f0 = mlp_forward(pre_mlp, d_mlp, stream2, fc1_w, fc2_w, 0)
    hidden1, activ1, result, fc2_n1, fc2_f1 = mlp_forward(pre_mlp, d_mlp, partial, fc1_w, fc2_w, 1, live)
    fc2_s = [Scatter(cube, fc2_n0, fc2_f0, 0), Scatter(cube, fc2_n1, fc2_f1, 1)]

    def pack(movers):
        for mover in movers:
            mover.pack()

    def settle(values, before=None):
        value = values[0] if len(values) == 1 else jnp.concatenate(values, 2)
        if before is not None:
            value, before = tie(value, before)
        return lax.psum_scatter(value, "sp", scatter_dimension=0, tiled=False)

    fc1_n0, fc1_f0, partial = mlp_backward(d_mlp, pre_mlp, hidden0, fc1_w, fc2_w, 0, None)
    partial = bind(partial, *fc2_s)
    pack(fc2_s)
    partial = bind(partial, *fc2_s)
    advance(fc2_s)
    fc1_n1, fc1_f1, grad2, d_cross, d_gain_mlp = mlp_backward(
        d_mlp, pre_mlp, hidden1, fc1_w, fc2_w, 1, partial, [stream2, g_mlp, grad3]
    )
    fc1_s = [Scatter(cube, fc1_n0, fc1_f0, 0), Scatter(cube, fc1_n1, fc1_f1, 1)]
    d_crossed = to_lanes(d_cross, [out2_w])
    d_crossed = bind(d_crossed, *fc2_s)
    pack(fc2_s)
    d_crossed = bind(d_crossed, *fc2_s)
    advance(fc2_s)
    d_query2, d_text_kv = cross_backward(
        query2, text_kv, lengths, d_crossed.reshape(parts, micros, slots, lanes), text_slots
    )
    d_query2 = bind(d_query2, *fc1_s)
    pack(fc1_s)
    d_query2 = bind(d_query2, *fc1_s)
    advance(fc1_s)
    d_query2 = d_query2.reshape(parts, rows, lanes)
    d_text_kv = d_text_kv.reshape(parts, -1, 2 * lanes)

    def go_back(sums, extra, out):
        add_norm_back(sums, *extra, *out)

    grad1, d_attn, d_gain_cross = to_features(
        d_query2, [query2_w], [stream1, g_cross, grad2], [wide_shape, low_shape, gain_shape], go_back
    )
    d_attended = to_lanes(d_attn, [out1_w])
    d_heads = exchange(d_attended.reshape(parts, micros, slots, lanes))

    def words_back(sums, extra, out):
        size = micros * text_strip
        for zone in range(parts):
            for side in range(2):
                out[0][zone, side] = sums[side][zone * size : (zone + 1) * size].astype(BF)

    words_shape = jax.ShapeDtypeStruct((parts, 2, micros * text_strip, features // 2), BF)
    d_words = to_features(d_text_kv, [text_w], [], [words_shape], words_back)[0]
    d_words = settle([d_words])
    text_s = Scatter(cube, *terms_of([(text_all, d_text_kv, 2 * lanes, 0)]), 1)
    cross_s = Scatter(
        cube,
        *terms_of([(d_attn, attended, lanes, 0), (pre_cross, d_query2, lanes, 0), (d_cross, crossed, lanes, 0)]),
        0,
    )
    total_fc2 = [mover.result() for mover in fc2_s]
    term_fc2 = settle(total_fc2)
    d_heads = bind(d_heads, text_s, cross_s)
    d_raw, d_gain_q, d_gain_k = self_backward(
        raw, counts, cosine, sine, gain_q, gain_k, turned_q, turned_k, norms, d_heads
    )
    d_raw = bind(d_raw, *fc1_s)
    d_projected = exchange(d_raw).reshape(parts, rows, 3 * lanes)
    pack(fc1_s)
    advance(fc1_s)
    pack([cross_s, text_s])
    advance([cross_s, text_s])
    total_fc1 = [mover.result() for mover in fc1_s]

    def last_norms(sums, extra, out):
        stream_ref, g1_ref, base_ref, g0_ref, add_ref = extra
        low_ref, d_shift_ref, d_g1_ref, d_g0_ref = out
        back, gains1 = norm_back([stream_ref[0], stream_ref[1]], g1_ref, sums)
        total = [add_ref[side] + back[side] for side in range(2)]
        back, gains0 = norm_back([base_ref[0], base_ref[1]], g0_ref, total)
        for side in range(2):
            low_ref[side] = back[side].astype(BF)
            d_g1_ref[side] = gains1[side]
            d_g0_ref[side] = gains0[side]
            for micro in range(micros):
                part = sums[side][micro * slots : (micro + 1) * slots]
                d_shift_ref[side, micro : micro + 1] = jnp.sum(part, 0, keepdims=True)

    qkv_t = [terms_of([(pre_attn, d_projected, 3 * lanes, 0)])]
    qkv_s = [Scatter(cube, *qkv_t[0], 0)]
    shift_shape = jax.ShapeDtypeStruct((2, micros, middle), F32)
    d_base, d_shift, d_gain_attn, d_gain_skip = to_features(
        d_projected,
        qkv_w,
        [stream, g_attn, base, g_skip, grad1],
        [low_shape, shift_shape, gain_shape, gain_shape],
        last_norms,
    )
    d_base = bind(d_base, *qkv_s)
    pack(qkv_s)
    d_base = bind(d_base, *qkv_s)
    advance(qkv_s)
    skip_s = [Scatter(cube, *terms_of([(d_base, joined, skip_lanes, 0)]), 1)]
    term_fc1 = settle(total_fc1, d_base)
    pack(skip_s)
    advance(skip_s)
    term_cross = settle([cross_s.result()])
    term_text = settle([text_s.result()])
    term_qkv = settle([mover.result() for mover in qkv_s])
    term_skip = settle([mover.result() for mover in skip_s])
    d_joined = to_inputs(d_base, skip_w, kept)
    result = (
        jnp.dot(result[0], turn[:, :middle].T, preferred_element_type=F32)
        + jnp.dot(result[1], turn[:, middle:].T, preferred_element_type=F32)
    ).astype(BF)
    d_words = d_words.reshape(2, micros * text_strip, features // 2)
    d_words = jnp.dot(
        d_words[0], text_turn[:, : features // 2].T, preferred_element_type=F32
    ) + jnp.dot(d_words[1], text_turn[:, features // 2 :].T, preferred_element_type=F32)
    d_words = d_words.reshape(micros, text_strip, features)[:, :text_slots]

    d_shift = jnp.transpose(d_shift.reshape(2, micros, ranks // 2, strip), (0, 2, 1, 3))
    d_shift = d_shift.reshape(ranks, micros, strip)
    d_shift = jnp.stack([d_shift[cube.masks.index(mask)] for mask in range(ranks)])
    d_shift = cube.add(cube.trade(d_shift), "sp").reshape(ranks * micros, strip)
    term_mod = lax.dot_general(
        time_part.astype(F32), d_shift, (((0,), (0,)), ((), ())), precision=lax.Precision.HIGHEST
    )

    places = jnp.array([cube.masks.index(mask) for mask in range(ranks)], jnp.int32)
    places = places[jnp.arange(ranks, dtype=jnp.int32) ^ cube.rank]
    gains = jnp.stack([d_gain_skip, d_gain_attn, d_gain_cross, d_gain_mlp])
    gains = gains.reshape(4, ranks, strip)[:, places].reshape(-1)
    heads = jnp.stack([jnp.sum(d_gain_q, (0, 1)), jnp.sum(d_gain_k, (0, 1))])
    heads = jnp.sum(heads[:, : local * HP].reshape(2, local, HP)[:, :, :HD], 1)
    packed = jnp.concatenate([gains, heads.reshape(-1)])
    packed = cube.add(cube.add(packed, "sp"), "dp")
    gains = packed[: 4 * width].reshape(4, ranks * parts, -1)
    gains = lax.dynamic_index_in_dim(gains, cube.rank * parts + zone, 1, keepdims=False)
    heads = packed[4 * width :].reshape(2, HD)

    def whole(term, groups):
        return cut_heads(term.astype(F32), local).reshape(term.shape[0], groups, -1)

    return (
        result.reshape(tokens.shape),
        d_joined[0].reshape(tokens.shape),
        d_joined[1].reshape(tokens.shape),
        d_words.reshape(text.shape),
        term_skip.astype(F32)[:, :kept].T,
        term_mod,
        whole(term_qkv, 3),
        cut_heads(term_cross[:, :lanes].astype(F32), local).T,
        cut_heads(term_cross[:, lanes : 2 * lanes].astype(F32), local),
        whole(term_text, 2),
        cut_heads(term_cross[:, 2 * lanes :].astype(F32), local).T,
        term_fc1.astype(F32),
        term_fc2.astype(F32).T,
        gains[0],
        gains[1],
        gains[2],
        gains[3],
        heads[0],
        heads[1],
    )


def solution(mesh):
    rows = P(None, ("dp", "sp"), None)
    column = P("sp", "dp")
    row = P("dp", "sp")
    grouped = P("dp", None, "sp")
    in_specs = (
        (rows, rows, rows, P(None, "dp"), P(None, "dp", None), P(None, "dp", None))
        + (column, column, grouped, column, row, grouped, column, row, column)
        + (P(),) * 6
        + (rows,)
    )
    out_specs = (
        (rows, rows, rows, rows)
        + (column, column, grouped, column, row, grouped, column, row, column)
        + (P(("dp", "sp")),) * 4
        + (P(), P())
    )
    return jax.shard_map(
        on_device, mesh=mesh, in_specs=in_specs, out_specs=out_specs, check_vma=False
    )
```

time: 1810 us -> 1740 us (0.961)
  Pallas kernels: 120 us -> 567 us
  waiting for transfers between devices: 467 us -> 814 us
  blocking collectives: 341 us -> 0 us
  matrix products: 287 us -> 13 us
  local copies, waits for them, and re-layouts: 303 us -> 124 us
  other arithmetic: 133 us -> 45.2 us
  starting transfers between devices: 122 us -> 152 us
    pallas_call x0 -> x54, Pallas kernels: none -> 453 us  [the longest x24 88.4 us: sum_rows(): pl.pallas_call(kernel, name=name, grid=(parts, count), in_specs=[spec(fir...]
    dot_general x36 -> x7, matrix products: 285 us -> 11.1 us  [the longest x2 4.26 us: on_device(): jnp.dot(cotangent.reshape(rows, width), side, preferred_element_type=F32)]
    all_gather x5 -> x0, blocking collectives: 197 us -> none  [spread(): return lax.all_gather(shard, 'sp', axis=0, tiled=False)]
    all_gather x3 -> x7, waiting for transfers between devices: 40.4 us -> 217 us  [spread(): return lax.all_gather(shard, 'sp', axis=0, tiled=False)]
    all_to_all x4, waiting for transfers between devices: 0.92 us -> 105 us  [exchange(): return lax.all_to_all(value, 'sp', split_axis=0, concat_axis=0, tiled=True)]
    concatenate x8 -> x2, local copies, waits for them, and re-layouts: 79.6 us -> 0.1 us  [the longest x1 0.09 us: spread(): held = jnp.concatenate([held, self.swap(held, bit)])]
    psum x3 -> x0, blocking collectives: 79 us -> none  [the longest x1 41.3 us: on_device(): packed = lax.psum(packed, ('dp', 'sp'))]
    ppermute x56 -> x78, waiting for transfers between devices: 424 us -> 491 us  [swap(): return lax.ppermute(value, axis, pairs)]
  transfers between devices with their start and end apart: 75 -> 96, of which waited for: 21 -> 45; matrix products, arithmetic and copies ran while one was open for 33% -> 6% of each run, Pallas kernels for 5% -> 28%
where the time goes in v4:
time: 1740 us; the launch traced here: 1730 us
  waiting for transfers between devices  814 us (47%)
  Pallas kernels  567 us (33%)
  starting transfers between devices  152 us (9%)
  local copies, waits for them, and re-layouts  124 us (7%)
  other arithmetic  45.2 us (3%)
    ppermute x78, waiting for transfers between devices, swap(): return lax.ppermute(value, axis, pairs)  491 us
    all_gather x7, waiting for transfers between devices, spread(): return lax.all_gather(shard, 'sp', axis=0, tiled=False)  217 us
    ppermute x78, starting transfers between devices, swap(): return lax.ppermute(value, axis, pairs)  122 us
    all_to_all x4, waiting for transfers between devices, exchange(): return lax.all_to_all(value, 'sp', split_axis=0, concat_axis=0, tiled=True)  105 us
    pallas_call x24, Pallas kernels, sum_rows(): pl.pallas_call(kernel, name=name, grid=(parts, count), in_specs=[spec(fir...  88.4 us
    unnamed x278, local copies, waits for them, and re-layouts  84.6 us
    pallas_call x6, Pallas kernels, to_features(): pl.pallas_call(kernel, name=name, grid=(parts,), in_specs=[pl.BlockSpec((...  78.4 us
    pallas_call x9, Pallas kernels, join_rows(): pl.pallas_call(kernel, name=name, grid=(parts, count), in_specs=[pl.Block...  77.7 us
  transfers between devices with their start and end apart: 96, of which 45 were waited for; matrix products, arithmetic and copies ran while one was open for 6% of the time, Pallas kernels for 28%

profile of v4, /device:TPU:0, one launch (start us, length us, event | category | flops | bytes accessed | tf_op | source)
XLA Modules:
  0.0 1732.4 jit_solution(5232863229215154369)
XLA Ops:
  12.2 29.2 %all-gather.15.cloned.1.call-done = bf16[704,768]{1,0:T(8,128)(2,1)} async-done(((bf16[176,768]{1,0:T(8,128)(2,1)}), bf16[704,768]{1,0:T(8,128)(2,1)}) %all-gather.15.cloned.1.call-update) | async-done | bytes 1081360 | tf_op jit(solution)/shard_map/all_gather | solution.py:968
  120.7 15.4 collective-permute-done.16.refs_1_
  140.3 14.7 to_features.6
  209.2 27.2 %all-gather.19.cloned.1.call-done = bf16[704,1536]{1,0:T(8,128)(2,1)} async-done(((bf16[176,1536]{1,0:T(8,128)(2,1)}), bf16[704,1536]{1,0:T(8,128)(2,1)}) %all-gather.19.cloned.1.call-update) | async-done | bytes 2162704 | tf_op jit(solution)/shard_map/all_gather | solution.py:968
  243.9 80.2 %all-gather.21.cloned.1.call-done = bf16[704,1536]{1,0:T(8,128)(2,1)} async-done(((bf16[176,1536]{1,0:T(8,128)(2,1)}), bf16[704,1536]{1,0:T(8,128)(2,1)}) %all-gather.21.cloned.1.call-update) | async-done | bytes 2162704 | tf_op jit(solution)/shard_map/all_gather | solution.py:968
  325.6 47.8 %collective-permute-done.25.refs_2_ = bf16[4,176,1536]{2,1,0:T(8,128)(2,1)} collective-permute-done((bf16[4,176,1536]{2,1,0:T(8,128)(2,1)}, bf16[4,176,1536]{2,1,0:T(8,128)(2,1)}, u32[]{:S(2)}, u32[]{:S(2)}) %collective-permute-start.25) | collective-permute-done | bytes 2162720 | tf_op jit(solution)/shard_map/ppermute | solution.py:817
  403.0 30.7 %self_forward.1 = (bf16[4,2,256,384]{3,2,1,0:T(8,128)(2,1)}, bf16[2,1024,384]{2,1,0:T(8,128)(2,1)S(1)}, bf16[2,1024,384]{2,1,0:T(8,128)(2,1)S(1)}, f32[2,4,1024]{2,1,0:T(4,128)S(1)}) custom-call(s32[2]{0:T(128)S(1)} %mul.78.count_ref, bf16[4,2,256,1152]{3,2,1,0:T(8,128)(2,1)} %all-to-all-done.raw_ref, f32[2,1024,384]{2,1,0:T(8,128)} %get-tuple-element.275.cos_ref, ...), custom_call_target="tpu_custom_call" | custom-call | flops 3221225472 | bytes 3221225 | tf_op jit(solution)/shard_map/self_forward/pallas_call | solution.py:150
  433.7 42.2 %collective-permute-done.27.refs_3_ = bf16[4,176,1536]{2,1,0:T(8,128)(2,1)} collective-permute-done((bf16[4,176,1536]{2,1,0:T(8,128)(2,1)}, bf16[4,176,1536]{2,1,0:T(8,128)(2,1)}, u32[]{:S(2)}, u32[]{:S(2)}) %collective-permute-start.27) | collective-permute-done | bytes 2162720 | tf_op jit(solution)/shard_map/ppermute | solution.py:817
  506.0 51.6 %all-gather.25.cloned.1.call-done = bf16[704,768]{1,0:T(8,128)(2,1)} async-done(((bf16[176,768]{1,0:T(8,128)(2,1)}), bf16[704,768]{1,0:T(8,128)(2,1)}) %all-gather.25.cloned.1.call-update) | async-done | bytes 1081360 | tf_op jit(solution)/shard_map/all_gather | solution.py:968
  562.4 16.9 collective-permute-done.35.refs_2_
  580.8 20.4 %collective-permute-done.32.refs_3_ = bf16[4,176,768]{2,1,0:T(8,128)(2,1)S(1)} collective-permute-done((bf16[4,176,768]{2,1,0:T(8,128)(2,1)}, bf16[4,176,768]{2,1,0:T(8,128)(2,1)S(1)}, u32[]{:S(2)}, u32[]{:S(2)}) %collective-permute-start.32) | collective-permute-done | bytes 1081376 | tf_op jit(solution)/shard_map/ppermute | solution.py:817
  684.6 28.4 %all-gather.27.cloned.1.call-done = bf16[768,1024]{1,0:T(8,128)(2,1)} async-done(((bf16[192,1024]{1,0:T(8,128)(2,1)}), bf16[768,1024]{1,0:T(8,128)(2,1)}) %all-gather.27.cloned.1.call-update) | async-done | bytes 1572880 | tf_op jit(solution)/shard_map/all_gather | solution.py:968
  742.0 17.3 cross_forward.1
  772.3 28.1 %mlp_forward.2 = (f32[4,512,768]{2,1,0:T(8,128)}, bf16[4,512,768]{2,1,0:T(8,128)(2,1)}, f32[2,512,704]{2,1,0:T(8,128)}, bf16[4,704,768]{2,1,0:T(8,128)(2,1)}, bf16[4,704,768]{2,1,0:T(8,128)(2,1)}) custom-call(bf16[2,512,704]{2,1,0:T(8,128)(2,1)S(1)} %copy-done.41, bf16[2,512,704]{2,1,0:T(8,128)(2,1)S(1)} %fusion.62.g_ref, ...), custom_call_target="tpu_custom_call" | custom-call | flops 13287555072 | bytes 13287555 | tf_op jit(solution)/shard_map/mlp_forward/pallas_call | solution.py:594
  800.5 27.1 %mlp_forward.3 = (f32[4,512,768]{2,1,0:T(8,128)}, bf16[4,512,768]{2,1,0:T(8,128)(2,1)}, bf16[2,512,704]{2,1,0:T(8,128)(2,1)S(1)}, bf16[4,704,768]{2,1,0:T(8,128)(2,1)}, bf16[4,704,768]{2,1,0:T(8,128)(2,1)}) custom-call(bf16[2,512,704]{2,1,0:T(8,128)(2,1)S(1)} %copy-done.41, bf16[2,512,704]{2,1,0:T(8,128)(2,1)S(1)} %fusion.62.g_ref, ...), custom_call_target="tpu_custom_call" | custom-call | flops 13287555072 | bytes 13287555 | tf_op jit(solution)/shard_map/mlp_forward/pallas_call | solution.py:594
  830.0 29.0 %mlp_backward.2 = (bf16[4,704,768]{2,1,0:T(8,128)(2,1)}, bf16[4,704,768]{2,1,0:T(8,128)(2,1)}, f32[2,512,704]{2,1,0:T(8,128)}) custom-call(bf16[2,512,704]{2,1,0:T(8,128)(2,1)} %copy-done.25, bf16[2,512,704]{2,1,0:T(8,128)(2,1)} %get-tuple-element.172.x_ref, f32[4,512,768]{2,1,0:T(8,128)} %get-tuple-element.188.hid_ref, ...), custom_call_target="tpu_custom_call" | custom-call | flops 13287555072 | bytes 13287555 | tf_op jit(solution)/shard_map/mlp_backward/pallas_call | solution.py:666
  873.5 34.9 %mlp_backward.3 = (bf16[4,704,768]{2,1,0:T(8,128)(2,1)}, bf16[4,704,768]{2,1,0:T(8,128)(2,1)}, f32[2,512,704]{2,1,0:T(8,128)}, bf16[2,512,704]{2,1,0:T(8,128)(2,1)}, f32[2,1,704]{2,1,0:T(1,128)}) custom-call(bf16[2,512,704]{2,1,0:T(8,128)(2,1)} %copy-done.25, bf16[2,512,704]{2,1,0:T(8,128)(2,1)} %get-tuple-element.172.x_ref, ...), custom_call_target="tpu_custom_call" | custom-call | flops 13287555072 | bytes 13287555 | tf_op jit(solution)/shard_map/mlp_backward/pallas_call | solution.py:666
  921.5 37.2 %collective-permute-done.46.refs_2_ = bf16[4,352,768]{2,1,0:T(8,128)(2,1)S(1)} collective-permute-done((bf16[4,352,768]{2,1,0:T(8,128)(2,1)}, bf16[4,352,768]{2,1,0:T(8,128)(2,1)S(1)}, u32[]{:S(2)}, u32[]{:S(2)}) %collective-permute-start.46) | collective-permute-done | bytes 2162720 | tf_op jit(solution)/shard_map/ppermute | solution.py:817
  976.2 20.6 %cross_backward.1 = (bf16[4,2,256,384]{3,2,1,0:T(8,128)(2,1)S(1)}, bf16[4,4,2,96,768]{4,3,2,1,0:T(8,128)(2,1)S(1)}) custom-call(s32[2,2]{1,0:T(2,128)S(1)} %bitcast.194, bf16[4,2,256,384]{3,2,1,0:T(8,128)(2,1)S(1)} %bitcast.177, bf16[4,4,2,96,768]{4,3,2,1,0:T(8,128)(2,1)S(1)} %bitcast.181, bf16[4,2,256,384]{3,2,1,0:T(8,128)(2,1)S(1)} %bitcast.197), custom_call_target="tpu_custom_call" | custom-call | flops 3019898880 | bytes 3019898 | tf_op jit(solution)/shard_map/cross_backward/pallas_call | solution.py:772
  1057.7 35.1 %all-to-all-done.2.in_ref = bf16[4,2,256,384]{3,2,1,0:T(8,128)(2,1)} async-done(((bf16[4,2,256,384]{3,2,1,0:T(8,128)(2,1)}), bf16[4,2,256,384]{3,2,1,0:T(8,128)(2,1)}, u32[]{:S(2)}, u32[]{:S(2)}) %all-to-all-start.2) | async-done | bytes 1572896 | tf_op jit(solution)/shard_map/all_to_all | solution.py:982
  1095.7 45.7 %self_backward.1 = (bf16[4,2,256,1152]{3,2,1,0:T(8,128)(2,1)}, f32[2,1,384]{2,1,0:T(1,128)S(1)}, f32[2,1,384]{2,1,0:T(1,128)S(1)}) custom-call(s32[2]{0:T(128)S(1)} %copy-done.67, bf16[4,2,256,1152]{3,2,1,0:T(8,128)(2,1)} %all-to-all-done.raw_ref, f32[2,1024,384]{2,1,0:T(8,128)} %get-tuple-element.275.cos_ref, f32[2,1024,384]{2,1,0:T(8,128)} %get-tuple-element.274.sin_ref, ...), custom_call_target="tpu_custom_call" | custom-call | flops 8053063680 | bytes 8053063 | tf_op jit(solution)/shard_map/self_backward/pallas_call | solution.py:260
  1172.5 18.2 %collective-permute-done.72.refs_3_ = bf16[4,176,768]{2,1,0:T(8,128)(2,1)S(1)} collective-permute-done((bf16[4,176,768]{2,1,0:T(8,128)(2,1)}, bf16[4,176,768]{2,1,0:T(8,128)(2,1)S(1)}, u32[]{:S(2)}, u32[]{:S(2)}) %collective-permute-start.72) | collective-permute-done | bytes 1081376 | tf_op jit(solution)/shard_map/ppermute | solution.py:817
  1214.5 62.0 %all-to-all-done.3 = bf16[4,2,256,1152]{3,2,1,0:T(8,128)(2,1)} async-done(((bf16[4,2,256,1152]{3,2,1,0:T(8,128)(2,1)}), bf16[4,2,256,1152]{3,2,1,0:T(8,128)(2,1)}, u32[]{:S(2)}, u32[]{:S(2)}) %all-to-all-start.3) | async-done | bytes 4718624 | tf_op jit(solution)/shard_map/all_to_all | solution.py:982
  1294.6 29.3 %collective-permute-start.67 = (bf16[4,256,768]{2,1,0:T(8,128)(2,1)S(1)}, bf16[4,256,768]{2,1,0:T(8,128)(2,1)S(1)}, u32[]{:S(2)}, u32[]{:S(2)}) collective-permute-start(bf16[4,256,768]{2,1,0:T(8,128)(2,1)S(1)} %sum_rows.39), channel_id=1, source_target_pairs={{0,8},{4,12},{8,0},{12,4},{16,24},{20,28},{24,16},{28,20},{1,9},{5... | collective-permute-start | bytes 4718600 | tf_op jit(solution)/shard_map/ppermute | solution.py:817
  1323.9 34.6 %collective-permute-done.67.refs_2_ = bf16[4,256,768]{2,1,0:T(8,128)(2,1)S(1)} collective-permute-done((bf16[4,256,768]{2,1,0:T(8,128)(2,1)S(1)}, bf16[4,256,768]{2,1,0:T(8,128)(2,1)S(1)}, u32[]{:S(2)}, u32[]{:S(2)}) %collective-permute-start.67) | collective-permute-done | bytes 1572896 | tf_op jit(solution)/shard_map/ppermute | solution.py:817
  1390.6 20.7 %collective-permute-done.66.refs_3_ = bf16[4,176,1152]{2,1,0:T(8,128)(2,1)} collective-permute-done((bf16[4,176,1152]{2,1,0:T(8,128)(2,1)}, bf16[4,176,1152]{2,1,0:T(8,128)(2,1)}, u32[]{:S(2)}, u32[]{:S(2)}) %collective-permute-start.66) | collective-permute-done | bytes 1622048 | tf_op jit(solution)/shard_map/ppermute | solution.py:817
  1433.0 15.0 collective-permute-done.70.refs_3_
  1459.4 20.5 %to_features.10 = (bf16[2,512,704]{2,1,0:T(8,128)(2,1)}, f32[2,2,704]{2,1,0:T(2,128)}, f32[2,1,704]{2,1,0:T(1,128)}, f32[2,1,704]{2,1,0:T(1,128)}) custom-call(bf16[4,512,1152]{2,1,0:T(8,128)(2,1)} %bitcast.57.refs_0_.refs_1_, bf16[4,704,640]{2,1,0:T(8,128)(2,1)} %join_rows.11.refs_0_.refs_1_, bf16[4,704,640]{2,1,0:T(8,128)(2,1)} %collective-permute-done.22.refs_1_.refs_2_, ...), custom_call_target="tpu_custom_call" | custom-call | flops 6643777536 | bytes 6643777 | tf_op jit(solution)/shard_map/to_features/pallas_call | solution.py:401
  1500.0 57.3 %collective-permute-done.63.refs_2_ = bf16[4,352,1152]{2,1,0:T(8,128)(2,1)S(1)} collective-permute-done((bf16[4,352,1152]{2,1,0:T(8,128)(2,1)}, bf16[4,352,1152]{2,1,0:T(8,128)(2,1)S(1)}, u32[]{:S(2)}, u32[]{:S(2)}) %collective-permute-start.63) | collective-permute-done | bytes 3244064 | tf_op jit(solution)/shard_map/ppermute | solution.py:817
  1583.5 19.5 %collective-permute-done.64.refs_3_ = bf16[4,176,1152]{2,1,0:T(8,128)(2,1)} collective-permute-done((bf16[4,176,1152]{2,1,0:T(8,128)(2,1)}, bf16[4,176,1152]{2,1,0:T(8,128)(2,1)}, u32[]{:S(2)}, u32[]{:S(2)}) %collective-permute-start.64) | collective-permute-done | bytes 1622048 | tf_op jit(solution)/shard_map/ppermute | solution.py:817
  1612.3 33.0 %collective-permute-done.59 = f32[4,2,176]{2,1,0:T(2,128)S(1)} collective-permute-done((f32[4,2,176]{2,1,0:T(2,128)S(1)}, f32[4,2,176]{2,1,0:T(2,128)S(1)}, u32[]{:S(2)}, u32[]{:S(2)}) %collective-permute-start.59) | collective-permute-done | bytes 5664 | tf_op jit(solution)/shard_map/ppermute | solution.py:817
  1666.3 22.3 %collective-permute-done.77 = f32[5808]{0:T(1024)S(1)} collective-permute-done((f32[5808]{0:T(1024)S(1)}, f32[5808]{0:T(1024)S(1)}, u32[]{:S(2)}, u32[]{:S(2)}) %collective-permute-start.77) | collective-permute-done | bytes 23264 | tf_op jit(solution)/shard_map/ppermute | solution.py:817
  (690 shorter events, 703.9 us)
Async XLA Ops:
  9.1 78.8 %all-gather.17.cloned.1.call-start = ((), (), s32[]{:S(2)}) async-start(), calls=%async_computation.19 | async-start | bytes 2027520 | tf_op jit(solution)/shard_map/all_gather | solution.py:968
  41.4 195.0 %all-gather.19.cloned.1.call-start = ((), (), s32[]{:S(2)}) async-start(), calls=%async_computation.20 | async-start | bytes 2703360 | tf_op jit(solution)/shard_map/all_gather | solution.py:968
  236.4 144.8 %all-to-all-start = ((bf16[4,2,256,1152]{3,2,1,0:T(8,128)(2,1)}), bf16[4,2,256,1152]{3,2,1,0:T(8,128)(2,1)}, u32[]{:S(2)}, u32[]{:S(2)}) async-start(bf16[4,2,256,1152]{3,2,1,0:T(8,128)(2,1)} %bitcast.198), calls=%async_computation | async-start | bytes 9437184 | tf_op jit(solution)/shard_map/all_to_all | solution.py:982
  241.7 82.4 %all-gather.21.cloned.1.call-start = ((), (), s32[]{:S(2)}) async-start(), calls=%async_computation.21 | async-start | bytes 2703360 | tf_op jit(solution)/shard_map/all_gather | solution.py:968
  242.3 258.5 %all-gather.23.cloned.1.call-start = ((), (), s32[]{:S(2)}) async-start(), calls=%async_computation.22 | async-start | bytes 2027520 | tf_op jit(solution)/shard_map/all_gather | solution.py:968
  242.4 83.2 %collective-permute-start.24 = (bf16[4,176,1536]{2,1,0:T(8,128)(2,1)}, bf16[4,176,1536]{2,1,0:T(8,128)(2,1)}, u32[]{:S(2)}, u32[]{:S(2)}) collective-permute-start(bf16[4,176,1536]{2,1,0:T(8,128)(2,1)} %bitcast.182), channel_id=1, source_target_pairs={{0,8},{4,12},{8,0},{12,4},{16,24},{20,28},{24,16},{28,20},{1,9},{5... | collective-permute-start | bytes 6488072 | tf_op jit(solution)/shard_map/ppermute | solution.py:817
  382.7 93.2 %collective-permute-start.27 = (bf16[4,176,1536]{2,1,0:T(8,128)(2,1)}, bf16[4,176,1536]{2,1,0:T(8,128)(2,1)}, u32[]{:S(2)}, u32[]{:S(2)}) collective-permute-start(bf16[4,176,1536]{2,1,0:T(8,128)(2,1)} %collective-permute-done.24.refs_1_), channel_id=1, source_target_pairs={{0,16},{4,20},{8,24},{12,28},{16,0},{20,4},{24,8},{28,12},{1,17},{... | collective-permute-start | bytes 6488072 | tf_op jit(solution)/shard_map/ppermute | solution.py:817
  383.2 92.7 %collective-permute-start.28 = (bf16[4,176,1536]{2,1,0:T(8,128)(2,1)}, bf16[4,176,1536]{2,1,0:T(8,128)(2,1)}, u32[]{:S(2)}, u32[]{:S(2)}) collective-permute-start(bf16[4,176,1536]{2,1,0:T(8,128)(2,1)} %bitcast.186), channel_id=1, source_target_pairs={{0,8},{4,12},{8,0},{12,4},{16,24},{20,28},{24,16},{28,20},{1,9},{5... | collective-permute-start | bytes 6488072 | tf_op jit(solution)/shard_map/ppermute | solution.py:817
  384.7 92.7 %collective-permute-start.29 = (bf16[4,176,1536]{2,1,0:T(8,128)(2,1)}, bf16[4,176,1536]{2,1,0:T(8,128)(2,1)}, u32[]{:S(2)}, u32[]{:S(2)}) collective-permute-start(bf16[4,176,1536]{2,1,0:T(8,128)(2,1)} %collective-permute-done.25.refs_2_), channel_id=1, source_target_pairs={{0,8},{4,12},{8,0},{12,4},{16,24},{20,28},{24,16},{28,20},{1,9},{5... | collective-permute-start | bytes 6488072 | tf_op jit(solution)/shard_map/ppermute | solution.py:817
  387.3 170.3 %all-gather.25.cloned.1.call-start = ((), (), s32[]{:S(2)}) async-start(), calls=%async_computation.23 | async-start | bytes 1351680 | tf_op jit(solution)/shard_map/all_gather | solution.py:968
  488.9 282.1 %collective-permute-start.42 = (bf16[4,704,1536]{2,1,0:T(8,128)(2,1)}, bf16[4,704,1536]{2,1,0:T(8,128)(2,1)}, u32[]{:S(2)}, u32[]{:S(2)}) collective-permute-start(bf16[4,704,1536]{2,1,0:T(8,128)(2,1)} %join_rows.16.n1_ref), channel_id=1, source_target_pairs={{0,4},{4,0},{8,12},{12,8},{16,20},{20,16},{24,28},{28,24},{1,5},{5... | collective-permute-start | bytes 25952264 | tf_op jit(solution)/shard_map/ppermute | solution.py:817
  500.3 270.7 %collective-permute-start.43 = (bf16[4,704,1536]{2,1,0:T(8,128)(2,1)}, bf16[4,704,1536]{2,1,0:T(8,128)(2,1)}, u32[]{:S(2)}, u32[]{:S(2)}) collective-permute-start(bf16[4,704,1536]{2,1,0:T(8,128)(2,1)} %join_rows.17.n2_ref), channel_id=1, source_target_pairs={{0,4},{4,0},{8,12},{12,8},{16,20},{20,16},{24,28},{28,24},{1,5},{5... | collective-permute-start | bytes 25952264 | tf_op jit(solution)/shard_map/ppermute | solution.py:817
  609.8 114.5 %collective-permute-start.33 = (bf16[4,704,768]{2,1,0:T(8,128)(2,1)}, bf16[4,704,768]{2,1,0:T(8,128)(2,1)}, u32[]{:S(2)}, u32[]{:S(2)}) collective-permute-start(bf16[4,704,768]{2,1,0:T(8,128)(2,1)} %join_rows.13.refs_1_.refs_0_), channel_id=1, source_target_pairs={{0,4},{4,0},{8,12},{12,8},{16,20},{20,16},{24,28},{28,24},{1,5},{5... | collective-permute-start | bytes 12976136 | tf_op jit(solution)/shard_map/ppermute | solution.py:817
  633.2 81.5 %collective-permute-start.37 = (bf16[4,512,768]{2,1,0:T(8,128)(2,1)}, bf16[4,512,768]{2,1,0:T(8,128)(2,1)}, u32[]{:S(2)}, u32[]{:S(2)}) collective-permute-start(bf16[4,512,768]{2,1,0:T(8,128)(2,1)} %join_rows.14.refs_0_.refs_1_), channel_id=1, source_target_pairs={{0,4},{4,0},{8,12},{12,8},{16,20},{20,16},{24,28},{28,24},{1,5},{5... | collective-permute-start | bytes 9437192 | tf_op jit(solution)/shard_map/ppermute | solution.py:817
  640.2 84.1 %all-to-all-start.1 = ((bf16[4,2,256,384]{3,2,1,0:T(8,128)(2,1)}), bf16[4,2,256,384]{3,2,1,0:T(8,128)(2,1)}, u32[]{:S(2)}, u32[]{:S(2)}) async-start(bf16[4,2,256,384]{3,2,1,0:T(8,128)(2,1)} %get-tuple-element.165), calls=%async_computation.1 | async-start | bytes 3145728 | tf_op jit(solution)/shard_map/all_to_all | solution.py:982
  677.3 83.2 %collective-permute-start.41 = (bf16[4,704,384]{2,1,0:T(8,128)(2,1)}, bf16[4,704,384]{2,1,0:T(8,128)(2,1)}, u32[]{:S(2)}, u32[]{:S(2)}) collective-permute-start(bf16[4,704,384]{2,1,0:T(8,128)(2,1)} %join_rows.15.refs_1_.refs_0_), channel_id=1, source_target_pairs={{0,4},{4,0},{8,12},{12,8},{16,20},{20,16},{24,28},{28,24},{1,5},{5... | collective-permute-start | bytes 6488072 | tf_op jit(solution)/shard_map/ppermute | solution.py:817
  859.0 137.8 %collective-permute-start.48 = (bf16[4,704,768]{2,1,0:T(8,128)(2,1)}, bf16[4,704,768]{2,1,0:T(8,128)(2,1)S(1)}, u32[]{:S(2)}, u32[]{:S(2)}) collective-permute-start(bf16[4,704,768]{2,1,0:T(8,128)(2,1)} %get-tuple-element.206), channel_id=1, source_target_pairs={{0,4},{4,0},{8,12},{12,8},{16,20},{20,16},{24,28},{28,24},{1,5},{5... | collective-permute-start | bytes 12976136 | tf_op jit(solution)/shard_map/ppermute | solution.py:817
  908.4 88.5 %collective-permute-start.49 = (bf16[4,704,768]{2,1,0:T(8,128)(2,1)}, bf16[4,704,768]{2,1,0:T(8,128)(2,1)}, u32[]{:S(2)}, u32[]{:S(2)}) collective-permute-start(bf16[4,704,768]{2,1,0:T(8,128)(2,1)} %get-tuple-element.207), channel_id=1, source_target_pairs={{0,4},{4,0},{8,12},{12,8},{16,20},{20,16},{24,28},{28,24},{1,5},{5... | collective-permute-start | bytes 12976136 | tf_op jit(solution)/shard_map/ppermute | solution.py:817
  1055.6 85.8 %collective-permute-start.52 = (bf16[4,352,768]{2,1,0:T(8,128)(2,1)}, bf16[4,352,768]{2,1,0:T(8,128)(2,1)}, u32[]{:S(2)}, u32[]{:S(2)}) collective-permute-start(bf16[4,352,768]{2,1,0:T(8,128)(2,1)} %copy-done.39), channel_id=1, source_target_pairs={{0,16},{4,20},{8,24},{12,28},{16,0},{20,4},{24,8},{28,12},{1,17},{... | collective-permute-start | bytes 6488072 | tf_op jit(solution)/shard_map/ppermute | solution.py:817
  1057.1 84.3 %collective-permute-start.53 = (bf16[4,352,768]{2,1,0:T(8,128)(2,1)}, bf16[4,352,768]{2,1,0:T(8,128)(2,1)}, u32[]{:S(2)}, u32[]{:S(2)}) collective-permute-start(bf16[4,352,768]{2,1,0:T(8,128)(2,1)} %copy-done.38), channel_id=1, source_target_pairs={{0,8},{4,12},{8,0},{12,4},{16,24},{20,28},{24,16},{28,20},{1,9},{5... | collective-permute-start | bytes 6488072 | tf_op jit(solution)/shard_map/ppermute | solution.py:817
  1141.4 135.0 %all-to-all-start.3 = ((bf16[4,2,256,1152]{3,2,1,0:T(8,128)(2,1)}), bf16[4,2,256,1152]{3,2,1,0:T(8,128)(2,1)}, u32[]{:S(2)}, u32[]{:S(2)}) async-start(bf16[4,2,256,1152]{3,2,1,0:T(8,128)(2,1)} %get-tuple-element.223), calls=%async_computation.3 | async-start | bytes 9437184 | tf_op jit(solution)/shard_map/all_to_all | solution.py:982
  1146.4 423.7 %reduce-scatter.8.cloned.1.call-start = ((), (), s32[]{:S(2)}) async-start(), calls=%async_computation.11 | async-start | bytes 1966080 | tf_op jit(solution)/shard_map/reduce_scatter | solution.py:1121
  1155.8 494.3 %reduce-scatter.20.cloned.1.call-start = ((), (), s32[]{:S(2)}) async-start(), calls=%async_computation.17 | async-start | bytes 2703360 | tf_op jit(solution)/shard_map/reduce_scatter | solution.py:1121
  1203.3 449.0 %reduce-scatter.16.cloned.1.call-start = ((), (), s32[]{:S(2)}) async-start(), calls=%async_computation.15 | async-start | bytes 983040 | tf_op jit(solution)/shard_map/reduce_scatter | solution.py:1121
  1213.0 156.8 %collective-permute-start.65 = (bf16[4,352,1152]{2,1,0:T(8,128)(2,1)}, bf16[4,352,1152]{2,1,0:T(8,128)(2,1)}, u32[]{:S(2)}, u32[]{:S(2)}) collective-permute-start(bf16[4,352,1152]{2,1,0:T(8,128)(2,1)} %sum_rows.36), channel_id=1, source_target_pairs={{0,16},{4,20},{8,24},{12,28},{16,0},{20,4},{24,8},{28,12},{1,17},{... | collective-permute-start | bytes 9732104 | tf_op jit(solution)/shard_map/ppermute | solution.py:817
  1289.4 190.6 %collective-permute-start.54 = (bf16[4,704,1152]{2,1,0:T(8,128)(2,1)}, bf16[4,704,1152]{2,1,0:T(8,128)(2,1)}, u32[]{:S(2)}, u32[]{:S(2)}) collective-permute-start(bf16[4,704,1152]{2,1,0:T(8,128)(2,1)} %get-tuple-element.227), channel_id=1, source_target_pairs={{0,4},{4,0},{8,12},{12,8},{16,20},{20,16},{24,28},{28,24},{1,5},{5... | collective-permute-start | bytes 19464200 | tf_op jit(solution)/shard_map/ppermute | solution.py:817
  1390.5 299.3 %reduce-scatter.14.cloned.1.call-start = ((), (), s32[]{:S(2)}) async-start(), calls=%async_computation.14 | async-start | bytes 2027520 | tf_op jit(solution)/shard_map/reduce_scatter | solution.py:1121
  1418.7 298.7 %reduce-scatter.18.cloned.1.call-start = ((), (), s32[]{:S(2)}) async-start(), calls=%async_computation.16 | async-start | bytes 2703360 | tf_op jit(solution)/shard_map/reduce_scatter | solution.py:1121
  1495.2 79.2 %collective-permute-start.55 = (bf16[4,704,768]{2,1,0:T(8,128)(2,1)}, bf16[4,704,768]{2,1,0:T(8,128)(2,1)}, u32[]{:S(2)}, u32[]{:S(2)}) collective-permute-start(bf16[4,704,768]{2,1,0:T(8,128)(2,1)} %get-tuple-element.233), channel_id=1, source_target_pairs={{0,4},{4,0},{8,12},{12,8},{16,20},{20,16},{24,28},{28,24},{1,5},{5... | collective-permute-start | bytes 12976136 | tf_op jit(solution)/shard_map/ppermute | solution.py:817
  1496.9 222.6 %reduce-scatter.12.cloned.1.call-start = ((), (), s32[]{:S(2)}) async-start(), calls=%async_computation.13 | async-start | bytes 2027520 | tf_op jit(solution)/shard_map/reduce_scatter | solution.py:1121
  1582.4 74.9 %collective-permute-start.56 = (bf16[4,352,768]{2,1,0:T(8,128)(2,1)}, bf16[4,352,768]{2,1,0:T(8,128)(2,1)}, u32[]{:S(2)}, u32[]{:S(2)}) collective-permute-start(bf16[4,352,768]{2,1,0:T(8,128)(2,1)} %sum_rows.31), channel_id=1, source_target_pairs={{0,8},{4,12},{8,0},{12,4},{16,24},{20,28},{24,16},{28,20},{1,9},{5... | collective-permute-start | bytes 6488072 | tf_op jit(solution)/shard_map/ppermute | solution.py:817
  1610.0 113.8 %reduce-scatter.10.cloned.1.call-start = ((), (), s32[]{:S(2)}) async-start(), calls=%async_computation.12 | async-start | bytes 1351680 | tf_op jit(solution)/shard_map/reduce_scatter | solution.py:1121
  (196 other events, 5320.3 us)
Sparse Core Ops, SparseCore 0:
  10.2 31.1 all-gather.14
  43.5 38.0 all-gather.16
  190.5 45.8 all-gather.18
  243.8 80.2 all-gather.20
  387.4 65.0 all-gather.22
  501.8 55.7 all-gather.24
  657.1 55.8 all-gather.26
  1155.9 100.9 reduce-scatter.7
  1259.2 58.3 reduce-scatter.19
  1390.7 21.7 reduce-scatter.15
  1418.8 33.5 reduce-scatter.13
  1497.0 42.2 reduce-scatter.17
  1610.2 33.5 reduce-scatter.11
  1697.4 26.3 reduce-scatter.9

commit v5 on v4

--- a/solution.py
+++ b/solution.py
@@ -292,7 +292,7 @@
 
 
 def cost(flops):
-    return pl.CostEstimate(flops=flops, bytes_accessed=flops // 1000, transcendentals=0)
+    return pl.CostEstimate(flops=flops // 16, bytes_accessed=flops // 16000, transcendentals=0)
 
 
 def full(shape):
@@ -483,17 +483,14 @@
 
     def kernel(*refs):
         for index in range(count):
-
-            @pl.when(pl.program_id(1) == index)
-            def _():
-                refs[-1][...] = refs[index][...]
+            refs[-1][0, index * rows : (index + 1) * rows] = refs[index][0]
 
     return pl.pallas_call(
         kernel,
         name=name,
-        grid=(parts, count),
-        in_specs=[pl.BlockSpec((1, rows, lanes), lambda p, i: (p, 0, 0))] * count,
-        out_specs=pl.BlockSpec((1, rows, lanes), lambda p, i: (p, i, 0)),
+        grid=(parts,),
+        in_specs=[pl.BlockSpec((1, rows, lanes), lambda p: (p, 0, 0))] * count,
+        out_specs=pl.BlockSpec((1, count * rows, lanes), lambda p: (p, 0, 0)),
         out_shape=jax.ShapeDtypeStruct((parts, count * rows, lanes), BF),
         compiler_params=params(24),
         cost_estimate=cost(parts * count * rows * lanes),
@@ -510,22 +507,25 @@
         return value.astype(BF).reshape(parts, count * rows, lanes)
 
     def kernel(*refs):
-        value = refs[0][...].astype(F32)
-        for ref in refs[1:-1]:
-            value = value + ref[...].astype(F32)
-        refs[-1][...] = value.astype(BF)
-
-    def spec(first, step):
-        return pl.BlockSpec((1, rows, lanes), lambda p, i: (p, first + step * i, 0))
+        for index in range(count):
+            value = None
+            for (array, first, step), ref in zip(terms, refs):
+                start = 0 if array.shape[1] == rows else (first + step * index) % (array.shape[1] // rows)
+                term = ref[0, start * rows : (start + 1) * rows].astype(F32)
+                value = term if value is None else value + term
+            refs[-1][0, index * rows : (index + 1) * rows] = value.astype(BF)
+
+    def spec(size):
+        return pl.BlockSpec((1, size, lanes), lambda p: (p, 0, 0))
 
     return pl.pallas_call(
         kernel,
         name=name,
-        grid=(parts, count),
-        in_specs=[spec(first, step) for _, first, step in terms],
-        out_specs=spec(0, 1),
+        grid=(parts,),
+        in_specs=[spec(term[0].shape[1]) for term in terms],
+        out_specs=spec(count * rows),
         out_shape=jax.ShapeDtypeStruct((parts, count * rows, lanes), BF),
-        compiler_params=params(24),
+        compiler_params=params(32),
         cost_estimate=cost(parts * count * rows * lanes),
     )(*[term[0] for term in terms])
 
@@ -907,6 +907,13 @@
         return self.total([0])
 
 
+def pin(value, *others):
+    flat = []
+    for other in others:
+        flat += other.pieces if hasattr(other, "pieces") else [other]
+    return tie(value, *flat)[0]
+
+
 def bind(value, *movers):
     flat = [piece for mover in movers for piece in mover.pieces]
     held = tie(value, *flat)
@@ -916,6 +923,11 @@
         mover.pieces = list(held[spot : spot + count])
         spot += count
     return held[0]
+
+
+def hold(movers, *others):
+    for mover in movers:
+        mover.pieces = [pin(piece, *others) for piece in mover.pieces]
 
 
 def on_device(
@@ -982,17 +994,18 @@
         return lax.all_to_all(value, "sp", split_axis=0, concat_axis=0, tiled=True)
 
     skip_z = spread(jnp.pad(w_skip.T, ((0, 0), (0, skip_lanes - kept))))
+    qkv_z = spread(pad_heads(w_qkv.reshape(strip, -1), local), skip_z)
+    fc1_z = spread(w_fc1, qkv_z)
+    fc2_z = spread(w_fc2.T, fc1_z)
     skip_m = fetch(skip_z, skip_cut)
-    qkv_z = spread(pad_heads(w_qkv.reshape(strip, -1), local), skip_z)
     while skip_m[0].todo:
         advance(skip_m)
-    qkv_z = bind(qkv_z, *skip_m)
-    fc1_z = spread(w_fc1, qkv_z)
-    fc2_z = spread(w_fc2.T, fc1_z)
+    qkv_m = fetch(qkv_z, qkv_cut)
+    hold(qkv_m, *skip_m)
+    advance(qkv_m)
+    hold(skip_m, qkv_z)
     join(skip_m)
     skip_w = [mover.weight() for mover in skip_m]
-    qkv_m = fetch(qkv_z, qkv_cut)
-    advance(qkv_m)
 
     def shuffle(count):
         block = count // ranks
@@ -1064,15 +1077,17 @@
     )
     while qkv_m[0].todo:
         advance(qkv_m)
-    pre_attn = bind(pre_attn, *qkv_m)
+    after_qkv = [mover.pieces[-1] for mover in qkv_m]
+    hold(qkv_m, pre_attn)
     join(qkv_m)
+    pre_attn, fc1_z = tie(pre_attn, fc1_z)
     qkv_w = [mover.weight() for mover in qkv_m]
+    projected = to_lanes(pre_attn, qkv_w)
+    projected, fc2_z = tie(projected, fc2_z)
     fc_m = [Gather(cube, fc1_z, 0), Gather(cube, fc2_z, 1)]
-    projected = to_lanes(pre_attn, qkv_w)
-    projected = bind(projected, fc_m[0])
+    hold(fc_m, *after_qkv)
     advance(fc_m)
     raw = exchange(projected.reshape(parts, micros, slots, 3 * lanes))
-    raw = bind(raw, *fc_m)
     cross_z = jnp.concatenate([pad_heads(side, local) for side in (w_out1.T, w_query2, w_out2.T)], 1)
     cross_z = spread(cross_z, raw)
     text_z = jnp.pad(pad_heads(w_text_kv.reshape(text_rows, -1), local), ((0, max(0, strip - text_rows)), (0, 0)))
@@ -1083,13 +1098,16 @@
     ).reshape(micros * text_strip, features)
     text_all = spread(text_own, text_z).reshape(-1, features)
     text_all = jnp.stack([text_all[:, : features // 2], text_all[:, features // 2 :]])
+    raw = pin(raw, *fc_m)
     while fc_m[0].todo:
         advance(fc_m)
     attended, turned_q, turned_k, norms = self_forward(raw, counts, cosine, sine, gain_q, gain_k)
-    attended = bind(attended, *fc_m)
-    attended = exchange(attended).reshape(parts, rows, lanes)
     cross_m = fetch(cross_z, 2 * lanes)
     text_m = Gather(cube, text_z[:, :text_rows], 1)
+    hold(cross_m, attended)
+    advance(cross_m)
+    attended = exchange(attended).reshape(parts, rows, lanes)
+    hold(fc_m + cross_m + [text_m], attended)
     join(cross_m)
     first_w, out2_w = [mover.weight() for mover in cross_m]
     out1_w, query2_w = (Lanes(first_w.near, first_w.far, lanes, index) for index in range(2))
@@ -1121,7 +1139,6 @@
         return lax.psum_scatter(value, "sp", scatter_dimension=0, tiled=False)
 
     fc1_n0, fc1_f0, partial = mlp_backward(d_mlp, pre_mlp, hidden0, fc1_w, fc2_w, 0, None)
-    partial = bind(partial, *fc2_s)
     pack(fc2_s)
     partial = bind(partial, *fc2_s)
     advance(fc2_s)
@@ -1131,15 +1148,13 @@
     fc1_s = [Scatter(cube, fc1_n0, fc1_f0, 0), Scatter(cube, fc1_n1, fc1_f1, 1)]
     d_crossed = to_lanes(d_cross, [out2_w])
     d_crossed = bind(d_crossed, *fc2_s)
-    pack(fc2_s)
-    d_crossed = bind(d_crossed, *fc2_s)
-    advance(fc2_s)
     d_query2, d_text_kv = cross_backward(
         query2, text_kv, lengths, d_crossed.reshape(parts, micros, slots, lanes), text_slots
     )
-    d_query2 = bind(d_query2, *fc1_s)
+    pack(fc2_s)
     pack(fc1_s)
-    d_query2 = bind(d_query2, *fc1_s)
+    d_query2 = bind(d_query2, *fc2_s, *fc1_s)
+    advance(fc2_s)
     advance(fc1_s)
     d_query2 = d_query2.reshape(parts, rows, lanes)
     d_text_kv = d_text_kv.reshape(parts, -1, 2 * lanes)
@@ -1170,16 +1185,17 @@
     )
     total_fc2 = [mover.result() for mover in fc2_s]
     term_fc2 = settle(total_fc2)
-    d_heads = bind(d_heads, text_s, cross_s)
     d_raw, d_gain_q, d_gain_k = self_backward(
         raw, counts, cosine, sine, gain_q, gain_k, turned_q, turned_k, norms, d_heads
     )
-    d_raw = bind(d_raw, *fc1_s)
+    d_raw, term_fc2, d_words = tie(d_raw, term_fc2, d_words)
+    d_raw = bind(d_raw, *fc1_s, cross_s, text_s)
     d_projected = exchange(d_raw).reshape(parts, rows, 3 * lanes)
-    pack(fc1_s)
     advance(fc1_s)
     pack([cross_s, text_s])
+    hold([cross_s, text_s], d_raw)
     advance([cross_s, text_s])
+    d_projected = bind(d_projected, *fc1_s, cross_s, text_s)
     total_fc1 = [mover.result() for mover in fc1_s]
 
     def last_norms(sums, extra, out):
@@ -1196,8 +1212,11 @@
                 part = sums[side][micro * slots : (micro + 1) * slots]
                 d_shift_ref[side, micro : micro + 1] = jnp.sum(part, 0, keepdims=True)
 
-    qkv_t = [terms_of([(pre_attn, d_projected, 3 * lanes, 0)])]
-    qkv_s = [Scatter(cube, *qkv_t[0], 0)]
+    qkv_s = [
+        Scatter(cube, *terms_of([(pre_attn, d_projected, 2 * lanes, 0)]), 0),
+        Scatter(cube, *terms_of([(pre_attn, d_projected, lanes, 2)]), 1),
+    ]
+    term_fc1 = settle(total_fc1, qkv_s[0].near)
     shift_shape = jax.ShapeDtypeStruct((2, micros, middle), F32)
     d_base, d_shift, d_gain_attn, d_gain_skip = to_features(
         d_projected,
@@ -1206,16 +1225,18 @@
         [low_shape, shift_shape, gain_shape, gain_shape],
         last_norms,
     )
-    d_base = bind(d_base, *qkv_s)
     pack(qkv_s)
     d_base = bind(d_base, *qkv_s)
     advance(qkv_s)
-    skip_s = [Scatter(cube, *terms_of([(d_base, joined, skip_lanes, 0)]), 1)]
-    term_fc1 = settle(total_fc1, d_base)
+    skip_s = [
+        Scatter(cube, *terms_of([(d_base, joined, skip_cut, flip)]), flip) for flip in range(2)
+    ]
+    total_cross, total_text = cross_s.result(), text_s.result()
     pack(skip_s)
+    hold(skip_s, total_cross, total_text, *qkv_s)
     advance(skip_s)
-    term_cross = settle([cross_s.result()])
-    term_text = settle([text_s.result()])
+    term_cross = settle([total_cross])
+    term_text = settle([total_text])
     term_qkv = settle([mover.result() for mover in qkv_s])
     term_skip = settle([mover.result() for mover in skip_s])
     d_joined = to_inputs(d_base, skip_w, kept)

time: 1740 us -> 1560 us (0.90)
  waiting for transfers between devices: 814 us -> 668 us
  starting transfers between devices: 152 us -> 113 us
    all_gather x7, waiting for transfers between devices: 217 us -> 82 us  [spread(): return lax.all_gather(shard, 'sp', axis=0, tiled=False)]
    ppermute x78 -> x84, waiting for transfers between devices: 491 us -> 432 us  [swap(): return lax.ppermute(value, axis, pairs)]
    all_to_all x4, waiting for transfers between devices: 105 us -> 148 us  [exchange(): return lax.all_to_all(value, 'sp', split_axis=0, concat_axis=0, tiled=True)]
    ppermute x78 -> x84, starting transfers between devices: 122 us -> 93.1 us  [swap(): return lax.ppermute(value, axis, pairs)]
    pallas_call x33 -> x39, Pallas kernels: 166 us -> 147 us  [the longest x30 109 us: sum_rows(): pl.pallas_call(kernel, name=name, grid=(parts,), in_specs=[spec(term[0].s...]
    pallas_call x4 -> x6, Pallas kernels: 40.3 us -> 49.8 us  [terms_of(): pl.pallas_call(kernel, name=name, grid=(parts,), in_specs=[full(pair[0].s...]
    unnamed x278 -> x284, local copies, waits for them, and re-layouts: 84.6 us -> 79.1 us
  transfers between devices with their start and end apart: 96 -> 102, of which waited for: 45 -> 42; matrix products, arithmetic and copies ran while one was open for 6% -> 6% of each run, Pallas kernels for 28% -> 32%
where the time goes in v5:
time: 1560 us; the launch traced here: 1540 us
  waiting for transfers between devices  668 us (43%)
  Pallas kernels  565 us (36%)
  local copies, waits for them, and re-layouts  122 us (8%)
  starting transfers between devices  113 us (7%)
  other arithmetic  47.3 us (3%)
  between operations  16.2 us (1%)
    ppermute x84, waiting for transfers between devices, swap(): return lax.ppermute(value, axis, pairs)  432 us
    all_to_all x4, waiting for transfers between devices, exchange(): return lax.all_to_all(value, 'sp', split_axis=0, concat_axis=0, tiled=True)  148 us
    pallas_call x30, Pallas kernels, sum_rows(): pl.pallas_call(kernel, name=name, grid=(parts,), in_specs=[spec(term[0].s...  109 us
    ppermute x84, starting transfers between devices, swap(): return lax.ppermute(value, axis, pairs)  93.1 us
    all_gather x7, waiting for transfers between devices, spread(): return lax.all_gather(shard, 'sp', axis=0, tiled=False)  82 us
    unnamed x284, local copies, waits for them, and re-layouts  79.1 us
    pallas_call x6, Pallas kernels, to_features(): pl.pallas_call(kernel, name=name, grid=(parts,), in_specs=[pl.BlockSpec((...  78.2 us
    pallas_call x2, Pallas kernels, mlp_backward(): pl.pallas_call(kernel, name='mlp_backward', grid=(parts, steps), in_specs...  63.7 us
  transfers between devices with their start and end apart: 102, of which 42 were waited for; matrix products, arithmetic and copies ran while one was open for 6% of the time, Pallas kernels for 32%

profile of v5, /device:TPU:0, one launch (start us, length us, event | category | flops | bytes accessed | tf_op | source)
XLA Modules:
  0.0 1542.1 jit_solution(3858727056954838068)
XLA Ops:
  12.2 29.2 %all-gather.15.cloned.1.call-done = bf16[704,768]{1,0:T(8,128)(2,1)} async-done(((bf16[176,768]{1,0:T(8,128)(2,1)}), bf16[704,768]{1,0:T(8,128)(2,1)}) %all-gather.15.cloned.1.call-update) | async-done | bytes 1081360 | tf_op jit(solution)/shard_map/all_gather | solution.py:980
  57.3 22.9 %all-gather.17.cloned.1.call-done = bf16[704,1152]{1,0:T(8,128)(2,1)} async-done(((bf16[176,1152]{1,0:T(8,128)(2,1)}), bf16[704,1152]{1,0:T(8,128)(2,1)}) %all-gather.17.cloned.1.call-update) | async-done | bytes 1622032 | tf_op jit(solution)/shard_map/all_gather | solution.py:980
  125.8 14.0 collective-permute-done.16.refs_1_
  142.3 19.8 %collective-permute-done.21.refs_2_ = bf16[4,176,512]{2,1,0:T(8,128)(2,1)} collective-permute-done((bf16[4,176,512]{2,1,0:T(8,128)(2,1)S(1)}, bf16[4,176,512]{2,1,0:T(8,128)(2,1)}, u32[]{:S(2)}, u32[]{:S(2)}) %collective-permute-start.21) | collective-permute-done | bytes 720928 | tf_op jit(solution)/shard_map/ppermute | solution.py:817
  164.2 14.7 to_features.6
  213.8 16.3 %all-gather.21.cloned.1.call-done = bf16[704,1536]{1,0:T(8,128)(2,1)} async-done(((bf16[176,1536]{1,0:T(8,128)(2,1)}), bf16[704,1536]{1,0:T(8,128)(2,1)}) %all-gather.21.cloned.1.call-update) | async-done | bytes 2162704 | tf_op jit(solution)/shard_map/all_gather | solution.py:980
  240.1 13.9 negate_select_fusion
  254.0 30.6 %collective-permute-done.24.refs_1_ = bf16[4,176,1536]{2,1,0:T(8,128)(2,1)} collective-permute-done((bf16[4,176,1536]{2,1,0:T(8,128)(2,1)}, bf16[4,176,1536]{2,1,0:T(8,128)(2,1)}, u32[]{:S(2)}, u32[]{:S(2)}) %collective-permute-start.24) | collective-permute-done | bytes 2162720 | tf_op jit(solution)/shard_map/ppermute | solution.py:817
  285.8 54.4 %all-to-all-done.raw_ref = bf16[4,2,256,1152]{3,2,1,0:T(8,128)(2,1)} async-done(((bf16[4,2,256,1152]{3,2,1,0:T(8,128)(2,1)}), bf16[4,2,256,1152]{3,2,1,0:T(8,128)(2,1)}, u32[]{:S(2)}, u32[]{:S(2)}) %all-to-all-start) | async-done | bytes 4718624 | tf_op jit(solution)/shard_map/all_to_all | solution.py:994
  340.2 34.2 %self_forward.1 = (bf16[4,2,256,384]{3,2,1,0:T(8,128)(2,1)}, bf16[2,1024,384]{2,1,0:T(8,128)(2,1)S(1)}, bf16[2,1024,384]{2,1,0:T(8,128)(2,1)S(1)}, f32[2,4,1024]{2,1,0:T(4,128)S(1)}) custom-call(s32[2]{0:T(128)S(1)} %mul.78.count_ref, bf16[4,2,256,1152]{3,2,1,0:T(8,128)(2,1)} %all-to-all-done.raw_ref, f32[2,1024,384]{2,1,0:T(8,128)} %get-tuple-element.301.cos_ref, ...), custom_call_target="tpu_custom_call" | custom-call | flops 201326592 | bytes 201326 | tf_op jit(solution)/shard_map/self_forward/pallas_call | solution.py:150
  393.8 41.1 %all-to-all-done.1 = bf16[4,2,256,384]{3,2,1,0:T(8,128)(2,1)S(1)} async-done(((bf16[4,2,256,384]{3,2,1,0:T(8,128)(2,1)}), bf16[4,2,256,384]{3,2,1,0:T(8,128)(2,1)S(1)}, u32[]{:S(2)}, u32[]{:S(2)}) %all-to-all-start.1) | async-done | bytes 1572896 | tf_op jit(solution)/shard_map/all_to_all | solution.py:994
  434.9 43.2 %collective-permute-done.39.refs_3_ = bf16[4,176,1536]{2,1,0:T(8,128)(2,1)} collective-permute-done((bf16[4,176,1536]{2,1,0:T(8,128)(2,1)}, bf16[4,176,1536]{2,1,0:T(8,128)(2,1)}, u32[]{:S(2)}, u32[]{:S(2)}) %collective-permute-start.39) | collective-permute-done | bytes 2162720 | tf_op jit(solution)/shard_map/ppermute | solution.py:817
  499.3 24.5 %collective-permute-done.26.refs_1_ = bf16[4,176,768]{2,1,0:T(8,128)(2,1)} collective-permute-done((bf16[4,176,768]{2,1,0:T(8,128)(2,1)S(1)}, bf16[4,176,768]{2,1,0:T(8,128)(2,1)}, u32[]{:S(2)}, u32[]{:S(2)}) %collective-permute-start.26) | collective-permute-done | bytes 1081376 | tf_op jit(solution)/shard_map/ppermute | solution.py:817
  529.6 36.9 %collective-permute-done.31.refs_2_ = bf16[4,128,768]{2,1,0:T(8,128)(2,1)S(1)} collective-permute-done((bf16[4,128,768]{2,1,0:T(8,128)(2,1)S(1)}, bf16[4,128,768]{2,1,0:T(8,128)(2,1)S(1)}, u32[]{:S(2)}, u32[]{:S(2)}) %collective-permute-start.31) | collective-permute-done | bytes 786464 | tf_op jit(solution)/shard_map/ppermute | solution.py:817
  626.1 13.6 all-gather.27.cloned.1.call-done
  668.1 17.3 %cross_forward.1 = bf16[4,2,256,384]{3,2,1,0:T(8,128)(2,1)S(1)} custom-call(s32[2,2]{1,0:T(2,128)S(1)} %bitcast.199, bf16[4,2,256,384]{3,2,1,0:T(8,128)(2,1)S(1)} %bitcast.184, bf16[4,4,2,96,768]{4,3,2,1,0:T(8,128)(2,1)S(1)} %bitcast.164), custom_call_target="tpu_custom_call" | custom-call | flops 75497472 | bytes 75497 | tf_op jit(solution)/shard_map/cross_forward/pallas_call | solution.py:723
  698.5 27.9 %mlp_forward.2 = (f32[4,512,768]{2,1,0:T(8,128)}, bf16[4,512,768]{2,1,0:T(8,128)(2,1)}, f32[2,512,704]{2,1,0:T(8,128)}, bf16[4,704,768]{2,1,0:T(8,128)(2,1)}, bf16[4,704,768]{2,1,0:T(8,128)(2,1)}) custom-call(bf16[2,512,704]{2,1,0:T(8,128)(2,1)S(1)} %copy-done.15, bf16[2,512,704]{2,1,0:T(8,128)(2,1)S(1)} %fusion.66.g_ref, ...), custom_call_target="tpu_custom_call" | custom-call | flops 830472192 | bytes 830472 | tf_op jit(solution)/shard_map/mlp_forward/pallas_call | solution.py:594
  726.4 27.1 %mlp_forward.3 = (f32[4,512,768]{2,1,0:T(8,128)}, bf16[4,512,768]{2,1,0:T(8,128)(2,1)}, bf16[2,512,704]{2,1,0:T(8,128)(2,1)S(1)}, bf16[4,704,768]{2,1,0:T(8,128)(2,1)}, bf16[4,704,768]{2,1,0:T(8,128)(2,1)}) custom-call(bf16[2,512,704]{2,1,0:T(8,128)(2,1)S(1)} %copy-done.15, bf16[2,512,704]{2,1,0:T(8,128)(2,1)S(1)} %fusion.66.g_ref, ...), custom_call_target="tpu_custom_call" | custom-call | flops 830472192 | bytes 830472 | tf_op jit(solution)/shard_map/mlp_forward/pallas_call | solution.py:594
  755.9 29.1 %mlp_backward.2 = (bf16[4,704,768]{2,1,0:T(8,128)(2,1)}, bf16[4,704,768]{2,1,0:T(8,128)(2,1)}, f32[2,512,704]{2,1,0:T(8,128)}) custom-call(bf16[2,512,704]{2,1,0:T(8,128)(2,1)} %copy-done.5, bf16[2,512,704]{2,1,0:T(8,128)(2,1)} %get-tuple-element.191.x_ref, f32[4,512,768]{2,1,0:T(8,128)} %get-tuple-element.207.hid_ref, ...), custom_call_target="tpu_custom_call" | custom-call | flops 830472192 | bytes 830472 | tf_op jit(solution)/shard_map/mlp_backward/pallas_call | solution.py:666
  796.9 34.7 %mlp_backward.3 = (bf16[4,704,768]{2,1,0:T(8,128)(2,1)}, bf16[4,704,768]{2,1,0:T(8,128)(2,1)}, f32[2,512,704]{2,1,0:T(8,128)}, bf16[2,512,704]{2,1,0:T(8,128)(2,1)}, f32[2,1,704]{2,1,0:T(1,128)}) custom-call(bf16[2,512,704]{2,1,0:T(8,128)(2,1)} %copy-done.5, bf16[2,512,704]{2,1,0:T(8,128)(2,1)} %get-tuple-element.191.x_ref, ...), custom_call_target="tpu_custom_call" | custom-call | flops 830472192 | bytes 830472 | tf_op jit(solution)/shard_map/mlp_backward/pallas_call | solution.py:666
  841.7 39.5 %collective-permute-done.46.refs_2_ = bf16[4,352,768]{2,1,0:T(8,128)(2,1)S(1)} collective-permute-done((bf16[4,352,768]{2,1,0:T(8,128)(2,1)}, bf16[4,352,768]{2,1,0:T(8,128)(2,1)S(1)}, u32[]{:S(2)}, u32[]{:S(2)}) %collective-permute-start.46) | collective-permute-done | bytes 2162720 | tf_op jit(solution)/shard_map/ppermute | solution.py:817
  882.6 20.6 %cross_backward.1 = (bf16[4,2,256,384]{3,2,1,0:T(8,128)(2,1)S(1)}, bf16[4,4,2,96,768]{4,3,2,1,0:T(8,128)(2,1)S(1)}) custom-call(s32[2,2]{1,0:T(2,128)S(1)} %bitcast.200, bf16[4,2,256,384]{3,2,1,0:T(8,128)(2,1)S(1)} %bitcast.185, bf16[4,4,2,96,768]{4,3,2,1,0:T(8,128)(2,1)S(1)} %bitcast.165, bf16[4,2,256,384]{3,2,1,0:T(8,128)(2,1)S(1)} %bitcast.188), custom_call_target="tpu_custom_call" | custom-call | flops 188743680 | bytes 188743 | tf_op jit(solution)/shard_map/cross_backward/pallas_call | solution.py:772
  939.5 12.7 to_features.9
  955.0 13.7 terms_of.6
  971.0 24.0 %collective-permute-done.51.refs_3_ = bf16[4,176,768]{2,1,0:T(8,128)(2,1)S(1)} collective-permute-done((bf16[4,176,768]{2,1,0:T(8,128)(2,1)S(1)}, bf16[4,176,768]{2,1,0:T(8,128)(2,1)S(1)}, u32[]{:S(2)}, u32[]{:S(2)}) %collective-permute-start.51) | collective-permute-done | bytes 1081376 | tf_op jit(solution)/shard_map/ppermute | solution.py:817
  1026.8 52.3 %all-to-all-done.2.in_ref = bf16[4,2,256,384]{3,2,1,0:T(8,128)(2,1)} async-done(((bf16[4,2,256,384]{3,2,1,0:T(8,128)(2,1)}), bf16[4,2,256,384]{3,2,1,0:T(8,128)(2,1)}, u32[]{:S(2)}, u32[]{:S(2)}) %all-to-all-start.2) | async-done | bytes 1572896 | tf_op jit(solution)/shard_map/all_to_all | solution.py:994
  1081.9 50.6 %self_backward.1 = (bf16[4,2,256,1152]{3,2,1,0:T(8,128)(2,1)}, f32[2,1,384]{2,1,0:T(1,128)S(1)}, f32[2,1,384]{2,1,0:T(1,128)S(1)}) custom-call(s32[2]{0:T(128)S(1)} %mul.78.count_ref, bf16[4,2,256,1152]{3,2,1,0:T(8,128)(2,1)} %all-to-all-done.raw_ref, f32[2,1024,384]{2,1,0:T(8,128)} %get-tuple-element.301.cos_ref, ...), custom_call_target="tpu_custom_call" | custom-call | flops 503316480 | bytes 503316 | tf_op jit(solution)/shard_map/self_backward/pallas_call | solution.py:260
  1165.0 43.9 %collective-permute-done.56.refs_3_ = bf16[4,176,768]{2,1,0:T(8,128)(2,1)S(1)} collective-permute-done((bf16[4,176,768]{2,1,0:T(8,128)(2,1)S(1)}, bf16[4,176,768]{2,1,0:T(8,128)(2,1)S(1)}, u32[]{:S(2)}, u32[]{:S(2)}) %collective-permute-start.56) | collective-permute-done | bytes 1081376 | tf_op jit(solution)/shard_map/ppermute | solution.py:817
  1209.8 32.0 %collective-permute-done.57.refs_3_ = bf16[4,176,768]{2,1,0:T(8,128)(2,1)S(1)} collective-permute-done((bf16[4,176,768]{2,1,0:T(8,128)(2,1)S(1)}, bf16[4,176,768]{2,1,0:T(8,128)(2,1)S(1)}, u32[]{:S(2)}, u32[]{:S(2)}) %collective-permute-start.57) | collective-permute-done | bytes 1081376 | tf_op jit(solution)/shard_map/ppermute | solution.py:817
  1254.0 16.6 %collective-permute-done.64.refs_3_ = bf16[4,128,768]{2,1,0:T(8,128)(2,1)S(1)} collective-permute-done((bf16[4,128,768]{2,1,0:T(8,128)(2,1)S(1)}, bf16[4,128,768]{2,1,0:T(8,128)(2,1)S(1)}, u32[]{:S(2)}, u32[]{:S(2)}) %collective-permute-start.64) | collective-permute-done | bytes 786464 | tf_op jit(solution)/shard_map/ppermute | solution.py:817
  1316.7 20.5 %to_features.11 = (bf16[2,512,704]{2,1,0:T(8,128)(2,1)}, f32[2,2,704]{2,1,0:T(2,128)}, f32[2,1,704]{2,1,0:T(1,128)}, f32[2,1,704]{2,1,0:T(1,128)}) custom-call(bf16[4,512,1152]{2,1,0:T(8,128)(2,1)} %bitcast.59.refs_0_.refs_1_, bf16[4,704,640]{2,1,0:T(8,128)(2,1)} %join_rows.11.refs_0_.refs_1_, bf16[4,704,640]{2,1,0:T(8,128)(2,1)} %collective-permute-done.19.refs_1_.refs_2_, ...), custom_call_target="tpu_custom_call" | custom-call | flops 415236096 | bytes 415236 | tf_op jit(solution)/shard_map/to_features/pallas_call | solution.py:401
  1375.5 18.2 %collective-permute-done.66.refs_2_ = bf16[4,352,384]{2,1,0:T(8,128)(2,1)S(1)} collective-permute-done((bf16[4,352,384]{2,1,0:T(8,128)(2,1)}, bf16[4,352,384]{2,1,0:T(8,128)(2,1)S(1)}, u32[]{:S(2)}, u32[]{:S(2)}) %collective-permute-start.66) | collective-permute-done | bytes 1081376 | tf_op jit(solution)/shard_map/ppermute | solution.py:817
  (720 shorter events, 636.1 us)
Async XLA Ops:
  9.1 71.1 %all-gather.17.cloned.1.call-start = ((), (), s32[]{:S(2)}) async-start(), calls=%async_computation.19 | async-start | bytes 2027520 | tf_op jit(solution)/shard_map/all_gather | solution.py:980
  41.4 141.9 %all-gather.19.cloned.1.call-start = ((), (), s32[]{:S(2)}) async-start(), calls=%async_computation.20 | async-start | bytes 2703360 | tf_op jit(solution)/shard_map/all_gather | solution.py:980
  80.2 149.9 %all-gather.21.cloned.1.call-start = ((), (), s32[]{:S(2)}) async-start(), calls=%async_computation.21 | async-start | bytes 2703360 | tf_op jit(solution)/shard_map/all_gather | solution.py:980
  230.2 110.0 %all-to-all-start = ((bf16[4,2,256,1152]{3,2,1,0:T(8,128)(2,1)}), bf16[4,2,256,1152]{3,2,1,0:T(8,128)(2,1)}, u32[]{:S(2)}, u32[]{:S(2)}) async-start(bf16[4,2,256,1152]{3,2,1,0:T(8,128)(2,1)} %bitcast.201), calls=%async_computation | async-start | bytes 9437184 | tf_op jit(solution)/shard_map/all_to_all | solution.py:994
  380.4 114.5 %all-gather.23.cloned.1.call-start = ((), (), s32[]{:S(2)}) async-start(), calls=%async_computation.22 | async-start | bytes 2027520 | tf_op jit(solution)/shard_map/all_gather | solution.py:980
  385.5 92.5 %collective-permute-start.39 = (bf16[4,176,1536]{2,1,0:T(8,128)(2,1)}, bf16[4,176,1536]{2,1,0:T(8,128)(2,1)}, u32[]{:S(2)}, u32[]{:S(2)}) collective-permute-start(bf16[4,176,1536]{2,1,0:T(8,128)(2,1)} %collective-permute-done.24.refs_1_), channel_id=1, source_target_pairs={{0,16},{4,20},{8,24},{12,28},{16,0},{20,4},{24,8},{28,12},{1,17},{... | collective-permute-start | bytes 6488072 | tf_op jit(solution)/shard_map/ppermute | solution.py:817
  385.5 102.6 %collective-permute-start.41 = (bf16[4,176,1536]{2,1,0:T(8,128)(2,1)}, bf16[4,176,1536]{2,1,0:T(8,128)(2,1)}, u32[]{:S(2)}, u32[]{:S(2)}) collective-permute-start(bf16[4,176,1536]{2,1,0:T(8,128)(2,1)} %bitcast.194), channel_id=1, source_target_pairs={{0,8},{4,12},{8,0},{12,4},{16,24},{20,28},{24,16},{28,20},{1,9},{5... | collective-permute-start | bytes 6488072 | tf_op jit(solution)/shard_map/ppermute | solution.py:817
  387.5 100.6 %collective-permute-start.42 = (bf16[4,176,1536]{2,1,0:T(8,128)(2,1)}, bf16[4,176,1536]{2,1,0:T(8,128)(2,1)}, u32[]{:S(2)}, u32[]{:S(2)}) collective-permute-start(bf16[4,176,1536]{2,1,0:T(8,128)(2,1)} %collective-permute-done.25.refs_2_), channel_id=1, source_target_pairs={{0,8},{4,12},{8,0},{12,4},{16,24},{20,28},{24,16},{28,20},{1,9},{5... | collective-permute-start | bytes 6488072 | tf_op jit(solution)/shard_map/ppermute | solution.py:817
  393.7 131.8 %all-gather.25.cloned.1.call-start = ((), (), s32[]{:S(2)}) async-start(), calls=%async_computation.23 | async-start | bytes 1351680 | tf_op jit(solution)/shard_map/all_gather | solution.py:980
  486.3 210.8 %collective-permute-start.40 = (bf16[4,704,1536]{2,1,0:T(8,128)(2,1)}, bf16[4,704,1536]{2,1,0:T(8,128)(2,1)}, u32[]{:S(2)}, u32[]{:S(2)}) collective-permute-start(bf16[4,704,1536]{2,1,0:T(8,128)(2,1)} %join_rows.16.n1_ref), channel_id=1, source_target_pairs={{0,4},{4,0},{8,12},{12,8},{16,20},{20,16},{24,28},{28,24},{1,5},{5... | collective-permute-start | bytes 25952264 | tf_op jit(solution)/shard_map/ppermute | solution.py:817
  494.7 202.4 %collective-permute-start.43 = (bf16[4,704,1536]{2,1,0:T(8,128)(2,1)}, bf16[4,704,1536]{2,1,0:T(8,128)(2,1)}, u32[]{:S(2)}, u32[]{:S(2)}) collective-permute-start(bf16[4,704,1536]{2,1,0:T(8,128)(2,1)} %join_rows.17.n2_ref), channel_id=1, source_target_pairs={{0,4},{4,0},{8,12},{12,8},{16,20},{20,16},{24,28},{28,24},{1,5},{5... | collective-permute-start | bytes 25952264 | tf_op jit(solution)/shard_map/ppermute | solution.py:817
  495.8 144.0 %all-gather.27.cloned.1.call-start = ((), (), s32[]{:S(2)}) async-start(), calls=%async_computation.24 | async-start | bytes 1966080 | tf_op jit(solution)/shard_map/all_gather | solution.py:980
  572.4 77.9 %collective-permute-start.29 = (bf16[4,704,768]{2,1,0:T(8,128)(2,1)}, bf16[4,704,768]{2,1,0:T(8,128)(2,1)}, u32[]{:S(2)}, u32[]{:S(2)}) collective-permute-start(bf16[4,704,768]{2,1,0:T(8,128)(2,1)} %join_rows.13.refs_1_.refs_0_), channel_id=1, source_target_pairs={{0,4},{4,0},{8,12},{12,8},{16,20},{20,16},{24,28},{28,24},{1,5},{5... | collective-permute-start | bytes 12976136 | tf_op jit(solution)/shard_map/ppermute | solution.py:817
  602.1 531.6 %reduce-scatter.10.cloned.1.call-start = ((), (), s32[]{:S(2)}) async-start(), calls=%async_computation.12 | async-start | bytes 1966080 | tf_op jit(solution)/shard_map/reduce_scatter | solution.py:1139
  619.6 67.0 %collective-permute-start.37 = (bf16[4,704,384]{2,1,0:T(8,128)(2,1)}, bf16[4,704,384]{2,1,0:T(8,128)(2,1)}, u32[]{:S(2)}, u32[]{:S(2)}) collective-permute-start(bf16[4,704,384]{2,1,0:T(8,128)(2,1)} %join_rows.15.refs_1_.refs_0_), channel_id=1, source_target_pairs={{0,4},{4,0},{8,12},{12,8},{16,20},{20,16},{24,28},{28,24},{1,5},{5... | collective-permute-start | bytes 6488072 | tf_op jit(solution)/shard_map/ppermute | solution.py:817
  785.0 131.0 %collective-permute-start.48 = (bf16[4,704,768]{2,1,0:T(8,128)(2,1)}, bf16[4,704,768]{2,1,0:T(8,128)(2,1)}, u32[]{:S(2)}, u32[]{:S(2)}) collective-permute-start(bf16[4,704,768]{2,1,0:T(8,128)(2,1)} %get-tuple-element.222), channel_id=1, source_target_pairs={{0,4},{4,0},{8,12},{12,8},{16,20},{20,16},{24,28},{28,24},{1,5},{5... | collective-permute-start | bytes 12976136 | tf_op jit(solution)/shard_map/ppermute | solution.py:817
  831.6 103.0 %collective-permute-start.49 = (bf16[4,704,768]{2,1,0:T(8,128)(2,1)}, bf16[4,704,768]{2,1,0:T(8,128)(2,1)}, u32[]{:S(2)}, u32[]{:S(2)}) collective-permute-start(bf16[4,704,768]{2,1,0:T(8,128)(2,1)} %get-tuple-element.224), channel_id=1, source_target_pairs={{0,4},{4,0},{8,12},{12,8},{16,20},{20,16},{24,28},{28,24},{1,5},{5... | collective-permute-start | bytes 12976136 | tf_op jit(solution)/shard_map/ppermute | solution.py:817
  916.0 217.7 %reduce-scatter.8.cloned.1.call-start = ((), (), s32[]{:S(2)}) async-start(), calls=%async_computation.11 | async-start | bytes 2703360 | tf_op jit(solution)/shard_map/reduce_scatter | solution.py:1139
  968.7 165.0 %collective-permute-start.54 = (bf16[4,704,1152]{2,1,0:T(8,128)(2,1)}, bf16[4,704,1152]{2,1,0:T(8,128)(2,1)}, u32[]{:S(2)}, u32[]{:S(2)}) collective-permute-start(bf16[4,704,1152]{2,1,0:T(8,128)(2,1)} %get-tuple-element.235), channel_id=1, source_target_pairs={{0,4},{4,0},{8,12},{12,8},{16,20},{20,16},{24,28},{28,24},{1,5},{5... | collective-permute-start | bytes 19464200 | tf_op jit(solution)/shard_map/ppermute | solution.py:817
  1013.4 120.3 %collective-permute-start.55 = (bf16[4,512,768]{2,1,0:T(8,128)(2,1)}, bf16[4,512,768]{2,1,0:T(8,128)(2,1)}, u32[]{:S(2)}, u32[]{:S(2)}) collective-permute-start(bf16[4,512,768]{2,1,0:T(8,128)(2,1)} %get-tuple-element.236), channel_id=1, source_target_pairs={{0,4},{4,0},{8,12},{12,8},{16,20},{20,16},{24,28},{28,24},{1,5},{5... | collective-permute-start | bytes 9437192 | tf_op jit(solution)/shard_map/ppermute | solution.py:817
  1020.0 59.1 %all-to-all-start.2 = ((bf16[4,2,256,384]{3,2,1,0:T(8,128)(2,1)}), bf16[4,2,256,384]{3,2,1,0:T(8,128)(2,1)}, u32[]{:S(2)}, u32[]{:S(2)}) async-start(bf16[4,2,256,384]{3,2,1,0:T(8,128)(2,1)} %bitcast.189), calls=%async_computation.2 | async-start | bytes 3145728 | tf_op jit(solution)/shard_map/all_to_all | solution.py:994
  1024.6 109.1 %collective-permute-start.52 = (bf16[4,352,768]{2,1,0:T(8,128)(2,1)}, bf16[4,352,768]{2,1,0:T(8,128)(2,1)}, u32[]{:S(2)}, u32[]{:S(2)}) collective-permute-start(bf16[4,352,768]{2,1,0:T(8,128)(2,1)} %copy-done.50), channel_id=1, source_target_pairs={{0,16},{4,20},{8,24},{12,28},{16,0},{20,4},{24,8},{28,12},{1,17},{... | collective-permute-start | bytes 6488072 | tf_op jit(solution)/shard_map/ppermute | solution.py:817
  1025.3 108.3 %collective-permute-start.53 = (bf16[4,352,768]{2,1,0:T(8,128)(2,1)}, bf16[4,352,768]{2,1,0:T(8,128)(2,1)}, u32[]{:S(2)}, u32[]{:S(2)}) collective-permute-start(bf16[4,352,768]{2,1,0:T(8,128)(2,1)} %copy-done.51), channel_id=1, source_target_pairs={{0,8},{4,12},{8,0},{12,4},{16,24},{20,28},{24,16},{28,20},{1,9},{5... | collective-permute-start | bytes 6488072 | tf_op jit(solution)/shard_map/ppermute | solution.py:817
  1133.7 112.0 %all-to-all-start.3 = ((bf16[4,2,256,1152]{3,2,1,0:T(8,128)(2,1)}), bf16[4,2,256,1152]{3,2,1,0:T(8,128)(2,1)}, u32[]{:S(2)}, u32[]{:S(2)}) async-start(bf16[4,2,256,1152]{3,2,1,0:T(8,128)(2,1)} %get-tuple-element.237), calls=%async_computation.5 | async-start | bytes 9437184 | tf_op jit(solution)/shard_map/all_to_all | solution.py:994
  1138.7 359.8 %reduce-scatter.18.cloned.1.call-start = ((), (), s32[]{:S(2)}) async-start(), calls=%async_computation.16 | async-start | bytes 983040 | tf_op jit(solution)/shard_map/reduce_scatter | solution.py:1139
  1145.4 98.6 %collective-permute-start.58 = (bf16[4,352,1152]{2,1,0:T(8,128)(2,1)S(1)}, bf16[4,352,1152]{2,1,0:T(8,128)(2,1)S(1)}, u32[]{:S(2)}, u32[]{:S(2)}) collective-permute-start(bf16[4,352,1152]{2,1,0:T(8,128)(2,1)S(1)} %sum_rows.40), channel_id=1, source_target_pairs={{0,16},{4,20},{8,24},{12,28},{16,0},{20,4},{24,8},{28,12},{1,17},{... | collective-permute-start | bytes 9732104 | tf_op jit(solution)/shard_map/ppermute | solution.py:817
  1155.5 87.3 %collective-permute-start.59 = (bf16[4,256,768]{2,1,0:T(8,128)(2,1)S(1)}, bf16[4,256,768]{2,1,0:T(8,128)(2,1)S(1)}, u32[]{:S(2)}, u32[]{:S(2)}) collective-permute-start(bf16[4,256,768]{2,1,0:T(8,128)(2,1)S(1)} %sum_rows.41), channel_id=1, source_target_pairs={{0,8},{4,12},{8,0},{12,4},{16,24},{20,28},{24,16},{28,20},{1,9},{5... | collective-permute-start | bytes 4718600 | tf_op jit(solution)/shard_map/ppermute | solution.py:817
  1164.9 77.0 %collective-permute-start.57 = (bf16[4,176,768]{2,1,0:T(8,128)(2,1)S(1)}, bf16[4,176,768]{2,1,0:T(8,128)(2,1)S(1)}, u32[]{:S(2)}, u32[]{:S(2)}) collective-permute-start(bf16[4,176,768]{2,1,0:T(8,128)(2,1)S(1)} %sum_rows.39), channel_id=1, source_target_pairs={{0,16},{4,20},{8,24},{12,28},{16,0},{20,4},{24,8},{28,12},{1,17},{... | collective-permute-start | bytes 3244040 | tf_op jit(solution)/shard_map/ppermute | solution.py:817
  1274.4 237.7 %reduce-scatter.20.cloned.1.call-start = ((), (), s32[]{:S(2)}) async-start(), calls=%async_computation.17 | async-start | bytes 2703360 | tf_op jit(solution)/shard_map/reduce_scatter | solution.py:1139
  1296.9 222.9 %reduce-scatter.16.cloned.1.call-start = ((), (), s32[]{:S(2)}) async-start(), calls=%async_computation.15 | async-start | bytes 2027520 | tf_op jit(solution)/shard_map/reduce_scatter | solution.py:1139
  1367.1 157.2 %reduce-scatter.12.cloned.1.call-start = ((), (), s32[]{:S(2)}) async-start(), calls=%async_computation.13 | async-start | bytes 1351680 | tf_op jit(solution)/shard_map/reduce_scatter | solution.py:1139
  1450.7 81.2 %reduce-scatter.14.cloned.1.call-start = ((), (), s32[]{:S(2)}) async-start(), calls=%async_computation.14 | async-start | bytes 2027520 | tf_op jit(solution)/shard_map/reduce_scatter | solution.py:1139
  (205 other events, 3759.5 us)
Sparse Core Ops, SparseCore 0:
  10.2 31.1 all-gather.14
  43.5 36.6 all-gather.16
  81.8 47.3 all-gather.18
  183.5 46.6 all-gather.20
  393.8 51.3 all-gather.22
  495.9 29.4 all-gather.24
  602.2 37.4 all-gather.26
  916.1 33.2 reduce-scatter.9
  1003.6 58.1 reduce-scatter.7
  1274.5 23.9 reduce-scatter.17
  1300.9 44.2 reduce-scatter.19
  1367.2 35.5 reduce-scatter.15
  1450.8 28.7 reduce-scatter.11
  1496.3 35.5 reduce-scatter.13

commit v6 on v5

--- a/solution.py
+++ b/solution.py
@@ -173,7 +173,7 @@
             jax.ShapeDtypeStruct((micros, sequence, lanes), BF),
             jax.ShapeDtypeStruct((micros, local, sequence), F32),
         ],
-        compiler_params=pltpu.CompilerParams(vmem_limit_bytes=48 << 20),
+        compiler_params=params(),
         cost_estimate=cost(4 * micros * local * sequence * sequence * HP),
     )(counts, raw, cosine, sine, gain_q, gain_k)
 
@@ -286,7 +286,7 @@
             jax.ShapeDtypeStruct((micros, 1, lanes), F32),
             jax.ShapeDtypeStruct((micros, 1, lanes), F32),
         ],
-        compiler_params=pltpu.CompilerParams(vmem_limit_bytes=48 << 20),
+        compiler_params=params(),
         cost_estimate=cost(10 * micros * local * sequence * sequence * HP),
     )(counts, raw, cosine, sine, gain_q, gain_k, turned_q, turned_k, norms, incoming)
 
@@ -299,7 +299,7 @@
     return pl.BlockSpec(shape, lambda *index: (0,) * len(shape))
 
 
-def params(megabytes=48):
+def params(megabytes=60):
     return pltpu.CompilerParams(vmem_limit_bytes=megabytes << 20)
 
 
@@ -408,7 +408,7 @@
         out_specs=[full(out.shape) for out in outs],
         out_shape=outs,
         scratch_shapes=[pltpu.VMEM((2, rows, half), F32)],
-        compiler_params=params(56),
+        compiler_params=params(),
         cost_estimate=cost(4 * rows * half * parts * total),
     )(value, *[side for weight in weights for side in (weight.near, weight.far)], *extras)
 
@@ -492,42 +492,51 @@
         in_specs=[pl.BlockSpec((1, rows, lanes), lambda p: (p, 0, 0))] * count,
         out_specs=pl.BlockSpec((1, count * rows, lanes), lambda p: (p, 0, 0)),
         out_shape=jax.ShapeDtypeStruct((parts, count * rows, lanes), BF),
-        compiler_params=params(24),
+        compiler_params=params(),
         cost_estimate=cost(parts * count * rows * lanes),
     )(*pieces)
 
 
-def sum_rows(terms, rows, count, name="sum_rows"):
-    parts, _, lanes = terms[0][0].shape
+def sum_rows(jobs, rows, name="sum_rows"):
+    parts = jobs[0][0][0].shape[0]
     if rows % 16:
-        value = 0.0
-        for array, first, step in terms:
-            blocks = array.reshape(parts, -1, rows, lanes)[:, first :: step][:, :count]
-            value = value + blocks.astype(F32)
-        return value.astype(BF).reshape(parts, count * rows, lanes)
+        results = []
+        for terms in jobs:
+            value = 0.0
+            for array, blocks in terms:
+                split = array.reshape(parts, -1, rows, array.shape[2])
+                value = value + jnp.stack([split[:, block] for block in blocks], 1).astype(F32)
+            results.append(value.astype(BF).reshape(parts, -1, value.shape[3]))
+        return results
+    arrays = [term[0] for terms in jobs for term in terms]
 
     def kernel(*refs):
-        for index in range(count):
-            value = None
-            for (array, first, step), ref in zip(terms, refs):
-                start = 0 if array.shape[1] == rows else (first + step * index) % (array.shape[1] // rows)
-                term = ref[0, start * rows : (start + 1) * rows].astype(F32)
-                value = term if value is None else value + term
-            refs[-1][0, index * rows : (index + 1) * rows] = value.astype(BF)
-
-    def spec(size):
+        at = 0
+        for spot, terms in enumerate(jobs):
+            out_ref = refs[len(arrays) + spot]
+            for index in range(len(terms[0][1])):
+                value = None
+                for offset, (_, blocks) in enumerate(terms):
+                    start = blocks[index] * rows
+                    term = refs[at + offset][0, start : start + rows].astype(F32)
+                    value = term if value is None else value + term
+                out_ref[0, index * rows : (index + 1) * rows] = value.astype(BF)
+            at += len(terms)
+
+    def spec(size, lanes):
         return pl.BlockSpec((1, size, lanes), lambda p: (p, 0, 0))
 
+    shapes = [(len(terms[0][1]) * rows, terms[0][0].shape[2]) for terms in jobs]
     return pl.pallas_call(
         kernel,
         name=name,
         grid=(parts,),
-        in_specs=[spec(term[0].shape[1]) for term in terms],
-        out_specs=spec(count * rows),
-        out_shape=jax.ShapeDtypeStruct((parts, count * rows, lanes), BF),
-        compiler_params=params(32),
-        cost_estimate=cost(parts * count * rows * lanes),
-    )(*[term[0] for term in terms])
+        in_specs=[spec(*array.shape[1:]) for array in arrays],
+        out_specs=[spec(*shape) for shape in shapes],
+        out_shape=[jax.ShapeDtypeStruct((parts, *shape), BF) for shape in shapes],
+        compiler_params=params(),
+        cost_estimate=cost(sum(parts * size * lanes for size, lanes in shapes)),
+    )(*arrays)
 
 
 def side_by_side(left, right, kept, lanes):
@@ -546,7 +555,7 @@
         kernel,
         name="side_by_side",
         out_shape=jax.ShapeDtypeStruct((2 * count, rows, lanes), BF),
-        compiler_params=params(24),
+        compiler_params=params(),
         cost_estimate=cost(4 * rows * lanes),
     )(left, right)
 
@@ -671,7 +680,7 @@
         out_specs=[grad, grad] + [full(out.shape) for out in outs],
         out_shape=[grad_shape, grad_shape] + outs,
         scratch_shapes=[pltpu.VMEM((2, half, rows), BF), pltpu.VMEM((2, rows, half), F32)],
-        compiler_params=params(56),
+        compiler_params=params(),
         cost_estimate=cost(12 * rows * half * parts * ff),
     )(grads, rows_in, hidden, weight1.near, weight1.far, weight2.near, weight2.far, *extras)
 
@@ -733,7 +742,7 @@
             out_specs=pl.BlockSpec((1, 1, slots, lanes), spot),
         ),
         out_shape=jax.ShapeDtypeStruct(query.shape, BF),
-        compiler_params=pltpu.CompilerParams(vmem_limit_bytes=32 << 20),
+        compiler_params=params(),
         cost_estimate=cost(4 * parts * micros * slots * words * lanes),
     )(lengths, query, text_kv)
 
@@ -789,7 +798,7 @@
             jax.ShapeDtypeStruct(query.shape, BF),
             jax.ShapeDtypeStruct(text_kv.shape, BF),
         ],
-        compiler_params=pltpu.CompilerParams(vmem_limit_bytes=32 << 20),
+        compiler_params=params(),
         cost_estimate=cost(10 * parts * micros * slots * words * lanes),
     )(lengths, query, text_kv, incoming)
 
@@ -870,41 +879,42 @@
         self.got = []
         self.pieces = [cube.swap(far, 0)]
         self.arriving = self.places
-        self.packed = False
-
-    def total(self, places):
-        first = places[0]
-        step = places[1] - first if len(places) > 1 else 1
-        terms = [(self.near, first, step)]
-        for value, held in self.got:
-            spots = [held.index(place) for place in places]
-            terms.append((value, spots[0], spots[1] - spots[0] if len(spots) > 1 else 1))
-        return sum_rows(terms, self.rows, len(places))
+
+    def job(self, places):
+        return [(self.near, places)] + [
+            (value, [held.index(place) for place in places]) for value, held in self.got
+        ]
 
     def absorb(self):
         self.got.append((self.pieces[0], self.arriving))
 
-    def pack(self):
-        self.absorb()
-        self.bit = self.todo.pop(0)
-        weight = 1 << (self.bit - 1)
-        sent = [place for place in self.places if place & weight]
-        self.places = [place for place in self.places if not place & weight]
-        self.arriving = [place ^ weight for place in sent]
-        self.pieces = [self.total(sent)]
-        self.packed = True
-
-    def move(self):
-        if not self.packed:
-            self.pack()
-        self.pieces = [self.cube.swap(self.pieces[0], self.bit)]
-        self.packed = False
-
-    def result(self):
-        while self.todo or self.packed:
-            self.move()
-        self.absorb()
-        return self.total([0])
+
+def pack(movers):
+    jobs = []
+    for mover in movers:
+        mover.absorb()
+        mover.bit = mover.todo.pop(0)
+        weight = 1 << (mover.bit - 1)
+        sent = [place for place in mover.places if place & weight]
+        mover.places = [place for place in mover.places if not place & weight]
+        mover.arriving = [place ^ weight for place in sent]
+        jobs.append(mover.job(sent))
+    for mover, value in zip(movers, sum_rows(jobs, movers[0].rows)):
+        mover.pieces = [value]
+
+
+def send(movers):
+    for mover in movers:
+        mover.pieces = [mover.cube.swap(mover.pieces[0], mover.bit)]
+
+
+def results(movers):
+    while movers[0].todo:
+        pack(movers)
+        send(movers)
+    for mover in movers:
+        mover.absorb()
+    return sum_rows([mover.job([0]) for mover in movers], movers[0].rows)
 
 
 def pin(value, *others):
@@ -994,16 +1004,27 @@
         return lax.all_to_all(value, "sp", split_axis=0, concat_axis=0, tiled=True)
 
     skip_z = spread(jnp.pad(w_skip.T, ((0, 0), (0, skip_lanes - kept))))
+    steps = cube.spread(timestep[:, 0])
+    skip_z, steps = tie(skip_z, steps)
+    skip_m = fetch(skip_z, skip_cut)
     qkv_z = spread(pad_heads(w_qkv.reshape(strip, -1), local), skip_z)
-    fc1_z = spread(w_fc1, qkv_z)
-    fc2_z = spread(w_fc2.T, fc1_z)
-    skip_m = fetch(skip_z, skip_cut)
+    advance(skip_m)
+
+    time_act = jax.nn.silu(time_embed(steps, width)).astype(BF).reshape(ranks * micros, parts, -1)
+    time_part = lax.dynamic_index_in_dim(time_act, zone, 1, keepdims=False)
+    shift = cube.add(jnp.dot(time_part, w_mod, preferred_element_type=F32), "sp")
+    skip_m[0].pieces[1], shift = tie(skip_m[0].pieces[1], shift)
     while skip_m[0].todo:
         advance(skip_m)
+    shift = cube.trade(shift.reshape(ranks, micros, strip))
+    skip_m[0].pieces[-1], shift = tie(skip_m[0].pieces[-1], shift)
+    shift = jnp.stack([shift[mask] for mask in cube.masks]).reshape(2, ranks // 2, micros, strip)
+    shift = jnp.transpose(shift, (0, 2, 1, 3)).reshape(2, micros, middle)
     qkv_m = fetch(qkv_z, qkv_cut)
     hold(qkv_m, *skip_m)
     advance(qkv_m)
-    hold(skip_m, qkv_z)
+    fc1_z = spread(pin(w_fc1, *skip_m))
+    fc2_z = spread(pin(w_fc2.T, *qkv_m))
     join(skip_m)
     skip_w = [mover.weight() for mover in skip_m]
 
@@ -1027,14 +1048,6 @@
     cosine, sine = rope_tables(sequence, wide, lanes)
     gain_q = pad_heads(jnp.tile(gain_query, local)[None, :], local)
     gain_k = pad_heads(jnp.tile(gain_key, local)[None, :], local)
-
-    steps = cube.spread(timestep[:, 0])
-    time_act = jax.nn.silu(time_embed(steps, width)).astype(BF).reshape(ranks * micros, parts, -1)
-    time_part = lax.dynamic_index_in_dim(time_act, zone, 1, keepdims=False)
-    shift = jnp.dot(time_part, w_mod, preferred_element_type=F32)
-    shift = cube.trade(cube.add(shift, "sp").reshape(ranks, micros, strip))
-    shift = jnp.stack([shift[mask] for mask in cube.masks]).reshape(2, ranks // 2, micros, strip)
-    shift = jnp.transpose(shift, (0, 2, 1, 3)).reshape(2, micros, middle)
 
     grad3 = jnp.stack(
         [
@@ -1089,32 +1102,34 @@
     advance(fc_m)
     raw = exchange(projected.reshape(parts, micros, slots, 3 * lanes))
     cross_z = jnp.concatenate([pad_heads(side, local) for side in (w_out1.T, w_query2, w_out2.T)], 1)
-    cross_z = spread(cross_z, raw)
-    text_z = jnp.pad(pad_heads(w_text_kv.reshape(text_rows, -1), local), ((0, max(0, strip - text_rows)), (0, 0)))
-    text_z = spread(text_z, cross_z)
+    cross_z = spread(pin(cross_z, *fc_m))
     text_own = jnp.dot(text.reshape(-1, features), text_turn, preferred_element_type=F32).astype(BF)
     text_own = jnp.pad(
         text_own.reshape(micros, text_slots, features), ((0, 0), (0, text_strip - text_slots), (0, 0))
     ).reshape(micros * text_strip, features)
-    text_all = spread(text_own, text_z).reshape(-1, features)
-    text_all = jnp.stack([text_all[:, : features // 2], text_all[:, features // 2 :]])
-    raw = pin(raw, *fc_m)
+    text_z = jnp.pad(pad_heads(w_text_kv.reshape(text_rows, -1), local), ((0, max(0, strip - text_rows)), (0, 0)))
     while fc_m[0].todo:
         advance(fc_m)
     attended, turned_q, turned_k, norms = self_forward(raw, counts, cosine, sine, gain_q, gain_k)
+    attended = bind(attended, *fc_m)
+    attended, cross_z = tie(attended, cross_z)
+    text_z = spread(text_z, cross_z)
     cross_m = fetch(cross_z, 2 * lanes)
-    text_m = Gather(cube, text_z[:, :text_rows], 1)
-    hold(cross_m, attended)
     advance(cross_m)
     attended = exchange(attended).reshape(parts, rows, lanes)
-    hold(fc_m + cross_m + [text_m], attended)
+    attended, text_z = tie(attended, text_z)
+    attended = bind(attended, *cross_m)
+    text_all = spread(text_own, text_z).reshape(-1, features)
+    text_all = jnp.stack([text_all[:, : features // 2], text_all[:, features // 2 :]])
+    text_m = Gather(cube, text_z[:, :text_rows], 1)
+    hold(fc_m, attended)
     join(cross_m)
     first_w, out2_w = [mover.weight() for mover in cross_m]
     out1_w, query2_w = (Lanes(first_w.near, first_w.far, lanes, index) for index in range(2))
+    text_m.join()
+    text_w = text_m.weight()
     join(fc_m)
     fc1_w, fc2_w = [mover.weight() for mover in fc_m]
-    text_m.join()
-    text_w = text_m.weight()
     stream1, pre_cross = to_features(
         attended, [out1_w], [stream, g_cross], [wide_shape, low_shape], next_norm
     )
@@ -1128,10 +1143,6 @@
     hidden1, activ1, result, fc2_n1, fc2_f1 = mlp_forward(pre_mlp, d_mlp, partial, fc1_w, fc2_w, 1, live)
     fc2_s = [Scatter(cube, fc2_n0, fc2_f0, 0), Scatter(cube, fc2_n1, fc2_f1, 1)]
 
-    def pack(movers):
-        for mover in movers:
-            mover.pack()
-
     def settle(values, before=None):
         value = values[0] if len(values) == 1 else jnp.concatenate(values, 2)
         if before is not None:
@@ -1139,25 +1150,27 @@
         return lax.psum_scatter(value, "sp", scatter_dimension=0, tiled=False)
 
     fc1_n0, fc1_f0, partial = mlp_backward(d_mlp, pre_mlp, hidden0, fc1_w, fc2_w, 0, None)
+    fc1_s = [Scatter(cube, fc1_n0, fc1_f0, 0)]
     pack(fc2_s)
     partial = bind(partial, *fc2_s)
-    advance(fc2_s)
+    send(fc2_s)
     fc1_n1, fc1_f1, grad2, d_cross, d_gain_mlp = mlp_backward(
         d_mlp, pre_mlp, hidden1, fc1_w, fc2_w, 1, partial, [stream2, g_mlp, grad3]
     )
-    fc1_s = [Scatter(cube, fc1_n0, fc1_f0, 0), Scatter(cube, fc1_n1, fc1_f1, 1)]
+    fc1_s.append(Scatter(cube, fc1_n1, fc1_f1, 1))
+    d_cross = bind(d_cross, *fc2_s)
     d_crossed = to_lanes(d_cross, [out2_w])
+    pack(fc2_s)
     d_crossed = bind(d_crossed, *fc2_s)
+    send(fc2_s)
     d_query2, d_text_kv = cross_backward(
         query2, text_kv, lengths, d_crossed.reshape(parts, micros, slots, lanes), text_slots
     )
-    pack(fc2_s)
-    pack(fc1_s)
-    d_query2 = bind(d_query2, *fc2_s, *fc1_s)
-    advance(fc2_s)
-    advance(fc1_s)
+    d_query2 = bind(d_query2, *fc2_s)
     d_query2 = d_query2.reshape(parts, rows, lanes)
     d_text_kv = d_text_kv.reshape(parts, -1, 2 * lanes)
+    total_fc2 = results(fc2_s)
+    term_fc2 = settle(total_fc2)
 
     def go_back(sums, extra, out):
         add_norm_back(sums, *extra, *out)
@@ -1165,7 +1178,12 @@
     grad1, d_attn, d_gain_cross = to_features(
         d_query2, [query2_w], [stream1, g_cross, grad2], [wide_shape, low_shape, gain_shape], go_back
     )
+    d_attn = bind(d_attn, *fc1_s)
+    pack(fc1_s)
+    d_attn = bind(d_attn, *fc1_s)
+    send(fc1_s)
     d_attended = to_lanes(d_attn, [out1_w])
+    d_attended, d_text_kv, pre_cross = tie(d_attended, d_text_kv, pre_cross)
     d_heads = exchange(d_attended.reshape(parts, micros, slots, lanes))
 
     def words_back(sums, extra, out):
@@ -1176,27 +1194,33 @@
 
     words_shape = jax.ShapeDtypeStruct((parts, 2, micros * text_strip, features // 2), BF)
     d_words = to_features(d_text_kv, [text_w], [], [words_shape], words_back)[0]
+    text_t = list(terms_of([(text_all, d_text_kv, 2 * lanes, 0)]))
+    cross_t = terms_of(
+        [(d_attn, attended, lanes, 0), (pre_cross, d_query2, lanes, 0), (d_cross, crossed, lanes, 0)]
+    )
+    cross_t = list(cross_t)
+    d_heads, d_words, text_t[1], cross_t[1] = tie(d_heads, d_words, text_t[1], cross_t[1])
     d_words = settle([d_words])
-    text_s = Scatter(cube, *terms_of([(text_all, d_text_kv, 2 * lanes, 0)]), 1)
-    cross_s = Scatter(
-        cube,
-        *terms_of([(d_attn, attended, lanes, 0), (pre_cross, d_query2, lanes, 0), (d_cross, crossed, lanes, 0)]),
-        0,
-    )
-    total_fc2 = [mover.result() for mover in fc2_s]
-    term_fc2 = settle(total_fc2)
+    text_s, cross_s = Scatter(cube, *text_t, 1), Scatter(cube, *cross_t, 0)
+    d_heads = bind(d_heads, *fc1_s)
+    pack(fc1_s)
+    d_heads = bind(d_heads, *fc1_s)
+    send(fc1_s)
     d_raw, d_gain_q, d_gain_k = self_backward(
         raw, counts, cosine, sine, gain_q, gain_k, turned_q, turned_k, norms, d_heads
     )
     d_raw, term_fc2, d_words = tie(d_raw, term_fc2, d_words)
-    d_raw = bind(d_raw, *fc1_s, cross_s, text_s)
+    d_raw = bind(d_raw, *fc1_s)
     d_projected = exchange(d_raw).reshape(parts, rows, 3 * lanes)
-    advance(fc1_s)
-    pack([cross_s, text_s])
-    hold([cross_s, text_s], d_raw)
-    advance([cross_s, text_s])
-    d_projected = bind(d_projected, *fc1_s, cross_s, text_s)
-    total_fc1 = [mover.result() for mover in fc1_s]
+    other_s = [cross_s, text_s]
+    total_fc1 = results(fc1_s)
+    pack([cross_s])
+    pack([text_s])
+    send(other_s)
+    d_projected = bind(d_projected, *other_s)
+    pack([cross_s])
+    pack([text_s])
+    send(other_s)
 
     def last_norms(sums, extra, out):
         stream_ref, g1_ref, base_ref, g0_ref, add_ref = extra
@@ -1225,20 +1249,21 @@
         [low_shape, shift_shape, gain_shape, gain_shape],
         last_norms,
     )
+    d_base = bind(d_base, *qkv_s, *other_s)
     pack(qkv_s)
     d_base = bind(d_base, *qkv_s)
-    advance(qkv_s)
+    send(qkv_s)
     skip_s = [
         Scatter(cube, *terms_of([(d_base, joined, skip_cut, flip)]), flip) for flip in range(2)
     ]
-    total_cross, total_text = cross_s.result(), text_s.result()
+    term_cross, term_text = settle(results([cross_s])), settle(results([text_s]))
     pack(skip_s)
-    hold(skip_s, total_cross, total_text, *qkv_s)
-    advance(skip_s)
-    term_cross = settle([total_cross])
-    term_text = settle([total_text])
-    term_qkv = settle([mover.result() for mover in qkv_s])
-    term_skip = settle([mover.result() for mover in skip_s])
+    hold(skip_s, *qkv_s)
+    send(skip_s)
+    pack(qkv_s)
+    send(qkv_s)
+    term_qkv = settle(results(qkv_s))
+    term_skip = settle(results(skip_s))
     d_joined = to_inputs(d_base, skip_w, kept)
     result = (
         jnp.dot(result[0], turn[:, :middle].T, preferred_element_type=F32)

time: 1560 us -> 1420 us (0.910)
  waiting for transfers between devices: 668 us -> 519 us
  local copies, waits for them, and re-layouts: 122 us -> 55.8 us
  Pallas kernels: 565 us -> 621 us
  starting transfers between devices: 113 us -> 133 us
    ppermute x84, waiting for transfers between devices: 432 us -> 349 us  [swap(): return lax.ppermute(value, axis, pairs)]
    all_to_all x4, waiting for transfers between devices: 148 us -> 79.5 us  [exchange(): return lax.all_to_all(value, 'sp', split_axis=0, concat_axis=0, tiled=True)]
    unnamed x284 -> x160, local copies, waits for them, and re-layouts: 79.1 us -> 11.4 us
    ppermute x84, starting transfers between devices: 93.1 us -> 115 us  [swap(): return lax.ppermute(value, axis, pairs)]
    pallas_call x30 -> x18, Pallas kernels: 109 us -> 127 us  [sum_rows(): pl.pallas_call(kernel, name=name, grid=(parts,), in_specs=[spec(*array.sh...]
  transfers between devices with their start and end apart: 102 -> 102, of which waited for: 42 -> 49; matrix products, arithmetic and copies ran while one was open for 6% -> 8% of each run, Pallas kernels for 32% -> 40%
where the time goes in v6:
time: 1420 us; the launch traced here: 1410 us
  Pallas kernels  621 us (44%)
  waiting for transfers between devices  519 us (37%)
  starting transfers between devices  133 us (9%)
  other arithmetic  56.7 us (4%)
  local copies, waits for them, and re-layouts  55.8 us (4%)
  between operations  15.6 us (1%)
    ppermute x84, waiting for transfers between devices, swap(): return lax.ppermute(value, axis, pairs)  349 us
    pallas_call x18, Pallas kernels, sum_rows(): pl.pallas_call(kernel, name=name, grid=(parts,), in_specs=[spec(*array.sh...  127 us
    ppermute x84, starting transfers between devices, swap(): return lax.ppermute(value, axis, pairs)  115 us
    all_gather x7, waiting for transfers between devices, spread(): return lax.all_gather(shard, 'sp', axis=0, tiled=False)  86.3 us
    all_to_all x4, waiting for transfers between devices, exchange(): return lax.all_to_all(value, 'sp', split_axis=0, concat_axis=0, tiled=True)  79.5 us
    pallas_call x6, Pallas kernels, to_features(): pl.pallas_call(kernel, name=name, grid=(parts,), in_specs=[pl.BlockSpec((...  78.5 us
    pallas_call x2, Pallas kernels, mlp_backward(): pl.pallas_call(kernel, name='mlp_backward', grid=(parts, steps), in_specs...  63.7 us
    pallas_call x2, Pallas kernels, mlp_forward(): pl.pallas_call(kernel, name='mlp_forward', grid=(parts, steps), in_specs=...  57.1 us
  transfers between devices with their start and end apart: 102, of which 49 were waited for; matrix products, arithmetic and copies ran while one was open for 8% of the time, Pallas kernels for 40%

profile of v6, /device:TPU:0, one launch (start us, length us, event | category | flops | bytes accessed | tf_op | source)
XLA Modules:
  0.0 1413.9 jit_solution(10218330713615907831)
XLA Ops:
  21.4 20.0 %all-gather.15.cloned.1.call-done = bf16[704,768]{1,0:T(8,128)(2,1)} async-done(((bf16[176,768]{1,0:T(8,128)(2,1)}), bf16[704,768]{1,0:T(8,128)(2,1)}) %all-gather.15.cloned.1.call-update) | async-done | bytes 1081360 | tf_op jit(solution)/shard_map/all_gather | solution.py:990
  62.5 22.0 %collective-permute-done.9 = f32[4,2,176]{2,1,0:T(2,128)S(1)} collective-permute-done((f32[4,2,176]{2,1,0:T(2,128)S(1)}, f32[4,2,176]{2,1,0:T(2,128)S(1)}, u32[]{:S(2)}, u32[]{:S(2)}) %collective-permute-start.9) | collective-permute-done | bytes 5664 | tf_op jit(solution)/shard_map/ppermute | solution.py:826
  112.3 11.2 collective-permute-done.16.refs_1_
  124.8 22.7 %collective-permute-done.21.refs_2_ = bf16[4,176,512]{2,1,0:T(8,128)(2,1)} collective-permute-done((bf16[4,176,512]{2,1,0:T(8,128)(2,1)S(1)}, bf16[4,176,512]{2,1,0:T(8,128)(2,1)}, u32[]{:S(2)}, u32[]{:S(2)}) %collective-permute-start.21) | collective-permute-done | bytes 720928 | tf_op jit(solution)/shard_map/ppermute | solution.py:826
  149.5 14.6 %to_features.6 = (f32[2,512,704]{2,1,0:T(8,128)}, f32[2,512,704]{2,1,0:T(8,128)}, bf16[2,512,704]{2,1,0:T(8,128)(2,1)}) custom-call(bf16[4,512,768]{2,1,0:T(8,128)(2,1)} %side_by_side.1.refs_0_.refs_1_, bf16[4,704,384]{2,1,0:T(8,128)(2,1)} %join_rows.9.refs_1_.refs_0_, bf16[4,704,384]{2,1,0:T(8,128)(2,1)} %collective-permute-done.11.refs_2_.refs_1_, ...), custom_call_target="tpu_custom_call" | custom-call | flops 276824064 | bytes 276824 | tf_op jit(solution)/shard_map/to_features/pallas_call | solution.py:401
  188.5 13.0 to_lanes.5
  201.5 14.3 %all-gather.21.cloned.1.call-done = bf16[704,1536]{1,0:T(8,128)(2,1)} async-done(((bf16[176,1536]{1,0:T(8,128)(2,1)}), bf16[704,1536]{1,0:T(8,128)(2,1)}) %all-gather.21.cloned.1.call-update) | async-done | bytes 2162704 | tf_op jit(solution)/shard_map/all_gather | solution.py:990
  226.3 44.1 %collective-permute-done.24.refs_1_ = bf16[4,176,1536]{2,1,0:T(8,128)(2,1)} collective-permute-done((bf16[4,176,1536]{2,1,0:T(8,128)(2,1)}, bf16[4,176,1536]{2,1,0:T(8,128)(2,1)}, u32[]{:S(2)}, u32[]{:S(2)}) %collective-permute-start.24) | collective-permute-done | bytes 2162720 | tf_op jit(solution)/shard_map/ppermute | solution.py:826
  279.0 13.9 negate_select_fusion
  292.9 59.0 %all-to-all-done.raw_ref = bf16[4,2,256,1152]{3,2,1,0:T(8,128)(2,1)} async-done(((bf16[4,2,256,1152]{3,2,1,0:T(8,128)(2,1)}), bf16[4,2,256,1152]{3,2,1,0:T(8,128)(2,1)}, u32[]{:S(2)}, u32[]{:S(2)}) %all-to-all-start) | async-done | bytes 4718624 | tf_op jit(solution)/shard_map/all_to_all | solution.py:1004
  351.9 38.4 %self_forward.1 = (bf16[4,2,256,384]{3,2,1,0:T(8,128)(2,1)}, bf16[2,1024,384]{2,1,0:T(8,128)(2,1)}, bf16[2,1024,384]{2,1,0:T(8,128)(2,1)}, f32[2,4,1024]{2,1,0:T(4,128)}) custom-call(s32[2]{0:T(128)} %mul.78.count_ref, bf16[4,2,256,1152]{3,2,1,0:T(8,128)(2,1)} %all-to-all-done.raw_ref, f32[2,1024,384]{2,1,0:T(8,128)} %get-tuple-element.403.cos_ref, ...), custom_call_target="tpu_custom_call" | custom-call | flops 201326592 | bytes 201326 | tf_op jit(solution)/shard_map/self_forward/pallas_call | solution.py:150
  407.0 41.0 %all-gather.25.cloned.1.call-done = bf16[704,768]{1,0:T(8,128)(2,1)} async-done(((bf16[176,768]{1,0:T(8,128)(2,1)}), bf16[704,768]{1,0:T(8,128)(2,1)}) %all-gather.25.cloned.1.call-update) | async-done | bytes 1081360 | tf_op jit(solution)/shard_map/all_gather | solution.py:990
  467.9 22.5 %collective-permute-done.32.refs_2_ = bf16[4,176,768]{2,1,0:T(8,128)(2,1)} collective-permute-done((bf16[4,176,768]{2,1,0:T(8,128)(2,1)}, bf16[4,176,768]{2,1,0:T(8,128)(2,1)}, u32[]{:S(2)}, u32[]{:S(2)}) %collective-permute-start.32) | collective-permute-done | bytes 1081376 | tf_op jit(solution)/shard_map/ppermute | solution.py:826
  495.8 17.8 %collective-permute-done.33.refs_3_ = bf16[4,176,768]{2,1,0:T(8,128)(2,1)} collective-permute-done((bf16[4,176,768]{2,1,0:T(8,128)(2,1)}, bf16[4,176,768]{2,1,0:T(8,128)(2,1)}, u32[]{:S(2)}, u32[]{:S(2)}) %collective-permute-start.33) | collective-permute-done | bytes 1081376 | tf_op jit(solution)/shard_map/ppermute | solution.py:826
  541.8 12.5 collective-permute-done.37.refs_3_
  631.3 19.1 %cross_forward.1 = bf16[4,2,256,384]{3,2,1,0:T(8,128)(2,1)} custom-call(s32[2,2]{1,0:T(2,128)} %bitcast.212, bf16[4,2,256,384]{3,2,1,0:T(8,128)(2,1)} %bitcast.167, bf16[4,4,2,96,768]{4,3,2,1,0:T(8,128)(2,1)} %bitcast.158), custom_call_target="tpu_custom_call" | custom-call | flops 75497472 | bytes 75497 | tf_op jit(solution)/shard_map/cross_forward/pallas_call | solution.py:732
  661.0 28.8 %mlp_forward.2 = (f32[4,512,768]{2,1,0:T(8,128)}, bf16[4,512,768]{2,1,0:T(8,128)(2,1)}, f32[2,512,704]{2,1,0:T(8,128)}, bf16[4,704,768]{2,1,0:T(8,128)(2,1)}, bf16[4,704,768]{2,1,0:T(8,128)(2,1)}) custom-call(bf16[2,512,704]{2,1,0:T(8,128)(2,1)} %get-tuple-element.242.x_ref, bf16[2,512,704]{2,1,0:T(8,128)(2,1)} %fusion.66.g_ref, ...), custom_call_target="tpu_custom_call" | custom-call | flops 830472192 | bytes 830472 | tf_op jit(solution)/shard_map/mlp_forward/pallas_call | solution.py:603
  689.8 28.4 %mlp_forward.3 = (f32[4,512,768]{2,1,0:T(8,128)}, bf16[4,512,768]{2,1,0:T(8,128)(2,1)}, bf16[2,512,704]{2,1,0:T(8,128)(2,1)}, bf16[4,704,768]{2,1,0:T(8,128)(2,1)}, bf16[4,704,768]{2,1,0:T(8,128)(2,1)}) custom-call(bf16[2,512,704]{2,1,0:T(8,128)(2,1)} %get-tuple-element.242.x_ref, bf16[2,512,704]{2,1,0:T(8,128)(2,1)} %fusion.66.g_ref, ...), custom_call_target="tpu_custom_call" | custom-call | flops 830472192 | bytes 830472 | tf_op jit(solution)/shard_map/mlp_forward/pallas_call | solution.py:603
  718.7 29.1 %mlp_backward.2 = (bf16[4,704,768]{2,1,0:T(8,128)(2,1)}, bf16[4,704,768]{2,1,0:T(8,128)(2,1)}, f32[2,512,704]{2,1,0:T(8,128)}) custom-call(bf16[2,512,704]{2,1,0:T(8,128)(2,1)} %fusion.66.g_ref, bf16[2,512,704]{2,1,0:T(8,128)(2,1)} %get-tuple-element.242.x_ref, f32[4,512,768]{2,1,0:T(8,128)} %get-tuple-element.266.hid_ref, ...), custom_call_target="tpu_custom_call" | custom-call | flops 830472192 | bytes 830472 | tf_op jit(solution)/shard_map/mlp_backward/pallas_call | solution.py:675
  762.7 34.7 %mlp_backward.3 = (bf16[4,704,768]{2,1,0:T(8,128)(2,1)}, bf16[4,704,768]{2,1,0:T(8,128)(2,1)}, f32[2,512,704]{2,1,0:T(8,128)}, bf16[2,512,704]{2,1,0:T(8,128)(2,1)}, f32[2,1,704]{2,1,0:T(1,128)}) custom-call(bf16[2,512,704]{2,1,0:T(8,128)(2,1)} %fusion.66.g_ref, bf16[2,512,704]{2,1,0:T(8,128)(2,1)} %get-tuple-element.242.x_ref, ...), custom_call_target="tpu_custom_call" | custom-call | flops 830472192 | bytes 830472 | tf_op jit(solution)/shard_map/mlp_backward/pallas_call | solution.py:675
  825.3 22.6 %cross_backward.1 = (bf16[4,2,256,384]{3,2,1,0:T(8,128)(2,1)}, bf16[4,4,2,96,768]{4,3,2,1,0:T(8,128)(2,1)}) custom-call(s32[2,2]{1,0:T(2,128)} %bitcast.213, bf16[4,2,256,384]{3,2,1,0:T(8,128)(2,1)} %bitcast.168, bf16[4,4,2,96,768]{4,3,2,1,0:T(8,128)(2,1)} %bitcast.159, bf16[4,2,256,384]{3,2,1,0:T(8,128)(2,1)} %bitcast.171), custom_call_target="tpu_custom_call" | custom-call | flops 188743680 | bytes 188743 | tf_op jit(solution)/shard_map/cross_backward/pallas_call | solution.py:781
  862.2 13.0 to_features.9
  914.6 15.4 %terms_of.7 = (bf16[4,704,1152]{2,1,0:T(8,128)(2,1)}, bf16[4,704,1152]{2,1,0:T(8,128)(2,1)}) custom-call(bf16[2,512,704]{2,1,0:T(8,128)(2,1)} %get-tuple-element.299.x_ref.refs_0_, bf16[2,512,704]{2,1,0:T(8,128)(2,1)} %get-tuple-element.304.x_ref.refs_1_, bf16[2,512,704]{2,1,0:T(8,128)(2,1)} %get-tuple-element.278.x_ref.refs_2_, ...), custom_call_target="tpu_custom_call" | custom-call | flops 415236096 | bytes 415236 | tf_op jit(solution)/shard_map/terms_of/pallas_call | solution.py:445
  954.0 56.5 %self_backward.1 = (bf16[4,2,256,1152]{3,2,1,0:T(8,128)(2,1)}, f32[2,1,384]{2,1,0:T(1,128)}, f32[2,1,384]{2,1,0:T(1,128)}) custom-call(s32[2]{0:T(128)} %mul.78.count_ref, bf16[4,2,256,1152]{3,2,1,0:T(8,128)(2,1)} %all-to-all-done.raw_ref, f32[2,1024,384]{2,1,0:T(8,128)} %get-tuple-element.403.cos_ref, f32[2,1024,384]{2,1,0:T(8,128)} %get-tuple-element.402.sin_ref, ...), custom_call_target="tpu_custom_call" | custom-call | flops 503316480 | bytes 503316 | tf_op jit(solution)/shard_map/self_backward/pallas_call | solution.py:260
  1049.1 27.2 %collective-permute-done.59.refs_2_ = bf16[4,256,768]{2,1,0:T(8,128)(2,1)S(1)} collective-permute-done((bf16[4,256,768]{2,1,0:T(8,128)(2,1)}, bf16[4,256,768]{2,1,0:T(8,128)(2,1)S(1)}, u32[]{:S(2)}, u32[]{:S(2)}) %collective-permute-start.59) | collective-permute-done | bytes 1572896 | tf_op jit(solution)/shard_map/ppermute | solution.py:826
  1076.2 29.9 %collective-permute-done.57.refs_2_ = bf16[4,352,1152]{2,1,0:T(8,128)(2,1)} collective-permute-done((bf16[4,352,1152]{2,1,0:T(8,128)(2,1)}, bf16[4,352,1152]{2,1,0:T(8,128)(2,1)}, u32[]{:S(2)}, u32[]{:S(2)}) %collective-permute-start.57) | collective-permute-done | bytes 3244064 | tf_op jit(solution)/shard_map/ppermute | solution.py:826
  1106.1 12.7 all-to-all-done.3
  1160.1 20.5 %to_features.11 = (bf16[2,512,704]{2,1,0:T(8,128)(2,1)}, f32[2,2,704]{2,1,0:T(2,128)}, f32[2,1,704]{2,1,0:T(1,128)}, f32[2,1,704]{2,1,0:T(1,128)}) custom-call(bf16[4,512,1152]{2,1,0:T(8,128)(2,1)} %bitcast.59.refs_0_.refs_1_, bf16[4,704,640]{2,1,0:T(8,128)(2,1)} %join_rows.11.refs_0_.refs_1_, bf16[4,704,640]{2,1,0:T(8,128)(2,1)} %collective-permute-done.19.refs_1_.refs_2_, ...), custom_call_target="tpu_custom_call" | custom-call | flops 415236096 | bytes 415236 | tf_op jit(solution)/shard_map/to_features/pallas_call | solution.py:401
  1235.4 15.9 %collective-permute-done.67.refs_5_.refs_6_ = bf16[4,352,384]{2,1,0:T(8,128)(2,1)S(1)} collective-permute-done((bf16[4,352,384]{2,1,0:T(8,128)(2,1)S(1)}, bf16[4,352,384]{2,1,0:T(8,128)(2,1)S(1)}, u32[]{:S(2)}, u32[]{:S(2)}) %collective-permute-start.67) | collective-permute-done | bytes 1081376 | tf_op jit(solution)/shard_map/ppermute | solution.py:826
  1251.3 14.4 %collective-permute-done.66.refs_2_ = bf16[4,352,768]{2,1,0:T(8,128)(2,1)} collective-permute-done((bf16[4,352,768]{2,1,0:T(8,128)(2,1)}, bf16[4,352,768]{2,1,0:T(8,128)(2,1)}, u32[]{:S(2)}, u32[]{:S(2)}) %collective-permute-start.66) | collective-permute-done | bytes 2162720 | tf_op jit(solution)/shard_map/ppermute | solution.py:826
  1276.8 14.3 %collective-permute-done.68.refs_2_ = bf16[4,352,384]{2,1,0:T(8,128)(2,1)S(1)} collective-permute-done((bf16[4,352,384]{2,1,0:T(8,128)(2,1)}, bf16[4,352,384]{2,1,0:T(8,128)(2,1)S(1)}, u32[]{:S(2)}, u32[]{:S(2)}) %collective-permute-start.68) | collective-permute-done | bytes 1081376 | tf_op jit(solution)/shard_map/ppermute | solution.py:826
  1371.2 12.2 to_inputs.1
  (577 shorter events, 636.8 us)
Async XLA Ops:
  9.1 91.1 %all-gather.19.cloned.1.call-start = ((), (), s32[]{:S(2)}) async-start(), calls=%async_computation.20 | async-start | bytes 2027520 | tf_op jit(solution)/shard_map/all_gather | solution.py:990
  41.4 141.5 %all-gather.17.cloned.1.call-start = ((), (), s32[]{:S(2)}) async-start(), calls=%async_computation.19 | async-start | bytes 2703360 | tf_op jit(solution)/shard_map/all_gather | solution.py:990
  90.1 125.7 %all-gather.21.cloned.1.call-start = ((), (), s32[]{:S(2)}) async-start(), calls=%async_computation.21 | async-start | bytes 2703360 | tf_op jit(solution)/shard_map/all_gather | solution.py:990
  215.8 136.1 %all-to-all-start = ((bf16[4,2,256,1152]{3,2,1,0:T(8,128)(2,1)}), bf16[4,2,256,1152]{3,2,1,0:T(8,128)(2,1)}, u32[]{:S(2)}, u32[]{:S(2)}) async-start(bf16[4,2,256,1152]{3,2,1,0:T(8,128)(2,1)} %bitcast.162), calls=%async_computation | async-start | bytes 9437184 | tf_op jit(solution)/shard_map/all_to_all | solution.py:1004
  221.2 169.2 %all-gather.23.cloned.1.call-start = ((), (), s32[]{:S(2)}) async-start(), calls=%async_computation.22 | async-start | bytes 2027520 | tf_op jit(solution)/shard_map/all_gather | solution.py:990
  271.6 118.7 %collective-permute-start.25 = (bf16[4,176,1536]{2,1,0:T(8,128)(2,1)}, bf16[4,176,1536]{2,1,0:T(8,128)(2,1)}, u32[]{:S(2)}, u32[]{:S(2)}) collective-permute-start(bf16[4,176,1536]{2,1,0:T(8,128)(2,1)} %bitcast.176), channel_id=1, source_target_pairs={{0,16},{4,20},{8,24},{12,28},{16,0},{20,4},{24,8},{28,12},{1,17},{... | collective-permute-start | bytes 6488072 | tf_op jit(solution)/shard_map/ppermute | solution.py:826
  273.1 117.2 %collective-permute-start.26 = (bf16[4,176,1536]{2,1,0:T(8,128)(2,1)}, bf16[4,176,1536]{2,1,0:T(8,128)(2,1)}, u32[]{:S(2)}, u32[]{:S(2)}) collective-permute-start(bf16[4,176,1536]{2,1,0:T(8,128)(2,1)} %collective-permute-done.24.refs_1_), channel_id=1, source_target_pairs={{0,16},{4,20},{8,24},{12,28},{16,0},{20,4},{24,8},{28,12},{1,17},{... | collective-permute-start | bytes 6488072 | tf_op jit(solution)/shard_map/ppermute | solution.py:826
  273.7 116.6 %collective-permute-start.28 = (bf16[4,176,1536]{2,1,0:T(8,128)(2,1)}, bf16[4,176,1536]{2,1,0:T(8,128)(2,1)}, u32[]{:S(2)}, u32[]{:S(2)}) collective-permute-start(bf16[4,176,1536]{2,1,0:T(8,128)(2,1)} %bitcast.179), channel_id=1, source_target_pairs={{0,8},{4,12},{8,0},{12,4},{16,24},{20,28},{24,16},{28,20},{1,9},{5... | collective-permute-start | bytes 6488072 | tf_op jit(solution)/shard_map/ppermute | solution.py:826
  274.2 116.1 %collective-permute-start.29 = (bf16[4,176,1536]{2,1,0:T(8,128)(2,1)}, bf16[4,176,1536]{2,1,0:T(8,128)(2,1)}, u32[]{:S(2)}, u32[]{:S(2)}) collective-permute-start(bf16[4,176,1536]{2,1,0:T(8,128)(2,1)} %collective-permute-done.27.refs_2_), channel_id=1, source_target_pairs={{0,8},{4,12},{8,0},{12,4},{16,24},{20,28},{24,16},{28,20},{1,9},{5... | collective-permute-start | bytes 6488072 | tf_op jit(solution)/shard_map/ppermute | solution.py:826
  390.3 57.7 %all-to-all-start.1 = ((bf16[4,2,256,384]{3,2,1,0:T(8,128)(2,1)}), bf16[4,2,256,384]{3,2,1,0:T(8,128)(2,1)S(1)}, u32[]{:S(2)}, u32[]{:S(2)}) async-start(bf16[4,2,256,384]{3,2,1,0:T(8,128)(2,1)} %get-tuple-element.228), calls=%async_computation.1 | async-start | bytes 3145728 | tf_op jit(solution)/shard_map/all_to_all | solution.py:1004
  394.9 207.2 %all-gather.27.cloned.1.call-start = ((), (), s32[]{:S(2)}) async-start(), calls=%async_computation.24 | async-start | bytes 1966080 | tf_op jit(solution)/shard_map/all_gather | solution.py:990
  455.8 205.2 %collective-permute-start.42 = (bf16[4,704,1536]{2,1,0:T(8,128)(2,1)}, bf16[4,704,1536]{2,1,0:T(8,128)(2,1)}, u32[]{:S(2)}, u32[]{:S(2)}) collective-permute-start(bf16[4,704,1536]{2,1,0:T(8,128)(2,1)} %join_rows.16.n1_ref), channel_id=1, source_target_pairs={{0,4},{4,0},{8,12},{12,8},{16,20},{20,16},{24,28},{28,24},{1,5},{5... | collective-permute-start | bytes 25952264 | tf_op jit(solution)/shard_map/ppermute | solution.py:826
  462.9 198.0 %collective-permute-start.43 = (bf16[4,704,1536]{2,1,0:T(8,128)(2,1)}, bf16[4,704,1536]{2,1,0:T(8,128)(2,1)}, u32[]{:S(2)}, u32[]{:S(2)}) collective-permute-start(bf16[4,704,1536]{2,1,0:T(8,128)(2,1)} %join_rows.17.n2_ref), channel_id=1, source_target_pairs={{0,4},{4,0},{8,12},{12,8},{16,20},{20,16},{24,28},{28,24},{1,5},{5... | collective-permute-start | bytes 25952264 | tf_op jit(solution)/shard_map/ppermute | solution.py:826
  466.6 62.9 %collective-permute-start.36 = (bf16[4,128,768]{2,1,0:T(8,128)(2,1)S(1)}, bf16[4,128,768]{2,1,0:T(8,128)(2,1)}, u32[]{:S(2)}, u32[]{:S(2)}) collective-permute-start(bf16[4,128,768]{2,1,0:T(8,128)(2,1)S(1)} %slice.338.refs_0_), channel_id=1, source_target_pairs={{0,16},{4,20},{8,24},{12,28},{16,0},{20,4},{24,8},{28,12},{1,17},{... | collective-permute-start | bytes 2359304 | tf_op jit(solution)/shard_map/ppermute | solution.py:826
  518.4 95.5 %collective-permute-start.34 = (bf16[4,704,768]{2,1,0:T(8,128)(2,1)}, bf16[4,704,768]{2,1,0:T(8,128)(2,1)}, u32[]{:S(2)}, u32[]{:S(2)}) collective-permute-start(bf16[4,704,768]{2,1,0:T(8,128)(2,1)} %join_rows.13.refs_1_.refs_0_), channel_id=1, source_target_pairs={{0,4},{4,0},{8,12},{12,8},{16,20},{20,16},{24,28},{28,24},{1,5},{5... | collective-permute-start | bytes 12976136 | tf_op jit(solution)/shard_map/ppermute | solution.py:826
  566.8 443.7 %reduce-scatter.8.cloned.1.call-start = ((), (), s32[]{:S(2)}) async-start(), calls=%async_computation.11 | async-start | bytes 2703360 | tf_op jit(solution)/shard_map/reduce_scatter | solution.py:1150
  583.5 66.8 %collective-permute-start.41 = (bf16[4,704,384]{2,1,0:T(8,128)(2,1)}, bf16[4,704,384]{2,1,0:T(8,128)(2,1)}, u32[]{:S(2)}, u32[]{:S(2)}) collective-permute-start(bf16[4,704,384]{2,1,0:T(8,128)(2,1)} %join_rows.15.refs_1_.refs_0_), channel_id=1, source_target_pairs={{0,4},{4,0},{8,12},{12,8},{16,20},{20,16},{24,28},{28,24},{1,5},{5... | collective-permute-start | bytes 6488072 | tf_op jit(solution)/shard_map/ppermute | solution.py:826
  689.7 58.0 %collective-permute-start.44 = (bf16[4,704,768]{2,1,0:T(8,128)(2,1)}, bf16[4,704,768]{2,1,0:T(8,128)(2,1)}, u32[]{:S(2)}, u32[]{:S(2)}) collective-permute-start(bf16[4,704,768]{2,1,0:T(8,128)(2,1)} %get-tuple-element.269), channel_id=1, source_target_pairs={{0,4},{4,0},{8,12},{12,8},{16,20},{20,16},{24,28},{28,24},{1,5},{5... | collective-permute-start | bytes 12976136 | tf_op jit(solution)/shard_map/ppermute | solution.py:826
  762.7 112.5 %collective-permute-start.50 = (bf16[4,704,768]{2,1,0:T(8,128)(2,1)}, bf16[4,704,768]{2,1,0:T(8,128)(2,1)}, u32[]{:S(2)}, u32[]{:S(2)}) collective-permute-start(bf16[4,704,768]{2,1,0:T(8,128)(2,1)} %get-tuple-element.290), channel_id=1, source_target_pairs={{0,4},{4,0},{8,12},{12,8},{16,20},{20,16},{24,28},{28,24},{1,5},{5... | collective-permute-start | bytes 12976136 | tf_op jit(solution)/shard_map/ppermute | solution.py:826
  797.4 77.8 %collective-permute-start.51 = (bf16[4,704,768]{2,1,0:T(8,128)(2,1)}, bf16[4,704,768]{2,1,0:T(8,128)(2,1)}, u32[]{:S(2)}, u32[]{:S(2)}) collective-permute-start(bf16[4,704,768]{2,1,0:T(8,128)(2,1)} %get-tuple-element.291), channel_id=1, source_target_pairs={{0,4},{4,0},{8,12},{12,8},{16,20},{20,16},{24,28},{28,24},{1,5},{5... | collective-permute-start | bytes 12976136 | tf_op jit(solution)/shard_map/ppermute | solution.py:826
  893.9 116.7 %reduce-scatter.10.cloned.1.call-start = ((), (), s32[]{:S(2)}) async-start(), calls=%async_computation.12 | async-start | bytes 1966080 | tf_op jit(solution)/shard_map/reduce_scatter | solution.py:1150
  938.0 79.1 %collective-permute-start.56 = (bf16[4,704,1152]{2,1,0:T(8,128)(2,1)}, bf16[4,704,1152]{2,1,0:T(8,128)(2,1)}, u32[]{:S(2)}, u32[]{:S(2)}) collective-permute-start(bf16[4,704,1152]{2,1,0:T(8,128)(2,1)} %get-tuple-element.326), channel_id=1, source_target_pairs={{0,4},{4,0},{8,12},{12,8},{16,20},{20,16},{24,28},{28,24},{1,5},{5... | collective-permute-start | bytes 19464200 | tf_op jit(solution)/shard_map/ppermute | solution.py:826
  952.0 58.6 %collective-permute-start.54 = (bf16[4,176,768]{2,1,0:T(8,128)(2,1)}, bf16[4,176,768]{2,1,0:T(8,128)(2,1)S(1)}, u32[]{:S(2)}, u32[]{:S(2)}) collective-permute-start(bf16[4,176,768]{2,1,0:T(8,128)(2,1)} %get-tuple-element.322), channel_id=1, source_target_pairs={{0,8},{4,12},{8,0},{12,4},{16,24},{20,28},{24,16},{28,20},{1,9},{5... | collective-permute-start | bytes 3244040 | tf_op jit(solution)/shard_map/ppermute | solution.py:826
  953.4 57.2 %collective-permute-start.55 = (bf16[4,176,768]{2,1,0:T(8,128)(2,1)}, bf16[4,176,768]{2,1,0:T(8,128)(2,1)S(1)}, u32[]{:S(2)}, u32[]{:S(2)}) collective-permute-start(bf16[4,176,768]{2,1,0:T(8,128)(2,1)} %get-tuple-element.323), channel_id=1, source_target_pairs={{0,16},{4,20},{8,24},{12,28},{16,0},{20,4},{24,8},{28,12},{1,17},{... | collective-permute-start | bytes 3244040 | tf_op jit(solution)/shard_map/ppermute | solution.py:826
  1011.9 106.9 %all-to-all-start.3 = ((bf16[4,2,256,1152]{3,2,1,0:T(8,128)(2,1)}), bf16[4,2,256,1152]{3,2,1,0:T(8,128)(2,1)}, u32[]{:S(2)}, u32[]{:S(2)}) async-start(bf16[4,2,256,1152]{3,2,1,0:T(8,128)(2,1)} %get-tuple-element.324), calls=%async_computation.5 | async-start | bytes 9437184 | tf_op jit(solution)/shard_map/all_to_all | solution.py:1004
  1016.9 366.4 %reduce-scatter.20.cloned.1.call-start = ((), (), s32[]{:S(2)}) async-start(), calls=%async_computation.17 | async-start | bytes 2703360 | tf_op jit(solution)/shard_map/reduce_scatter | solution.py:1150
  1023.8 82.3 %collective-permute-start.57 = (bf16[4,352,1152]{2,1,0:T(8,128)(2,1)}, bf16[4,352,1152]{2,1,0:T(8,128)(2,1)}, u32[]{:S(2)}, u32[]{:S(2)}) collective-permute-start(bf16[4,352,1152]{2,1,0:T(8,128)(2,1)} %sum_rows.23), channel_id=1, source_target_pairs={{0,16},{4,20},{8,24},{12,28},{16,0},{20,4},{24,8},{28,12},{1,17},{... | collective-permute-start | bytes 9732104 | tf_op jit(solution)/shard_map/ppermute | solution.py:826
  1130.4 260.7 %reduce-scatter.18.cloned.1.call-start = ((), (), s32[]{:S(2)}) async-start(), calls=%async_computation.16 | async-start | bytes 983040 | tf_op jit(solution)/shard_map/reduce_scatter | solution.py:1150
  1188.8 204.2 %reduce-scatter.16.cloned.1.call-start = ((), (), s32[]{:S(2)}) async-start(), calls=%async_computation.15 | async-start | bytes 2027520 | tf_op jit(solution)/shard_map/reduce_scatter | solution.py:1150
  1209.5 56.1 %collective-permute-start.66 = (bf16[4,352,768]{2,1,0:T(8,128)(2,1)}, bf16[4,352,768]{2,1,0:T(8,128)(2,1)}, u32[]{:S(2)}, u32[]{:S(2)}) collective-permute-start(bf16[4,352,768]{2,1,0:T(8,128)(2,1)} %get-tuple-element.351), channel_id=1, source_target_pairs={{0,16},{4,20},{8,24},{12,28},{16,0},{20,4},{24,8},{28,12},{1,17},{... | collective-permute-start | bytes 6488072 | tf_op jit(solution)/shard_map/ppermute | solution.py:826
  1225.6 171.8 %reduce-scatter.12.cloned.1.call-start = ((), (), s32[]{:S(2)}) async-start(), calls=%async_computation.13 | async-start | bytes 1351680 | tf_op jit(solution)/shard_map/reduce_scatter | solution.py:1150
  1321.0 82.7 %reduce-scatter.14.cloned.1.call-start = ((), (), s32[]{:S(2)}) async-start(), calls=%async_computation.14 | async-start | bytes 2027520 | tf_op jit(solution)/shard_map/reduce_scatter | solution.py:1150
  (143 other events, 3673.5 us)
Sparse Core Ops, SparseCore 0:
  10.2 31.1 all-gather.14
  43.0 37.7 all-gather.18
  90.2 46.1 all-gather.16
  170.3 45.4 all-gather.20
  271.7 69.3 all-gather.22
  396.6 51.3 all-gather.24
  566.9 35.1 all-gather.26
  862.3 53.4 reduce-scatter.7
  938.1 34.2 reduce-scatter.9
  1130.5 51.6 reduce-scatter.19
  1188.9 29.6 reduce-scatter.17
  1225.7 34.6 reduce-scatter.15
  1321.1 27.3 reduce-scatter.11
  1369.0 34.6 reduce-scatter.13

commit v7 on v6

--- a/solution.py
+++ b/solution.py
@@ -508,35 +508,38 @@
                 value = value + jnp.stack([split[:, block] for block in blocks], 1).astype(F32)
             results.append(value.astype(BF).reshape(parts, -1, value.shape[3]))
         return results
-    arrays = [term[0] for terms in jobs for term in terms]
+    spots = [
+        (array, blocks[index])
+        for terms in jobs
+        for index in range(len(terms[0][1]))
+        for array, blocks in terms
+    ]
 
     def kernel(*refs):
         at = 0
         for spot, terms in enumerate(jobs):
-            out_ref = refs[len(arrays) + spot]
+            out_ref = refs[len(spots) + spot]
             for index in range(len(terms[0][1])):
-                value = None
-                for offset, (_, blocks) in enumerate(terms):
-                    start = blocks[index] * rows
-                    term = refs[at + offset][0, start : start + rows].astype(F32)
-                    value = term if value is None else value + term
+                value = refs[at][0].astype(F32)
+                for offset in range(1, len(terms)):
+                    value = value + refs[at + offset][0].astype(F32)
                 out_ref[0, index * rows : (index + 1) * rows] = value.astype(BF)
-            at += len(terms)
-
-    def spec(size, lanes):
-        return pl.BlockSpec((1, size, lanes), lambda p: (p, 0, 0))
+                at += len(terms)
+
+    def spec(block, lanes):
+        return pl.BlockSpec((1, rows, lanes), lambda p: (p, block, 0))
 
     shapes = [(len(terms[0][1]) * rows, terms[0][0].shape[2]) for terms in jobs]
     return pl.pallas_call(
         kernel,
         name=name,
         grid=(parts,),
-        in_specs=[spec(*array.shape[1:]) for array in arrays],
-        out_specs=[spec(*shape) for shape in shapes],
+        in_specs=[spec(block, array.shape[2]) for array, block in spots],
+        out_specs=[pl.BlockSpec((1, *shape), lambda p: (p, 0, 0)) for shape in shapes],
         out_shape=[jax.ShapeDtypeStruct((parts, *shape), BF) for shape in shapes],
         compiler_params=params(),
         cost_estimate=cost(sum(parts * size * lanes for size, lanes in shapes)),
-    )(*arrays)
+    )(*[array for array, _ in spots])
 
 
 def side_by_side(left, right, kept, lanes):
@@ -1005,7 +1008,8 @@
 
     skip_z = spread(jnp.pad(w_skip.T, ((0, 0), (0, skip_lanes - kept))))
     steps = cube.spread(timestep[:, 0])
-    skip_z, steps = tie(skip_z, steps)
+    joined = side_by_side(tokens.reshape(rows, width), skip_tokens.reshape(rows, width), kept, skip_lanes)
+    skip_z, steps, joined = tie(skip_z, steps, joined)
     skip_m = fetch(skip_z, skip_cut)
     qkv_z = spread(pad_heads(w_qkv.reshape(strip, -1), local), skip_z)
     advance(skip_m)
@@ -1060,7 +1064,6 @@
     wide_shape = jax.ShapeDtypeStruct((2, rows, middle), F32)
     low_shape = jax.ShapeDtypeStruct((2, rows, middle), BF)
     gain_shape = jax.ShapeDtypeStruct((2, 1, middle), F32)
-    joined = side_by_side(tokens.reshape(rows, width), skip_tokens.reshape(rows, width), kept, skip_lanes)
 
     def first_norms(sums, extra, out):
         g0_ref, g1_ref, shift_ref = extra
@@ -1110,30 +1113,38 @@
     text_z = jnp.pad(pad_heads(w_text_kv.reshape(text_rows, -1), local), ((0, max(0, strip - text_rows)), (0, 0)))
     while fc_m[0].todo:
         advance(fc_m)
-    attended, turned_q, turned_k, norms = self_forward(raw, counts, cosine, sine, gain_q, gain_k)
-    attended = bind(attended, *fc_m)
-    attended, cross_z = tie(attended, cross_z)
     text_z = spread(text_z, cross_z)
     cross_m = fetch(cross_z, 2 * lanes)
     advance(cross_m)
+    raw, d_mlp = tie(raw, d_mlp)
+    attended, turned_q, turned_k, norms = self_forward(raw, counts, cosine, sine, gain_q, gain_k)
+    attended = bind(attended, *fc_m, *cross_m)
+    attended, text_z = tie(attended, text_z)
+    text_m = Gather(cube, text_z[:, :text_rows], 1)
+    text_m.move()
     attended = exchange(attended).reshape(parts, rows, lanes)
-    attended, text_z = tie(attended, text_z)
-    attended = bind(attended, *cross_m)
-    text_all = spread(text_own, text_z).reshape(-1, features)
-    text_all = jnp.stack([text_all[:, : features // 2], text_all[:, features // 2 :]])
-    text_m = Gather(cube, text_z[:, :text_rows], 1)
-    hold(fc_m, attended)
+    while cross_m[0].todo:
+        advance(cross_m)
+    text_all = spread(text_own, text_z)
+    hold(cross_m, attended)
     join(cross_m)
     first_w, out2_w = [mover.weight() for mover in cross_m]
     out1_w, query2_w = (Lanes(first_w.near, first_w.far, lanes, index) for index in range(2))
+    attended, text_all = tie(attended, text_all)
+    stream1, pre_cross = to_features(
+        attended, [out1_w], [stream, g_cross], [wide_shape, low_shape], next_norm
+    )
+    pre_cross = bind(pre_cross, text_m, *fc_m)
+    while text_m.todo:
+        text_m.move()
+    query2 = to_lanes(pre_cross, [query2_w]).reshape(parts, micros, slots, lanes)
+    query2 = bind(query2, text_m)
+    text_all = text_all.reshape(-1, features)
+    text_all = jnp.stack([text_all[:, : features // 2], text_all[:, features // 2 :]])
     text_m.join()
     text_w = text_m.weight()
     join(fc_m)
     fc1_w, fc2_w = [mover.weight() for mover in fc_m]
-    stream1, pre_cross = to_features(
-        attended, [out1_w], [stream, g_cross], [wide_shape, low_shape], next_norm
-    )
-    query2 = to_lanes(pre_cross, [query2_w]).reshape(parts, micros, slots, lanes)
     text_kv = to_lanes(text_all, [text_w]).reshape(parts, parts, micros, text_strip, 2 * lanes)
     crossed = cross_forward(query2, text_kv, lengths, text_slots).reshape(parts, rows, lanes)
     stream2, pre_mlp = to_features(
@@ -1218,9 +1229,17 @@
     pack([text_s])
     send(other_s)
     d_projected = bind(d_projected, *other_s)
+    term_fc1 = settle(total_fc1, d_projected)
+    qkv_s = [
+        Scatter(cube, *terms_of([(pre_attn, d_projected, 2 * lanes, 0)]), 0),
+        Scatter(cube, *terms_of([(pre_attn, d_projected, lanes, 2)]), 1),
+    ]
     pack([cross_s])
     pack([text_s])
     send(other_s)
+    pack(qkv_s)
+    d_projected = bind(d_projected, *qkv_s)
+    send(qkv_s)
 
     def last_norms(sums, extra, out):
         stream_ref, g1_ref, base_ref, g0_ref, add_ref = extra
@@ -1236,11 +1255,6 @@
                 part = sums[side][micro * slots : (micro + 1) * slots]
                 d_shift_ref[side, micro : micro + 1] = jnp.sum(part, 0, keepdims=True)
 
-    qkv_s = [
-        Scatter(cube, *terms_of([(pre_attn, d_projected, 2 * lanes, 0)]), 0),
-        Scatter(cube, *terms_of([(pre_attn, d_projected, lanes, 2)]), 1),
-    ]
-    term_fc1 = settle(total_fc1, qkv_s[0].near)
     shift_shape = jax.ShapeDtypeStruct((2, micros, middle), F32)
     d_base, d_shift, d_gain_attn, d_gain_skip = to_features(
         d_projected,
@@ -1249,19 +1263,16 @@
         [low_shape, shift_shape, gain_shape, gain_shape],
         last_norms,
     )
-    d_base = bind(d_base, *qkv_s, *other_s)
-    pack(qkv_s)
-    d_base = bind(d_base, *qkv_s)
-    send(qkv_s)
+    d_base = bind(d_base, *other_s)
     skip_s = [
         Scatter(cube, *terms_of([(d_base, joined, skip_cut, flip)]), flip) for flip in range(2)
     ]
-    term_cross, term_text = settle(results([cross_s])), settle(results([text_s]))
     pack(skip_s)
     hold(skip_s, *qkv_s)
-    send(skip_s)
     pack(qkv_s)
     send(qkv_s)
+    term_cross, term_text = settle(results([cross_s])), settle(results([text_s]))
+    send(skip_s)
     term_qkv = settle(results(qkv_s))
     term_skip = settle(results(skip_s))
     d_joined = to_inputs(d_base, skip_w, kept)

time: 1420 us -> 1390 us (0.979)
  Pallas kernels: 621 us -> 569 us
  waiting for transfers between devices: 519 us -> 552 us
    all_gather x7, waiting for transfers between devices: 86.3 us -> 129 us  [spread(): return lax.all_gather(shard, 'sp', axis=0, tiled=False)]
    pallas_call x18, Pallas kernels: 127 us -> 85.2 us  [sum_rows(): pl.pallas_call(kernel, name=name, grid=(parts,), in_specs=[spec(block, ar...]
  transfers between devices with their start and end apart: 102 -> 102, of which waited for: 49 -> 46; matrix products, arithmetic and copies ran while one was open for 8% -> 8% of each run, Pallas kernels for 40% -> 37%
where the time goes in v7:
time: 1390 us; the launch traced here: 1380 us
  Pallas kernels  569 us (41%)
  waiting for transfers between devices  552 us (40%)
  starting transfers between devices  125 us (9%)
  other arithmetic  56.1 us (4%)
  local copies, waits for them, and re-layouts  51 us (4%)
  between operations  16 us (1%)
    ppermute x84, waiting for transfers between devices, swap(): return lax.ppermute(value, axis, pairs)  342 us
    all_gather x7, waiting for transfers between devices, spread(): return lax.all_gather(shard, 'sp', axis=0, tiled=False)  129 us
    ppermute x84, starting transfers between devices, swap(): return lax.ppermute(value, axis, pairs)  107 us
    pallas_call x18, Pallas kernels, sum_rows(): pl.pallas_call(kernel, name=name, grid=(parts,), in_specs=[spec(block, ar...  85.2 us
    pallas_call x6, Pallas kernels, to_features(): pl.pallas_call(kernel, name=name, grid=(parts,), in_specs=[pl.BlockSpec((...  78.2 us
    all_to_all x4, waiting for transfers between devices, exchange(): return lax.all_to_all(value, 'sp', split_axis=0, concat_axis=0, tiled=True)  69.2 us
    pallas_call x2, Pallas kernels, mlp_backward(): pl.pallas_call(kernel, name='mlp_backward', grid=(parts, steps), in_specs...  63.5 us
    pallas_call x2, Pallas kernels, mlp_forward(): pl.pallas_call(kernel, name='mlp_forward', grid=(parts, steps), in_specs=...  57.6 us
  transfers between devices with their start and end apart: 102, of which 46 were waited for; matrix products, arithmetic and copies ran while one was open for 8% of the time, Pallas kernels for 37%

profile of v7, /device:TPU:0, one launch (start us, length us, event | category | flops | bytes accessed | tf_op | source)
XLA Modules:
  0.0 1382.5 jit_solution(10929614492730179307)
XLA Ops:
  23.8 17.6 %all-gather.15.cloned.1.call-done = bf16[704,768]{1,0:T(8,128)(2,1)} async-done(((bf16[176,768]{1,0:T(8,128)(2,1)}), bf16[704,768]{1,0:T(8,128)(2,1)}) %all-gather.15.cloned.1.call-update) | async-done | bytes 1081360 | tf_op jit(solution)/shard_map/all_gather | solution.py:993
  62.5 22.0 %collective-permute-done.9 = f32[4,2,176]{2,1,0:T(2,128)S(1)} collective-permute-done((f32[4,2,176]{2,1,0:T(2,128)S(1)}, f32[4,2,176]{2,1,0:T(2,128)S(1)}, u32[]{:S(2)}, u32[]{:S(2)}) %collective-permute-start.9) | collective-permute-done | bytes 5664 | tf_op jit(solution)/shard_map/ppermute | solution.py:829
  107.8 15.2 %collective-permute-done.16.refs_1_ = bf16[4,176,640]{2,1,0:T(8,128)(2,1)} collective-permute-done((bf16[4,176,640]{2,1,0:T(8,128)(2,1)S(1)}, bf16[4,176,640]{2,1,0:T(8,128)(2,1)}, u32[]{:S(2)}, u32[]{:S(2)}) %collective-permute-start.16) | collective-permute-done | bytes 901152 | tf_op jit(solution)/shard_map/ppermute | solution.py:829
  124.3 18.7 %collective-permute-done.21.refs_2_ = bf16[4,176,512]{2,1,0:T(8,128)(2,1)} collective-permute-done((bf16[4,176,512]{2,1,0:T(8,128)(2,1)S(1)}, bf16[4,176,512]{2,1,0:T(8,128)(2,1)}, u32[]{:S(2)}, u32[]{:S(2)}) %collective-permute-start.21) | collective-permute-done | bytes 720928 | tf_op jit(solution)/shard_map/ppermute | solution.py:829
  145.1 14.6 %to_features.6 = (f32[2,512,704]{2,1,0:T(8,128)}, f32[2,512,704]{2,1,0:T(8,128)}, bf16[2,512,704]{2,1,0:T(8,128)(2,1)}) custom-call(bf16[4,512,768]{2,1,0:T(8,128)(2,1)} %side_by_side.1.refs_0_.refs_1_, bf16[4,704,384]{2,1,0:T(8,128)(2,1)} %join_rows.9.refs_1_.refs_0_, bf16[4,704,384]{2,1,0:T(8,128)(2,1)} %collective-permute-done.11.refs_2_.refs_1_, ...), custom_call_target="tpu_custom_call" | custom-call | flops 276824064 | bytes 276824 | tf_op jit(solution)/shard_map/to_features/pallas_call | solution.py:401
  184.0 13.0 to_lanes.5
  197.0 14.3 %all-gather.21.cloned.1.call-done = bf16[704,1536]{1,0:T(8,128)(2,1)} async-done(((bf16[176,1536]{1,0:T(8,128)(2,1)}), bf16[704,1536]{1,0:T(8,128)(2,1)}) %all-gather.21.cloned.1.call-update) | async-done | bytes 2162704 | tf_op jit(solution)/shard_map/all_gather | solution.py:993
  221.8 44.1 %collective-permute-done.24.refs_1_ = bf16[4,176,1536]{2,1,0:T(8,128)(2,1)} collective-permute-done((bf16[4,176,1536]{2,1,0:T(8,128)(2,1)}, bf16[4,176,1536]{2,1,0:T(8,128)(2,1)}, u32[]{:S(2)}, u32[]{:S(2)}) %collective-permute-start.24) | collective-permute-done | bytes 2162720 | tf_op jit(solution)/shard_map/ppermute | solution.py:829
  282.4 54.3 %all-gather.23.cloned.1.call-done = bf16[704,1152]{1,0:T(8,128)(2,1)} async-done(((bf16[176,1152]{1,0:T(8,128)(2,1)}), bf16[704,1152]{1,0:T(8,128)(2,1)}) %all-gather.23.cloned.1.call-update) | async-done | bytes 1622032 | tf_op jit(solution)/shard_map/all_gather | solution.py:993
  349.5 14.3 %negate_select_fusion = (f32[2,1024,384]{2,1,0:T(8,128)}, f32[2,1024,384]{2,1,0:T(8,128)}) fusion(f32[384]{0:T(512)S(1)} %fusion.52, s32[2,1024]{1,0:T(2,128)S(1)} %copy-done.56, s32[2,1024]{1,0:T(2,128)S(1)} %copy-done.57, pred[384]{0:T(512)(128)(4,1)S(1)} %get-tuple-element.478, pred[384]{0:T(512)(128)(4,1)S(1)} %get-tuple-element.479), kind=kLoop, calls=%fused_computation.4 | loop fusion | flops 3932160 | bytes 6310144 | tf_op jit(solution)/shard_map/jit(_where)/select_n | solution.py:41
  363.8 34.8 %self_forward.1 = (bf16[4,2,256,384]{3,2,1,0:T(8,128)(2,1)}, bf16[2,1024,384]{2,1,0:T(8,128)(2,1)}, bf16[2,1024,384]{2,1,0:T(8,128)(2,1)}, f32[2,4,1024]{2,1,0:T(4,128)}) custom-call(s32[2]{0:T(128)} %copy-done.72, bf16[4,2,256,1152]{3,2,1,0:T(8,128)(2,1)} %all-to-all-done.raw_ref, f32[2,1024,384]{2,1,0:T(8,128)} %get-tuple-element.435.cos_ref, ...), custom_call_target="tpu_custom_call" | custom-call | flops 201326592 | bytes 201326 | tf_op jit(solution)/shard_map/self_forward/pallas_call | solution.py:150
  404.5 35.1 %all-to-all-done.1 = bf16[4,2,256,384]{3,2,1,0:T(8,128)(2,1)S(1)} async-done(((bf16[4,2,256,384]{3,2,1,0:T(8,128)(2,1)}), bf16[4,2,256,384]{3,2,1,0:T(8,128)(2,1)S(1)}, u32[]{:S(2)}, u32[]{:S(2)}) %all-to-all-start.1) | async-done | bytes 1572896 | tf_op jit(solution)/shard_map/all_to_all | solution.py:1007
  465.8 43.2 %all-gather.27.cloned.1.call-done = bf16[768,1024]{1,0:T(8,128)(2,1)} async-done(((bf16[192,1024]{1,0:T(8,128)(2,1)}), bf16[768,1024]{1,0:T(8,128)(2,1)}) %all-gather.27.cloned.1.call-update) | async-done | bytes 1572880 | tf_op jit(solution)/shard_map/all_gather | solution.py:993
  554.9 16.1 %collective-permute-done.37.refs_3_ = bf16[4,128,768]{2,1,0:T(8,128)(2,1)} collective-permute-done((bf16[4,128,768]{2,1,0:T(8,128)(2,1)S(1)}, bf16[4,128,768]{2,1,0:T(8,128)(2,1)}, u32[]{:S(2)}, u32[]{:S(2)}) %collective-permute-start.37) | collective-permute-done | bytes 786464 | tf_op jit(solution)/shard_map/ppermute | solution.py:829
  577.5 13.1 collective-permute-done.39.refs_1_
  618.4 19.1 %cross_forward.1 = bf16[4,2,256,384]{3,2,1,0:T(8,128)(2,1)} custom-call(s32[2,2]{1,0:T(2,128)} %bitcast.208, bf16[4,2,256,384]{3,2,1,0:T(8,128)(2,1)} %bitcast.169, bf16[4,4,2,96,768]{4,3,2,1,0:T(8,128)(2,1)} %bitcast.160), custom_call_target="tpu_custom_call" | custom-call | flops 75497472 | bytes 75497 | tf_op jit(solution)/shard_map/cross_forward/pallas_call | solution.py:735
  648.0 28.9 %mlp_forward.2 = (f32[4,512,768]{2,1,0:T(8,128)}, bf16[4,512,768]{2,1,0:T(8,128)(2,1)}, f32[2,512,704]{2,1,0:T(8,128)}, bf16[4,704,768]{2,1,0:T(8,128)(2,1)}, bf16[4,704,768]{2,1,0:T(8,128)(2,1)}) custom-call(bf16[2,512,704]{2,1,0:T(8,128)(2,1)} %get-tuple-element.283.x_ref, bf16[2,512,704]{2,1,0:T(8,128)(2,1)} %fusion.66.g_ref, ...), custom_call_target="tpu_custom_call" | custom-call | flops 830472192 | bytes 830472 | tf_op jit(solution)/shard_map/mlp_forward/pallas_call | solution.py:606
  677.3 28.8 %mlp_forward.3 = (f32[4,512,768]{2,1,0:T(8,128)}, bf16[4,512,768]{2,1,0:T(8,128)(2,1)}, bf16[2,512,704]{2,1,0:T(8,128)(2,1)}, bf16[4,704,768]{2,1,0:T(8,128)(2,1)}, bf16[4,704,768]{2,1,0:T(8,128)(2,1)}) custom-call(bf16[2,512,704]{2,1,0:T(8,128)(2,1)} %get-tuple-element.283.x_ref, bf16[2,512,704]{2,1,0:T(8,128)(2,1)} %fusion.66.g_ref, ...), custom_call_target="tpu_custom_call" | custom-call | flops 830472192 | bytes 830472 | tf_op jit(solution)/shard_map/mlp_forward/pallas_call | solution.py:606
  706.2 29.1 %mlp_backward.2 = (bf16[4,704,768]{2,1,0:T(8,128)(2,1)}, bf16[4,704,768]{2,1,0:T(8,128)(2,1)}, f32[2,512,704]{2,1,0:T(8,128)}) custom-call(bf16[2,512,704]{2,1,0:T(8,128)(2,1)} %fusion.66.g_ref, bf16[2,512,704]{2,1,0:T(8,128)(2,1)} %get-tuple-element.283.x_ref, f32[4,512,768]{2,1,0:T(8,128)} %get-tuple-element.300.hid_ref, ...), custom_call_target="tpu_custom_call" | custom-call | flops 830472192 | bytes 830472 | tf_op jit(solution)/shard_map/mlp_backward/pallas_call | solution.py:678
  747.9 34.5 %mlp_backward.3 = (bf16[4,704,768]{2,1,0:T(8,128)(2,1)}, bf16[4,704,768]{2,1,0:T(8,128)(2,1)}, f32[2,512,704]{2,1,0:T(8,128)}, bf16[2,512,704]{2,1,0:T(8,128)(2,1)}, f32[2,1,704]{2,1,0:T(1,128)}) custom-call(bf16[2,512,704]{2,1,0:T(8,128)(2,1)} %fusion.66.g_ref, bf16[2,512,704]{2,1,0:T(8,128)(2,1)} %get-tuple-element.283.x_ref, ...), custom_call_target="tpu_custom_call" | custom-call | flops 830472192 | bytes 830472 | tf_op jit(solution)/shard_map/mlp_backward/pallas_call | solution.py:678
  807.1 22.6 %cross_backward.1 = (bf16[4,2,256,384]{3,2,1,0:T(8,128)(2,1)}, bf16[4,4,2,96,768]{4,3,2,1,0:T(8,128)(2,1)}) custom-call(s32[2,2]{1,0:T(2,128)} %bitcast.209, bf16[4,2,256,384]{3,2,1,0:T(8,128)(2,1)} %bitcast.170, bf16[4,4,2,96,768]{4,3,2,1,0:T(8,128)(2,1)} %bitcast.161, bf16[4,2,256,384]{3,2,1,0:T(8,128)(2,1)} %bitcast.173), custom_call_target="tpu_custom_call" | custom-call | flops 188743680 | bytes 188743 | tf_op jit(solution)/shard_map/cross_backward/pallas_call | solution.py:784
  840.3 12.6 to_features.9
  890.3 15.3 %terms_of.7 = (bf16[4,704,1152]{2,1,0:T(8,128)(2,1)}, bf16[4,704,1152]{2,1,0:T(8,128)(2,1)}) custom-call(bf16[2,512,704]{2,1,0:T(8,128)(2,1)} %get-tuple-element.333.x_ref.refs_0_, bf16[2,512,704]{2,1,0:T(8,128)(2,1)} %get-tuple-element.338.x_ref.refs_1_, bf16[2,512,704]{2,1,0:T(8,128)(2,1)} %get-tuple-element.312.x_ref.refs_2_, ...), custom_call_target="tpu_custom_call" | custom-call | flops 415236096 | bytes 415236 | tf_op jit(solution)/shard_map/terms_of/pallas_call | solution.py:445
  925.4 51.8 %self_backward.1 = (bf16[4,2,256,1152]{3,2,1,0:T(8,128)(2,1)}, f32[2,1,384]{2,1,0:T(1,128)}, f32[2,1,384]{2,1,0:T(1,128)}) custom-call(s32[2]{0:T(128)} %copy-done.72, bf16[4,2,256,1152]{3,2,1,0:T(8,128)(2,1)} %all-to-all-done.raw_ref, f32[2,1024,384]{2,1,0:T(8,128)} %get-tuple-element.435.cos_ref, f32[2,1024,384]{2,1,0:T(8,128)} %get-tuple-element.434.sin_ref, ...), custom_call_target="tpu_custom_call" | custom-call | flops 503316480 | bytes 503316 | tf_op jit(solution)/shard_map/self_backward/pallas_call | solution.py:260
  1012.5 29.7 %collective-permute-done.59.refs_2_ = bf16[4,256,768]{2,1,0:T(8,128)(2,1)} collective-permute-done((bf16[4,256,768]{2,1,0:T(8,128)(2,1)}, bf16[4,256,768]{2,1,0:T(8,128)(2,1)}, u32[]{:S(2)}, u32[]{:S(2)}) %collective-permute-start.59) | collective-permute-done | bytes 1572896 | tf_op jit(solution)/shard_map/ppermute | solution.py:829
  1042.3 22.4 %collective-permute-done.57.refs_2_ = bf16[4,352,1152]{2,1,0:T(8,128)(2,1)} collective-permute-done((bf16[4,352,1152]{2,1,0:T(8,128)(2,1)}, bf16[4,352,1152]{2,1,0:T(8,128)(2,1)}, u32[]{:S(2)}, u32[]{:S(2)}) %collective-permute-start.57) | collective-permute-done | bytes 3244064 | tf_op jit(solution)/shard_map/ppermute | solution.py:829
  1064.7 23.7 %all-to-all-done.3 = bf16[4,2,256,1152]{3,2,1,0:T(8,128)(2,1)} async-done(((bf16[4,2,256,1152]{3,2,1,0:T(8,128)(2,1)}), bf16[4,2,256,1152]{3,2,1,0:T(8,128)(2,1)}, u32[]{:S(2)}, u32[]{:S(2)}) %all-to-all-start.3) | async-done | bytes 4718624 | tf_op jit(solution)/shard_map/all_to_all | solution.py:1007
  1133.2 20.5 %to_features.11 = (bf16[2,512,704]{2,1,0:T(8,128)(2,1)}, f32[2,2,704]{2,1,0:T(2,128)}, f32[2,1,704]{2,1,0:T(1,128)}, f32[2,1,704]{2,1,0:T(1,128)}) custom-call(bf16[4,512,1152]{2,1,0:T(8,128)(2,1)} %bitcast.61.refs_1_.refs_0_, bf16[4,704,640]{2,1,0:T(8,128)(2,1)} %join_rows.11.refs_0_.refs_1_, bf16[4,704,640]{2,1,0:T(8,128)(2,1)} %collective-permute-done.19.refs_1_.refs_2_, ...), custom_call_target="tpu_custom_call" | custom-call | flops 415236096 | bytes 415236 | tf_op jit(solution)/shard_map/to_features/pallas_call | solution.py:401
  1191.5 16.9 %collective-permute-done.67.refs_5_.refs_6_ = bf16[4,352,384]{2,1,0:T(8,128)(2,1)S(1)} collective-permute-done((bf16[4,352,384]{2,1,0:T(8,128)(2,1)S(1)}, bf16[4,352,384]{2,1,0:T(8,128)(2,1)S(1)}, u32[]{:S(2)}, u32[]{:S(2)}) %collective-permute-start.67) | collective-permute-done | bytes 1081376 | tf_op jit(solution)/shard_map/ppermute | solution.py:829
  1208.4 17.1 %collective-permute-done.66.refs_2_ = bf16[4,352,768]{2,1,0:T(8,128)(2,1)} collective-permute-done((bf16[4,352,768]{2,1,0:T(8,128)(2,1)}, bf16[4,352,768]{2,1,0:T(8,128)(2,1)}, u32[]{:S(2)}, u32[]{:S(2)}) %collective-permute-start.66) | collective-permute-done | bytes 2162720 | tf_op jit(solution)/shard_map/ppermute | solution.py:829
  1235.5 15.4 %collective-permute-done.68.refs_2_ = bf16[4,352,384]{2,1,0:T(8,128)(2,1)S(1)} collective-permute-done((bf16[4,352,384]{2,1,0:T(8,128)(2,1)}, bf16[4,352,384]{2,1,0:T(8,128)(2,1)S(1)}, u32[]{:S(2)}, u32[]{:S(2)}) %collective-permute-start.68) | collective-permute-done | bytes 1081376 | tf_op jit(solution)/shard_map/ppermute | solution.py:829
  1289.1 22.7 %collective-permute-done.73 = f32[4,2,176]{2,1,0:T(2,128)S(1)} collective-permute-done((f32[4,2,176]{2,1,0:T(2,128)S(1)}, f32[4,2,176]{2,1,0:T(2,128)S(1)}, u32[]{:S(2)}, u32[]{:S(2)}) %collective-permute-start.73) | collective-permute-done | bytes 5664 | tf_op jit(solution)/shard_map/ppermute | solution.py:829
  (601 shorter events, 585.2 us)
Async XLA Ops:
  9.1 90.6 %all-gather.19.cloned.1.call-start = ((), (), s32[]{:S(2)}) async-start(), calls=%async_computation.20 | async-start | bytes 2027520 | tf_op jit(solution)/shard_map/all_gather | solution.py:993
  41.4 137.0 %all-gather.17.cloned.1.call-start = ((), (), s32[]{:S(2)}) async-start(), calls=%async_computation.19 | async-start | bytes 2703360 | tf_op jit(solution)/shard_map/all_gather | solution.py:993
  90.1 121.3 %all-gather.21.cloned.1.call-start = ((), (), s32[]{:S(2)}) async-start(), calls=%async_computation.21 | async-start | bytes 2703360 | tf_op jit(solution)/shard_map/all_gather | solution.py:993
  104.5 55.2 %collective-permute-start.17 = (bf16[4,176,640]{2,1,0:T(8,128)(2,1)S(1)}, bf16[4,176,640]{2,1,0:T(8,128)(2,1)}, u32[]{:S(2)}, u32[]{:S(2)}) collective-permute-start(bf16[4,176,640]{2,1,0:T(8,128)(2,1)S(1)} %slice.413.refs_0_), channel_id=1, source_target_pairs={{0,16},{4,20},{8,24},{12,28},{16,0},{20,4},{24,8},{28,12},{1,17},{... | collective-permute-start | bytes 2703368 | tf_op jit(solution)/shard_map/ppermute | solution.py:829
  211.4 152.4 %all-to-all-start = ((bf16[4,2,256,1152]{3,2,1,0:T(8,128)(2,1)}), bf16[4,2,256,1152]{3,2,1,0:T(8,128)(2,1)}, u32[]{:S(2)}, u32[]{:S(2)}) async-start(bf16[4,2,256,1152]{3,2,1,0:T(8,128)(2,1)} %bitcast.164), calls=%async_computation | async-start | bytes 9437184 | tf_op jit(solution)/shard_map/all_to_all | solution.py:1007
  216.7 120.0 %all-gather.23.cloned.1.call-start = ((), (), s32[]{:S(2)}) async-start(), calls=%async_computation.22 | async-start | bytes 2027520 | tf_op jit(solution)/shard_map/all_gather | solution.py:993
  267.1 131.5 %all-gather.25.cloned.1.call-start = ((), (), s32[]{:S(2)}) async-start(), calls=%async_computation.23 | async-start | bytes 1351680 | tf_op jit(solution)/shard_map/all_gather | solution.py:993
  275.7 70.8 %collective-permute-start.25 = (bf16[4,176,1536]{2,1,0:T(8,128)(2,1)}, bf16[4,176,1536]{2,1,0:T(8,128)(2,1)}, u32[]{:S(2)}, u32[]{:S(2)}) collective-permute-start(bf16[4,176,1536]{2,1,0:T(8,128)(2,1)} %bitcast.17.refs_0_), channel_id=1, source_target_pairs={{0,16},{4,20},{8,24},{12,28},{16,0},{20,4},{24,8},{28,12},{1,17},{... | collective-permute-start | bytes 6488072 | tf_op jit(solution)/shard_map/ppermute | solution.py:829
  278.8 119.8 %collective-permute-start.26 = (bf16[4,176,1536]{2,1,0:T(8,128)(2,1)}, bf16[4,176,1536]{2,1,0:T(8,128)(2,1)}, u32[]{:S(2)}, u32[]{:S(2)}) collective-permute-start(bf16[4,176,1536]{2,1,0:T(8,128)(2,1)} %collective-permute-done.24.refs_1_), channel_id=1, source_target_pairs={{0,16},{4,20},{8,24},{12,28},{16,0},{20,4},{24,8},{28,12},{1,17},{... | collective-permute-start | bytes 6488072 | tf_op jit(solution)/shard_map/ppermute | solution.py:829
  279.3 119.3 %collective-permute-start.28 = (bf16[4,176,1536]{2,1,0:T(8,128)(2,1)}, bf16[4,176,1536]{2,1,0:T(8,128)(2,1)}, u32[]{:S(2)}, u32[]{:S(2)}) collective-permute-start(bf16[4,176,1536]{2,1,0:T(8,128)(2,1)} %bitcast.20.refs_0_), channel_id=1, source_target_pairs={{0,8},{4,12},{8,0},{12,4},{16,24},{20,28},{24,16},{28,20},{1,9},{5... | collective-permute-start | bytes 6488072 | tf_op jit(solution)/shard_map/ppermute | solution.py:829
  279.9 118.7 %collective-permute-start.29 = (bf16[4,176,1536]{2,1,0:T(8,128)(2,1)}, bf16[4,176,1536]{2,1,0:T(8,128)(2,1)}, u32[]{:S(2)}, u32[]{:S(2)}) collective-permute-start(bf16[4,176,1536]{2,1,0:T(8,128)(2,1)} %collective-permute-done.27.refs_2_), channel_id=1, source_target_pairs={{0,8},{4,12},{8,0},{12,4},{16,24},{20,28},{24,16},{28,20},{1,9},{5... | collective-permute-start | bytes 6488072 | tf_op jit(solution)/shard_map/ppermute | solution.py:829
  342.3 56.3 %collective-permute-start.30 = (bf16[4,176,768]{2,1,0:T(8,128)(2,1)S(1)}, bf16[4,176,768]{2,1,0:T(8,128)(2,1)}, u32[]{:S(2)}, u32[]{:S(2)}) collective-permute-start(bf16[4,176,768]{2,1,0:T(8,128)(2,1)S(1)} %slice.417.refs_0_), channel_id=1, source_target_pairs={{0,8},{4,12},{8,0},{12,4},{16,24},{20,28},{24,16},{28,20},{1,9},{5... | collective-permute-start | bytes 3244040 | tf_op jit(solution)/shard_map/ppermute | solution.py:829
  402.3 106.6 %all-gather.27.cloned.1.call-start = ((), (), s32[]{:S(2)}) async-start(), calls=%async_computation.24 | async-start | bytes 1966080 | tf_op jit(solution)/shard_map/all_gather | solution.py:993
  454.8 54.2 %collective-permute-start.34 = (bf16[4,704,768]{2,1,0:T(8,128)(2,1)}, bf16[4,704,768]{2,1,0:T(8,128)(2,1)}, u32[]{:S(2)}, u32[]{:S(2)}) collective-permute-start(bf16[4,704,768]{2,1,0:T(8,128)(2,1)} %join_rows.13.refs_1_.refs_0_), channel_id=1, source_target_pairs={{0,4},{4,0},{8,12},{12,8},{16,20},{20,16},{24,28},{28,24},{1,5},{5... | collective-permute-start | bytes 12976136 | tf_op jit(solution)/shard_map/ppermute | solution.py:829
  464.3 512.9 %reduce-scatter.8.cloned.1.call-start = ((), (), s32[]{:S(2)}) async-start(), calls=%async_computation.11 | async-start | bytes 2703360 | tf_op jit(solution)/shard_map/reduce_scatter | solution.py:1161
  464.5 55.2 %collective-permute-start.35 = (bf16[4,128,768]{2,1,0:T(8,128)(2,1)S(1)}, bf16[4,128,768]{2,1,0:T(8,128)(2,1)S(1)}, u32[]{:S(2)}, u32[]{:S(2)}) collective-permute-start(bf16[4,128,768]{2,1,0:T(8,128)(2,1)S(1)} %slice.338.refs_0_), channel_id=1, source_target_pairs={{0,16},{4,20},{8,24},{12,28},{16,0},{20,4},{24,8},{28,12},{1,17},{... | collective-permute-start | bytes 2359304 | tf_op jit(solution)/shard_map/ppermute | solution.py:829
  527.0 121.0 %collective-permute-start.42 = (bf16[4,704,1536]{2,1,0:T(8,128)(2,1)}, bf16[4,704,1536]{2,1,0:T(8,128)(2,1)}, u32[]{:S(2)}, u32[]{:S(2)}) collective-permute-start(bf16[4,704,1536]{2,1,0:T(8,128)(2,1)} %join_rows.16.n1_ref), channel_id=1, source_target_pairs={{0,4},{4,0},{8,12},{12,8},{16,20},{20,16},{24,28},{28,24},{1,5},{5... | collective-permute-start | bytes 25952264 | tf_op jit(solution)/shard_map/ppermute | solution.py:829
  534.0 113.9 %collective-permute-start.43 = (bf16[4,704,1536]{2,1,0:T(8,128)(2,1)}, bf16[4,704,1536]{2,1,0:T(8,128)(2,1)}, u32[]{:S(2)}, u32[]{:S(2)}) collective-permute-start(bf16[4,704,1536]{2,1,0:T(8,128)(2,1)} %join_rows.17.n2_ref), channel_id=1, source_target_pairs={{0,4},{4,0},{8,12},{12,8},{16,20},{20,16},{24,28},{28,24},{1,5},{5... | collective-permute-start | bytes 25952264 | tf_op jit(solution)/shard_map/ppermute | solution.py:829
  676.8 58.5 %collective-permute-start.44 = (bf16[4,704,768]{2,1,0:T(8,128)(2,1)}, bf16[4,704,768]{2,1,0:T(8,128)(2,1)}, u32[]{:S(2)}, u32[]{:S(2)}) collective-permute-start(bf16[4,704,768]{2,1,0:T(8,128)(2,1)} %get-tuple-element.303), channel_id=1, source_target_pairs={{0,4},{4,0},{8,12},{12,8},{16,20},{20,16},{24,28},{28,24},{1,5},{5... | collective-permute-start | bytes 12976136 | tf_op jit(solution)/shard_map/ppermute | solution.py:829
  747.9 105.0 %collective-permute-start.50 = (bf16[4,704,768]{2,1,0:T(8,128)(2,1)}, bf16[4,704,768]{2,1,0:T(8,128)(2,1)}, u32[]{:S(2)}, u32[]{:S(2)}) collective-permute-start(bf16[4,704,768]{2,1,0:T(8,128)(2,1)} %get-tuple-element.324), channel_id=1, source_target_pairs={{0,4},{4,0},{8,12},{12,8},{16,20},{20,16},{24,28},{28,24},{1,5},{5... | collective-permute-start | bytes 12976136 | tf_op jit(solution)/shard_map/ppermute | solution.py:829
  782.4 70.5 %collective-permute-start.51 = (bf16[4,704,768]{2,1,0:T(8,128)(2,1)}, bf16[4,704,768]{2,1,0:T(8,128)(2,1)}, u32[]{:S(2)}, u32[]{:S(2)}) collective-permute-start(bf16[4,704,768]{2,1,0:T(8,128)(2,1)} %get-tuple-element.325), channel_id=1, source_target_pairs={{0,4},{4,0},{8,12},{12,8},{16,20},{20,16},{24,28},{28,24},{1,5},{5... | collective-permute-start | bytes 12976136 | tf_op jit(solution)/shard_map/ppermute | solution.py:829
  869.4 107.8 %reduce-scatter.10.cloned.1.call-start = ((), (), s32[]{:S(2)}) async-start(), calls=%async_computation.12 | async-start | bytes 1966080 | tf_op jit(solution)/shard_map/reduce_scatter | solution.py:1161
  916.1 71.0 %collective-permute-start.56 = (bf16[4,704,1152]{2,1,0:T(8,128)(2,1)}, bf16[4,704,1152]{2,1,0:T(8,128)(2,1)}, u32[]{:S(2)}, u32[]{:S(2)}) collective-permute-start(bf16[4,704,1152]{2,1,0:T(8,128)(2,1)} %get-tuple-element.360), channel_id=1, source_target_pairs={{0,4},{4,0},{8,12},{12,8},{16,20},{20,16},{24,28},{28,24},{1,5},{5... | collective-permute-start | bytes 19464200 | tf_op jit(solution)/shard_map/ppermute | solution.py:829
  923.6 53.6 %collective-permute-start.54 = (bf16[4,176,768]{2,1,0:T(8,128)(2,1)}, bf16[4,176,768]{2,1,0:T(8,128)(2,1)S(1)}, u32[]{:S(2)}, u32[]{:S(2)}) collective-permute-start(bf16[4,176,768]{2,1,0:T(8,128)(2,1)} %get-tuple-element.356), channel_id=1, source_target_pairs={{0,8},{4,12},{8,0},{12,4},{16,24},{20,28},{24,16},{28,20},{1,9},{5... | collective-permute-start | bytes 3244040 | tf_op jit(solution)/shard_map/ppermute | solution.py:829
  978.6 109.7 %all-to-all-start.3 = ((bf16[4,2,256,1152]{3,2,1,0:T(8,128)(2,1)}), bf16[4,2,256,1152]{3,2,1,0:T(8,128)(2,1)}, u32[]{:S(2)}, u32[]{:S(2)}) async-start(bf16[4,2,256,1152]{3,2,1,0:T(8,128)(2,1)} %get-tuple-element.358), calls=%async_computation.5 | async-start | bytes 9437184 | tf_op jit(solution)/shard_map/all_to_all | solution.py:1007
  983.6 360.7 %reduce-scatter.20.cloned.1.call-start = ((), (), s32[]{:S(2)}) async-start(), calls=%async_computation.17 | async-start | bytes 2703360 | tf_op jit(solution)/shard_map/reduce_scatter | solution.py:1161
  992.2 72.5 %collective-permute-start.57 = (bf16[4,352,1152]{2,1,0:T(8,128)(2,1)}, bf16[4,352,1152]{2,1,0:T(8,128)(2,1)}, u32[]{:S(2)}, u32[]{:S(2)}) collective-permute-start(bf16[4,352,1152]{2,1,0:T(8,128)(2,1)} %sum_rows.23), channel_id=1, source_target_pairs={{0,16},{4,20},{8,24},{12,28},{16,0},{20,4},{24,8},{28,12},{1,17},{... | collective-permute-start | bytes 9732104 | tf_op jit(solution)/shard_map/ppermute | solution.py:829
  1099.6 253.0 %reduce-scatter.18.cloned.1.call-start = ((), (), s32[]{:S(2)}) async-start(), calls=%async_computation.16 | async-start | bytes 983040 | tf_op jit(solution)/shard_map/reduce_scatter | solution.py:1161
  1158.6 195.9 %reduce-scatter.16.cloned.1.call-start = ((), (), s32[]{:S(2)}) async-start(), calls=%async_computation.15 | async-start | bytes 2027520 | tf_op jit(solution)/shard_map/reduce_scatter | solution.py:1161
  1172.9 52.5 %collective-permute-start.66 = (bf16[4,352,768]{2,1,0:T(8,128)(2,1)}, bf16[4,352,768]{2,1,0:T(8,128)(2,1)}, u32[]{:S(2)}, u32[]{:S(2)}) collective-permute-start(bf16[4,352,768]{2,1,0:T(8,128)(2,1)} %get-tuple-element.383), channel_id=1, source_target_pairs={{0,16},{4,20},{8,24},{12,28},{16,0},{20,4},{24,8},{28,12},{1,17},{... | collective-permute-start | bytes 6488072 | tf_op jit(solution)/shard_map/ppermute | solution.py:829
  1182.7 176.3 %reduce-scatter.12.cloned.1.call-start = ((), (), s32[]{:S(2)}) async-start(), calls=%async_computation.13 | async-start | bytes 1351680 | tf_op jit(solution)/shard_map/reduce_scatter | solution.py:1161
  1278.0 94.1 %reduce-scatter.14.cloned.1.call-start = ((), (), s32[]{:S(2)}) async-start(), calls=%async_computation.14 | async-start | bytes 2027520 | tf_op jit(solution)/shard_map/reduce_scatter | solution.py:1161
  (155 other events, 3787.4 us)
Sparse Core Ops, SparseCore 0:
  10.2 31.1 all-gather.14
  43.0 37.7 all-gather.18
  90.2 46.1 all-gather.16
  165.7 45.5 all-gather.20
  267.2 69.3 all-gather.22
  338.6 26.6 all-gather.24
  464.5 44.4 all-gather.26
  840.4 54.8 reduce-scatter.7
  916.2 34.2 reduce-scatter.9
  1099.7 53.1 reduce-scatter.19
  1158.7 26.1 reduce-scatter.17
  1187.0 35.4 reduce-scatter.15
  1278.0 26.4 reduce-scatter.11
  1336.4 35.5 reduce-scatter.13

commit v8 on v7

--- a/solution.py
+++ b/solution.py
@@ -1009,7 +1009,10 @@
     skip_z = spread(jnp.pad(w_skip.T, ((0, 0), (0, skip_lanes - kept))))
     steps = cube.spread(timestep[:, 0])
     joined = side_by_side(tokens.reshape(rows, width), skip_tokens.reshape(rows, width), kept, skip_lanes)
-    skip_z, steps, joined = tie(skip_z, steps, joined)
+    wide = grid[:, 0, 1]
+    counts = grid[:, 0, 0] * wide
+    cosine, sine = rope_tables(sequence, wide, lanes)
+    skip_z, steps, joined, cosine, sine = tie(skip_z, steps, joined, cosine, sine)
     skip_m = fetch(skip_z, skip_cut)
     qkv_z = spread(pad_heads(w_qkv.reshape(strip, -1), local), skip_z)
     advance(skip_m)
@@ -1044,12 +1047,9 @@
     gains = gains.reshape(4, ranks, strip)[:, cube.owners].reshape(4, 2, 1, middle)
     g_skip, g_attn, g_cross, g_mlp = gains
 
-    wide = grid[:, 0, 1]
-    counts = grid[:, 0, 0] * wide
     lengths = text_len[:, 0, :]
     place = zone * slots + jnp.arange(slots, dtype=jnp.int32)
     live = (place[None, :] < counts[:, None]).astype(F32).reshape(rows, 1)
-    cosine, sine = rope_tables(sequence, wide, lanes)
     gain_q = pad_heads(jnp.tile(gain_query, local)[None, :], local)
     gain_k = pad_heads(jnp.tile(gain_key, local)[None, :], local)
 
@@ -1114,36 +1114,39 @@
     while fc_m[0].todo:
         advance(fc_m)
     text_z = spread(text_z, cross_z)
+    text_all = spread(text_own, cross_z)
     cross_m = fetch(cross_z, 2 * lanes)
     advance(cross_m)
-    raw, d_mlp = tie(raw, d_mlp)
+    raw, d_mlp, turn, text_turn = tie(raw, d_mlp, turn, text_turn)
+    text_m = Gather(cube, text_z[:, :text_rows], 1)
     attended, turned_q, turned_k, norms = self_forward(raw, counts, cosine, sine, gain_q, gain_k)
-    attended = bind(attended, *fc_m, *cross_m)
-    attended, text_z = tie(attended, text_z)
-    text_m = Gather(cube, text_z[:, :text_rows], 1)
+    attended = bind(attended, *fc_m, *cross_m, text_m)
+    attended, text_all = tie(attended, text_all)
     text_m.move()
     attended = exchange(attended).reshape(parts, rows, lanes)
     while cross_m[0].todo:
         advance(cross_m)
-    text_all = spread(text_own, text_z)
+    join(fc_m)
     hold(cross_m, attended)
-    join(cross_m)
-    first_w, out2_w = [mover.weight() for mover in cross_m]
+    attended = bind(attended, text_m, *fc_m)
+    while text_m.todo:
+        text_m.move()
+    join(cross_m[:1])
+    first_w = cross_m[0].weight()
     out1_w, query2_w = (Lanes(first_w.near, first_w.far, lanes, index) for index in range(2))
-    attended, text_all = tie(attended, text_all)
+    attended, first_w.far = tie(attended, first_w.far)
+    out1_w.far = query2_w.far = first_w.far
+    text_all = text_all.reshape(-1, features)
+    text_all = jnp.stack([text_all[:, : features // 2], text_all[:, features // 2 :]])
     stream1, pre_cross = to_features(
         attended, [out1_w], [stream, g_cross], [wide_shape, low_shape], next_norm
     )
-    pre_cross = bind(pre_cross, text_m, *fc_m)
-    while text_m.todo:
-        text_m.move()
-    query2 = to_lanes(pre_cross, [query2_w]).reshape(parts, micros, slots, lanes)
-    query2 = bind(query2, text_m)
-    text_all = text_all.reshape(-1, features)
-    text_all = jnp.stack([text_all[:, : features // 2], text_all[:, features // 2 :]])
+    pre_cross = bind(pre_cross, text_m, *cross_m[1:])
     text_m.join()
     text_w = text_m.weight()
-    join(fc_m)
+    join(cross_m[1:])
+    out2_w = cross_m[1].weight()
+    query2 = to_lanes(pre_cross, [query2_w]).reshape(parts, micros, slots, lanes)
     fc1_w, fc2_w = [mover.weight() for mover in fc_m]
     text_kv = to_lanes(text_all, [text_w]).reshape(parts, parts, micros, text_strip, 2 * lanes)
     crossed = cross_forward(query2, text_kv, lengths, text_slots).reshape(parts, rows, lanes)
@@ -1264,13 +1267,12 @@
         last_norms,
     )
     d_base = bind(d_base, *other_s)
-    skip_s = [
-        Scatter(cube, *terms_of([(d_base, joined, skip_cut, flip)]), flip) for flip in range(2)
-    ]
-    pack(skip_s)
-    hold(skip_s, *qkv_s)
+    skip_t = [list(terms_of([(d_base, joined, skip_cut, flip)])) for flip in range(2)]
+    skip_t[0][1] = bind(skip_t[0][1], *qkv_s)
+    skip_s = [Scatter(cube, *pair, flip) for flip, pair in enumerate(skip_t)]
     pack(qkv_s)
     send(qkv_s)
+    pack(skip_s)
     term_cross, term_text = settle(results([cross_s])), settle(results([text_s]))
     send(skip_s)
     term_qkv = settle(results(qkv_s))

time: 1390 us -> 1410 us (1.014)
  waiting for transfers between devices: 552 us -> 570 us
    ppermute x84, waiting for transfers between devices: 342 us -> 422 us  [swap(): return lax.ppermute(value, axis, pairs)]
    all_gather x7, waiting for transfers between devices: 129 us -> 91.9 us  [spread(): return lax.all_gather(shard, 'sp', axis=0, tiled=False)]
    all_to_all x4, waiting for transfers between devices: 69.2 us -> 46 us  [exchange(): return lax.all_to_all(value, 'sp', split_axis=0, concat_axis=0, tiled=True)]
  transfers between devices with their start and end apart: 102 -> 102, of which waited for: 46 -> 49; matrix products, arithmetic and copies ran while one was open for 8% -> 8% of each run, Pallas kernels for 37% -> 37%
where the time goes in v8:
time: 1410 us; the launch traced here: 1400 us
  waiting for transfers between devices  570 us (40%)
  Pallas kernels  562 us (40%)
  starting transfers between devices  123 us (9%)
  other arithmetic  58.6 us (4%)
  local copies, waits for them, and re-layouts  52.4 us (4%)
  matrix products  18.5 us (1%)
  between operations  15.7 us (1%)
    ppermute x84, waiting for transfers between devices, swap(): return lax.ppermute(value, axis, pairs)  422 us
    ppermute x84, starting transfers between devices, swap(): return lax.ppermute(value, axis, pairs)  105 us
    all_gather x7, waiting for transfers between devices, spread(): return lax.all_gather(shard, 'sp', axis=0, tiled=False)  91.9 us
    pallas_call x18, Pallas kernels, sum_rows(): pl.pallas_call(kernel, name=name, grid=(parts,), in_specs=[spec(block, ar...  85.3 us
    pallas_call x6, Pallas kernels, to_features(): pl.pallas_call(kernel, name=name, grid=(parts,), in_specs=[pl.BlockSpec((...  78.3 us
    pallas_call x2, Pallas kernels, mlp_backward(): pl.pallas_call(kernel, name='mlp_backward', grid=(parts, steps), in_specs...  63.4 us
    pallas_call x2, Pallas kernels, mlp_forward(): pl.pallas_call(kernel, name='mlp_forward', grid=(parts, steps), in_specs=...  57.6 us
    pallas_call x6, Pallas kernels, terms_of(): pl.pallas_call(kernel, name=name, grid=(parts,), in_specs=[full(pair[0].s...  54 us
  transfers between devices with their start and end apart: 102, of which 49 were waited for; matrix products, arithmetic and copies ran while one was open for 8% of the time, Pallas kernels for 37%

profile of v8, /device:TPU:0, one launch (start us, length us, event | category | flops | bytes accessed | tf_op | source)
XLA Modules:
  0.0 1399.5 jit_solution(3046662398139302763)
XLA Ops:
  17.2 13.9 negate_select_fusion
  62.6 22.0 %collective-permute-done.9 = f32[4,2,176]{2,1,0:T(2,128)S(1)} collective-permute-done((f32[4,2,176]{2,1,0:T(2,128)S(1)}, f32[4,2,176]{2,1,0:T(2,128)S(1)}, u32[]{:S(2)}, u32[]{:S(2)}) %collective-permute-start.9) | collective-permute-done | bytes 5664 | tf_op jit(solution)/shard_map/ppermute | solution.py:829
  108.4 15.1 %collective-permute-done.16.refs_1_ = bf16[4,176,640]{2,1,0:T(8,128)(2,1)} collective-permute-done((bf16[4,176,640]{2,1,0:T(8,128)(2,1)S(1)}, bf16[4,176,640]{2,1,0:T(8,128)(2,1)}, u32[]{:S(2)}, u32[]{:S(2)}) %collective-permute-start.16) | collective-permute-done | bytes 901152 | tf_op jit(solution)/shard_map/ppermute | solution.py:829
  124.9 18.7 %collective-permute-done.21.refs_2_ = bf16[4,176,512]{2,1,0:T(8,128)(2,1)} collective-permute-done((bf16[4,176,512]{2,1,0:T(8,128)(2,1)S(1)}, bf16[4,176,512]{2,1,0:T(8,128)(2,1)}, u32[]{:S(2)}, u32[]{:S(2)}) %collective-permute-start.21) | collective-permute-done | bytes 720928 | tf_op jit(solution)/shard_map/ppermute | solution.py:829
  145.6 14.8 %to_features.6 = (f32[2,512,704]{2,1,0:T(8,128)}, f32[2,512,704]{2,1,0:T(8,128)}, bf16[2,512,704]{2,1,0:T(8,128)(2,1)}) custom-call(bf16[4,512,768]{2,1,0:T(8,128)(2,1)} %side_by_side.1.refs_0_.refs_1_, bf16[4,704,384]{2,1,0:T(8,128)(2,1)} %join_rows.9.refs_1_.refs_0_, bf16[4,704,384]{2,1,0:T(8,128)(2,1)} %collective-permute-done.11.refs_2_.refs_1_, ...), custom_call_target="tpu_custom_call" | custom-call | flops 276824064 | bytes 276824 | tf_op jit(solution)/shard_map/to_features/pallas_call | solution.py:401
  184.6 13.0 to_lanes.5
  197.6 14.3 %all-gather.21.cloned.1.call-done = bf16[704,1536]{1,0:T(8,128)(2,1)} async-done(((bf16[176,1536]{1,0:T(8,128)(2,1)}), bf16[704,1536]{1,0:T(8,128)(2,1)}) %all-gather.21.cloned.1.call-update) | async-done | bytes 2162704 | tf_op jit(solution)/shard_map/all_gather | solution.py:993
  228.7 32.2 %collective-permute-done.27.refs_2_ = bf16[4,176,1536]{2,1,0:T(8,128)(2,1)} collective-permute-done((bf16[4,176,1536]{2,1,0:T(8,128)(2,1)}, bf16[4,176,1536]{2,1,0:T(8,128)(2,1)}, u32[]{:S(2)}, u32[]{:S(2)}) %collective-permute-start.27) | collective-permute-done | bytes 2162720 | tf_op jit(solution)/shard_map/ppermute | solution.py:829
  261.1 75.3 %all-gather.23.cloned.1.call-done = bf16[704,1152]{1,0:T(8,128)(2,1)} async-done(((bf16[176,1152]{1,0:T(8,128)(2,1)}), bf16[704,1152]{1,0:T(8,128)(2,1)}) %all-gather.23.cloned.1.call-update) | async-done | bytes 1622032 | tf_op jit(solution)/shard_map/all_gather | solution.py:993
  363.7 29.8 %collective-permute-done.25.refs_2_ = bf16[4,176,1536]{2,1,0:T(8,128)(2,1)} collective-permute-done((bf16[4,176,1536]{2,1,0:T(8,128)(2,1)}, bf16[4,176,1536]{2,1,0:T(8,128)(2,1)}, u32[]{:S(2)}, u32[]{:S(2)}) %collective-permute-start.25) | collective-permute-done | bytes 2162720 | tf_op jit(solution)/shard_map/ppermute | solution.py:829
  406.4 31.3 %self_forward.1 = (bf16[4,2,256,384]{3,2,1,0:T(8,128)(2,1)}, bf16[2,1024,384]{2,1,0:T(8,128)(2,1)}, bf16[2,1024,384]{2,1,0:T(8,128)(2,1)}, f32[2,4,1024]{2,1,0:T(4,128)}) custom-call(s32[2]{0:T(128)} %copy-done.63, bf16[4,2,256,1152]{3,2,1,0:T(8,128)(2,1)} %all-to-all-done.raw_ref, f32[2,1024,384]{2,1,0:T(8,128)} %get-tuple-element.243.cos_ref, ...), custom_call_target="tpu_custom_call" | custom-call | flops 201326592 | bytes 201326 | tf_op jit(solution)/shard_map/self_forward/pallas_call | solution.py:150
  450.5 21.1 %collective-permute-done.30.refs_1_ = bf16[4,176,768]{2,1,0:T(8,128)(2,1)} collective-permute-done((bf16[4,176,768]{2,1,0:T(8,128)(2,1)}, bf16[4,176,768]{2,1,0:T(8,128)(2,1)}, u32[]{:S(2)}, u32[]{:S(2)}) %collective-permute-start.30) | collective-permute-done | bytes 1081376 | tf_op jit(solution)/shard_map/ppermute | solution.py:829
  493.4 17.7 %all-to-all-done.1 = bf16[4,2,256,384]{3,2,1,0:T(8,128)(2,1)S(1)} async-done(((bf16[4,2,256,384]{3,2,1,0:T(8,128)(2,1)}), bf16[4,2,256,384]{3,2,1,0:T(8,128)(2,1)S(1)}, u32[]{:S(2)}, u32[]{:S(2)}) %all-to-all-start.1) | async-done | bytes 1572896 | tf_op jit(solution)/shard_map/all_to_all | solution.py:1007
  513.7 25.0 %collective-permute-done.33.refs_2_ = bf16[4,176,768]{2,1,0:T(8,128)(2,1)} collective-permute-done((bf16[4,176,768]{2,1,0:T(8,128)(2,1)}, bf16[4,176,768]{2,1,0:T(8,128)(2,1)}, u32[]{:S(2)}, u32[]{:S(2)}) %collective-permute-start.33) | collective-permute-done | bytes 1081376 | tf_op jit(solution)/shard_map/ppermute | solution.py:829
  538.7 22.3 %collective-permute-done.34.refs_3_ = bf16[4,176,768]{2,1,0:T(8,128)(2,1)} collective-permute-done((bf16[4,176,768]{2,1,0:T(8,128)(2,1)}, bf16[4,176,768]{2,1,0:T(8,128)(2,1)}, u32[]{:S(2)}, u32[]{:S(2)}) %collective-permute-start.34) | collective-permute-done | bytes 1081376 | tf_op jit(solution)/shard_map/ppermute | solution.py:829
  567.9 13.1 collective-permute-done.38.refs_1_
  609.4 16.4 %collective-permute-done.37.refs_3_ = bf16[4,128,768]{2,1,0:T(8,128)(2,1)S(1)} collective-permute-done((bf16[4,128,768]{2,1,0:T(8,128)(2,1)}, bf16[4,128,768]{2,1,0:T(8,128)(2,1)S(1)}, u32[]{:S(2)}, u32[]{:S(2)}) %collective-permute-start.37) | collective-permute-done | bytes 786464 | tf_op jit(solution)/shard_map/ppermute | solution.py:829
  654.3 19.1 %cross_forward.1 = bf16[4,2,256,384]{3,2,1,0:T(8,128)(2,1)} custom-call(s32[2,2]{1,0:T(2,128)} %bitcast.216, bf16[4,2,256,384]{3,2,1,0:T(8,128)(2,1)} %bitcast.169, bf16[4,4,2,96,768]{4,3,2,1,0:T(8,128)(2,1)} %bitcast.160), custom_call_target="tpu_custom_call" | custom-call | flops 75497472 | bytes 75497 | tf_op jit(solution)/shard_map/cross_forward/pallas_call | solution.py:735
  683.9 28.7 %mlp_forward.2 = (f32[4,512,768]{2,1,0:T(8,128)}, bf16[4,512,768]{2,1,0:T(8,128)(2,1)}, f32[2,512,704]{2,1,0:T(8,128)}, bf16[4,704,768]{2,1,0:T(8,128)(2,1)}, bf16[4,704,768]{2,1,0:T(8,128)(2,1)}) custom-call(bf16[2,512,704]{2,1,0:T(8,128)(2,1)} %get-tuple-element.294.x_ref, bf16[2,512,704]{2,1,0:T(8,128)(2,1)} %fusion.65.g_ref, ...), custom_call_target="tpu_custom_call" | custom-call | flops 830472192 | bytes 830472 | tf_op jit(solution)/shard_map/mlp_forward/pallas_call | solution.py:606
  712.8 28.9 %mlp_forward.3 = (f32[4,512,768]{2,1,0:T(8,128)}, bf16[4,512,768]{2,1,0:T(8,128)(2,1)}, bf16[2,512,704]{2,1,0:T(8,128)(2,1)}, bf16[4,704,768]{2,1,0:T(8,128)(2,1)}, bf16[4,704,768]{2,1,0:T(8,128)(2,1)}) custom-call(bf16[2,512,704]{2,1,0:T(8,128)(2,1)} %get-tuple-element.294.x_ref, bf16[2,512,704]{2,1,0:T(8,128)(2,1)} %fusion.65.g_ref, ...), custom_call_target="tpu_custom_call" | custom-call | flops 830472192 | bytes 830472 | tf_op jit(solution)/shard_map/mlp_forward/pallas_call | solution.py:606
  742.1 29.0 %mlp_backward.2 = (bf16[4,704,768]{2,1,0:T(8,128)(2,1)}, bf16[4,704,768]{2,1,0:T(8,128)(2,1)}, f32[2,512,704]{2,1,0:T(8,128)}) custom-call(bf16[2,512,704]{2,1,0:T(8,128)(2,1)} %fusion.65.g_ref, bf16[2,512,704]{2,1,0:T(8,128)(2,1)} %get-tuple-element.294.x_ref, f32[4,512,768]{2,1,0:T(8,128)} %get-tuple-element.306.hid_ref, ...), custom_call_target="tpu_custom_call" | custom-call | flops 830472192 | bytes 830472 | tf_op jit(solution)/shard_map/mlp_backward/pallas_call | solution.py:678
  783.3 34.5 %mlp_backward.3 = (bf16[4,704,768]{2,1,0:T(8,128)(2,1)}, bf16[4,704,768]{2,1,0:T(8,128)(2,1)}, f32[2,512,704]{2,1,0:T(8,128)}, bf16[2,512,704]{2,1,0:T(8,128)(2,1)}, f32[2,1,704]{2,1,0:T(1,128)}) custom-call(bf16[2,512,704]{2,1,0:T(8,128)(2,1)} %fusion.65.g_ref, bf16[2,512,704]{2,1,0:T(8,128)(2,1)} %get-tuple-element.294.x_ref, ...), custom_call_target="tpu_custom_call" | custom-call | flops 830472192 | bytes 830472 | tf_op jit(solution)/shard_map/mlp_backward/pallas_call | solution.py:678
  842.1 22.6 %cross_backward.1 = (bf16[4,2,256,384]{3,2,1,0:T(8,128)(2,1)}, bf16[4,4,2,96,768]{4,3,2,1,0:T(8,128)(2,1)}) custom-call(s32[2,2]{1,0:T(2,128)} %bitcast.217, bf16[4,2,256,384]{3,2,1,0:T(8,128)(2,1)} %bitcast.170, bf16[4,4,2,96,768]{4,3,2,1,0:T(8,128)(2,1)} %bitcast.161, bf16[4,2,256,384]{3,2,1,0:T(8,128)(2,1)} %bitcast.173), custom_call_target="tpu_custom_call" | custom-call | flops 188743680 | bytes 188743 | tf_op jit(solution)/shard_map/cross_backward/pallas_call | solution.py:784
  925.0 15.2 %terms_of.7 = (bf16[4,704,1152]{2,1,0:T(8,128)(2,1)}, bf16[4,704,1152]{2,1,0:T(8,128)(2,1)}) custom-call(bf16[2,512,704]{2,1,0:T(8,128)(2,1)} %get-tuple-element.339.x_ref.refs_0_, bf16[2,512,704]{2,1,0:T(8,128)(2,1)} %get-tuple-element.344.x_ref.refs_1_, bf16[2,512,704]{2,1,0:T(8,128)(2,1)} %get-tuple-element.318.x_ref.refs_2_, ...), custom_call_target="tpu_custom_call" | custom-call | flops 415236096 | bytes 415236 | tf_op jit(solution)/shard_map/terms_of/pallas_call | solution.py:445
  960.0 46.7 %self_backward.1 = (bf16[4,2,256,1152]{3,2,1,0:T(8,128)(2,1)}, f32[2,1,384]{2,1,0:T(1,128)}, f32[2,1,384]{2,1,0:T(1,128)}) custom-call(s32[2]{0:T(128)} %copy-done.63, bf16[4,2,256,1152]{3,2,1,0:T(8,128)(2,1)} %all-to-all-done.raw_ref, f32[2,1024,384]{2,1,0:T(8,128)} %get-tuple-element.243.cos_ref, f32[2,1024,384]{2,1,0:T(8,128)} %get-tuple-element.244.sin_ref, ...), custom_call_target="tpu_custom_call" | custom-call | flops 503316480 | bytes 503316 | tf_op jit(solution)/shard_map/self_backward/pallas_call | solution.py:260
  1044.1 29.6 %collective-permute-done.59.refs_2_ = bf16[4,256,768]{2,1,0:T(8,128)(2,1)} collective-permute-done((bf16[4,256,768]{2,1,0:T(8,128)(2,1)}, bf16[4,256,768]{2,1,0:T(8,128)(2,1)}, u32[]{:S(2)}, u32[]{:S(2)}) %collective-permute-start.59) | collective-permute-done | bytes 1572896 | tf_op jit(solution)/shard_map/ppermute | solution.py:829
  1073.7 26.5 %collective-permute-done.57.refs_2_ = bf16[4,352,1152]{2,1,0:T(8,128)(2,1)} collective-permute-done((bf16[4,352,1152]{2,1,0:T(8,128)(2,1)}, bf16[4,352,1152]{2,1,0:T(8,128)(2,1)}, u32[]{:S(2)}, u32[]{:S(2)}) %collective-permute-start.57) | collective-permute-done | bytes 3244064 | tf_op jit(solution)/shard_map/ppermute | solution.py:829
  1100.2 17.6 %all-to-all-done.3 = bf16[4,2,256,1152]{3,2,1,0:T(8,128)(2,1)} async-done(((bf16[4,2,256,1152]{3,2,1,0:T(8,128)(2,1)}), bf16[4,2,256,1152]{3,2,1,0:T(8,128)(2,1)}, u32[]{:S(2)}, u32[]{:S(2)}) %all-to-all-start.3) | async-done | bytes 4718624 | tf_op jit(solution)/shard_map/all_to_all | solution.py:1007
  1162.8 20.5 %to_features.11 = (bf16[2,512,704]{2,1,0:T(8,128)(2,1)}, f32[2,2,704]{2,1,0:T(2,128)}, f32[2,1,704]{2,1,0:T(1,128)}, f32[2,1,704]{2,1,0:T(1,128)}) custom-call(bf16[4,512,1152]{2,1,0:T(8,128)(2,1)} %bitcast.61.refs_1_.refs_0_, bf16[4,704,640]{2,1,0:T(8,128)(2,1)} %join_rows.11.refs_0_.refs_1_, bf16[4,704,640]{2,1,0:T(8,128)(2,1)} %collective-permute-done.19.refs_1_.refs_2_, ...), custom_call_target="tpu_custom_call" | custom-call | flops 415236096 | bytes 415236 | tf_op jit(solution)/shard_map/to_features/pallas_call | solution.py:401
  1207.7 15.9 %collective-permute-done.65.refs_5_.refs_6_ = bf16[4,352,384]{2,1,0:T(8,128)(2,1)S(1)} collective-permute-done((bf16[4,352,384]{2,1,0:T(8,128)(2,1)S(1)}, bf16[4,352,384]{2,1,0:T(8,128)(2,1)S(1)}, u32[]{:S(2)}, u32[]{:S(2)}) %collective-permute-start.65) | collective-permute-done | bytes 1081376 | tf_op jit(solution)/shard_map/ppermute | solution.py:829
  1223.7 17.1 %collective-permute-done.64.refs_2_ = bf16[4,352,768]{2,1,0:T(8,128)(2,1)} collective-permute-done((bf16[4,352,768]{2,1,0:T(8,128)(2,1)}, bf16[4,352,768]{2,1,0:T(8,128)(2,1)}, u32[]{:S(2)}, u32[]{:S(2)}) %collective-permute-start.64) | collective-permute-done | bytes 2162720 | tf_op jit(solution)/shard_map/ppermute | solution.py:829
  1298.4 23.4 %collective-permute-done.73 = f32[4,2,176]{2,1,0:T(2,128)S(1)} collective-permute-done((f32[4,2,176]{2,1,0:T(2,128)S(1)}, f32[4,2,176]{2,1,0:T(2,128)S(1)}, u32[]{:S(2)}, u32[]{:S(2)}) %collective-permute-start.73) | collective-permute-done | bytes 5664 | tf_op jit(solution)/shard_map/ppermute | solution.py:829
  (579 shorter events, 612.7 us)
Async XLA Ops:
  9.1 91.1 %all-gather.19.cloned.1.call-start = ((), (), s32[]{:S(2)}) async-start(), calls=%async_computation.20 | async-start | bytes 2027520 | tf_op jit(solution)/shard_map/all_gather | solution.py:993
  41.5 137.5 %all-gather.17.cloned.1.call-start = ((), (), s32[]{:S(2)}) async-start(), calls=%async_computation.19 | async-start | bytes 2703360 | tf_op jit(solution)/shard_map/all_gather | solution.py:993
  90.1 121.8 %all-gather.21.cloned.1.call-start = ((), (), s32[]{:S(2)}) async-start(), calls=%async_computation.21 | async-start | bytes 2703360 | tf_op jit(solution)/shard_map/all_gather | solution.py:993
  105.1 55.4 %collective-permute-start.17 = (bf16[4,176,640]{2,1,0:T(8,128)(2,1)S(1)}, bf16[4,176,640]{2,1,0:T(8,128)(2,1)}, u32[]{:S(2)}, u32[]{:S(2)}) collective-permute-start(bf16[4,176,640]{2,1,0:T(8,128)(2,1)S(1)} %slice.419.refs_0_), channel_id=1, source_target_pairs={{0,16},{4,20},{8,24},{12,28},{16,0},{20,4},{24,8},{28,12},{1,17},{... | collective-permute-start | bytes 2703368 | tf_op jit(solution)/shard_map/ppermute | solution.py:829
  179.0 49.8 %collective-permute-start.24 = (bf16[4,176,1536]{2,1,0:T(8,128)(2,1)}, bf16[4,176,1536]{2,1,0:T(8,128)(2,1)}, u32[]{:S(2)}, u32[]{:S(2)}) collective-permute-start(bf16[4,176,1536]{2,1,0:T(8,128)(2,1)} %bitcast.178), channel_id=1, source_target_pairs={{0,8},{4,12},{8,0},{12,4},{16,24},{20,28},{24,16},{28,20},{1,9},{5... | collective-permute-start | bytes 6488072 | tf_op jit(solution)/shard_map/ppermute | solution.py:829
  213.3 193.1 %all-to-all-start = ((bf16[4,2,256,1152]{3,2,1,0:T(8,128)(2,1)}), bf16[4,2,256,1152]{3,2,1,0:T(8,128)(2,1)}, u32[]{:S(2)}, u32[]{:S(2)}) async-start(bf16[4,2,256,1152]{3,2,1,0:T(8,128)(2,1)} %bitcast.164), calls=%async_computation | async-start | bytes 9437184 | tf_op jit(solution)/shard_map/all_to_all | solution.py:1007
  218.4 118.0 %all-gather.23.cloned.1.call-start = ((), (), s32[]{:S(2)}) async-start(), calls=%async_computation.22 | async-start | bytes 2027520 | tf_op jit(solution)/shard_map/all_gather | solution.py:993
  261.0 144.2 %all-gather.25.cloned.1.call-start = ((), (), s32[]{:S(2)}) async-start(), calls=%async_computation.23 | async-start | bytes 1351680 | tf_op jit(solution)/shard_map/all_gather | solution.py:993
  337.2 134.4 %all-gather.27.cloned.1.call-start = ((), (), s32[]{:S(2)}) async-start(), calls=%async_computation.24 | async-start | bytes 1966080 | tf_op jit(solution)/shard_map/all_gather | solution.py:993
  343.2 50.3 %collective-permute-start.25 = (bf16[4,176,1536]{2,1,0:T(8,128)(2,1)}, bf16[4,176,1536]{2,1,0:T(8,128)(2,1)}, u32[]{:S(2)}, u32[]{:S(2)}) collective-permute-start(bf16[4,176,1536]{2,1,0:T(8,128)(2,1)} %bitcast.179), channel_id=1, source_target_pairs={{0,16},{4,20},{8,24},{12,28},{16,0},{20,4},{24,8},{28,12},{1,17},{... | collective-permute-start | bytes 6488072 | tf_op jit(solution)/shard_map/ppermute | solution.py:829
  352.3 87.5 %collective-permute-start.26 = (bf16[4,176,1536]{2,1,0:T(8,128)(2,1)}, bf16[4,176,1536]{2,1,0:T(8,128)(2,1)}, u32[]{:S(2)}, u32[]{:S(2)}) collective-permute-start(bf16[4,176,1536]{2,1,0:T(8,128)(2,1)} %collective-permute-done.24.refs_1_), channel_id=1, source_target_pairs={{0,16},{4,20},{8,24},{12,28},{16,0},{20,4},{24,8},{28,12},{1,17},{... | collective-permute-start | bytes 6488072 | tf_op jit(solution)/shard_map/ppermute | solution.py:829
  353.3 86.5 %collective-permute-start.28 = (bf16[4,176,1536]{2,1,0:T(8,128)(2,1)}, bf16[4,176,1536]{2,1,0:T(8,128)(2,1)}, u32[]{:S(2)}, u32[]{:S(2)}) collective-permute-start(bf16[4,176,1536]{2,1,0:T(8,128)(2,1)} %bitcast.182), channel_id=1, source_target_pairs={{0,8},{4,12},{8,0},{12,4},{16,24},{20,28},{24,16},{28,20},{1,9},{5... | collective-permute-start | bytes 6488072 | tf_op jit(solution)/shard_map/ppermute | solution.py:829
  354.8 95.2 %collective-permute-start.29 = (bf16[4,176,1536]{2,1,0:T(8,128)(2,1)}, bf16[4,176,1536]{2,1,0:T(8,128)(2,1)}, u32[]{:S(2)}, u32[]{:S(2)}) collective-permute-start(bf16[4,176,1536]{2,1,0:T(8,128)(2,1)} %collective-permute-done.27.refs_2_), channel_id=1, source_target_pairs={{0,8},{4,12},{8,0},{12,4},{16,24},{20,28},{24,16},{28,20},{1,9},{5... | collective-permute-start | bytes 6488072 | tf_op jit(solution)/shard_map/ppermute | solution.py:829
  360.4 111.2 %collective-permute-start.30 = (bf16[4,176,768]{2,1,0:T(8,128)(2,1)}, bf16[4,176,768]{2,1,0:T(8,128)(2,1)}, u32[]{:S(2)}, u32[]{:S(2)}) collective-permute-start(bf16[4,176,768]{2,1,0:T(8,128)(2,1)} %slice.423.refs_0_), channel_id=1, source_target_pairs={{0,8},{4,12},{8,0},{12,4},{16,24},{20,28},{24,16},{28,20},{1,9},{5... | collective-permute-start | bytes 3244040 | tf_op jit(solution)/shard_map/ppermute | solution.py:829
  393.4 57.0 %collective-permute-start.31 = (bf16[4,176,384]{2,1,0:T(8,128)(2,1)S(1)}, bf16[4,176,384]{2,1,0:T(8,128)(2,1)}, u32[]{:S(2)}, u32[]{:S(2)}) collective-permute-start(bf16[4,176,384]{2,1,0:T(8,128)(2,1)S(1)} %slice.424.refs_0_), channel_id=1, source_target_pairs={{0,16},{4,20},{8,24},{12,28},{16,0},{20,4},{24,8},{28,12},{1,17},{... | collective-permute-start | bytes 1622024 | tf_op jit(solution)/shard_map/ppermute | solution.py:829
  475.2 531.5 %reduce-scatter.8.cloned.1.call-start = ((), (), s32[]{:S(2)}) async-start(), calls=%async_computation.11 | async-start | bytes 2703360 | tf_op jit(solution)/shard_map/reduce_scatter | solution.py:1164
  511.1 172.8 %collective-permute-start.42 = (bf16[4,704,1536]{2,1,0:T(8,128)(2,1)}, bf16[4,704,1536]{2,1,0:T(8,128)(2,1)}, u32[]{:S(2)}, u32[]{:S(2)}) collective-permute-start(bf16[4,704,1536]{2,1,0:T(8,128)(2,1)} %join_rows.13.n1_ref), channel_id=1, source_target_pairs={{0,4},{4,0},{8,12},{12,8},{16,20},{20,16},{24,28},{28,24},{1,5},{5... | collective-permute-start | bytes 25952264 | tf_op jit(solution)/shard_map/ppermute | solution.py:829
  511.1 172.8 %collective-permute-start.43 = (bf16[4,704,1536]{2,1,0:T(8,128)(2,1)}, bf16[4,704,1536]{2,1,0:T(8,128)(2,1)}, u32[]{:S(2)}, u32[]{:S(2)}) collective-permute-start(bf16[4,704,1536]{2,1,0:T(8,128)(2,1)} %join_rows.14.n2_ref), channel_id=1, source_target_pairs={{0,4},{4,0},{8,12},{12,8},{16,20},{20,16},{24,28},{28,24},{1,5},{5... | collective-permute-start | bytes 25952264 | tf_op jit(solution)/shard_map/ppermute | solution.py:829
  712.6 58.4 %collective-permute-start.44 = (bf16[4,704,768]{2,1,0:T(8,128)(2,1)}, bf16[4,704,768]{2,1,0:T(8,128)(2,1)}, u32[]{:S(2)}, u32[]{:S(2)}) collective-permute-start(bf16[4,704,768]{2,1,0:T(8,128)(2,1)} %get-tuple-element.309), channel_id=1, source_target_pairs={{0,4},{4,0},{8,12},{12,8},{16,20},{20,16},{24,28},{28,24},{1,5},{5... | collective-permute-start | bytes 12976136 | tf_op jit(solution)/shard_map/ppermute | solution.py:829
  783.3 104.7 %collective-permute-start.50 = (bf16[4,704,768]{2,1,0:T(8,128)(2,1)}, bf16[4,704,768]{2,1,0:T(8,128)(2,1)}, u32[]{:S(2)}, u32[]{:S(2)}) collective-permute-start(bf16[4,704,768]{2,1,0:T(8,128)(2,1)} %get-tuple-element.330), channel_id=1, source_target_pairs={{0,4},{4,0},{8,12},{12,8},{16,20},{20,16},{24,28},{28,24},{1,5},{5... | collective-permute-start | bytes 12976136 | tf_op jit(solution)/shard_map/ppermute | solution.py:829
  817.8 70.2 %collective-permute-start.51 = (bf16[4,704,768]{2,1,0:T(8,128)(2,1)}, bf16[4,704,768]{2,1,0:T(8,128)(2,1)}, u32[]{:S(2)}, u32[]{:S(2)}) collective-permute-start(bf16[4,704,768]{2,1,0:T(8,128)(2,1)} %get-tuple-element.331), channel_id=1, source_target_pairs={{0,4},{4,0},{8,12},{12,8},{16,20},{20,16},{24,28},{28,24},{1,5},{5... | collective-permute-start | bytes 12976136 | tf_op jit(solution)/shard_map/ppermute | solution.py:829
  901.0 50.0 %all-to-all-start.2 = ((bf16[4,2,256,384]{3,2,1,0:T(8,128)(2,1)}), bf16[4,2,256,384]{3,2,1,0:T(8,128)(2,1)S(1)}, u32[]{:S(2)}, u32[]{:S(2)}) async-start(bf16[4,2,256,384]{3,2,1,0:T(8,128)(2,1)} %bitcast.174), calls=%async_computation.2 | async-start | bytes 3145728 | tf_op jit(solution)/shard_map/all_to_all | solution.py:1007
  904.6 102.2 %reduce-scatter.10.cloned.1.call-start = ((), (), s32[]{:S(2)}) async-start(), calls=%async_computation.12 | async-start | bytes 1966080 | tf_op jit(solution)/shard_map/reduce_scatter | solution.py:1164
  951.0 70.7 %collective-permute-start.56 = (bf16[4,704,1152]{2,1,0:T(8,128)(2,1)}, bf16[4,704,1152]{2,1,0:T(8,128)(2,1)}, u32[]{:S(2)}, u32[]{:S(2)}) collective-permute-start(bf16[4,704,1152]{2,1,0:T(8,128)(2,1)} %get-tuple-element.366), channel_id=1, source_target_pairs={{0,4},{4,0},{8,12},{12,8},{16,20},{20,16},{24,28},{28,24},{1,5},{5... | collective-permute-start | bytes 19464200 | tf_op jit(solution)/shard_map/ppermute | solution.py:829
  1008.1 109.7 %all-to-all-start.3 = ((bf16[4,2,256,1152]{3,2,1,0:T(8,128)(2,1)}), bf16[4,2,256,1152]{3,2,1,0:T(8,128)(2,1)}, u32[]{:S(2)}, u32[]{:S(2)}) async-start(bf16[4,2,256,1152]{3,2,1,0:T(8,128)(2,1)} %get-tuple-element.364), calls=%async_computation.5 | async-start | bytes 9437184 | tf_op jit(solution)/shard_map/all_to_all | solution.py:1007
  1013.0 350.8 %reduce-scatter.20.cloned.1.call-start = ((), (), s32[]{:S(2)}) async-start(), calls=%async_computation.17 | async-start | bytes 2703360 | tf_op jit(solution)/shard_map/reduce_scatter | solution.py:1164
  1026.9 73.4 %collective-permute-start.57 = (bf16[4,352,1152]{2,1,0:T(8,128)(2,1)}, bf16[4,352,1152]{2,1,0:T(8,128)(2,1)}, u32[]{:S(2)}, u32[]{:S(2)}) collective-permute-start(bf16[4,352,1152]{2,1,0:T(8,128)(2,1)} %sum_rows.23), channel_id=1, source_target_pairs={{0,16},{4,20},{8,24},{12,28},{16,0},{20,4},{24,8},{28,12},{1,17},{... | collective-permute-start | bytes 9732104 | tf_op jit(solution)/shard_map/ppermute | solution.py:829
  1129.1 242.2 %reduce-scatter.18.cloned.1.call-start = ((), (), s32[]{:S(2)}) async-start(), calls=%async_computation.16 | async-start | bytes 983040 | tf_op jit(solution)/shard_map/reduce_scatter | solution.py:1164
  1189.5 183.6 %reduce-scatter.16.cloned.1.call-start = ((), (), s32[]{:S(2)}) async-start(), calls=%async_computation.15 | async-start | bytes 2027520 | tf_op jit(solution)/shard_map/reduce_scatter | solution.py:1164
  1189.6 51.2 %collective-permute-start.64 = (bf16[4,352,768]{2,1,0:T(8,128)(2,1)}, bf16[4,352,768]{2,1,0:T(8,128)(2,1)}, u32[]{:S(2)}, u32[]{:S(2)}) collective-permute-start(bf16[4,352,768]{2,1,0:T(8,128)(2,1)} %get-tuple-element.387), channel_id=1, source_target_pairs={{0,16},{4,20},{8,24},{12,28},{16,0},{20,4},{24,8},{28,12},{1,17},{... | collective-permute-start | bytes 6488072 | tf_op jit(solution)/shard_map/ppermute | solution.py:829
  1198.2 179.4 %reduce-scatter.14.cloned.1.call-start = ((), (), s32[]{:S(2)}) async-start(), calls=%async_computation.14 | async-start | bytes 2027520 | tf_op jit(solution)/shard_map/reduce_scatter | solution.py:1164
  1287.4 103.6 %reduce-scatter.12.cloned.1.call-start = ((), (), s32[]{:S(2)}) async-start(), calls=%async_computation.13 | async-start | bytes 1351680 | tf_op jit(solution)/shard_map/reduce_scatter | solution.py:1164
  (144 other events, 3596.1 us)
Sparse Core Ops, SparseCore 0:
  10.2 31.2 all-gather.14
  43.0 37.7 all-gather.18
  90.2 46.1 all-gather.16
  166.3 45.5 all-gather.20
  261.1 75.2 all-gather.22
  338.4 28.1 all-gather.24
  368.7 35.5 all-gather.26
  875.6 54.7 reduce-scatter.7
  951.1 34.2 reduce-scatter.9
  1129.2 52.9 reduce-scatter.19
  1189.6 24.8 reduce-scatter.17
  1216.7 35.4 reduce-scatter.15
  1287.5 35.1 reduce-scatter.13
  1364.0 26.9 reduce-scatter.11

commit v9 on v8

--- a/solution.py
+++ b/solution.py
@@ -475,26 +475,29 @@
     return back, gains
 
 
-def join_rows(pieces, name="join_rows"):
-    parts, rows, lanes = pieces[0].shape
+def join_rows(pieces, rows, name="join_rows"):
+    parts, _, lanes = pieces[0][0].shape
     count = len(pieces)
     if rows % 16:
-        return jnp.concatenate(pieces, 1)
+        return jnp.concatenate([array[:, block * rows : (block + 1) * rows] for array, block in pieces], 1)
 
     def kernel(*refs):
         for index in range(count):
             refs[-1][0, index * rows : (index + 1) * rows] = refs[index][0]
+
+    def spec(block):
+        return pl.BlockSpec((1, rows, lanes), lambda p: (p, block, 0))
 
     return pl.pallas_call(
         kernel,
         name=name,
         grid=(parts,),
-        in_specs=[pl.BlockSpec((1, rows, lanes), lambda p: (p, 0, 0))] * count,
+        in_specs=[spec(block) for _, block in pieces],
         out_specs=pl.BlockSpec((1, count * rows, lanes), lambda p: (p, 0, 0)),
         out_shape=jax.ShapeDtypeStruct((parts, count * rows, lanes), BF),
         compiler_params=params(),
         cost_estimate=cost(parts * count * rows * lanes),
-    )(*pieces)
+    )(*[array for array, _ in pieces])
 
 
 def sum_rows(jobs, rows, name="sum_rows"):
@@ -850,22 +853,34 @@
 
 
 class Gather:
-    def __init__(self, cube, shard, flip):
+    def __init__(self, cube, shard, flip, joined=False):
         self.cube = cube
-        self.masks = [0]
+        self.rows = shard.shape[1]
+        self.masks = [[0]]
         self.pieces = [shard]
         self.todo = cube.outer[::-1] if flip else list(cube.outer)
+        self.joined = joined
+
+    def blocks(self, order):
+        spots = {
+            mask: (piece, index)
+            for piece, masks in zip(self.pieces, self.masks)
+            for index, mask in enumerate(masks)
+        }
+        return join_rows([spots[mask] for mask in order], self.rows)
 
     def move(self):
         bit = self.todo.pop(0)
-        self.masks = self.masks + [mask | (1 << bit) for mask in self.masks]
+        if self.joined and len(self.pieces) > 1:
+            order = [mask for masks in self.masks for mask in masks]
+            self.pieces, self.masks = [self.blocks(order)], [order]
+        self.masks = self.masks + [[mask | (1 << bit) for mask in masks] for masks in self.masks]
         self.pieces = self.pieces + [self.cube.swap(piece, bit) for piece in self.pieces]
 
     def join(self):
         while self.todo:
             self.move()
-        order = sorted(range(len(self.masks)), key=lambda i: self.cube.masks.index(self.masks[i]))
-        self.pieces = [join_rows([self.pieces[i] for i in order])]
+        self.pieces = [self.blocks(self.cube.masks[: self.cube.size // 2])]
 
     def weight(self):
         near = self.pieces[0]
@@ -992,8 +1007,8 @@
             shard, before = tie(shard, before)
         return lax.all_gather(shard, "sp", axis=0, tiled=False)
 
-    def fetch(value, cut):
-        return [Gather(cube, value[:, :, :cut], 0), Gather(cube, value[:, :, cut:], 1)]
+    def fetch(value, cut, joined=False):
+        return [Gather(cube, value[:, :, :cut], 0, joined), Gather(cube, value[:, :, cut:], 1, joined)]
 
     def advance(movers):
         for mover in movers:
@@ -1100,12 +1115,13 @@
     qkv_w = [mover.weight() for mover in qkv_m]
     projected = to_lanes(pre_attn, qkv_w)
     projected, fc2_z = tie(projected, fc2_z)
-    fc_m = [Gather(cube, fc1_z, 0), Gather(cube, fc2_z, 1)]
+    fc_m = [Gather(cube, fc1_z, 0, True), Gather(cube, fc2_z, 1, True)]
     hold(fc_m, *after_qkv)
     advance(fc_m)
     raw = exchange(projected.reshape(parts, micros, slots, 3 * lanes))
     cross_z = jnp.concatenate([pad_heads(side, local) for side in (w_out1.T, w_query2, w_out2.T)], 1)
-    cross_z = spread(pin(cross_z, *fc_m))
+    arrived = fc_m[0].pieces + fc_m[1].pieces
+    cross_z = spread(pin(cross_z, *arrived))
     text_own = jnp.dot(text.reshape(-1, features), text_turn, preferred_element_type=F32).astype(BF)
     text_own = jnp.pad(
         text_own.reshape(micros, text_slots, features), ((0, 0), (0, text_strip - text_slots), (0, 0))
@@ -1113,22 +1129,21 @@
     text_z = jnp.pad(pad_heads(w_text_kv.reshape(text_rows, -1), local), ((0, max(0, strip - text_rows)), (0, 0)))
     while fc_m[0].todo:
         advance(fc_m)
-    text_z = spread(text_z, cross_z)
-    text_all = spread(text_own, cross_z)
-    cross_m = fetch(cross_z, 2 * lanes)
+    text_z = spread(pin(text_z, *arrived))
+    text_all = spread(pin(text_own, *arrived))
+    cross_m = fetch(cross_z, 2 * lanes, True)
     advance(cross_m)
     raw, d_mlp, turn, text_turn = tie(raw, d_mlp, turn, text_turn)
-    text_m = Gather(cube, text_z[:, :text_rows], 1)
     attended, turned_q, turned_k, norms = self_forward(raw, counts, cosine, sine, gain_q, gain_k)
-    attended = bind(attended, *fc_m, *cross_m, text_m)
-    attended, text_all = tie(attended, text_all)
+    attended = bind(attended, *fc_m, *cross_m)
+    attended, text_all, text_z = tie(attended, text_all, text_z)
+    text_m = Gather(cube, text_z[:, :text_rows], 1, True)
     text_m.move()
     attended = exchange(attended).reshape(parts, rows, lanes)
     while cross_m[0].todo:
         advance(cross_m)
     join(fc_m)
-    hold(cross_m, attended)
-    attended = bind(attended, text_m, *fc_m)
+    attended = bind(attended, text_m, *fc_m, cross_m[0])
     while text_m.todo:
         text_m.move()
     join(cross_m[:1])
@@ -1141,13 +1156,14 @@
     stream1, pre_cross = to_features(
         attended, [out1_w], [stream, g_cross], [wide_shape, low_shape], next_norm
     )
-    pre_cross = bind(pre_cross, text_m, *cross_m[1:])
+    hold(fc_m, out1_w.far)
+    fc1_w, fc2_w = [mover.weight() for mover in fc_m]
     text_m.join()
     text_w = text_m.weight()
+    query2 = to_lanes(pre_cross, [query2_w]).reshape(parts, micros, slots, lanes)
+    query2 = bind(query2, *cross_m[1:])
     join(cross_m[1:])
     out2_w = cross_m[1].weight()
-    query2 = to_lanes(pre_cross, [query2_w]).reshape(parts, micros, slots, lanes)
-    fc1_w, fc2_w = [mover.weight() for mover in fc_m]
     text_kv = to_lanes(text_all, [text_w]).reshape(parts, parts, micros, text_strip, 2 * lanes)
     crossed = cross_forward(query2, text_kv, lengths, text_slots).reshape(parts, rows, lanes)
     stream2, pre_mlp = to_features(

time: 1410 us -> 1330 us (0.943)
  waiting for transfers between devices: 570 us -> 464 us
  Pallas kernels: 562 us -> 591 us
    ppermute x84 -> x79, waiting for transfers between devices: 422 us -> 355 us  [swap(): return lax.ppermute(value, axis, pairs)]
    all_to_all x4, waiting for transfers between devices: 46 us -> 24.8 us  [exchange(): return lax.all_to_all(value, 'sp', split_axis=0, concat_axis=0, tiled=True)]
    pallas_call x9 -> x14, Pallas kernels: 43.9 us -> 65 us  [join_rows(): pl.pallas_call(kernel, name=name, grid=(parts,), in_specs=[spec(block) fo...]
    all_gather x7, waiting for transfers between devices: 91.9 us -> 73.4 us  [spread(): return lax.all_gather(shard, 'sp', axis=0, tiled=False)]
    ppermute x84 -> x79, starting transfers between devices: 105 us -> 103 us  [swap(): return lax.ppermute(value, axis, pairs)]
  transfers between devices with their start and end apart: 102 -> 97, of which waited for: 49 -> 37; matrix products, arithmetic and copies ran while one was open for 8% -> 9% of each run, Pallas kernels for 37% -> 41%
where the time goes in v9:
time: 1330 us
  Pallas kernels  591 us (44%)
  waiting for transfers between devices  464 us (35%)
  starting transfers between devices  122 us (9%)
  other arithmetic  59.2 us (4%)
  local copies, waits for them, and re-layouts  56.8 us (4%)
  matrix products  18.4 us (1%)
  between operations  15.7 us (1%)
    ppermute x79, waiting for transfers between devices, swap(): return lax.ppermute(value, axis, pairs)  355 us
    ppermute x79, starting transfers between devices, swap(): return lax.ppermute(value, axis, pairs)  103 us
    pallas_call x18, Pallas kernels, sum_rows(): pl.pallas_call(kernel, name=name, grid=(parts,), in_specs=[spec(block, ar...  85.2 us
    pallas_call x6, Pallas kernels, to_features(): pl.pallas_call(kernel, name=name, grid=(parts,), in_specs=[pl.BlockSpec((...  78.3 us
    all_gather x7, waiting for transfers between devices, spread(): return lax.all_gather(shard, 'sp', axis=0, tiled=False)  73.4 us
    pallas_call x14, Pallas kernels, join_rows(): pl.pallas_call(kernel, name=name, grid=(parts,), in_specs=[spec(block) fo...  65 us
    pallas_call x2, Pallas kernels, mlp_backward(): pl.pallas_call(kernel, name='mlp_backward', grid=(parts, steps), in_specs...  63.6 us
    pallas_call x2, Pallas kernels, mlp_forward(): pl.pallas_call(kernel, name='mlp_forward', grid=(parts, steps), in_specs=...  57.6 us
  transfers between devices with their start and end apart: 97, of which 37 were waited for; matrix products, arithmetic and copies ran while one was open for 9% of the time, Pallas kernels for 41%

profile of v9, /device:TPU:0, one launch (start us, length us, event | category | flops | bytes accessed | tf_op | source)
XLA Modules:
  0.0 1328.1 jit_solution(5782958619014734786)
XLA Ops:
  17.2 13.9 %negate_select_fusion = (f32[2,1024,384]{2,1,0:T(8,128)}, f32[2,1024,384]{2,1,0:T(8,128)}) fusion(f32[384]{0:T(512)S(1)} %fusion.51, s32[2,1024]{1,0:T(2,128)S(1)} %and_select_fusion.2, s32[2,1024]{1,0:T(2,128)S(1)} %and_select_fusion.3, pred[384]{0:T(512)(128)(4,1)S(1)} %get-tuple-element.460, pred[384]{0:T(512)(128)(4,1)S(1)} %get-tuple-element.461), kind=kLoop, calls=%fused_computation.4 | loop fusion | flops 3932160 | bytes 6310144 | tf_op jit(solution)/shard_map/jit(_where)/select_n | solution.py:41
  62.5 22.1 %collective-permute-done.9 = f32[4,2,176]{2,1,0:T(2,128)S(1)} collective-permute-done((f32[4,2,176]{2,1,0:T(2,128)S(1)}, f32[4,2,176]{2,1,0:T(2,128)S(1)}, u32[]{:S(2)}, u32[]{:S(2)}) %collective-permute-start.9) | collective-permute-done | bytes 5664 | tf_op jit(solution)/shard_map/ppermute | solution.py:832
  108.4 15.2 %collective-permute-done.16.refs_1_ = bf16[4,176,640]{2,1,0:T(8,128)(2,1)} collective-permute-done((bf16[4,176,640]{2,1,0:T(8,128)(2,1)S(1)}, bf16[4,176,640]{2,1,0:T(8,128)(2,1)}, u32[]{:S(2)}, u32[]{:S(2)}) %collective-permute-start.16) | collective-permute-done | bytes 901152 | tf_op jit(solution)/shard_map/ppermute | solution.py:832
  124.9 18.7 %collective-permute-done.21.refs_2_ = bf16[4,176,512]{2,1,0:T(8,128)(2,1)} collective-permute-done((bf16[4,176,512]{2,1,0:T(8,128)(2,1)S(1)}, bf16[4,176,512]{2,1,0:T(8,128)(2,1)}, u32[]{:S(2)}, u32[]{:S(2)}) %collective-permute-start.21) | collective-permute-done | bytes 720928 | tf_op jit(solution)/shard_map/ppermute | solution.py:832
  145.6 14.6 %to_features.6 = (f32[2,512,704]{2,1,0:T(8,128)}, f32[2,512,704]{2,1,0:T(8,128)}, bf16[2,512,704]{2,1,0:T(8,128)(2,1)}) custom-call(bf16[4,512,768]{2,1,0:T(8,128)(2,1)} %side_by_side.1.refs_0_.refs_1_, bf16[4,704,384]{2,1,0:T(8,128)(2,1)} %join_rows.14.refs_1_.refs_0_, bf16[4,704,384]{2,1,0:T(8,128)(2,1)} %collective-permute-done.11.refs_2_.refs_1_, ...), custom_call_target="tpu_custom_call" | custom-call | flops 276824064 | bytes 276824 | tf_op jit(solution)/shard_map/to_features/pallas_call | solution.py:401
  184.5 13.0 to_lanes.5
  197.5 14.3 %all-gather.21.cloned.1.call-done = bf16[704,1536]{1,0:T(8,128)(2,1)} async-done(((bf16[176,1536]{1,0:T(8,128)(2,1)}), bf16[704,1536]{1,0:T(8,128)(2,1)}) %all-gather.21.cloned.1.call-update) | async-done | bytes 2162704 | tf_op jit(solution)/shard_map/all_gather | solution.py:1008
  228.7 32.2 %collective-permute-done.26.refs_1_ = bf16[4,176,1536]{2,1,0:T(8,128)(2,1)} collective-permute-done((bf16[4,176,1536]{2,1,0:T(8,128)(2,1)}, bf16[4,176,1536]{2,1,0:T(8,128)(2,1)}, u32[]{:S(2)}, u32[]{:S(2)}) %collective-permute-start.26) | collective-permute-done | bytes 2162720 | tf_op jit(solution)/shard_map/ppermute | solution.py:832
  293.7 42.7 %all-gather.23.cloned.1.call-done = bf16[704,1152]{1,0:T(8,128)(2,1)} async-done(((bf16[176,1152]{1,0:T(8,128)(2,1)}), bf16[704,1152]{1,0:T(8,128)(2,1)}) %all-gather.23.cloned.1.call-update) | async-done | bytes 1622032 | tf_op jit(solution)/shard_map/all_gather | solution.py:1008
  355.3 34.8 %self_forward.1 = (bf16[4,2,256,384]{3,2,1,0:T(8,128)(2,1)}, bf16[2,1024,384]{2,1,0:T(8,128)(2,1)}, bf16[2,1024,384]{2,1,0:T(8,128)(2,1)}, f32[2,4,1024]{2,1,0:T(4,128)}) custom-call(s32[2]{0:T(128)} %copy-done.62, bf16[4,2,256,1152]{3,2,1,0:T(8,128)(2,1)} %all-to-all-done.raw_ref, f32[2,1024,384]{2,1,0:T(8,128)} %get-tuple-element.229.cos_ref, ...), custom_call_target="tpu_custom_call" | custom-call | flops 201326592 | bytes 201326 | tf_op jit(solution)/shard_map/self_forward/pallas_call | solution.py:150
  390.2 14.1 %all-gather.25.cloned.1.call-done = bf16[768,1024]{1,0:T(8,128)(2,1)} async-done(((bf16[192,1024]{1,0:T(8,128)(2,1)}), bf16[768,1024]{1,0:T(8,128)(2,1)}) %all-gather.25.cloned.1.call-update) | async-done | bytes 1572880 | tf_op jit(solution)/shard_map/all_gather | solution.py:1008
  429.5 48.0 %collective-permute-done.30.refs_1_ = bf16[4,128,768]{2,1,0:T(8,128)(2,1)} collective-permute-done((bf16[4,128,768]{2,1,0:T(8,128)(2,1)S(1)}, bf16[4,128,768]{2,1,0:T(8,128)(2,1)}, u32[]{:S(2)}, u32[]{:S(2)}) %collective-permute-start.30) | collective-permute-done | bytes 786464 | tf_op jit(solution)/shard_map/ppermute | solution.py:832
  500.1 32.0 %collective-permute-done.34.refs_1_.refs_3_ = bf16[4,256,768]{2,1,0:T(8,128)(2,1)S(1)} collective-permute-done((bf16[4,256,768]{2,1,0:T(8,128)(2,1)}, bf16[4,256,768]{2,1,0:T(8,128)(2,1)S(1)}, u32[]{:S(2)}, u32[]{:S(2)}) %collective-permute-start.34) | collective-permute-done | bytes 1572896 | tf_op jit(solution)/shard_map/ppermute | solution.py:832
  573.1 19.1 %cross_forward.1 = bf16[4,2,256,384]{3,2,1,0:T(8,128)(2,1)} custom-call(s32[2,2]{1,0:T(2,128)} %bitcast.214, bf16[4,2,256,384]{3,2,1,0:T(8,128)(2,1)} %bitcast.169, bf16[4,4,2,96,768]{4,3,2,1,0:T(8,128)(2,1)} %bitcast.160), custom_call_target="tpu_custom_call" | custom-call | flops 75497472 | bytes 75497 | tf_op jit(solution)/shard_map/cross_forward/pallas_call | solution.py:738
  602.7 28.7 %mlp_forward.2 = (f32[4,512,768]{2,1,0:T(8,128)}, bf16[4,512,768]{2,1,0:T(8,128)(2,1)}, f32[2,512,704]{2,1,0:T(8,128)}, bf16[4,704,768]{2,1,0:T(8,128)(2,1)}, bf16[4,704,768]{2,1,0:T(8,128)(2,1)}) custom-call(bf16[2,512,704]{2,1,0:T(8,128)(2,1)} %get-tuple-element.264.x_ref, bf16[2,512,704]{2,1,0:T(8,128)(2,1)} %fusion.65.g_ref, ...), custom_call_target="tpu_custom_call" | custom-call | flops 830472192 | bytes 830472 | tf_op jit(solution)/shard_map/mlp_forward/pallas_call | solution.py:609
  631.4 28.9 %mlp_forward.3 = (f32[4,512,768]{2,1,0:T(8,128)}, bf16[4,512,768]{2,1,0:T(8,128)(2,1)}, bf16[2,512,704]{2,1,0:T(8,128)(2,1)}, bf16[4,704,768]{2,1,0:T(8,128)(2,1)}, bf16[4,704,768]{2,1,0:T(8,128)(2,1)}) custom-call(bf16[2,512,704]{2,1,0:T(8,128)(2,1)} %get-tuple-element.264.x_ref, bf16[2,512,704]{2,1,0:T(8,128)(2,1)} %fusion.65.g_ref, ...), custom_call_target="tpu_custom_call" | custom-call | flops 830472192 | bytes 830472 | tf_op jit(solution)/shard_map/mlp_forward/pallas_call | solution.py:609
  660.9 29.1 %mlp_backward.2 = (bf16[4,704,768]{2,1,0:T(8,128)(2,1)}, bf16[4,704,768]{2,1,0:T(8,128)(2,1)}, f32[2,512,704]{2,1,0:T(8,128)}) custom-call(bf16[2,512,704]{2,1,0:T(8,128)(2,1)} %fusion.65.g_ref, bf16[2,512,704]{2,1,0:T(8,128)(2,1)} %get-tuple-element.264.x_ref, f32[4,512,768]{2,1,0:T(8,128)} %get-tuple-element.278.hid_ref, ...), custom_call_target="tpu_custom_call" | custom-call | flops 830472192 | bytes 830472 | tf_op jit(solution)/shard_map/mlp_backward/pallas_call | solution.py:681
  702.8 34.5 %mlp_backward.3 = (bf16[4,704,768]{2,1,0:T(8,128)(2,1)}, bf16[4,704,768]{2,1,0:T(8,128)(2,1)}, f32[2,512,704]{2,1,0:T(8,128)}, bf16[2,512,704]{2,1,0:T(8,128)(2,1)}, f32[2,1,704]{2,1,0:T(1,128)}) custom-call(bf16[2,512,704]{2,1,0:T(8,128)(2,1)} %fusion.65.g_ref, bf16[2,512,704]{2,1,0:T(8,128)(2,1)} %get-tuple-element.264.x_ref, ...), custom_call_target="tpu_custom_call" | custom-call | flops 830472192 | bytes 830472 | tf_op jit(solution)/shard_map/mlp_backward/pallas_call | solution.py:681
  761.6 22.6 %cross_backward.1 = (bf16[4,2,256,384]{3,2,1,0:T(8,128)(2,1)}, bf16[4,4,2,96,768]{4,3,2,1,0:T(8,128)(2,1)}) custom-call(s32[2,2]{1,0:T(2,128)} %bitcast.215, bf16[4,2,256,384]{3,2,1,0:T(8,128)(2,1)} %bitcast.170, bf16[4,4,2,96,768]{4,3,2,1,0:T(8,128)(2,1)} %bitcast.161, bf16[4,2,256,384]{3,2,1,0:T(8,128)(2,1)} %bitcast.173), custom_call_target="tpu_custom_call" | custom-call | flops 188743680 | bytes 188743 | tf_op jit(solution)/shard_map/cross_backward/pallas_call | solution.py:787
  794.4 12.8 to_features.9
  845.3 15.3 %terms_of.7 = (bf16[4,704,1152]{2,1,0:T(8,128)(2,1)}, bf16[4,704,1152]{2,1,0:T(8,128)(2,1)}) custom-call(bf16[2,512,704]{2,1,0:T(8,128)(2,1)} %get-tuple-element.311.x_ref.refs_0_, bf16[2,512,704]{2,1,0:T(8,128)(2,1)} %get-tuple-element.316.x_ref.refs_1_, bf16[2,512,704]{2,1,0:T(8,128)(2,1)} %get-tuple-element.290.x_ref.refs_2_, ...), custom_call_target="tpu_custom_call" | custom-call | flops 415236096 | bytes 415236 | tf_op jit(solution)/shard_map/terms_of/pallas_call | solution.py:445
  860.6 11.7 all-to-all-done.2.in_ref
  880.7 51.6 %self_backward.1 = (bf16[4,2,256,1152]{3,2,1,0:T(8,128)(2,1)}, f32[2,1,384]{2,1,0:T(1,128)}, f32[2,1,384]{2,1,0:T(1,128)}) custom-call(s32[2]{0:T(128)} %copy-done.62, bf16[4,2,256,1152]{3,2,1,0:T(8,128)(2,1)} %all-to-all-done.raw_ref, f32[2,1024,384]{2,1,0:T(8,128)} %get-tuple-element.229.cos_ref, f32[2,1024,384]{2,1,0:T(8,128)} %get-tuple-element.230.sin_ref, ...), custom_call_target="tpu_custom_call" | custom-call | flops 503316480 | bytes 503316 | tf_op jit(solution)/shard_map/self_backward/pallas_call | solution.py:260
  968.7 31.4 %collective-permute-done.54.refs_2_ = bf16[4,256,768]{2,1,0:T(8,128)(2,1)} collective-permute-done((bf16[4,256,768]{2,1,0:T(8,128)(2,1)}, bf16[4,256,768]{2,1,0:T(8,128)(2,1)}, u32[]{:S(2)}, u32[]{:S(2)}) %collective-permute-start.54) | collective-permute-done | bytes 1572896 | tf_op jit(solution)/shard_map/ppermute | solution.py:832
  1000.1 30.3 %collective-permute-done.52.refs_2_ = bf16[4,352,1152]{2,1,0:T(8,128)(2,1)} collective-permute-done((bf16[4,352,1152]{2,1,0:T(8,128)(2,1)}, bf16[4,352,1152]{2,1,0:T(8,128)(2,1)}, u32[]{:S(2)}, u32[]{:S(2)}) %collective-permute-start.52) | collective-permute-done | bytes 3244064 | tf_op jit(solution)/shard_map/ppermute | solution.py:832
  1030.4 13.1 all-to-all-done.3
  1070.7 13.9 %collective-permute-start.58 = (bf16[4,128,768]{2,1,0:T(8,128)(2,1)}, bf16[4,128,768]{2,1,0:T(8,128)(2,1)S(1)}, u32[]{:S(2)}, u32[]{:S(2)}) collective-permute-start(bf16[4,128,768]{2,1,0:T(8,128)(2,1)} %sum_rows.27), channel_id=1, source_target_pairs={{0,16},{4,20},{8,24},{12,28},{16,0},{20,4},{24,8},{28,12},{1,17},{... | collective-permute-start | bytes 2359304 | tf_op jit(solution)/shard_map/ppermute | solution.py:832
  1090.9 20.5 %to_features.11 = (bf16[2,512,704]{2,1,0:T(8,128)(2,1)}, f32[2,2,704]{2,1,0:T(2,128)}, f32[2,1,704]{2,1,0:T(1,128)}, f32[2,1,704]{2,1,0:T(1,128)}) custom-call(bf16[4,512,1152]{2,1,0:T(8,128)(2,1)} %bitcast.61.refs_1_.refs_0_, bf16[4,704,640]{2,1,0:T(8,128)(2,1)} %join_rows.16.refs_0_.refs_1_, bf16[4,704,640]{2,1,0:T(8,128)(2,1)} %collective-permute-done.19.refs_1_.refs_2_, ...), custom_call_target="tpu_custom_call" | custom-call | flops 415236096 | bytes 415236 | tf_op jit(solution)/shard_map/to_features/pallas_call | solution.py:401
  1135.6 16.7 %collective-permute-done.60.refs_5_.refs_6_ = bf16[4,352,384]{2,1,0:T(8,128)(2,1)S(1)} collective-permute-done((bf16[4,352,384]{2,1,0:T(8,128)(2,1)S(1)}, bf16[4,352,384]{2,1,0:T(8,128)(2,1)S(1)}, u32[]{:S(2)}, u32[]{:S(2)}) %collective-permute-start.60) | collective-permute-done | bytes 1081376 | tf_op jit(solution)/shard_map/ppermute | solution.py:832
  1152.3 17.1 %collective-permute-done.59.refs_2_ = bf16[4,352,768]{2,1,0:T(8,128)(2,1)} collective-permute-done((bf16[4,352,768]{2,1,0:T(8,128)(2,1)}, bf16[4,352,768]{2,1,0:T(8,128)(2,1)}, u32[]{:S(2)}, u32[]{:S(2)}) %collective-permute-start.59) | collective-permute-done | bytes 2162720 | tf_op jit(solution)/shard_map/ppermute | solution.py:832
  1225.9 23.6 %collective-permute-done.68 = f32[4,2,176]{2,1,0:T(2,128)S(1)} collective-permute-done((f32[4,2,176]{2,1,0:T(2,128)S(1)}, f32[4,2,176]{2,1,0:T(2,128)S(1)}, u32[]{:S(2)}, u32[]{:S(2)}) %collective-permute-start.68) | collective-permute-done | bytes 5664 | tf_op jit(solution)/shard_map/ppermute | solution.py:832
  1250.0 12.2 to_inputs.1
  (572 shorter events, 563.7 us)
Async XLA Ops:
  9.1 91.2 %all-gather.19.cloned.1.call-start = ((), (), s32[]{:S(2)}) async-start(), calls=%async_computation.20 | async-start | bytes 2027520 | tf_op jit(solution)/shard_map/all_gather | solution.py:1008
  41.4 137.5 %all-gather.17.cloned.1.call-start = ((), (), s32[]{:S(2)}) async-start(), calls=%async_computation.19 | async-start | bytes 2703360 | tf_op jit(solution)/shard_map/all_gather | solution.py:1008
  90.1 121.7 %all-gather.21.cloned.1.call-start = ((), (), s32[]{:S(2)}) async-start(), calls=%async_computation.21 | async-start | bytes 2703360 | tf_op jit(solution)/shard_map/all_gather | solution.py:1008
  105.0 55.1 %collective-permute-start.17 = (bf16[4,176,640]{2,1,0:T(8,128)(2,1)S(1)}, bf16[4,176,640]{2,1,0:T(8,128)(2,1)}, u32[]{:S(2)}, u32[]{:S(2)}) collective-permute-start(bf16[4,176,640]{2,1,0:T(8,128)(2,1)S(1)} %slice.419.refs_0_), channel_id=1, source_target_pairs={{0,16},{4,20},{8,24},{12,28},{16,0},{20,4},{24,8},{28,12},{1,17},{... | collective-permute-start | bytes 2703368 | tf_op jit(solution)/shard_map/ppermute | solution.py:832
  213.3 142.0 %all-to-all-start = ((bf16[4,2,256,1152]{3,2,1,0:T(8,128)(2,1)}), bf16[4,2,256,1152]{3,2,1,0:T(8,128)(2,1)}, u32[]{:S(2)}, u32[]{:S(2)}) async-start(bf16[4,2,256,1152]{3,2,1,0:T(8,128)(2,1)} %bitcast.164), calls=%async_computation | async-start | bytes 9437184 | tf_op jit(solution)/shard_map/all_to_all | solution.py:1022
  218.4 117.9 %all-gather.23.cloned.1.call-start = ((), (), s32[]{:S(2)}) async-start(), calls=%async_computation.22 | async-start | bytes 2027520 | tf_op jit(solution)/shard_map/all_gather | solution.py:1008
  260.9 129.2 %all-gather.27.cloned.1.call-start = ((), (), s32[]{:S(2)}) async-start(), calls=%async_computation.24 | async-start | bytes 1351680 | tf_op jit(solution)/shard_map/all_gather | solution.py:1008
  265.7 124.3 %collective-permute-start.25 = (bf16[4,352,1536]{2,1,0:T(8,128)(2,1)}, bf16[4,352,1536]{2,1,0:T(8,128)(2,1)}, u32[]{:S(2)}, u32[]{:S(2)}) collective-permute-start(bf16[4,352,1536]{2,1,0:T(8,128)(2,1)} %join_rows.18.refs_0_.refs_1_), channel_id=1, source_target_pairs={{0,16},{4,20},{8,24},{12,28},{16,0},{20,4},{24,8},{28,12},{1,17},{... | collective-permute-start | bytes 12976136 | tf_op jit(solution)/shard_map/ppermute | solution.py:832
  272.0 118.1 %collective-permute-start.27 = (bf16[4,352,1536]{2,1,0:T(8,128)(2,1)}, bf16[4,352,1536]{2,1,0:T(8,128)(2,1)}, u32[]{:S(2)}, u32[]{:S(2)}) collective-permute-start(bf16[4,352,1536]{2,1,0:T(8,128)(2,1)} %join_rows.19.refs_0_.refs_2_), channel_id=1, source_target_pairs={{0,8},{4,12},{8,0},{12,4},{16,24},{20,28},{24,16},{28,20},{1,9},{5... | collective-permute-start | bytes 12976136 | tf_op jit(solution)/shard_map/ppermute | solution.py:832
  274.5 129.8 %all-gather.25.cloned.1.call-start = ((), (), s32[]{:S(2)}) async-start(), calls=%async_computation.23 | async-start | bytes 1966080 | tf_op jit(solution)/shard_map/all_gather | solution.py:1008
  404.3 73.2 %all-to-all-start.1 = ((bf16[4,2,256,384]{3,2,1,0:T(8,128)(2,1)}), bf16[4,2,256,384]{3,2,1,0:T(8,128)(2,1)S(1)}, u32[]{:S(2)}, u32[]{:S(2)}) async-start(bf16[4,2,256,384]{3,2,1,0:T(8,128)(2,1)} %get-tuple-element.240), calls=%async_computation.1 | async-start | bytes 3145728 | tf_op jit(solution)/shard_map/all_to_all | solution.py:1022
  407.8 524.5 %reduce-scatter.8.cloned.1.call-start = ((), (), s32[]{:S(2)}) async-start(), calls=%async_computation.11 | async-start | bytes 2703360 | tf_op jit(solution)/shard_map/reduce_scatter | solution.py:1180
  411.9 65.6 %collective-permute-start.31 = (bf16[4,352,768]{2,1,0:T(8,128)(2,1)}, bf16[4,352,768]{2,1,0:T(8,128)(2,1)}, u32[]{:S(2)}, u32[]{:S(2)}) collective-permute-start(bf16[4,352,768]{2,1,0:T(8,128)(2,1)} %join_rows.22.refs_0_.refs_1_), channel_id=1, source_target_pairs={{0,16},{4,20},{8,24},{12,28},{16,0},{20,4},{24,8},{28,12},{1,17},{... | collective-permute-start | bytes 6488072 | tf_op jit(solution)/shard_map/ppermute | solution.py:832
  414.6 62.9 %collective-permute-start.30 = (bf16[4,128,768]{2,1,0:T(8,128)(2,1)S(1)}, bf16[4,128,768]{2,1,0:T(8,128)(2,1)}, u32[]{:S(2)}, u32[]{:S(2)}) collective-permute-start(bf16[4,128,768]{2,1,0:T(8,128)(2,1)S(1)} %slice.342.refs_0_), channel_id=1, source_target_pairs={{0,16},{4,20},{8,24},{12,28},{16,0},{20,4},{24,8},{28,12},{1,17},{... | collective-permute-start | bytes 2359304 | tf_op jit(solution)/shard_map/ppermute | solution.py:832
  490.5 112.2 %collective-permute-start.37 = (bf16[4,704,1536]{2,1,0:T(8,128)(2,1)}, bf16[4,704,1536]{2,1,0:T(8,128)(2,1)}, u32[]{:S(2)}, u32[]{:S(2)}) collective-permute-start(bf16[4,704,1536]{2,1,0:T(8,128)(2,1)} %join_rows.20.n1_ref), channel_id=1, source_target_pairs={{0,4},{4,0},{8,12},{12,8},{16,20},{20,16},{24,28},{28,24},{1,5},{5... | collective-permute-start | bytes 25952264 | tf_op jit(solution)/shard_map/ppermute | solution.py:832
  490.6 112.0 %collective-permute-start.38 = (bf16[4,704,1536]{2,1,0:T(8,128)(2,1)}, bf16[4,704,1536]{2,1,0:T(8,128)(2,1)}, u32[]{:S(2)}, u32[]{:S(2)}) collective-permute-start(bf16[4,704,1536]{2,1,0:T(8,128)(2,1)} %join_rows.21.n2_ref), channel_id=1, source_target_pairs={{0,4},{4,0},{8,12},{12,8},{16,20},{20,16},{24,28},{28,24},{1,5},{5... | collective-permute-start | bytes 25952264 | tf_op jit(solution)/shard_map/ppermute | solution.py:832
  499.8 55.8 %collective-permute-start.33 = (bf16[4,352,384]{2,1,0:T(8,128)(2,1)}, bf16[4,352,384]{2,1,0:T(8,128)(2,1)S(1)}, u32[]{:S(2)}, u32[]{:S(2)}) collective-permute-start(bf16[4,352,384]{2,1,0:T(8,128)(2,1)} %join_rows.24.refs_0_.refs_2_), channel_id=1, source_target_pairs={{0,8},{4,12},{8,0},{12,4},{16,24},{20,28},{24,16},{28,20},{1,9},{5... | collective-permute-start | bytes 3244040 | tf_op jit(solution)/shard_map/ppermute | solution.py:832
  631.4 58.5 %collective-permute-start.39 = (bf16[4,704,768]{2,1,0:T(8,128)(2,1)}, bf16[4,704,768]{2,1,0:T(8,128)(2,1)}, u32[]{:S(2)}, u32[]{:S(2)}) collective-permute-start(bf16[4,704,768]{2,1,0:T(8,128)(2,1)} %get-tuple-element.281), channel_id=1, source_target_pairs={{0,4},{4,0},{8,12},{12,8},{16,20},{20,16},{24,28},{28,24},{1,5},{5... | collective-permute-start | bytes 12976136 | tf_op jit(solution)/shard_map/ppermute | solution.py:832
  702.8 104.4 %collective-permute-start.45 = (bf16[4,704,768]{2,1,0:T(8,128)(2,1)}, bf16[4,704,768]{2,1,0:T(8,128)(2,1)}, u32[]{:S(2)}, u32[]{:S(2)}) collective-permute-start(bf16[4,704,768]{2,1,0:T(8,128)(2,1)} %get-tuple-element.302), channel_id=1, source_target_pairs={{0,4},{4,0},{8,12},{12,8},{16,20},{20,16},{24,28},{28,24},{1,5},{5... | collective-permute-start | bytes 12976136 | tf_op jit(solution)/shard_map/ppermute | solution.py:832
  737.4 69.9 %collective-permute-start.46 = (bf16[4,704,768]{2,1,0:T(8,128)(2,1)}, bf16[4,704,768]{2,1,0:T(8,128)(2,1)}, u32[]{:S(2)}, u32[]{:S(2)}) collective-permute-start(bf16[4,704,768]{2,1,0:T(8,128)(2,1)} %get-tuple-element.303), channel_id=1, source_target_pairs={{0,4},{4,0},{8,12},{12,8},{16,20},{20,16},{24,28},{28,24},{1,5},{5... | collective-permute-start | bytes 12976136 | tf_op jit(solution)/shard_map/ppermute | solution.py:832
  824.9 107.4 %reduce-scatter.10.cloned.1.call-start = ((), (), s32[]{:S(2)}) async-start(), calls=%async_computation.12 | async-start | bytes 1966080 | tf_op jit(solution)/shard_map/reduce_scatter | solution.py:1180
  872.4 75.7 %collective-permute-start.51 = (bf16[4,704,1152]{2,1,0:T(8,128)(2,1)}, bf16[4,704,1152]{2,1,0:T(8,128)(2,1)}, u32[]{:S(2)}, u32[]{:S(2)}) collective-permute-start(bf16[4,704,1152]{2,1,0:T(8,128)(2,1)} %get-tuple-element.338), channel_id=1, source_target_pairs={{0,4},{4,0},{8,12},{12,8},{16,20},{20,16},{24,28},{28,24},{1,5},{5... | collective-permute-start | bytes 19464200 | tf_op jit(solution)/shard_map/ppermute | solution.py:832
  877.8 54.6 %collective-permute-start.49 = (bf16[4,176,768]{2,1,0:T(8,128)(2,1)}, bf16[4,176,768]{2,1,0:T(8,128)(2,1)S(1)}, u32[]{:S(2)}, u32[]{:S(2)}) collective-permute-start(bf16[4,176,768]{2,1,0:T(8,128)(2,1)} %get-tuple-element.334), channel_id=1, source_target_pairs={{0,8},{4,12},{8,0},{12,4},{16,24},{20,28},{24,16},{28,20},{1,9},{5... | collective-permute-start | bytes 3244040 | tf_op jit(solution)/shard_map/ppermute | solution.py:832
  879.2 53.2 %collective-permute-start.50 = (bf16[4,176,768]{2,1,0:T(8,128)(2,1)}, bf16[4,176,768]{2,1,0:T(8,128)(2,1)S(1)}, u32[]{:S(2)}, u32[]{:S(2)}) collective-permute-start(bf16[4,176,768]{2,1,0:T(8,128)(2,1)} %get-tuple-element.335), channel_id=1, source_target_pairs={{0,16},{4,20},{8,24},{12,28},{16,0},{20,4},{24,8},{28,12},{1,17},{... | collective-permute-start | bytes 3244040 | tf_op jit(solution)/shard_map/ppermute | solution.py:832
  933.7 109.7 %all-to-all-start.3 = ((bf16[4,2,256,1152]{3,2,1,0:T(8,128)(2,1)}), bf16[4,2,256,1152]{3,2,1,0:T(8,128)(2,1)}, u32[]{:S(2)}, u32[]{:S(2)}) async-start(bf16[4,2,256,1152]{3,2,1,0:T(8,128)(2,1)} %get-tuple-element.336), calls=%async_computation.5 | async-start | bytes 9437184 | tf_op jit(solution)/shard_map/all_to_all | solution.py:1022
  938.7 352.9 %reduce-scatter.20.cloned.1.call-start = ((), (), s32[]{:S(2)}) async-start(), calls=%async_computation.17 | async-start | bytes 2703360 | tf_op jit(solution)/shard_map/reduce_scatter | solution.py:1180
  953.2 77.1 %collective-permute-start.52 = (bf16[4,352,1152]{2,1,0:T(8,128)(2,1)}, bf16[4,352,1152]{2,1,0:T(8,128)(2,1)}, u32[]{:S(2)}, u32[]{:S(2)}) collective-permute-start(bf16[4,352,1152]{2,1,0:T(8,128)(2,1)} %sum_rows.23), channel_id=1, source_target_pairs={{0,16},{4,20},{8,24},{12,28},{16,0},{20,4},{24,8},{28,12},{1,17},{... | collective-permute-start | bytes 9732104 | tf_op jit(solution)/shard_map/ppermute | solution.py:832
  1054.7 244.2 %reduce-scatter.18.cloned.1.call-start = ((), (), s32[]{:S(2)}) async-start(), calls=%async_computation.16 | async-start | bytes 983040 | tf_op jit(solution)/shard_map/reduce_scatter | solution.py:1180
  1116.3 184.5 %reduce-scatter.16.cloned.1.call-start = ((), (), s32[]{:S(2)}) async-start(), calls=%async_computation.15 | async-start | bytes 2027520 | tf_op jit(solution)/shard_map/reduce_scatter | solution.py:1180
  1116.4 53.0 %collective-permute-start.59 = (bf16[4,352,768]{2,1,0:T(8,128)(2,1)}, bf16[4,352,768]{2,1,0:T(8,128)(2,1)}, u32[]{:S(2)}, u32[]{:S(2)}) collective-permute-start(bf16[4,352,768]{2,1,0:T(8,128)(2,1)} %get-tuple-element.359), channel_id=1, source_target_pairs={{0,16},{4,20},{8,24},{12,28},{16,0},{20,4},{24,8},{28,12},{1,17},{... | collective-permute-start | bytes 6488072 | tf_op jit(solution)/shard_map/ppermute | solution.py:832
  1127.6 177.7 %reduce-scatter.14.cloned.1.call-start = ((), (), s32[]{:S(2)}) async-start(), calls=%async_computation.14 | async-start | bytes 2027520 | tf_op jit(solution)/shard_map/reduce_scatter | solution.py:1180
  1215.1 104.5 %reduce-scatter.12.cloned.1.call-start = ((), (), s32[]{:S(2)}) async-start(), calls=%async_computation.13 | async-start | bytes 1351680 | tf_op jit(solution)/shard_map/reduce_scatter | solution.py:1180
  (138 other events, 2810.2 us)
Sparse Core Ops, SparseCore 0:
  10.2 31.1 all-gather.14
  42.9 37.8 all-gather.18
  90.3 46.0 all-gather.16
  166.3 45.4 all-gather.20
  261.1 75.2 all-gather.22
  338.3 28.2 all-gather.26
  368.7 35.4 all-gather.24
  794.6 57.3 reduce-scatter.7
  872.5 34.2 reduce-scatter.9
  1054.8 55.6 reduce-scatter.19
  1116.4 26.1 reduce-scatter.17
  1144.8 35.4 reduce-scatter.15
  1215.2 35.8 reduce-scatter.13
  1291.7 27.8 reduce-scatter.11

commit v10 on v9

--- a/solution.py
+++ b/solution.py
@@ -501,27 +501,27 @@
 
 
 def sum_rows(jobs, rows, name="sum_rows"):
-    parts = jobs[0][0][0].shape[0]
+    parts = jobs[0][1][0][0].shape[0]
     if rows % 16:
         results = []
-        for terms in jobs:
+        for lanes, terms in jobs:
             value = 0.0
-            for array, blocks in terms:
-                split = array.reshape(parts, -1, rows, array.shape[2])
+            for array, blocks, spot in terms:
+                split = array[:, :, spot * lanes : (spot + 1) * lanes].reshape(parts, -1, rows, lanes)
                 value = value + jnp.stack([split[:, block] for block in blocks], 1).astype(F32)
-            results.append(value.astype(BF).reshape(parts, -1, value.shape[3]))
+            results.append(value.astype(BF).reshape(parts, -1, lanes))
         return results
     spots = [
-        (array, blocks[index])
-        for terms in jobs
+        (array, blocks[index], spot, lanes)
+        for lanes, terms in jobs
         for index in range(len(terms[0][1]))
-        for array, blocks in terms
+        for array, blocks, spot in terms
     ]
 
     def kernel(*refs):
         at = 0
-        for spot, terms in enumerate(jobs):
-            out_ref = refs[len(spots) + spot]
+        for order, (_, terms) in enumerate(jobs):
+            out_ref = refs[len(spots) + order]
             for index in range(len(terms[0][1])):
                 value = refs[at][0].astype(F32)
                 for offset in range(1, len(terms)):
@@ -529,20 +529,20 @@
                 out_ref[0, index * rows : (index + 1) * rows] = value.astype(BF)
                 at += len(terms)
 
-    def spec(block, lanes):
-        return pl.BlockSpec((1, rows, lanes), lambda p: (p, block, 0))
-
-    shapes = [(len(terms[0][1]) * rows, terms[0][0].shape[2]) for terms in jobs]
+    def spec(block, spot, lanes):
+        return pl.BlockSpec((1, rows, lanes), lambda p: (p, block, spot))
+
+    shapes = [(len(terms[0][1]) * rows, lanes) for lanes, terms in jobs]
     return pl.pallas_call(
         kernel,
         name=name,
         grid=(parts,),
-        in_specs=[spec(block, array.shape[2]) for array, block in spots],
+        in_specs=[spec(*rest) for _, *rest in spots],
         out_specs=[pl.BlockSpec((1, *shape), lambda p: (p, 0, 0)) for shape in shapes],
         out_shape=[jax.ShapeDtypeStruct((parts, *shape), BF) for shape in shapes],
         compiler_params=params(),
         cost_estimate=cost(sum(parts * size * lanes for size, lanes in shapes)),
-    )(*[array for array, _ in spots])
+    )(*[array for array, *_ in spots])
 
 
 def side_by_side(left, right, kept, lanes):
@@ -570,7 +570,7 @@
     _, rows, half = rows_in.shape
     parts, _, lanes = weight1.near.shape
     ff = lanes // 2
-    step = 384 if ff % 384 == 0 else ff
+    step = 768 if ff % 768 == 0 else ff
     steps = ff // step
     extras = [] if live is None else [live]
 
@@ -638,7 +638,7 @@
     _, rows, half = rows_in.shape
     parts, _, lanes = weight1.near.shape
     ff = lanes // 2
-    step = 384 if ff % 384 == 0 else ff
+    step = 768 if ff % 768 == 0 else ff
     steps = ff // step
     extras = list(finish or []) + ([] if start is None else [start])
 
@@ -888,23 +888,32 @@
 
 
 class Scatter:
-    def __init__(self, cube, near, far, flip):
+    def __init__(self, cube, near, other, flip, lanes=None, spot=0):
         self.cube = cube
         self.todo = list(cube.outer) if flip else cube.outer[::-1]
         self.rows = near.shape[1] // (cube.size // 2)
         self.places = list(range(cube.size // 2))
         self.near = near
+        self.lanes = lanes or near.shape[2]
+        self.spot = spot
         self.got = []
-        self.pieces = [cube.swap(far, 0)]
+        self.pieces = [other]
         self.arriving = self.places
 
     def job(self, places):
-        return [(self.near, places)] + [
-            (value, [held.index(place) for place in places]) for value, held in self.got
-        ]
+        terms = [(self.near, places, self.spot)]
+        for value, held, spot in self.got:
+            terms.append((value, [held.index(place) for place in places], spot))
+        return self.lanes, terms
 
     def absorb(self):
-        self.got.append((self.pieces[0], self.arriving))
+        self.got.append((self.pieces[0], self.arriving, 0 if self.got else self.spot))
+
+
+def scatter(cube, terms, *shares):
+    near, far = terms
+    other = cube.swap(far, 0)
+    return [Scatter(cube, near, other, flip, lanes, spot) for lanes, spot, flip in shares]
 
 
 def pack(movers):
@@ -1131,13 +1140,13 @@
         advance(fc_m)
     text_z = spread(pin(text_z, *arrived))
     text_all = spread(pin(text_own, *arrived))
+    cross_z, d_mlp, turn, text_turn = tie(cross_z, d_mlp, turn, text_turn)
     cross_m = fetch(cross_z, 2 * lanes, True)
     advance(cross_m)
-    raw, d_mlp, turn, text_turn = tie(raw, d_mlp, turn, text_turn)
     attended, turned_q, turned_k, norms = self_forward(raw, counts, cosine, sine, gain_q, gain_k)
     attended = bind(attended, *fc_m, *cross_m)
     attended, text_all, text_z = tie(attended, text_all, text_z)
-    text_m = Gather(cube, text_z[:, :text_rows], 1, True)
+    text_m = Gather(cube, text_z[:, :text_rows], 0, True)
     text_m.move()
     attended = exchange(attended).reshape(parts, rows, lanes)
     while cross_m[0].todo:
@@ -1158,6 +1167,7 @@
     )
     hold(fc_m, out1_w.far)
     fc1_w, fc2_w = [mover.weight() for mover in fc_m]
+    hold([text_m], pre_cross)
     text_m.join()
     text_w = text_m.weight()
     query2 = to_lanes(pre_cross, [query2_w]).reshape(parts, micros, slots, lanes)
@@ -1171,7 +1181,8 @@
     )
     hidden0, activ0, partial, fc2_n0, fc2_f0 = mlp_forward(pre_mlp, d_mlp, stream2, fc1_w, fc2_w, 0)
     hidden1, activ1, result, fc2_n1, fc2_f1 = mlp_forward(pre_mlp, d_mlp, partial, fc1_w, fc2_w, 1, live)
-    fc2_s = [Scatter(cube, fc2_n0, fc2_f0, 0), Scatter(cube, fc2_n1, fc2_f1, 1)]
+    share = fc2_n0.shape[2]
+    fc2_s = scatter(cube, (fc2_n0, fc2_f0), (share, 0, 0)) + scatter(cube, (fc2_n1, fc2_f1), (share, 0, 1))
 
     def settle(values, before=None):
         value = values[0] if len(values) == 1 else jnp.concatenate(values, 2)
@@ -1180,14 +1191,14 @@
         return lax.psum_scatter(value, "sp", scatter_dimension=0, tiled=False)
 
     fc1_n0, fc1_f0, partial = mlp_backward(d_mlp, pre_mlp, hidden0, fc1_w, fc2_w, 0, None)
-    fc1_s = [Scatter(cube, fc1_n0, fc1_f0, 0)]
+    fc1_s = scatter(cube, (fc1_n0, fc1_f0), (share, 0, 0))
     pack(fc2_s)
     partial = bind(partial, *fc2_s)
     send(fc2_s)
     fc1_n1, fc1_f1, grad2, d_cross, d_gain_mlp = mlp_backward(
         d_mlp, pre_mlp, hidden1, fc1_w, fc2_w, 1, partial, [stream2, g_mlp, grad3]
     )
-    fc1_s.append(Scatter(cube, fc1_n1, fc1_f1, 1))
+    fc1_s += scatter(cube, (fc1_n1, fc1_f1), (share, 0, 1))
     d_cross = bind(d_cross, *fc2_s)
     d_crossed = to_lanes(d_cross, [out2_w])
     pack(fc2_s)
@@ -1231,7 +1242,8 @@
     cross_t = list(cross_t)
     d_heads, d_words, text_t[1], cross_t[1] = tie(d_heads, d_words, text_t[1], cross_t[1])
     d_words = settle([d_words])
-    text_s, cross_s = Scatter(cube, *text_t, 1), Scatter(cube, *cross_t, 0)
+    text_s = scatter(cube, text_t, (lanes, 0, 0), (lanes, 1, 1))
+    cross_s = scatter(cube, cross_t, (2 * lanes, 0, 0), (lanes, 2, 1))
     d_heads = bind(d_heads, *fc1_s)
     pack(fc1_s)
     d_heads = bind(d_heads, *fc1_s)
@@ -1242,19 +1254,17 @@
     d_raw, term_fc2, d_words = tie(d_raw, term_fc2, d_words)
     d_raw = bind(d_raw, *fc1_s)
     d_projected = exchange(d_raw).reshape(parts, rows, 3 * lanes)
-    other_s = [cross_s, text_s]
+    other_s = cross_s + text_s
     total_fc1 = results(fc1_s)
-    pack([cross_s])
-    pack([text_s])
+    pack(cross_s)
+    pack(text_s)
     send(other_s)
     d_projected = bind(d_projected, *other_s)
     term_fc1 = settle(total_fc1, d_projected)
-    qkv_s = [
-        Scatter(cube, *terms_of([(pre_attn, d_projected, 2 * lanes, 0)]), 0),
-        Scatter(cube, *terms_of([(pre_attn, d_projected, lanes, 2)]), 1),
-    ]
-    pack([cross_s])
-    pack([text_s])
+    qkv_t = terms_of([(pre_attn, d_projected, 3 * lanes, 0)])
+    qkv_s = scatter(cube, qkv_t, (2 * lanes, 0, 0), (lanes, 2, 1))
+    pack(cross_s)
+    pack(text_s)
     send(other_s)
     pack(qkv_s)
     d_projected = bind(d_projected, *qkv_s)
@@ -1283,16 +1293,17 @@
         last_norms,
     )
     d_base = bind(d_base, *other_s)
-    skip_t = [list(terms_of([(d_base, joined, skip_cut, flip)])) for flip in range(2)]
-    skip_t[0][1] = bind(skip_t[0][1], *qkv_s)
-    skip_s = [Scatter(cube, *pair, flip) for flip, pair in enumerate(skip_t)]
+    skip_t = terms_of([(d_base, joined, skip_lanes, 0)])
+    skip_s = scatter(cube, skip_t, (skip_cut, 0, 0), (skip_cut, 1, 1))
+    pack(skip_s)
     pack(qkv_s)
+    skip_s[0].pieces[0] = bind(skip_s[0].pieces[0], *qkv_s)
     send(qkv_s)
-    pack(skip_s)
-    term_cross, term_text = settle(results([cross_s])), settle(results([text_s]))
     send(skip_s)
-    term_qkv = settle(results(qkv_s))
-    term_skip = settle(results(skip_s))
+    term_cross, term_text = settle(results(cross_s)), settle(results(text_s))
+    total_qkv = results(qkv_s)
+    term_qkv = settle(total_qkv)
+    term_skip = settle(results(skip_s), total_qkv[0])
     d_joined = to_inputs(d_base, skip_w, kept)
     result = (
         jnp.dot(result[0], turn[:, :middle].T, preferred_element_type=F32)

time: 1330 us -> 1300 us (0.977)
  Pallas kernels: 591 us -> 567 us
    all_to_all x4, waiting for transfers between devices: 24.8 us -> 38.8 us  [exchange(): return lax.all_to_all(value, 'sp', split_axis=0, concat_axis=0, tiled=True)]
    pallas_call x6 -> x4, Pallas kernels: 54.1 us -> 45.3 us  [terms_of(): pl.pallas_call(kernel, name=name, grid=(parts,), in_specs=[full(pair[0].s...]
    ppermute x79 -> x81, starting transfers between devices: 103 us -> 99.5 us  [swap(): return lax.ppermute(value, axis, pairs)]
    ppermute x79 -> x81, waiting for transfers between devices: 355 us -> 352 us  [swap(): return lax.ppermute(value, axis, pairs)]
  transfers between devices with their start and end apart: 97 -> 99, of which waited for: 37 -> 46; matrix products, arithmetic and copies ran while one was open for 9% -> 9% of each run, Pallas kernels for 41% -> 40%
where the time goes in v10:
time: 1300 us; the launch traced here: 1290 us
  Pallas kernels  567 us (44%)
  waiting for transfers between devices  465 us (36%)
  starting transfers between devices  119 us (9%)
  other arithmetic  62.6 us (5%)
  local copies, waits for them, and re-layouts  50.7 us (4%)
  between operations  15.8 us (1%)
  matrix products  13 us (1%)
    ppermute x81, waiting for transfers between devices, swap(): return lax.ppermute(value, axis, pairs)  352 us
    ppermute x81, starting transfers between devices, swap(): return lax.ppermute(value, axis, pairs)  99.5 us
    pallas_call x18, Pallas kernels, sum_rows(): pl.pallas_call(kernel, name=name, grid=(parts,), in_specs=[spec(*rest) fo...  84.8 us
    pallas_call x6, Pallas kernels, to_features(): pl.pallas_call(kernel, name=name, grid=(parts,), in_specs=[pl.BlockSpec((...  78.3 us
    pallas_call x14, Pallas kernels, join_rows(): pl.pallas_call(kernel, name=name, grid=(parts,), in_specs=[spec(block) fo...  64.7 us
    all_gather x7, waiting for transfers between devices, spread(): return lax.all_gather(shard, 'sp', axis=0, tiled=False)  61.9 us
    pallas_call x2, Pallas kernels, mlp_backward(): pl.pallas_call(kernel, name='mlp_backward', grid=(parts, steps), in_specs...  54.3 us
    pallas_call x1, Pallas kernels, self_backward(): pl.pallas_call(kernel, name='self_backward', grid_spec=pltpu.PrefetchScal...  51.6 us
  transfers between devices with their start and end apart: 99, of which 46 were waited for; matrix products, arithmetic and copies ran while one was open for 9% of the time, Pallas kernels for 40%

profile of v10, /device:TPU:0, one launch (start us, length us, event | category | flops | bytes accessed | tf_op | source)
XLA Modules:
  0.0 1292.0 jit_solution(11338060475303224144)
XLA Ops:
  17.2 13.9 %negate_select_fusion = (f32[2,1024,384]{2,1,0:T(8,128)}, f32[2,1024,384]{2,1,0:T(8,128)}) fusion(f32[384]{0:T(512)S(1)} %fusion.51, s32[2,1024]{1,0:T(2,128)S(1)} %and_select_fusion.2, s32[2,1024]{1,0:T(2,128)S(1)} %and_select_fusion.3, pred[384]{0:T(512)(128)(4,1)S(1)} %get-tuple-element.490, pred[384]{0:T(512)(128)(4,1)S(1)} %get-tuple-element.491), kind=kLoop, calls=%fused_computation.4 | loop fusion | flops 3932160 | bytes 6310144 | tf_op jit(solution)/shard_map/jit(_where)/select_n | solution.py:41
  62.5 22.0 %collective-permute-done.9 = f32[4,2,176]{2,1,0:T(2,128)S(1)} collective-permute-done((f32[4,2,176]{2,1,0:T(2,128)S(1)}, f32[4,2,176]{2,1,0:T(2,128)S(1)}, u32[]{:S(2)}, u32[]{:S(2)}) %collective-permute-start.9) | collective-permute-done | bytes 5664 | tf_op jit(solution)/shard_map/ppermute | solution.py:832
  108.1 15.2 %collective-permute-done.16.refs_1_ = bf16[4,176,640]{2,1,0:T(8,128)(2,1)} collective-permute-done((bf16[4,176,640]{2,1,0:T(8,128)(2,1)S(1)}, bf16[4,176,640]{2,1,0:T(8,128)(2,1)}, u32[]{:S(2)}, u32[]{:S(2)}) %collective-permute-start.16) | collective-permute-done | bytes 901152 | tf_op jit(solution)/shard_map/ppermute | solution.py:832
  124.6 19.9 %collective-permute-done.21.refs_2_ = bf16[4,176,512]{2,1,0:T(8,128)(2,1)} collective-permute-done((bf16[4,176,512]{2,1,0:T(8,128)(2,1)S(1)}, bf16[4,176,512]{2,1,0:T(8,128)(2,1)}, u32[]{:S(2)}, u32[]{:S(2)}) %collective-permute-start.21) | collective-permute-done | bytes 720928 | tf_op jit(solution)/shard_map/ppermute | solution.py:832
  146.5 14.7 %to_features.6 = (f32[2,512,704]{2,1,0:T(8,128)}, f32[2,512,704]{2,1,0:T(8,128)}, bf16[2,512,704]{2,1,0:T(8,128)(2,1)}) custom-call(bf16[4,512,768]{2,1,0:T(8,128)(2,1)} %side_by_side.1.refs_0_.refs_1_, bf16[4,704,384]{2,1,0:T(8,128)(2,1)} %join_rows.14.refs_1_.refs_0_, bf16[4,704,384]{2,1,0:T(8,128)(2,1)} %collective-permute-done.11.refs_2_.refs_1_, ...), custom_call_target="tpu_custom_call" | custom-call | flops 276824064 | bytes 276824 | tf_op jit(solution)/shard_map/to_features/pallas_call | solution.py:401
  185.5 13.0 %to_lanes.5 = bf16[4,512,1152]{2,1,0:T(8,128)(2,1)} custom-call(bf16[2,512,704]{2,1,0:T(8,128)(2,1)} %get-tuple-element.229.x_ref.refs_0_, bf16[4,704,640]{2,1,0:T(8,128)(2,1)} %join_rows.16.refs_0_.refs_1_, bf16[4,704,640]{2,1,0:T(8,128)(2,1)} %collective-permute-done.19.refs_1_.refs_2_, bf16[4,704,512]{2,1,0:T(8,128)(2,1)} %join_rows.17.refs_2_.refs_3_, ...), custom_call_target="tpu_custom_call" | custom-call | flops 415236096 | bytes 415236 | tf_op jit(solution)/shard_map/to_lanes/pallas_call | solution.py:330
  198.4 14.4 %all-gather.21.cloned.1.call-done = bf16[704,1536]{1,0:T(8,128)(2,1)} async-done(((bf16[176,1536]{1,0:T(8,128)(2,1)}), bf16[704,1536]{1,0:T(8,128)(2,1)}) %all-gather.21.cloned.1.call-update) | async-done | bytes 2162704 | tf_op jit(solution)/shard_map/all_gather | solution.py:1017
  229.6 32.3 %collective-permute-done.26.refs_1_ = bf16[4,176,1536]{2,1,0:T(8,128)(2,1)} collective-permute-done((bf16[4,176,1536]{2,1,0:T(8,128)(2,1)}, bf16[4,176,1536]{2,1,0:T(8,128)(2,1)}, u32[]{:S(2)}, u32[]{:S(2)}) %collective-permute-start.26) | collective-permute-done | bytes 2162720 | tf_op jit(solution)/shard_map/ppermute | solution.py:832
  300.8 36.5 %all-gather.23.cloned.1.call-done = bf16[704,1152]{1,0:T(8,128)(2,1)} async-done(((bf16[176,1152]{1,0:T(8,128)(2,1)}), bf16[704,1152]{1,0:T(8,128)(2,1)}) %all-gather.23.cloned.1.call-update) | async-done | bytes 1622032 | tf_op jit(solution)/shard_map/all_gather | solution.py:1017
  351.5 34.9 %self_forward.1 = (bf16[4,2,256,384]{3,2,1,0:T(8,128)(2,1)}, bf16[2,1024,384]{2,1,0:T(8,128)(2,1)}, bf16[2,1024,384]{2,1,0:T(8,128)(2,1)}, f32[2,4,1024]{2,1,0:T(4,128)}) custom-call(s32[2]{0:T(128)} %copy-done.66, bf16[4,2,256,1152]{3,2,1,0:T(8,128)(2,1)} %all-to-all-done.raw_ref, f32[2,1024,384]{2,1,0:T(8,128)} %get-tuple-element.243.cos_ref, ...), custom_call_target="tpu_custom_call" | custom-call | flops 201326592 | bytes 201326 | tf_op jit(solution)/shard_map/self_forward/pallas_call | solution.py:150
  434.6 27.2 %collective-permute-done.31.refs_2_.refs_3_ = bf16[4,352,768]{2,1,0:T(8,128)(2,1)} collective-permute-done((bf16[4,352,768]{2,1,0:T(8,128)(2,1)}, bf16[4,352,768]{2,1,0:T(8,128)(2,1)}, u32[]{:S(2)}, u32[]{:S(2)}) %collective-permute-start.31) | collective-permute-done | bytes 2162720 | tf_op jit(solution)/shard_map/ppermute | solution.py:832
  496.5 19.1 %collective-permute-done.34.refs_2_.refs_3_ = bf16[4,256,768]{2,1,0:T(8,128)(2,1)S(1)} collective-permute-done((bf16[4,256,768]{2,1,0:T(8,128)(2,1)}, bf16[4,256,768]{2,1,0:T(8,128)(2,1)S(1)}, u32[]{:S(2)}, u32[]{:S(2)}) %collective-permute-start.34) | collective-permute-done | bytes 1572896 | tf_op jit(solution)/shard_map/ppermute | solution.py:832
  545.5 19.1 %cross_forward.1 = bf16[4,2,256,384]{3,2,1,0:T(8,128)(2,1)} custom-call(s32[2,2]{1,0:T(2,128)} %bitcast.214, bf16[4,2,256,384]{3,2,1,0:T(8,128)(2,1)} %bitcast.169, bf16[4,4,2,96,768]{4,3,2,1,0:T(8,128)(2,1)} %bitcast.160), custom_call_target="tpu_custom_call" | custom-call | flops 75497472 | bytes 75497 | tf_op jit(solution)/shard_map/cross_forward/pallas_call | solution.py:738
  575.1 26.0 %mlp_forward.2 = (f32[4,512,768]{2,1,0:T(8,128)}, bf16[4,512,768]{2,1,0:T(8,128)(2,1)}, f32[2,512,704]{2,1,0:T(8,128)}, bf16[4,704,768]{2,1,0:T(8,128)(2,1)}, bf16[4,704,768]{2,1,0:T(8,128)(2,1)}) custom-call(bf16[2,512,704]{2,1,0:T(8,128)(2,1)} %get-tuple-element.281.x_ref, bf16[2,512,704]{2,1,0:T(8,128)(2,1)} %fusion.65.g_ref, ...), custom_call_target="tpu_custom_call" | custom-call | flops 830472192 | bytes 830472 | tf_op jit(solution)/shard_map/mlp_forward/pallas_call | solution.py:609
  601.1 25.5 %mlp_forward.3 = (f32[4,512,768]{2,1,0:T(8,128)}, bf16[4,512,768]{2,1,0:T(8,128)(2,1)}, bf16[2,512,704]{2,1,0:T(8,128)(2,1)}, bf16[4,704,768]{2,1,0:T(8,128)(2,1)}, bf16[4,704,768]{2,1,0:T(8,128)(2,1)}) custom-call(bf16[2,512,704]{2,1,0:T(8,128)(2,1)} %get-tuple-element.281.x_ref, bf16[2,512,704]{2,1,0:T(8,128)(2,1)} %fusion.65.g_ref, ...), custom_call_target="tpu_custom_call" | custom-call | flops 830472192 | bytes 830472 | tf_op jit(solution)/shard_map/mlp_forward/pallas_call | solution.py:609
  627.1 24.6 %mlp_backward.2 = (bf16[4,704,768]{2,1,0:T(8,128)(2,1)}, bf16[4,704,768]{2,1,0:T(8,128)(2,1)}, f32[2,512,704]{2,1,0:T(8,128)}) custom-call(bf16[2,512,704]{2,1,0:T(8,128)(2,1)} %fusion.65.g_ref, bf16[2,512,704]{2,1,0:T(8,128)(2,1)} %get-tuple-element.281.x_ref, f32[4,512,768]{2,1,0:T(8,128)} %get-tuple-element.295.hid_ref, ...), custom_call_target="tpu_custom_call" | custom-call | flops 830472192 | bytes 830472 | tf_op jit(solution)/shard_map/mlp_backward/pallas_call | solution.py:681
  664.4 29.6 %mlp_backward.3 = (bf16[4,704,768]{2,1,0:T(8,128)(2,1)}, bf16[4,704,768]{2,1,0:T(8,128)(2,1)}, f32[2,512,704]{2,1,0:T(8,128)}, bf16[2,512,704]{2,1,0:T(8,128)(2,1)}, f32[2,1,704]{2,1,0:T(1,128)}) custom-call(bf16[2,512,704]{2,1,0:T(8,128)(2,1)} %fusion.65.g_ref, bf16[2,512,704]{2,1,0:T(8,128)(2,1)} %get-tuple-element.281.x_ref, ...), custom_call_target="tpu_custom_call" | custom-call | flops 830472192 | bytes 830472 | tf_op jit(solution)/shard_map/mlp_backward/pallas_call | solution.py:681
  694.6 12.3 collective-permute-done.41.refs_2_
  723.1 22.6 %cross_backward.1 = (bf16[4,2,256,384]{3,2,1,0:T(8,128)(2,1)}, bf16[4,4,2,96,768]{4,3,2,1,0:T(8,128)(2,1)}) custom-call(s32[2,2]{1,0:T(2,128)} %bitcast.215, bf16[4,2,256,384]{3,2,1,0:T(8,128)(2,1)} %bitcast.170, bf16[4,4,2,96,768]{4,3,2,1,0:T(8,128)(2,1)} %bitcast.161, bf16[4,2,256,384]{3,2,1,0:T(8,128)(2,1)} %bitcast.173), custom_call_target="tpu_custom_call" | custom-call | flops 188743680 | bytes 188743 | tf_op jit(solution)/shard_map/cross_backward/pallas_call | solution.py:787
  755.9 12.8 to_features.9
  806.8 15.3 %terms_of.5 = (bf16[4,704,1152]{2,1,0:T(8,128)(2,1)}, bf16[4,704,1152]{2,1,0:T(8,128)(2,1)}) custom-call(bf16[2,512,704]{2,1,0:T(8,128)(2,1)} %get-tuple-element.328.x_ref.refs_0_, bf16[2,512,704]{2,1,0:T(8,128)(2,1)} %get-tuple-element.333.x_ref.refs_1_, bf16[2,512,704]{2,1,0:T(8,128)(2,1)} %get-tuple-element.307.x_ref.refs_2_, ...), custom_call_target="tpu_custom_call" | custom-call | flops 415236096 | bytes 415236 | tf_op jit(solution)/shard_map/terms_of/pallas_call | solution.py:445
  822.1 11.7 all-to-all-done.2.in_ref
  842.1 51.6 %self_backward.1 = (bf16[4,2,256,1152]{3,2,1,0:T(8,128)(2,1)}, f32[2,1,384]{2,1,0:T(1,128)}, f32[2,1,384]{2,1,0:T(1,128)}) custom-call(s32[2]{0:T(128)} %copy-done.66, bf16[4,2,256,1152]{3,2,1,0:T(8,128)(2,1)} %all-to-all-done.raw_ref, f32[2,1024,384]{2,1,0:T(8,128)} %get-tuple-element.243.cos_ref, f32[2,1024,384]{2,1,0:T(8,128)} %get-tuple-element.244.sin_ref, ...), custom_call_target="tpu_custom_call" | custom-call | flops 503316480 | bytes 503316 | tf_op jit(solution)/shard_map/self_backward/pallas_call | solution.py:260
  900.2 14.2 %collective-permute-start.54 = (bf16[4,512,768]{2,1,0:T(8,128)(2,1)}, bf16[4,512,768]{2,1,0:T(8,128)(2,1)}, u32[]{:S(2)}, u32[]{:S(2)}) collective-permute-start(bf16[4,512,768]{2,1,0:T(8,128)(2,1)} %get-tuple-element.359), channel_id=1, source_target_pairs={{0,4},{4,0},{8,12},{12,8},{16,20},{20,16},{24,28},{28,24},{1,5},{5... | collective-permute-start | bytes 9437192 | tf_op jit(solution)/shard_map/ppermute | solution.py:832
  927.5 58.0 %collective-permute-done.55.refs_2_ = bf16[4,256,384]{2,1,0:T(8,128)(2,1)S(1)} collective-permute-done((bf16[4,256,384]{2,1,0:T(8,128)(2,1)}, bf16[4,256,384]{2,1,0:T(8,128)(2,1)S(1)}, u32[]{:S(2)}, u32[]{:S(2)}) %collective-permute-start.55) | collective-permute-done | bytes 786464 | tf_op jit(solution)/shard_map/ppermute | solution.py:832
  985.5 19.4 %all-to-all-done.3 = bf16[4,2,256,1152]{3,2,1,0:T(8,128)(2,1)} async-done(((bf16[4,2,256,1152]{3,2,1,0:T(8,128)(2,1)}), bf16[4,2,256,1152]{3,2,1,0:T(8,128)(2,1)}, u32[]{:S(2)}, u32[]{:S(2)}) %all-to-all-start.3) | async-done | bytes 4718624 | tf_op jit(solution)/shard_map/all_to_all | solution.py:1031
  1050.5 20.5 %to_features.11 = (bf16[2,512,704]{2,1,0:T(8,128)(2,1)}, f32[2,2,704]{2,1,0:T(2,128)}, f32[2,1,704]{2,1,0:T(1,128)}, f32[2,1,704]{2,1,0:T(1,128)}) custom-call(bf16[4,512,1152]{2,1,0:T(8,128)(2,1)} %bitcast.61.refs_1_.refs_0_, bf16[4,704,640]{2,1,0:T(8,128)(2,1)} %join_rows.16.refs_0_.refs_1_, bf16[4,704,640]{2,1,0:T(8,128)(2,1)} %collective-permute-done.19.refs_1_.refs_2_, ...), custom_call_target="tpu_custom_call" | custom-call | flops 415236096 | bytes 415236 | tf_op jit(solution)/shard_map/to_features/pallas_call | solution.py:401
  1098.6 23.8 %collective-permute-done.64.refs_5_.refs_6_ = bf16[4,352,384]{2,1,0:T(8,128)(2,1)S(1)} collective-permute-done((bf16[4,352,384]{2,1,0:T(8,128)(2,1)S(1)}, bf16[4,352,384]{2,1,0:T(8,128)(2,1)S(1)}, u32[]{:S(2)}, u32[]{:S(2)}) %collective-permute-start.64) | collective-permute-done | bytes 1081376 | tf_op jit(solution)/shard_map/ppermute | solution.py:832
  1122.4 15.8 %collective-permute-done.63.refs_2_ = bf16[4,352,768]{2,1,0:T(8,128)(2,1)} collective-permute-done((bf16[4,352,768]{2,1,0:T(8,128)(2,1)}, bf16[4,352,768]{2,1,0:T(8,128)(2,1)}, u32[]{:S(2)}, u32[]{:S(2)}) %collective-permute-start.63) | collective-permute-done | bytes 2162720 | tf_op jit(solution)/shard_map/ppermute | solution.py:832
  1157.9 16.4 %collective-permute-done.65.refs_2_ = bf16[4,352,384]{2,1,0:T(8,128)(2,1)S(1)} collective-permute-done((bf16[4,352,384]{2,1,0:T(8,128)(2,1)}, bf16[4,352,384]{2,1,0:T(8,128)(2,1)S(1)}, u32[]{:S(2)}, u32[]{:S(2)}) %collective-permute-start.65) | collective-permute-done | bytes 1081376 | tf_op jit(solution)/shard_map/ppermute | solution.py:832
  1185.9 11.8 collective-permute-done.69.refs_3_
  1234.1 12.4 to_inputs.1
  (584 shorter events, 569.8 us)
Async XLA Ops:
  9.1 90.9 %all-gather.19.cloned.1.call-start = ((), (), s32[]{:S(2)}) async-start(), calls=%async_computation.20 | async-start | bytes 2027520 | tf_op jit(solution)/shard_map/all_gather | solution.py:1017
  41.5 138.4 %all-gather.17.cloned.1.call-start = ((), (), s32[]{:S(2)}) async-start(), calls=%async_computation.19 | async-start | bytes 2703360 | tf_op jit(solution)/shard_map/all_gather | solution.py:1017
  90.1 122.7 %all-gather.21.cloned.1.call-start = ((), (), s32[]{:S(2)}) async-start(), calls=%async_computation.21 | async-start | bytes 2703360 | tf_op jit(solution)/shard_map/all_gather | solution.py:1017
  106.0 55.2 %collective-permute-start.17 = (bf16[4,176,640]{2,1,0:T(8,128)(2,1)S(1)}, bf16[4,176,640]{2,1,0:T(8,128)(2,1)}, u32[]{:S(2)}, u32[]{:S(2)}) collective-permute-start(bf16[4,176,640]{2,1,0:T(8,128)(2,1)S(1)} %slice.419.refs_0_), channel_id=1, source_target_pairs={{0,16},{4,20},{8,24},{12,28},{16,0},{20,4},{24,8},{28,12},{1,17},{... | collective-permute-start | bytes 2703368 | tf_op jit(solution)/shard_map/ppermute | solution.py:832
  214.3 137.3 %all-to-all-start = ((bf16[4,2,256,1152]{3,2,1,0:T(8,128)(2,1)}), bf16[4,2,256,1152]{3,2,1,0:T(8,128)(2,1)}, u32[]{:S(2)}, u32[]{:S(2)}) async-start(bf16[4,2,256,1152]{3,2,1,0:T(8,128)(2,1)} %bitcast.164), calls=%async_computation | async-start | bytes 9437184 | tf_op jit(solution)/shard_map/all_to_all | solution.py:1031
  219.4 117.9 %all-gather.23.cloned.1.call-start = ((), (), s32[]{:S(2)}) async-start(), calls=%async_computation.22 | async-start | bytes 2027520 | tf_op jit(solution)/shard_map/all_gather | solution.py:1017
  261.9 134.6 %all-gather.27.cloned.1.call-start = ((), (), s32[]{:S(2)}) async-start(), calls=%async_computation.24 | async-start | bytes 1351680 | tf_op jit(solution)/shard_map/all_gather | solution.py:1017
  272.8 113.6 %collective-permute-start.25 = (bf16[4,352,1536]{2,1,0:T(8,128)(2,1)}, bf16[4,352,1536]{2,1,0:T(8,128)(2,1)}, u32[]{:S(2)}, u32[]{:S(2)}) collective-permute-start(bf16[4,352,1536]{2,1,0:T(8,128)(2,1)} %join_rows.18.refs_0_.refs_1_), channel_id=1, source_target_pairs={{0,16},{4,20},{8,24},{12,28},{16,0},{20,4},{24,8},{28,12},{1,17},{... | collective-permute-start | bytes 12976136 | tf_op jit(solution)/shard_map/ppermute | solution.py:832
  279.1 117.4 %collective-permute-start.27 = (bf16[4,352,1536]{2,1,0:T(8,128)(2,1)}, bf16[4,352,1536]{2,1,0:T(8,128)(2,1)}, u32[]{:S(2)}, u32[]{:S(2)}) collective-permute-start(bf16[4,352,1536]{2,1,0:T(8,128)(2,1)} %join_rows.19.refs_0_.refs_2_), channel_id=1, source_target_pairs={{0,8},{4,12},{8,0},{12,4},{16,24},{20,28},{24,16},{28,20},{1,9},{5... | collective-permute-start | bytes 12976136 | tf_op jit(solution)/shard_map/ppermute | solution.py:832
  281.5 123.8 %all-gather.25.cloned.1.call-start = ((), (), s32[]{:S(2)}) async-start(), calls=%async_computation.23 | async-start | bytes 1966080 | tf_op jit(solution)/shard_map/all_gather | solution.py:1017
  338.6 57.9 %collective-permute-start.28 = (bf16[4,176,768]{2,1,0:T(8,128)(2,1)S(1)}, bf16[4,176,768]{2,1,0:T(8,128)(2,1)S(1)}, u32[]{:S(2)}, u32[]{:S(2)}) collective-permute-start(bf16[4,176,768]{2,1,0:T(8,128)(2,1)S(1)} %slice.340.refs_0_), channel_id=1, source_target_pairs={{0,8},{4,12},{8,0},{12,4},{16,24},{20,28},{24,16},{28,20},{1,9},{5... | collective-permute-start | bytes 3244040 | tf_op jit(solution)/shard_map/ppermute | solution.py:832
  405.2 56.6 %all-to-all-start.1 = ((bf16[4,2,256,384]{3,2,1,0:T(8,128)(2,1)}), bf16[4,2,256,384]{3,2,1,0:T(8,128)(2,1)S(1)}, u32[]{:S(2)}, u32[]{:S(2)}) async-start(bf16[4,2,256,384]{3,2,1,0:T(8,128)(2,1)} %get-tuple-element.255), calls=%async_computation.1 | async-start | bytes 3145728 | tf_op jit(solution)/shard_map/all_to_all | solution.py:1031
  408.8 484.9 %reduce-scatter.8.cloned.1.call-start = ((), (), s32[]{:S(2)}) async-start(), calls=%async_computation.11 | async-start | bytes 2703360 | tf_op jit(solution)/shard_map/reduce_scatter | solution.py:1191
  474.9 100.2 %collective-permute-start.37 = (bf16[4,704,1536]{2,1,0:T(8,128)(2,1)}, bf16[4,704,1536]{2,1,0:T(8,128)(2,1)}, u32[]{:S(2)}, u32[]{:S(2)}) collective-permute-start(bf16[4,704,1536]{2,1,0:T(8,128)(2,1)} %join_rows.20.n1_ref), channel_id=1, source_target_pairs={{0,4},{4,0},{8,12},{12,8},{16,20},{20,16},{24,28},{28,24},{1,5},{5... | collective-permute-start | bytes 25952264 | tf_op jit(solution)/shard_map/ppermute | solution.py:832
  475.0 100.1 %collective-permute-start.38 = (bf16[4,704,1536]{2,1,0:T(8,128)(2,1)}, bf16[4,704,1536]{2,1,0:T(8,128)(2,1)}, u32[]{:S(2)}, u32[]{:S(2)}) collective-permute-start(bf16[4,704,1536]{2,1,0:T(8,128)(2,1)} %join_rows.21.n2_ref), channel_id=1, source_target_pairs={{0,4},{4,0},{8,12},{12,8},{16,20},{20,16},{24,28},{28,24},{1,5},{5... | collective-permute-start | bytes 25952264 | tf_op jit(solution)/shard_map/ppermute | solution.py:832
  664.4 104.3 %collective-permute-start.45 = (bf16[4,704,768]{2,1,0:T(8,128)(2,1)}, bf16[4,704,768]{2,1,0:T(8,128)(2,1)}, u32[]{:S(2)}, u32[]{:S(2)}) collective-permute-start(bf16[4,704,768]{2,1,0:T(8,128)(2,1)} %get-tuple-element.319), channel_id=1, source_target_pairs={{0,4},{4,0},{8,12},{12,8},{16,20},{20,16},{24,28},{28,24},{1,5},{5... | collective-permute-start | bytes 12976136 | tf_op jit(solution)/shard_map/ppermute | solution.py:832
  694.1 74.6 %collective-permute-start.46 = (bf16[4,704,768]{2,1,0:T(8,128)(2,1)}, bf16[4,704,768]{2,1,0:T(8,128)(2,1)}, u32[]{:S(2)}, u32[]{:S(2)}) collective-permute-start(bf16[4,704,768]{2,1,0:T(8,128)(2,1)} %get-tuple-element.320), channel_id=1, source_target_pairs={{0,4},{4,0},{8,12},{12,8},{16,20},{20,16},{24,28},{28,24},{1,5},{5... | collective-permute-start | bytes 12976136 | tf_op jit(solution)/shard_map/ppermute | solution.py:832
  786.4 107.4 %reduce-scatter.10.cloned.1.call-start = ((), (), s32[]{:S(2)}) async-start(), calls=%async_computation.12 | async-start | bytes 1966080 | tf_op jit(solution)/shard_map/reduce_scatter | solution.py:1191
  833.8 80.6 %collective-permute-start.51 = (bf16[4,704,1152]{2,1,0:T(8,128)(2,1)}, bf16[4,704,1152]{2,1,0:T(8,128)(2,1)}, u32[]{:S(2)}, u32[]{:S(2)}) collective-permute-start(bf16[4,704,1152]{2,1,0:T(8,128)(2,1)} %get-tuple-element.355), channel_id=1, source_target_pairs={{0,4},{4,0},{8,12},{12,8},{16,20},{20,16},{24,28},{28,24},{1,5},{5... | collective-permute-start | bytes 19464200 | tf_op jit(solution)/shard_map/ppermute | solution.py:832
  839.2 54.6 %collective-permute-start.49 = (bf16[4,176,768]{2,1,0:T(8,128)(2,1)}, bf16[4,176,768]{2,1,0:T(8,128)(2,1)S(1)}, u32[]{:S(2)}, u32[]{:S(2)}) collective-permute-start(bf16[4,176,768]{2,1,0:T(8,128)(2,1)} %get-tuple-element.351), channel_id=1, source_target_pairs={{0,8},{4,12},{8,0},{12,4},{16,24},{20,28},{24,16},{28,20},{1,9},{5... | collective-permute-start | bytes 3244040 | tf_op jit(solution)/shard_map/ppermute | solution.py:832
  840.6 53.2 %collective-permute-start.50 = (bf16[4,176,768]{2,1,0:T(8,128)(2,1)}, bf16[4,176,768]{2,1,0:T(8,128)(2,1)S(1)}, u32[]{:S(2)}, u32[]{:S(2)}) collective-permute-start(bf16[4,176,768]{2,1,0:T(8,128)(2,1)} %get-tuple-element.352), channel_id=1, source_target_pairs={{0,16},{4,20},{8,24},{12,28},{16,0},{20,4},{24,8},{28,12},{1,17},{... | collective-permute-start | bytes 3244040 | tf_op jit(solution)/shard_map/ppermute | solution.py:832
  895.2 109.7 %all-to-all-start.3 = ((bf16[4,2,256,1152]{3,2,1,0:T(8,128)(2,1)}), bf16[4,2,256,1152]{3,2,1,0:T(8,128)(2,1)}, u32[]{:S(2)}, u32[]{:S(2)}) async-start(bf16[4,2,256,1152]{3,2,1,0:T(8,128)(2,1)} %get-tuple-element.353), calls=%async_computation.5 | async-start | bytes 9437184 | tf_op jit(solution)/shard_map/all_to_all | solution.py:1031
  900.1 317.9 %reduce-scatter.20.cloned.1.call-start = ((), (), s32[]{:S(2)}) async-start(), calls=%async_computation.17 | async-start | bytes 2703360 | tf_op jit(solution)/shard_map/reduce_scatter | solution.py:1191
  919.4 66.1 %collective-permute-start.52 = (bf16[4,352,768]{2,1,0:T(8,128)(2,1)}, bf16[4,352,768]{2,1,0:T(8,128)(2,1)}, u32[]{:S(2)}, u32[]{:S(2)}) collective-permute-start(bf16[4,352,768]{2,1,0:T(8,128)(2,1)} %get-tuple-element.356), channel_id=1, source_target_pairs={{0,16},{4,20},{8,24},{12,28},{16,0},{20,4},{24,8},{28,12},{1,17},{... | collective-permute-start | bytes 6488072 | tf_op jit(solution)/shard_map/ppermute | solution.py:832
  919.5 66.0 %collective-permute-start.53 = (bf16[4,352,384]{2,1,0:T(8,128)(2,1)}, bf16[4,352,384]{2,1,0:T(8,128)(2,1)S(1)}, u32[]{:S(2)}, u32[]{:S(2)}) collective-permute-start(bf16[4,352,384]{2,1,0:T(8,128)(2,1)} %get-tuple-element.357), channel_id=1, source_target_pairs={{0,8},{4,12},{8,0},{12,4},{16,24},{20,28},{24,16},{28,20},{1,9},{5... | collective-permute-start | bytes 3244040 | tf_op jit(solution)/shard_map/ppermute | solution.py:832
  924.0 61.5 %collective-permute-start.55 = (bf16[4,256,384]{2,1,0:T(8,128)(2,1)}, bf16[4,256,384]{2,1,0:T(8,128)(2,1)S(1)}, u32[]{:S(2)}, u32[]{:S(2)}) collective-permute-start(bf16[4,256,384]{2,1,0:T(8,128)(2,1)} %get-tuple-element.360), channel_id=1, source_target_pairs={{0,16},{4,20},{8,24},{12,28},{16,0},{20,4},{24,8},{28,12},{1,17},{... | collective-permute-start | bytes 2359304 | tf_op jit(solution)/shard_map/ppermute | solution.py:832
  925.5 60.0 %collective-permute-start.56 = (bf16[4,256,384]{2,1,0:T(8,128)(2,1)}, bf16[4,256,384]{2,1,0:T(8,128)(2,1)S(1)}, u32[]{:S(2)}, u32[]{:S(2)}) collective-permute-start(bf16[4,256,384]{2,1,0:T(8,128)(2,1)} %get-tuple-element.361), channel_id=1, source_target_pairs={{0,8},{4,12},{8,0},{12,4},{16,24},{20,28},{24,16},{28,20},{1,9},{5... | collective-permute-start | bytes 2359304 | tf_op jit(solution)/shard_map/ppermute | solution.py:832
  1025.9 236.2 %reduce-scatter.18.cloned.1.call-start = ((), (), s32[]{:S(2)}) async-start(), calls=%async_computation.16 | async-start | bytes 983040 | tf_op jit(solution)/shard_map/reduce_scatter | solution.py:1191
  1082.4 60.4 %collective-permute-start.62 = (bf16[4,704,768]{2,1,0:T(8,128)(2,1)}, bf16[4,704,768]{2,1,0:T(8,128)(2,1)}, u32[]{:S(2)}, u32[]{:S(2)}) collective-permute-start(bf16[4,704,768]{2,1,0:T(8,128)(2,1)} %get-tuple-element.383), channel_id=1, source_target_pairs={{0,4},{4,0},{8,12},{12,8},{16,20},{20,16},{24,28},{28,24},{1,5},{5... | collective-permute-start | bytes 12976136 | tf_op jit(solution)/shard_map/ppermute | solution.py:832
  1088.4 175.6 %reduce-scatter.16.cloned.1.call-start = ((), (), s32[]{:S(2)}) async-start(), calls=%async_computation.15 | async-start | bytes 2027520 | tf_op jit(solution)/shard_map/reduce_scatter | solution.py:1191
  1096.1 172.3 %reduce-scatter.12.cloned.1.call-start = ((), (), s32[]{:S(2)}) async-start(), calls=%async_computation.13 | async-start | bytes 1351680 | tf_op jit(solution)/shard_map/reduce_scatter | solution.py:1191
  1216.0 65.9 %reduce-scatter.14.cloned.1.call-start = ((), (), s32[]{:S(2)}) async-start(), calls=%async_computation.14 | async-start | bytes 2027520 | tf_op jit(solution)/shard_map/reduce_scatter | solution.py:1191
  (144 other events, 3057.8 us)
Sparse Core Ops, SparseCore 0:
  10.2 31.2 all-gather.14
  43.0 37.7 all-gather.18
  90.2 46.1 all-gather.16
  167.2 45.5 all-gather.20
  262.0 75.2 all-gather.22
  339.3 28.2 all-gather.26
  369.7 35.4 all-gather.24
  756.0 57.3 reduce-scatter.7
  834.0 34.2 reduce-scatter.9
  1026.0 50.7 reduce-scatter.19
  1088.5 21.7 reduce-scatter.17
  1112.5 35.4 reduce-scatter.15
  1216.1 28.4 reduce-scatter.11
  1246.9 34.9 reduce-scatter.13

commit v11 on v10

--- a/solution.py
+++ b/solution.py
@@ -1054,8 +1054,9 @@
     qkv_m = fetch(qkv_z, qkv_cut)
     hold(qkv_m, *skip_m)
     advance(qkv_m)
+    cross_z = jnp.concatenate([pad_heads(side, local) for side in (w_out1.T, w_query2, w_out2.T)], 1)
+    cross_z = spread(pin(cross_z, *skip_m))
     fc1_z = spread(pin(w_fc1, *skip_m))
-    fc2_z = spread(pin(w_fc2.T, *qkv_m))
     join(skip_m)
     skip_w = [mover.weight() for mover in skip_m]
 
@@ -1120,17 +1121,20 @@
     after_qkv = [mover.pieces[-1] for mover in qkv_m]
     hold(qkv_m, pre_attn)
     join(qkv_m)
-    pre_attn, fc1_z = tie(pre_attn, fc1_z)
+    fc2_z = spread(pin(w_fc2.T, *after_qkv))
+    pre_attn, cross_z, fc1_z = tie(pre_attn, cross_z, fc1_z)
+    cross_m = fetch(cross_z, 2 * lanes, True)
+    hold(cross_m, *after_qkv)
+    advance(cross_m)
     qkv_w = [mover.weight() for mover in qkv_m]
     projected = to_lanes(pre_attn, qkv_w)
+    projected = bind(projected, *cross_m)
     projected, fc2_z = tie(projected, fc2_z)
     fc_m = [Gather(cube, fc1_z, 0, True), Gather(cube, fc2_z, 1, True)]
-    hold(fc_m, *after_qkv)
     advance(fc_m)
     raw = exchange(projected.reshape(parts, micros, slots, 3 * lanes))
-    cross_z = jnp.concatenate([pad_heads(side, local) for side in (w_out1.T, w_query2, w_out2.T)], 1)
+    cross_m[0].pieces[0], d_mlp, turn, text_turn = tie(cross_m[0].pieces[0], d_mlp, turn, text_turn)
     arrived = fc_m[0].pieces + fc_m[1].pieces
-    cross_z = spread(pin(cross_z, *arrived))
     text_own = jnp.dot(text.reshape(-1, features), text_turn, preferred_element_type=F32).astype(BF)
     text_own = jnp.pad(
         text_own.reshape(micros, text_slots, features), ((0, 0), (0, text_strip - text_slots), (0, 0))
@@ -1140,40 +1144,32 @@
         advance(fc_m)
     text_z = spread(pin(text_z, *arrived))
     text_all = spread(pin(text_own, *arrived))
-    cross_z, d_mlp, turn, text_turn = tie(cross_z, d_mlp, turn, text_turn)
-    cross_m = fetch(cross_z, 2 * lanes, True)
-    advance(cross_m)
+    while cross_m[0].todo:
+        advance(cross_m)
+    join(cross_m)
+    first_w, out2_w = [mover.weight() for mover in cross_m]
+    out1_w, query2_w = (Lanes(first_w.near, first_w.far, lanes, index) for index in range(2))
     attended, turned_q, turned_k, norms = self_forward(raw, counts, cosine, sine, gain_q, gain_k)
-    attended = bind(attended, *fc_m, *cross_m)
-    attended, text_all, text_z = tie(attended, text_all, text_z)
+    attended = bind(attended, *fc_m)
+    attended, text_all, text_z, first_w.far, out2_w.far = tie(attended, text_all, text_z, first_w.far, out2_w.far)
+    out1_w.far = query2_w.far = first_w.far
     text_m = Gather(cube, text_z[:, :text_rows], 0, True)
     text_m.move()
     attended = exchange(attended).reshape(parts, rows, lanes)
-    while cross_m[0].todo:
-        advance(cross_m)
     join(fc_m)
-    attended = bind(attended, text_m, *fc_m, cross_m[0])
+    attended = bind(attended, text_m, *fc_m)
     while text_m.todo:
         text_m.move()
-    join(cross_m[:1])
-    first_w = cross_m[0].weight()
-    out1_w, query2_w = (Lanes(first_w.near, first_w.far, lanes, index) for index in range(2))
-    attended, first_w.far = tie(attended, first_w.far)
-    out1_w.far = query2_w.far = first_w.far
     text_all = text_all.reshape(-1, features)
     text_all = jnp.stack([text_all[:, : features // 2], text_all[:, features // 2 :]])
     stream1, pre_cross = to_features(
         attended, [out1_w], [stream, g_cross], [wide_shape, low_shape], next_norm
     )
-    hold(fc_m, out1_w.far)
     fc1_w, fc2_w = [mover.weight() for mover in fc_m]
     hold([text_m], pre_cross)
     text_m.join()
     text_w = text_m.weight()
     query2 = to_lanes(pre_cross, [query2_w]).reshape(parts, micros, slots, lanes)
-    query2 = bind(query2, *cross_m[1:])
-    join(cross_m[1:])
-    out2_w = cross_m[1].weight()
     text_kv = to_lanes(text_all, [text_w]).reshape(parts, parts, micros, text_strip, 2 * lanes)
     crossed = cross_forward(query2, text_kv, lengths, text_slots).reshape(parts, rows, lanes)
     stream2, pre_mlp = to_features(
@@ -1293,17 +1289,22 @@
         last_norms,
     )
     d_base = bind(d_base, *other_s)
+    total_cross, total_text = list(results(cross_s)), list(results(text_s))
+    d_base = bind(d_base, *qkv_s)
+    d_base, total_cross[0], total_text[0] = tie(d_base, total_cross[0], total_text[0])
+    term_cross, term_text = settle(total_cross), settle(total_text)
     skip_t = terms_of([(d_base, joined, skip_lanes, 0)])
     skip_s = scatter(cube, skip_t, (skip_cut, 0, 0), (skip_cut, 1, 1))
+    pack(qkv_s)
+    send(qkv_s)
     pack(skip_s)
-    pack(qkv_s)
-    skip_s[0].pieces[0] = bind(skip_s[0].pieces[0], *qkv_s)
-    send(qkv_s)
     send(skip_s)
-    term_cross, term_text = settle(results(cross_s)), settle(results(text_s))
-    total_qkv = results(qkv_s)
-    term_qkv = settle(total_qkv)
-    term_skip = settle(results(skip_s), total_qkv[0])
+    total_qkv = list(results(qkv_s))
+    total_qkv[0] = bind(total_qkv[0], *skip_s)
+    total_skip = list(results(skip_s))
+    total_skip[0], term_cross, term_text = tie(total_skip[0], term_cross, term_text)
+    term_qkv = settle(total_qkv + total_skip)
+    term_qkv, term_skip = term_qkv[:, : 3 * lanes], term_qkv[:, 3 * lanes :]
     d_joined = to_inputs(d_base, skip_w, kept)
     result = (
         jnp.dot(result[0], turn[:, :middle].T, preferred_element_type=F32)

time: 1300 us -> 1340 us (1.031)
  waiting for transfers between devices: 465 us -> 493 us
    ppermute x81, waiting for transfers between devices: 352 us -> 420 us  [swap(): return lax.ppermute(value, axis, pairs)]
    all_gather x7, waiting for transfers between devices: 61.9 us -> 14.2 us  [spread(): return lax.all_gather(shard, 'sp', axis=0, tiled=False)]
  transfers between devices with their start and end apart: 99 -> 98, of which waited for: 46 -> 44; matrix products, arithmetic and copies ran while one was open for 9% -> 9% of each run, Pallas kernels for 40% -> 39%
where the time goes in v11:
time: 1340 us; the launch traced here: 1330 us
  Pallas kernels  565 us (42%)
  waiting for transfers between devices  493 us (37%)
  starting transfers between devices  115 us (9%)
  other arithmetic  62.2 us (5%)
  local copies, waits for them, and re-layouts  56.6 us (4%)
  matrix products  17.9 us (1%)
  between operations  15.9 us (1%)
    ppermute x81, waiting for transfers between devices, swap(): return lax.ppermute(value, axis, pairs)  420 us
    ppermute x81, starting transfers between devices, swap(): return lax.ppermute(value, axis, pairs)  95.7 us
    pallas_call x18, Pallas kernels, sum_rows(): pl.pallas_call(kernel, name=name, grid=(parts,), in_specs=[spec(*rest) fo...  84.5 us
    pallas_call x6, Pallas kernels, to_features(): pl.pallas_call(kernel, name=name, grid=(parts,), in_specs=[pl.BlockSpec((...  78.1 us
    pallas_call x14, Pallas kernels, join_rows(): pl.pallas_call(kernel, name=name, grid=(parts,), in_specs=[spec(block) fo...  64.3 us
    pallas_call x2, Pallas kernels, mlp_backward(): pl.pallas_call(kernel, name='mlp_backward', grid=(parts, steps), in_specs...  54.2 us
    pallas_call x1, Pallas kernels, self_backward(): pl.pallas_call(kernel, name='self_backward', grid_spec=pltpu.PrefetchScal...  51.6 us
    pallas_call x2, Pallas kernels, mlp_forward(): pl.pallas_call(kernel, name='mlp_forward', grid=(parts, steps), in_specs=...  51.4 us
  transfers between devices with their start and end apart: 98, of which 44 were waited for; matrix products, arithmetic and copies ran while one was open for 9% of the time, Pallas kernels for 39%

profile of v11, /device:TPU:0, one launch (start us, length us, event | category | flops | bytes accessed | tf_op | source)
XLA Modules:
  0.0 1325.7 jit_solution(916627187917592764)
XLA Ops:
  17.2 13.9 %negate_select_fusion = (f32[2,1024,384]{2,1,0:T(8,128)}, f32[2,1024,384]{2,1,0:T(8,128)}) fusion(f32[384]{0:T(512)S(1)} %fusion.48, s32[2,1024]{1,0:T(2,128)S(1)} %and_select_fusion.2, s32[2,1024]{1,0:T(2,128)S(1)} %and_select_fusion.3, pred[384]{0:T(512)(128)(4,1)S(1)} %get-tuple-element.496, pred[384]{0:T(512)(128)(4,1)S(1)} %get-tuple-element.497), kind=kLoop, calls=%fused_computation.4 | loop fusion | flops 3932160 | bytes 6310144 | tf_op jit(solution)/shard_map/jit(_where)/select_n | solution.py:41
  72.3 18.5 %collective-permute-done.10 = f32[4,2,176]{2,1,0:T(2,128)S(1)} collective-permute-done((f32[4,2,176]{2,1,0:T(2,128)S(1)}, f32[4,2,176]{2,1,0:T(2,128)S(1)}, u32[]{:S(2)}, u32[]{:S(2)}) %collective-permute-start.10) | collective-permute-done | bytes 5664 | tf_op jit(solution)/shard_map/ppermute | solution.py:832
  108.9 16.7 %collective-permute-done.16.refs_1_ = bf16[4,176,640]{2,1,0:T(8,128)(2,1)} collective-permute-done((bf16[4,176,640]{2,1,0:T(8,128)(2,1)S(1)}, bf16[4,176,640]{2,1,0:T(8,128)(2,1)}, u32[]{:S(2)}, u32[]{:S(2)}) %collective-permute-start.16) | collective-permute-done | bytes 901152 | tf_op jit(solution)/shard_map/ppermute | solution.py:832
  129.0 14.7 %to_features.6 = (f32[2,512,704]{2,1,0:T(8,128)}, f32[2,512,704]{2,1,0:T(8,128)}, bf16[2,512,704]{2,1,0:T(8,128)(2,1)}) custom-call(bf16[4,512,768]{2,1,0:T(8,128)(2,1)} %side_by_side.1.refs_0_.refs_1_, bf16[4,704,384]{2,1,0:T(8,128)(2,1)} %join_rows.14.refs_1_.refs_0_, bf16[4,704,384]{2,1,0:T(8,128)(2,1)} %collective-permute-done.11.refs_2_.refs_1_, ...), custom_call_target="tpu_custom_call" | custom-call | flops 276824064 | bytes 276824 | tf_op jit(solution)/shard_map/to_features/pallas_call | solution.py:401
  145.3 18.1 %collective-permute-done.18.refs_3_ = bf16[4,176,640]{2,1,0:T(8,128)(2,1)} collective-permute-done((bf16[4,176,640]{2,1,0:T(8,128)(2,1)}, bf16[4,176,640]{2,1,0:T(8,128)(2,1)}, u32[]{:S(2)}, u32[]{:S(2)}) %collective-permute-start.18) | collective-permute-done | bytes 901152 | tf_op jit(solution)/shard_map/ppermute | solution.py:832
  194.3 13.0 to_lanes.5
  210.9 11.9 all-gather.23.cloned.1.call-done
  242.5 41.8 %collective-permute-done.26.refs_1_ = bf16[4,176,1536]{2,1,0:T(8,128)(2,1)} collective-permute-done((bf16[4,176,1536]{2,1,0:T(8,128)(2,1)}, bf16[4,176,1536]{2,1,0:T(8,128)(2,1)}, u32[]{:S(2)}, u32[]{:S(2)}) %collective-permute-start.26) | collective-permute-done | bytes 2162720 | tf_op jit(solution)/shard_map/ppermute | solution.py:832
  296.9 36.4 %collective-permute-done.30.refs_2_.refs_3_ = bf16[4,352,768]{2,1,0:T(8,128)(2,1)S(1)} collective-permute-done((bf16[4,352,768]{2,1,0:T(8,128)(2,1)}, bf16[4,352,768]{2,1,0:T(8,128)(2,1)S(1)}, u32[]{:S(2)}, u32[]{:S(2)}) %collective-permute-start.30) | collective-permute-done | bytes 2162720 | tf_op jit(solution)/shard_map/ppermute | solution.py:832
  350.7 62.1 %collective-permute-done.32.refs_1_.refs_3_ = bf16[4,352,384]{2,1,0:T(8,128)(2,1)S(1)} collective-permute-done((bf16[4,352,384]{2,1,0:T(8,128)(2,1)}, bf16[4,352,384]{2,1,0:T(8,128)(2,1)S(1)}, u32[]{:S(2)}, u32[]{:S(2)}) %collective-permute-start.32) | collective-permute-done | bytes 1081376 | tf_op jit(solution)/shard_map/ppermute | solution.py:832
  419.0 34.8 %self_forward.1 = (bf16[4,2,256,384]{3,2,1,0:T(8,128)(2,1)}, bf16[2,1024,384]{2,1,0:T(8,128)(2,1)}, bf16[2,1024,384]{2,1,0:T(8,128)(2,1)}, f32[2,4,1024]{2,1,0:T(4,128)}) custom-call(s32[2]{0:T(128)} %copy-done.64, bf16[4,2,256,1152]{3,2,1,0:T(8,128)(2,1)} %all-to-all-done.raw_ref, f32[2,1024,384]{2,1,0:T(8,128)} %get-tuple-element.251.cos_ref, ...), custom_call_target="tpu_custom_call" | custom-call | flops 201326592 | bytes 201326 | tf_op jit(solution)/shard_map/self_forward/pallas_call | solution.py:150
  481.4 13.2 all-to-all-done.1
  515.4 23.7 %collective-permute-done.35.refs_2_.refs_3_ = bf16[4,256,768]{2,1,0:T(8,128)(2,1)} collective-permute-done((bf16[4,256,768]{2,1,0:T(8,128)(2,1)}, bf16[4,256,768]{2,1,0:T(8,128)(2,1)}, u32[]{:S(2)}, u32[]{:S(2)}) %collective-permute-start.35) | collective-permute-done | bytes 1572896 | tf_op jit(solution)/shard_map/ppermute | solution.py:832
  562.3 19.1 %cross_forward.1 = bf16[4,2,256,384]{3,2,1,0:T(8,128)(2,1)} custom-call(s32[2,2]{1,0:T(2,128)} %bitcast.218, bf16[4,2,256,384]{3,2,1,0:T(8,128)(2,1)} %bitcast.171, bf16[4,4,2,96,768]{4,3,2,1,0:T(8,128)(2,1)} %bitcast.162), custom_call_target="tpu_custom_call" | custom-call | flops 75497472 | bytes 75497 | tf_op jit(solution)/shard_map/cross_forward/pallas_call | solution.py:738
  581.4 10.5 to_features.8
  591.9 25.9 %mlp_forward.2 = (f32[4,512,768]{2,1,0:T(8,128)}, bf16[4,512,768]{2,1,0:T(8,128)(2,1)}, f32[2,512,704]{2,1,0:T(8,128)}, bf16[4,704,768]{2,1,0:T(8,128)(2,1)}, bf16[4,704,768]{2,1,0:T(8,128)(2,1)}) custom-call(bf16[2,512,704]{2,1,0:T(8,128)(2,1)} %get-tuple-element.282.x_ref, bf16[2,512,704]{2,1,0:T(8,128)(2,1)} %fusion.62.g_ref, ...), custom_call_target="tpu_custom_call" | custom-call | flops 830472192 | bytes 830472 | tf_op jit(solution)/shard_map/mlp_forward/pallas_call | solution.py:609
  618.3 25.5 %mlp_forward.3 = (f32[4,512,768]{2,1,0:T(8,128)}, bf16[4,512,768]{2,1,0:T(8,128)(2,1)}, bf16[2,512,704]{2,1,0:T(8,128)(2,1)}, bf16[4,704,768]{2,1,0:T(8,128)(2,1)}, bf16[4,704,768]{2,1,0:T(8,128)(2,1)}) custom-call(bf16[2,512,704]{2,1,0:T(8,128)(2,1)} %get-tuple-element.282.x_ref, bf16[2,512,704]{2,1,0:T(8,128)(2,1)} %fusion.62.g_ref, ...), custom_call_target="tpu_custom_call" | custom-call | flops 830472192 | bytes 830472 | tf_op jit(solution)/shard_map/mlp_forward/pallas_call | solution.py:609
  643.9 24.6 %mlp_backward.2 = (bf16[4,704,768]{2,1,0:T(8,128)(2,1)}, bf16[4,704,768]{2,1,0:T(8,128)(2,1)}, f32[2,512,704]{2,1,0:T(8,128)}) custom-call(bf16[2,512,704]{2,1,0:T(8,128)(2,1)} %fusion.62.g_ref, bf16[2,512,704]{2,1,0:T(8,128)(2,1)} %get-tuple-element.282.x_ref, f32[4,512,768]{2,1,0:T(8,128)} %get-tuple-element.294.hid_ref, ...), custom_call_target="tpu_custom_call" | custom-call | flops 830472192 | bytes 830472 | tf_op jit(solution)/shard_map/mlp_backward/pallas_call | solution.py:681
  682.0 29.6 %mlp_backward.3 = (bf16[4,704,768]{2,1,0:T(8,128)(2,1)}, bf16[4,704,768]{2,1,0:T(8,128)(2,1)}, f32[2,512,704]{2,1,0:T(8,128)}, bf16[2,512,704]{2,1,0:T(8,128)(2,1)}, f32[2,1,704]{2,1,0:T(1,128)}) custom-call(bf16[2,512,704]{2,1,0:T(8,128)(2,1)} %fusion.62.g_ref, bf16[2,512,704]{2,1,0:T(8,128)(2,1)} %get-tuple-element.282.x_ref, ...), custom_call_target="tpu_custom_call" | custom-call | flops 830472192 | bytes 830472 | tf_op jit(solution)/shard_map/mlp_backward/pallas_call | solution.py:681
  712.2 11.9 collective-permute-done.41.refs_2_
  741.3 22.5 %cross_backward.1 = (bf16[4,2,256,384]{3,2,1,0:T(8,128)(2,1)}, bf16[4,4,2,96,768]{4,3,2,1,0:T(8,128)(2,1)}) custom-call(s32[2,2]{1,0:T(2,128)} %bitcast.219, bf16[4,2,256,384]{3,2,1,0:T(8,128)(2,1)} %bitcast.172, bf16[4,4,2,96,768]{4,3,2,1,0:T(8,128)(2,1)} %bitcast.163, bf16[4,2,256,384]{3,2,1,0:T(8,128)(2,1)} %bitcast.175), custom_call_target="tpu_custom_call" | custom-call | flops 188743680 | bytes 188743 | tf_op jit(solution)/shard_map/cross_backward/pallas_call | solution.py:787
  775.0 12.6 to_features.9
  824.8 15.3 %terms_of.5 = (bf16[4,704,1152]{2,1,0:T(8,128)(2,1)}, bf16[4,704,1152]{2,1,0:T(8,128)(2,1)}) custom-call(bf16[2,512,704]{2,1,0:T(8,128)(2,1)} %get-tuple-element.327.x_ref.refs_0_, bf16[2,512,704]{2,1,0:T(8,128)(2,1)} %get-tuple-element.332.x_ref.refs_1_, bf16[2,512,704]{2,1,0:T(8,128)(2,1)} %get-tuple-element.306.x_ref.refs_2_, ...), custom_call_target="tpu_custom_call" | custom-call | flops 415236096 | bytes 415236 | tf_op jit(solution)/shard_map/terms_of/pallas_call | solution.py:445
  840.1 10.5 all-to-all-done.2.in_ref
  860.0 51.6 %self_backward.1 = (bf16[4,2,256,1152]{3,2,1,0:T(8,128)(2,1)}, f32[2,1,384]{2,1,0:T(1,128)}, f32[2,1,384]{2,1,0:T(1,128)}) custom-call(s32[2]{0:T(128)} %copy-done.64, bf16[4,2,256,1152]{3,2,1,0:T(8,128)(2,1)} %all-to-all-done.raw_ref, f32[2,1024,384]{2,1,0:T(8,128)} %get-tuple-element.251.cos_ref, f32[2,1024,384]{2,1,0:T(8,128)} %get-tuple-element.252.sin_ref, ...), custom_call_target="tpu_custom_call" | custom-call | flops 503316480 | bytes 503316 | tf_op jit(solution)/shard_map/self_backward/pallas_call | solution.py:260
  941.9 55.7 %collective-permute-done.55.refs_2_ = bf16[4,256,384]{2,1,0:T(8,128)(2,1)S(1)} collective-permute-done((bf16[4,256,384]{2,1,0:T(8,128)(2,1)}, bf16[4,256,384]{2,1,0:T(8,128)(2,1)S(1)}, u32[]{:S(2)}, u32[]{:S(2)}) %collective-permute-start.55) | collective-permute-done | bytes 786464 | tf_op jit(solution)/shard_map/ppermute | solution.py:832
  997.6 25.1 %all-to-all-done.3 = bf16[4,2,256,1152]{3,2,1,0:T(8,128)(2,1)} async-done(((bf16[4,2,256,1152]{3,2,1,0:T(8,128)(2,1)}), bf16[4,2,256,1152]{3,2,1,0:T(8,128)(2,1)}, u32[]{:S(2)}, u32[]{:S(2)}) %all-to-all-start.3) | async-done | bytes 4718624 | tf_op jit(solution)/shard_map/all_to_all | solution.py:1031
  1022.7 11.6 terms_of.6
  1067.8 50.2 %collective-permute-done.60.refs_3_ = bf16[4,128,384]{2,1,0:T(8,128)(2,1)S(1)} collective-permute-done((bf16[4,128,384]{2,1,0:T(8,128)(2,1)}, bf16[4,128,384]{2,1,0:T(8,128)(2,1)S(1)}, u32[]{:S(2)}, u32[]{:S(2)}) %collective-permute-start.60) | collective-permute-done | bytes 393248 | tf_op jit(solution)/shard_map/ppermute | solution.py:832
  1118.3 20.5 %to_features.11 = (bf16[2,512,704]{2,1,0:T(8,128)(2,1)}, f32[2,2,704]{2,1,0:T(2,128)}, f32[2,1,704]{2,1,0:T(1,128)}, f32[2,1,704]{2,1,0:T(1,128)}) custom-call(bf16[4,512,1152]{2,1,0:T(8,128)(2,1)} %bitcast.61.refs_1_.refs_0_, bf16[4,704,640]{2,1,0:T(8,128)(2,1)} %join_rows.16.refs_0_.refs_1_, bf16[4,704,640]{2,1,0:T(8,128)(2,1)} %collective-permute-done.19.refs_1_.refs_2_, ...), custom_call_target="tpu_custom_call" | custom-call | flops 415236096 | bytes 415236 | tf_op jit(solution)/shard_map/to_features/pallas_call | solution.py:401
  1188.0 29.8 %collective-permute-done.65.refs_7_ = bf16[4,176,384]{2,1,0:T(8,128)(2,1)S(1)} collective-permute-done((bf16[4,176,384]{2,1,0:T(8,128)(2,1)}, bf16[4,176,384]{2,1,0:T(8,128)(2,1)S(1)}, u32[]{:S(2)}, u32[]{:S(2)}) %collective-permute-start.65) | collective-permute-done | bytes 540704 | tf_op jit(solution)/shard_map/ppermute | solution.py:832
  1282.2 12.4 to_inputs.1
  (573 shorter events, 526.4 us)
Async XLA Ops:
  9.1 93.2 %all-gather.21.cloned.1.call-start = ((), (), s32[]{:S(2)}) async-start(), calls=%async_computation.19 | async-start | bytes 2027520 | tf_op jit(solution)/shard_map/all_gather | solution.py:1017
  41.4 142.1 %all-gather.17.cloned.1.call-start = ((), (), s32[]{:S(2)}) async-start(), calls=%async_computation.17 | async-start | bytes 2027520 | tf_op jit(solution)/shard_map/all_gather | solution.py:1017
  91.9 91.6 %all-gather.19.cloned.1.call-start = ((), (), s32[]{:S(2)}) async-start(), calls=%async_computation.18 | async-start | bytes 2703360 | tf_op jit(solution)/shard_map/all_gather | solution.py:1017
  92.5 130.3 %all-gather.23.cloned.1.call-start = ((), (), s32[]{:S(2)}) async-start(), calls=%async_computation.20 | async-start | bytes 2703360 | tf_op jit(solution)/shard_map/all_gather | solution.py:1017
  222.8 196.2 %all-to-all-start = ((bf16[4,2,256,1152]{3,2,1,0:T(8,128)(2,1)}), bf16[4,2,256,1152]{3,2,1,0:T(8,128)(2,1)}, u32[]{:S(2)}, u32[]{:S(2)}) async-start(bf16[4,2,256,1152]{3,2,1,0:T(8,128)(2,1)} %bitcast.166), calls=%async_computation | async-start | bytes 9437184 | tf_op jit(solution)/shard_map/all_to_all | solution.py:1031
  227.8 226.1 %all-gather.27.cloned.1.call-start = ((), (), s32[]{:S(2)}) async-start(), calls=%async_computation.22 | async-start | bytes 1351680 | tf_op jit(solution)/shard_map/all_gather | solution.py:1017
  242.0 91.3 %collective-permute-start.30 = (bf16[4,352,768]{2,1,0:T(8,128)(2,1)}, bf16[4,352,768]{2,1,0:T(8,128)(2,1)S(1)}, u32[]{:S(2)}, u32[]{:S(2)}) collective-permute-start(bf16[4,352,768]{2,1,0:T(8,128)(2,1)} %join_rows.20.refs_0_.refs_1_), channel_id=1, source_target_pairs={{0,16},{4,20},{8,24},{12,28},{16,0},{20,4},{24,8},{28,12},{1,17},{... | collective-permute-start | bytes 6488072 | tf_op jit(solution)/shard_map/ppermute | solution.py:832
  289.1 164.7 %collective-permute-start.27 = (bf16[4,352,1536]{2,1,0:T(8,128)(2,1)}, bf16[4,352,1536]{2,1,0:T(8,128)(2,1)}, u32[]{:S(2)}, u32[]{:S(2)}) collective-permute-start(bf16[4,352,1536]{2,1,0:T(8,128)(2,1)} %join_rows.18.refs_0_.refs_1_), channel_id=1, source_target_pairs={{0,16},{4,20},{8,24},{12,28},{16,0},{20,4},{24,8},{28,12},{1,17},{... | collective-permute-start | bytes 12976136 | tf_op jit(solution)/shard_map/ppermute | solution.py:832
  295.4 158.4 %collective-permute-start.29 = (bf16[4,352,1536]{2,1,0:T(8,128)(2,1)}, bf16[4,352,1536]{2,1,0:T(8,128)(2,1)}, u32[]{:S(2)}, u32[]{:S(2)}) collective-permute-start(bf16[4,352,1536]{2,1,0:T(8,128)(2,1)} %join_rows.19.refs_0_.refs_2_), channel_id=1, source_target_pairs={{0,8},{4,12},{8,0},{12,4},{16,24},{20,28},{24,16},{28,20},{1,9},{5... | collective-permute-start | bytes 12976136 | tf_op jit(solution)/shard_map/ppermute | solution.py:832
  339.4 114.5 %collective-permute-start.31 = (bf16[4,704,768]{2,1,0:T(8,128)(2,1)}, bf16[4,704,768]{2,1,0:T(8,128)(2,1)}, u32[]{:S(2)}, u32[]{:S(2)}) collective-permute-start(bf16[4,704,768]{2,1,0:T(8,128)(2,1)} %join_rows.21.refs_1_.refs_0_), channel_id=1, source_target_pairs={{0,4},{4,0},{8,12},{12,8},{16,20},{20,16},{24,28},{28,24},{1,5},{5... | collective-permute-start | bytes 12976136 | tf_op jit(solution)/shard_map/ppermute | solution.py:832
  340.4 113.5 %all-gather.25.cloned.1.call-start = ((), (), s32[]{:S(2)}) async-start(), calls=%async_computation.21 | async-start | bytes 1966080 | tf_op jit(solution)/shard_map/all_gather | solution.py:1017
  344.1 68.6 %collective-permute-start.32 = (bf16[4,352,384]{2,1,0:T(8,128)(2,1)}, bf16[4,352,384]{2,1,0:T(8,128)(2,1)S(1)}, u32[]{:S(2)}, u32[]{:S(2)}) collective-permute-start(bf16[4,352,384]{2,1,0:T(8,128)(2,1)} %join_rows.22.refs_0_.refs_2_), channel_id=1, source_target_pairs={{0,8},{4,12},{8,0},{12,4},{16,24},{20,28},{24,16},{28,20},{1,9},{5... | collective-permute-start | bytes 3244040 | tf_op jit(solution)/shard_map/ppermute | solution.py:832
  458.3 453.2 %reduce-scatter.7.cloned.1.call-start = ((), (), s32[]{:S(2)}) async-start(), calls=%async_computation.10 | async-start | bytes 2703360 | tf_op jit(solution)/shard_map/reduce_scatter | solution.py:1187
  494.6 97.3 %collective-permute-start.37 = (bf16[4,704,1536]{2,1,0:T(8,128)(2,1)}, bf16[4,704,1536]{2,1,0:T(8,128)(2,1)}, u32[]{:S(2)}, u32[]{:S(2)}) collective-permute-start(bf16[4,704,1536]{2,1,0:T(8,128)(2,1)} %join_rows.24.n1_ref), channel_id=1, source_target_pairs={{0,4},{4,0},{8,12},{12,8},{16,20},{20,16},{24,28},{28,24},{1,5},{5... | collective-permute-start | bytes 25952264 | tf_op jit(solution)/shard_map/ppermute | solution.py:832
  496.5 95.3 %collective-permute-start.38 = (bf16[4,704,1536]{2,1,0:T(8,128)(2,1)}, bf16[4,704,1536]{2,1,0:T(8,128)(2,1)}, u32[]{:S(2)}, u32[]{:S(2)}) collective-permute-start(bf16[4,704,1536]{2,1,0:T(8,128)(2,1)} %join_rows.25.n2_ref), channel_id=1, source_target_pairs={{0,4},{4,0},{8,12},{12,8},{16,20},{20,16},{24,28},{28,24},{1,5},{5... | collective-permute-start | bytes 25952264 | tf_op jit(solution)/shard_map/ppermute | solution.py:832
  682.0 105.5 %collective-permute-start.45 = (bf16[4,704,768]{2,1,0:T(8,128)(2,1)}, bf16[4,704,768]{2,1,0:T(8,128)(2,1)}, u32[]{:S(2)}, u32[]{:S(2)}) collective-permute-start(bf16[4,704,768]{2,1,0:T(8,128)(2,1)} %get-tuple-element.318), channel_id=1, source_target_pairs={{0,4},{4,0},{8,12},{12,8},{16,20},{20,16},{24,28},{28,24},{1,5},{5... | collective-permute-start | bytes 12976136 | tf_op jit(solution)/shard_map/ppermute | solution.py:832
  711.6 76.0 %collective-permute-start.46 = (bf16[4,704,768]{2,1,0:T(8,128)(2,1)}, bf16[4,704,768]{2,1,0:T(8,128)(2,1)}, u32[]{:S(2)}, u32[]{:S(2)}) collective-permute-start(bf16[4,704,768]{2,1,0:T(8,128)(2,1)} %get-tuple-element.319), channel_id=1, source_target_pairs={{0,4},{4,0},{8,12},{12,8},{16,20},{20,16},{24,28},{28,24},{1,5},{5... | collective-permute-start | bytes 12976136 | tf_op jit(solution)/shard_map/ppermute | solution.py:832
  804.1 107.5 %reduce-scatter.9.cloned.1.call-start = ((), (), s32[]{:S(2)}) async-start(), calls=%async_computation.11 | async-start | bytes 1966080 | tf_op jit(solution)/shard_map/reduce_scatter | solution.py:1187
  850.6 75.6 %collective-permute-start.51 = (bf16[4,704,1152]{2,1,0:T(8,128)(2,1)}, bf16[4,704,1152]{2,1,0:T(8,128)(2,1)}, u32[]{:S(2)}, u32[]{:S(2)}) collective-permute-start(bf16[4,704,1152]{2,1,0:T(8,128)(2,1)} %get-tuple-element.354), channel_id=1, source_target_pairs={{0,4},{4,0},{8,12},{12,8},{16,20},{20,16},{24,28},{28,24},{1,5},{5... | collective-permute-start | bytes 19464200 | tf_op jit(solution)/shard_map/ppermute | solution.py:832
  913.0 109.7 %all-to-all-start.3 = ((bf16[4,2,256,1152]{3,2,1,0:T(8,128)(2,1)}), bf16[4,2,256,1152]{3,2,1,0:T(8,128)(2,1)}, u32[]{:S(2)}, u32[]{:S(2)}) async-start(bf16[4,2,256,1152]{3,2,1,0:T(8,128)(2,1)} %get-tuple-element.352), calls=%async_computation.5 | async-start | bytes 9437184 | tf_op jit(solution)/shard_map/all_to_all | solution.py:1031
  917.9 331.4 %reduce-scatter.13.cloned.1.call-start = ((), (), s32[]{:S(2)}) async-start(), calls=%async_computation.13 | async-start | bytes 983040 | tf_op jit(solution)/shard_map/reduce_scatter | solution.py:1187
  931.5 66.1 %collective-permute-start.52 = (bf16[4,352,768]{2,1,0:T(8,128)(2,1)}, bf16[4,352,768]{2,1,0:T(8,128)(2,1)}, u32[]{:S(2)}, u32[]{:S(2)}) collective-permute-start(bf16[4,352,768]{2,1,0:T(8,128)(2,1)} %get-tuple-element.355), channel_id=1, source_target_pairs={{0,16},{4,20},{8,24},{12,28},{16,0},{20,4},{24,8},{28,12},{1,17},{... | collective-permute-start | bytes 6488072 | tf_op jit(solution)/shard_map/ppermute | solution.py:832
  931.5 66.0 %collective-permute-start.53 = (bf16[4,352,384]{2,1,0:T(8,128)(2,1)}, bf16[4,352,384]{2,1,0:T(8,128)(2,1)S(1)}, u32[]{:S(2)}, u32[]{:S(2)}) collective-permute-start(bf16[4,352,384]{2,1,0:T(8,128)(2,1)} %get-tuple-element.356), channel_id=1, source_target_pairs={{0,8},{4,12},{8,0},{12,4},{16,24},{20,28},{24,16},{28,20},{1,9},{5... | collective-permute-start | bytes 3244040 | tf_op jit(solution)/shard_map/ppermute | solution.py:832
  941.5 56.1 %collective-permute-start.55 = (bf16[4,256,384]{2,1,0:T(8,128)(2,1)}, bf16[4,256,384]{2,1,0:T(8,128)(2,1)S(1)}, u32[]{:S(2)}, u32[]{:S(2)}) collective-permute-start(bf16[4,256,384]{2,1,0:T(8,128)(2,1)} %get-tuple-element.359), channel_id=1, source_target_pairs={{0,16},{4,20},{8,24},{12,28},{16,0},{20,4},{24,8},{28,12},{1,17},{... | collective-permute-start | bytes 2359304 | tf_op jit(solution)/shard_map/ppermute | solution.py:832
  941.6 56.0 %collective-permute-start.56 = (bf16[4,256,384]{2,1,0:T(8,128)(2,1)}, bf16[4,256,384]{2,1,0:T(8,128)(2,1)S(1)}, u32[]{:S(2)}, u32[]{:S(2)}) collective-permute-start(bf16[4,256,384]{2,1,0:T(8,128)(2,1)} %get-tuple-element.360), channel_id=1, source_target_pairs={{0,8},{4,12},{8,0},{12,4},{16,24},{20,28},{24,16},{28,20},{1,9},{5... | collective-permute-start | bytes 2359304 | tf_op jit(solution)/shard_map/ppermute | solution.py:832
  1050.7 97.5 %collective-permute-start.62 = (bf16[4,352,768]{2,1,0:T(8,128)(2,1)}, bf16[4,352,768]{2,1,0:T(8,128)(2,1)}, u32[]{:S(2)}, u32[]{:S(2)}) collective-permute-start(bf16[4,352,768]{2,1,0:T(8,128)(2,1)} %get-tuple-element.379), channel_id=1, source_target_pairs={{0,16},{4,20},{8,24},{12,28},{16,0},{20,4},{24,8},{28,12},{1,17},{... | collective-permute-start | bytes 6488072 | tf_op jit(solution)/shard_map/ppermute | solution.py:832
  1058.4 80.4 %collective-permute-start.58 = (bf16[4,176,768]{2,1,0:T(8,128)(2,1)}, bf16[4,176,768]{2,1,0:T(8,128)(2,1)S(1)}, u32[]{:S(2)}, u32[]{:S(2)}) collective-permute-start(bf16[4,176,768]{2,1,0:T(8,128)(2,1)} %get-tuple-element.372), channel_id=1, source_target_pairs={{0,8},{4,12},{8,0},{12,4},{16,24},{20,28},{24,16},{28,20},{1,9},{5... | collective-permute-start | bytes 3244040 | tf_op jit(solution)/shard_map/ppermute | solution.py:832
  1062.0 86.1 %collective-permute-start.63 = (bf16[4,352,384]{2,1,0:T(8,128)(2,1)}, bf16[4,352,384]{2,1,0:T(8,128)(2,1)S(1)}, u32[]{:S(2)}, u32[]{:S(2)}) collective-permute-start(bf16[4,352,384]{2,1,0:T(8,128)(2,1)} %get-tuple-element.380), channel_id=1, source_target_pairs={{0,8},{4,12},{8,0},{12,4},{16,24},{20,28},{24,16},{28,20},{1,9},{5... | collective-permute-start | bytes 3244040 | tf_op jit(solution)/shard_map/ppermute | solution.py:832
  1067.7 71.0 %collective-permute-start.59 = (bf16[4,176,384]{2,1,0:T(8,128)(2,1)}, bf16[4,176,384]{2,1,0:T(8,128)(2,1)S(1)}, u32[]{:S(2)}, u32[]{:S(2)}) collective-permute-start(bf16[4,176,384]{2,1,0:T(8,128)(2,1)} %get-tuple-element.373), channel_id=1, source_target_pairs={{0,16},{4,20},{8,24},{12,28},{16,0},{20,4},{24,8},{28,12},{1,17},{... | collective-permute-start | bytes 1622024 | tf_op jit(solution)/shard_map/ppermute | solution.py:832
  1150.5 98.8 %reduce-scatter.11.cloned.1.call-start = ((), (), s32[]{:S(2)}) async-start(), calls=%async_computation.12 | async-start | bytes 2027520 | tf_op jit(solution)/shard_map/reduce_scatter | solution.py:1187
  1152.0 122.1 %reduce-scatter.17.cloned.1.call-start = ((), (), s32[]{:S(2)}) async-start(), calls=%async_computation.15 | async-start | bytes 2703360 | tf_op jit(solution)/shard_map/reduce_scatter | solution.py:1187
  1169.6 143.8 %reduce-scatter.15.cloned.1.call-start = ((), (), s32[]{:S(2)}) async-start(), calls=%async_computation.14 | async-start | bytes 3379200 | tf_op jit(solution)/shard_map/reduce_scatter | solution.py:1187
  (139 other events, 2676.1 us)
Sparse Core Ops, SparseCore 0:
  10.2 31.1 all-gather.14
  43.5 37.6 all-gather.20
  92.0 35.8 all-gather.16
  129.3 46.0 all-gather.18
  176.9 45.8 all-gather.22
  340.5 29.0 all-gather.26
  371.7 36.5 all-gather.24
  775.1 54.6 reduce-scatter.6
  850.7 34.2 reduce-scatter.8
  1150.7 22.8 reduce-scatter.12
  1176.0 35.4 reduce-scatter.10
  1213.6 43.9 reduce-scatter.16
  1260.1 53.2 reduce-scatter.14

commit v12 on v11

--- a/solution.py
+++ b/solution.py
@@ -1130,11 +1130,13 @@
     projected = to_lanes(pre_attn, qkv_w)
     projected = bind(projected, *cross_m)
     projected, fc2_z = tie(projected, fc2_z)
+    while cross_m[0].todo:
+        advance(cross_m)
     fc_m = [Gather(cube, fc1_z, 0, True), Gather(cube, fc2_z, 1, True)]
+    hold(fc_m, cross_m[0].pieces[-1], cross_m[1].pieces[-1])
     advance(fc_m)
     raw = exchange(projected.reshape(parts, micros, slots, 3 * lanes))
-    cross_m[0].pieces[0], d_mlp, turn, text_turn = tie(cross_m[0].pieces[0], d_mlp, turn, text_turn)
-    arrived = fc_m[0].pieces + fc_m[1].pieces
+    arrived = [mover.pieces[-1] for mover in cross_m]
     text_own = jnp.dot(text.reshape(-1, features), text_turn, preferred_element_type=F32).astype(BF)
     text_own = jnp.pad(
         text_own.reshape(micros, text_slots, features), ((0, 0), (0, text_strip - text_slots), (0, 0))
@@ -1144,22 +1146,20 @@
         advance(fc_m)
     text_z = spread(pin(text_z, *arrived))
     text_all = spread(pin(text_own, *arrived))
-    while cross_m[0].todo:
-        advance(cross_m)
+    fc_m[0].pieces[0], d_mlp, turn, text_turn = tie(fc_m[0].pieces[0], d_mlp, turn, text_turn)
     join(cross_m)
     first_w, out2_w = [mover.weight() for mover in cross_m]
     out1_w, query2_w = (Lanes(first_w.near, first_w.far, lanes, index) for index in range(2))
     attended, turned_q, turned_k, norms = self_forward(raw, counts, cosine, sine, gain_q, gain_k)
-    attended = bind(attended, *fc_m)
     attended, text_all, text_z, first_w.far, out2_w.far = tie(attended, text_all, text_z, first_w.far, out2_w.far)
     out1_w.far = query2_w.far = first_w.far
     text_m = Gather(cube, text_z[:, :text_rows], 0, True)
     text_m.move()
     attended = exchange(attended).reshape(parts, rows, lanes)
-    join(fc_m)
     attended = bind(attended, text_m, *fc_m)
     while text_m.todo:
         text_m.move()
+    join(fc_m)
     text_all = text_all.reshape(-1, features)
     text_all = jnp.stack([text_all[:, : features // 2], text_all[:, features // 2 :]])
     stream1, pre_cross = to_features(
@@ -1238,7 +1238,7 @@
     cross_t = list(cross_t)
     d_heads, d_words, text_t[1], cross_t[1] = tie(d_heads, d_words, text_t[1], cross_t[1])
     d_words = settle([d_words])
-    text_s = scatter(cube, text_t, (lanes, 0, 0), (lanes, 1, 1))
+    text_s = scatter(cube, text_t, (2 * lanes, 0, 1))
     cross_s = scatter(cube, cross_t, (2 * lanes, 0, 0), (lanes, 2, 1))
     d_heads = bind(d_heads, *fc1_s)
     pack(fc1_s)
@@ -1289,22 +1289,17 @@
         last_norms,
     )
     d_base = bind(d_base, *other_s)
-    total_cross, total_text = list(results(cross_s)), list(results(text_s))
-    d_base = bind(d_base, *qkv_s)
-    d_base, total_cross[0], total_text[0] = tie(d_base, total_cross[0], total_text[0])
-    term_cross, term_text = settle(total_cross), settle(total_text)
     skip_t = terms_of([(d_base, joined, skip_lanes, 0)])
     skip_s = scatter(cube, skip_t, (skip_cut, 0, 0), (skip_cut, 1, 1))
+    pack(skip_s)
     pack(qkv_s)
+    skip_s[0].pieces[0] = bind(skip_s[0].pieces[0], *qkv_s)
     send(qkv_s)
-    pack(skip_s)
     send(skip_s)
-    total_qkv = list(results(qkv_s))
-    total_qkv[0] = bind(total_qkv[0], *skip_s)
-    total_skip = list(results(skip_s))
-    total_skip[0], term_cross, term_text = tie(total_skip[0], term_cross, term_text)
-    term_qkv = settle(total_qkv + total_skip)
-    term_qkv, term_skip = term_qkv[:, : 3 * lanes], term_qkv[:, 3 * lanes :]
+    term_cross, term_text = settle(results(cross_s)), settle(results(text_s))
+    total_qkv = results(qkv_s)
+    last = settle(list(total_qkv) + list(results(skip_s)))
+    term_qkv, term_skip = last[:, : 3 * lanes], last[:, 3 * lanes :]
     d_joined = to_inputs(d_base, skip_w, kept)
     result = (
         jnp.dot(result[0], turn[:, :middle].T, preferred_element_type=F32)

time: 1340 us -> 1290 us (0.963)
  waiting for transfers between devices: 493 us -> 461 us
  starting transfers between devices: 115 us -> 95.3 us
    ppermute x81 -> x79, waiting for transfers between devices: 420 us -> 385 us  [swap(): return lax.ppermute(value, axis, pairs)]
    ppermute x81 -> x79, starting transfers between devices: 95.7 us -> 76.5 us  [swap(): return lax.ppermute(value, axis, pairs)]
  transfers between devices with their start and end apart: 98 -> 96, of which waited for: 44 -> 45; matrix products, arithmetic and copies ran while one was open for 9% -> 9% of each run, Pallas kernels for 39% -> 41%
where the time goes in v12:
time: 1290 us; the launch traced here: 1280 us
  Pallas kernels  576 us (45%)
  waiting for transfers between devices  461 us (36%)
  starting transfers between devices  95.3 us (7%)
  other arithmetic  61 us (5%)
  local copies, waits for them, and re-layouts  55 us (4%)
  between operations  15.6 us (1%)
  matrix products  13.1 us (1%)
    ppermute x79, waiting for transfers between devices, swap(): return lax.ppermute(value, axis, pairs)  385 us
    pallas_call x18, Pallas kernels, sum_rows(): pl.pallas_call(kernel, name=name, grid=(parts,), in_specs=[spec(*rest) fo...  85.3 us
    pallas_call x6, Pallas kernels, to_features(): pl.pallas_call(kernel, name=name, grid=(parts,), in_specs=[pl.BlockSpec((...  78.4 us
    ppermute x79, starting transfers between devices, swap(): return lax.ppermute(value, axis, pairs)  76.5 us
    pallas_call x14, Pallas kernels, join_rows(): pl.pallas_call(kernel, name=name, grid=(parts,), in_specs=[spec(block) fo...  65 us
    pallas_call x1, Pallas kernels, self_backward(): pl.pallas_call(kernel, name='self_backward', grid_spec=pltpu.PrefetchScal...  56.5 us
    pallas_call x2, Pallas kernels, mlp_backward(): pl.pallas_call(kernel, name='mlp_backward', grid=(parts, steps), in_specs...  54.4 us
    pallas_call x2, Pallas kernels, mlp_forward(): pl.pallas_call(kernel, name='mlp_forward', grid=(parts, steps), in_specs=...  51.5 us
  transfers between devices with their start and end apart: 96, of which 45 were waited for; matrix products, arithmetic and copies ran while one was open for 9% of the time, Pallas kernels for 41%

profile of v12, /device:TPU:0, one launch (start us, length us, event | category | flops | bytes accessed | tf_op | source)
XLA Modules:
  0.0 1276.7 jit_solution(14900579951135204380)
XLA Ops:
  17.6 13.9 %negate_select_fusion = (f32[2,1024,384]{2,1,0:T(8,128)}, f32[2,1024,384]{2,1,0:T(8,128)}) fusion(f32[384]{0:T(512)S(1)} %fusion.51, s32[2,1024]{1,0:T(2,128)S(1)} %and_select_fusion.2, s32[2,1024]{1,0:T(2,128)S(1)} %and_select_fusion.3, pred[384]{0:T(512)(128)(4,1)S(1)} %get-tuple-element.460, pred[384]{0:T(512)(128)(4,1)S(1)} %get-tuple-element.461), kind=kLoop, calls=%fused_computation.4 | loop fusion | flops 3932160 | bytes 6310144 | tf_op jit(solution)/shard_map/jit(_where)/select_n | solution.py:41
  72.3 18.4 %collective-permute-done.10 = f32[4,2,176]{2,1,0:T(2,128)S(1)} collective-permute-done((f32[4,2,176]{2,1,0:T(2,128)S(1)}, f32[4,2,176]{2,1,0:T(2,128)S(1)}, u32[]{:S(2)}, u32[]{:S(2)}) %collective-permute-start.10) | collective-permute-done | bytes 5664 | tf_op jit(solution)/shard_map/ppermute | solution.py:832
  110.0 16.2 %collective-permute-done.16.refs_1_ = bf16[4,176,640]{2,1,0:T(8,128)(2,1)} collective-permute-done((bf16[4,176,640]{2,1,0:T(8,128)(2,1)S(1)}, bf16[4,176,640]{2,1,0:T(8,128)(2,1)}, u32[]{:S(2)}, u32[]{:S(2)}) %collective-permute-start.16) | collective-permute-done | bytes 901152 | tf_op jit(solution)/shard_map/ppermute | solution.py:832
  129.8 14.8 %to_features.6 = (f32[2,512,704]{2,1,0:T(8,128)}, f32[2,512,704]{2,1,0:T(8,128)}, bf16[2,512,704]{2,1,0:T(8,128)(2,1)}) custom-call(bf16[4,512,768]{2,1,0:T(8,128)(2,1)} %side_by_side.1.refs_0_.refs_1_, bf16[4,704,384]{2,1,0:T(8,128)(2,1)} %join_rows.14.refs_1_.refs_0_, bf16[4,704,384]{2,1,0:T(8,128)(2,1)} %collective-permute-done.11.refs_2_.refs_1_, ...), custom_call_target="tpu_custom_call" | custom-call | flops 276824064 | bytes 276824 | tf_op jit(solution)/shard_map/to_features/pallas_call | solution.py:401
  146.4 18.1 %collective-permute-done.18.refs_3_ = bf16[4,176,640]{2,1,0:T(8,128)(2,1)} collective-permute-done((bf16[4,176,640]{2,1,0:T(8,128)(2,1)}, bf16[4,176,640]{2,1,0:T(8,128)(2,1)}, u32[]{:S(2)}, u32[]{:S(2)}) %collective-permute-start.18) | collective-permute-done | bytes 901152 | tf_op jit(solution)/shard_map/ppermute | solution.py:832
  180.9 13.3 %to_lanes.5 = bf16[4,512,1152]{2,1,0:T(8,128)(2,1)} custom-call(bf16[2,512,704]{2,1,0:T(8,128)(2,1)} %get-tuple-element.215.x_ref.refs_0_, bf16[4,704,640]{2,1,0:T(8,128)(2,1)} %join_rows.16.refs_0_.refs_1_, bf16[4,704,640]{2,1,0:T(8,128)(2,1)} %collective-permute-done.19.refs_1_.refs_2_, bf16[4,704,512]{2,1,0:T(8,128)(2,1)} %join_rows.17.refs_2_.refs_3_, ...), custom_call_target="tpu_custom_call" | custom-call | flops 415236096 | bytes 415236 | tf_op jit(solution)/shard_map/to_lanes/pallas_call | solution.py:330
  202.6 20.3 %all-gather.23.cloned.1.call-done = bf16[704,1536]{1,0:T(8,128)(2,1)} async-done(((bf16[176,1536]{1,0:T(8,128)(2,1)}), bf16[704,1536]{1,0:T(8,128)(2,1)}) %all-gather.23.cloned.1.call-update) | async-done | bytes 2162704 | tf_op jit(solution)/shard_map/all_gather | solution.py:1017
  238.1 42.6 %collective-permute-done.26.refs_2_.refs_3_ = bf16[4,352,768]{2,1,0:T(8,128)(2,1)S(1)} collective-permute-done((bf16[4,352,768]{2,1,0:T(8,128)(2,1)}, bf16[4,352,768]{2,1,0:T(8,128)(2,1)S(1)}, u32[]{:S(2)}, u32[]{:S(2)}) %collective-permute-start.26) | collective-permute-done | bytes 2162720 | tf_op jit(solution)/shard_map/ppermute | solution.py:832
  302.6 34.0 %collective-permute-done.31.refs_1_ = bf16[4,176,1536]{2,1,0:T(8,128)(2,1)} collective-permute-done((bf16[4,176,1536]{2,1,0:T(8,128)(2,1)}, bf16[4,176,1536]{2,1,0:T(8,128)(2,1)}, u32[]{:S(2)}, u32[]{:S(2)}) %collective-permute-start.31) | collective-permute-done | bytes 2162720 | tf_op jit(solution)/shard_map/ppermute | solution.py:832
  361.6 38.4 %self_forward.1 = (bf16[4,2,256,384]{3,2,1,0:T(8,128)(2,1)}, bf16[2,1024,384]{2,1,0:T(8,128)(2,1)}, bf16[2,1024,384]{2,1,0:T(8,128)(2,1)}, f32[2,4,1024]{2,1,0:T(4,128)}) custom-call(s32[2]{0:T(128)} %copy-done.57, bf16[4,2,256,1152]{3,2,1,0:T(8,128)(2,1)} %all-to-all-done.raw_ref, f32[2,1024,384]{2,1,0:T(8,128)} %get-tuple-element.233.cos_ref, ...), custom_call_target="tpu_custom_call" | custom-call | flops 201326592 | bytes 201326 | tf_op jit(solution)/shard_map/self_forward/pallas_call | solution.py:150
  415.1 44.5 %collective-permute-done.30.refs_1_ = bf16[4,128,768]{2,1,0:T(8,128)(2,1)S(1)} collective-permute-done((bf16[4,128,768]{2,1,0:T(8,128)(2,1)S(1)}, bf16[4,128,768]{2,1,0:T(8,128)(2,1)S(1)}, u32[]{:S(2)}, u32[]{:S(2)}) %collective-permute-start.30) | collective-permute-done | bytes 786464 | tf_op jit(solution)/shard_map/ppermute | solution.py:832
  491.3 24.8 %collective-permute-done.35.refs_2_.refs_3_ = bf16[4,256,768]{2,1,0:T(8,128)(2,1)S(1)} collective-permute-done((bf16[4,256,768]{2,1,0:T(8,128)(2,1)}, bf16[4,256,768]{2,1,0:T(8,128)(2,1)S(1)}, u32[]{:S(2)}, u32[]{:S(2)}) %collective-permute-start.35) | collective-permute-done | bytes 1572896 | tf_op jit(solution)/shard_map/ppermute | solution.py:832
  541.8 19.1 %cross_forward.1 = bf16[4,2,256,384]{3,2,1,0:T(8,128)(2,1)} custom-call(s32[2,2]{1,0:T(2,128)} %bitcast.215, bf16[4,2,256,384]{3,2,1,0:T(8,128)(2,1)} %bitcast.169, bf16[4,4,2,96,768]{4,3,2,1,0:T(8,128)(2,1)} %bitcast.160), custom_call_target="tpu_custom_call" | custom-call | flops 75497472 | bytes 75497 | tf_op jit(solution)/shard_map/cross_forward/pallas_call | solution.py:738
  571.3 26.0 %mlp_forward.2 = (f32[4,512,768]{2,1,0:T(8,128)}, bf16[4,512,768]{2,1,0:T(8,128)(2,1)}, f32[2,512,704]{2,1,0:T(8,128)}, bf16[4,704,768]{2,1,0:T(8,128)(2,1)}, bf16[4,704,768]{2,1,0:T(8,128)(2,1)}) custom-call(bf16[2,512,704]{2,1,0:T(8,128)(2,1)} %get-tuple-element.260.x_ref, bf16[2,512,704]{2,1,0:T(8,128)(2,1)} %fusion.65.g_ref, ...), custom_call_target="tpu_custom_call" | custom-call | flops 830472192 | bytes 830472 | tf_op jit(solution)/shard_map/mlp_forward/pallas_call | solution.py:609
  597.9 25.5 %mlp_forward.3 = (f32[4,512,768]{2,1,0:T(8,128)}, bf16[4,512,768]{2,1,0:T(8,128)(2,1)}, bf16[2,512,704]{2,1,0:T(8,128)(2,1)}, bf16[4,704,768]{2,1,0:T(8,128)(2,1)}, bf16[4,704,768]{2,1,0:T(8,128)(2,1)}) custom-call(bf16[2,512,704]{2,1,0:T(8,128)(2,1)} %get-tuple-element.260.x_ref, bf16[2,512,704]{2,1,0:T(8,128)(2,1)} %fusion.65.g_ref, ...), custom_call_target="tpu_custom_call" | custom-call | flops 830472192 | bytes 830472 | tf_op jit(solution)/shard_map/mlp_forward/pallas_call | solution.py:609
  623.4 24.7 %mlp_backward.2 = (bf16[4,704,768]{2,1,0:T(8,128)(2,1)}, bf16[4,704,768]{2,1,0:T(8,128)(2,1)}, f32[2,512,704]{2,1,0:T(8,128)}) custom-call(bf16[2,512,704]{2,1,0:T(8,128)(2,1)} %fusion.65.g_ref, bf16[2,512,704]{2,1,0:T(8,128)(2,1)} %get-tuple-element.260.x_ref, f32[4,512,768]{2,1,0:T(8,128)} %get-tuple-element.274.hid_ref, ...), custom_call_target="tpu_custom_call" | custom-call | flops 830472192 | bytes 830472 | tf_op jit(solution)/shard_map/mlp_backward/pallas_call | solution.py:681
  659.9 29.7 %mlp_backward.3 = (bf16[4,704,768]{2,1,0:T(8,128)(2,1)}, bf16[4,704,768]{2,1,0:T(8,128)(2,1)}, f32[2,512,704]{2,1,0:T(8,128)}, bf16[2,512,704]{2,1,0:T(8,128)(2,1)}, f32[2,1,704]{2,1,0:T(1,128)}) custom-call(bf16[2,512,704]{2,1,0:T(8,128)(2,1)} %fusion.65.g_ref, bf16[2,512,704]{2,1,0:T(8,128)(2,1)} %get-tuple-element.260.x_ref, ...), custom_call_target="tpu_custom_call" | custom-call | flops 830472192 | bytes 830472 | tf_op jit(solution)/shard_map/mlp_backward/pallas_call | solution.py:681
  690.1 13.5 %collective-permute-done.41.refs_2_ = bf16[4,352,768]{2,1,0:T(8,128)(2,1)S(1)} collective-permute-done((bf16[4,352,768]{2,1,0:T(8,128)(2,1)}, bf16[4,352,768]{2,1,0:T(8,128)(2,1)S(1)}, u32[]{:S(2)}, u32[]{:S(2)}) %collective-permute-start.41) | collective-permute-done | bytes 2162720 | tf_op jit(solution)/shard_map/ppermute | solution.py:832
  719.0 22.5 %cross_backward.1 = (bf16[4,2,256,384]{3,2,1,0:T(8,128)(2,1)}, bf16[4,4,2,96,768]{4,3,2,1,0:T(8,128)(2,1)}) custom-call(s32[2,2]{1,0:T(2,128)} %bitcast.216, bf16[4,2,256,384]{3,2,1,0:T(8,128)(2,1)} %bitcast.170, bf16[4,4,2,96,768]{4,3,2,1,0:T(8,128)(2,1)} %bitcast.161, bf16[4,2,256,384]{3,2,1,0:T(8,128)(2,1)} %bitcast.173), custom_call_target="tpu_custom_call" | custom-call | flops 188743680 | bytes 188743 | tf_op jit(solution)/shard_map/cross_backward/pallas_call | solution.py:787
  753.2 12.8 %to_features.9 = (f32[2,512,704]{2,1,0:T(8,128)}, bf16[2,512,704]{2,1,0:T(8,128)(2,1)}, f32[2,1,704]{2,1,0:T(1,128)}) custom-call(bf16[4,512,384]{2,1,0:T(8,128)(2,1)} %bitcast.171, bf16[4,704,768]{2,1,0:T(8,128)(2,1)} %join_rows.20.refs_1_.refs_0_, bf16[4,704,768]{2,1,0:T(8,128)(2,1)} %collective-permute-done.28.refs_2_.refs_1_, ...), custom_call_target="tpu_custom_call" | custom-call | flops 138412032 | bytes 138412 | tf_op jit(solution)/shard_map/to_features/pallas_call | solution.py:401
  803.0 15.3 %terms_of.5 = (bf16[4,704,1152]{2,1,0:T(8,128)(2,1)}, bf16[4,704,1152]{2,1,0:T(8,128)(2,1)}) custom-call(bf16[2,512,704]{2,1,0:T(8,128)(2,1)} %get-tuple-element.307.x_ref.refs_0_, bf16[2,512,704]{2,1,0:T(8,128)(2,1)} %get-tuple-element.312.x_ref.refs_1_, bf16[2,512,704]{2,1,0:T(8,128)(2,1)} %get-tuple-element.286.x_ref.refs_2_, ...), custom_call_target="tpu_custom_call" | custom-call | flops 415236096 | bytes 415236 | tf_op jit(solution)/shard_map/terms_of/pallas_call | solution.py:445
  818.4 11.8 all-to-all-done.2.in_ref
  838.7 56.5 %self_backward.1 = (bf16[4,2,256,1152]{3,2,1,0:T(8,128)(2,1)}, f32[2,1,384]{2,1,0:T(1,128)}, f32[2,1,384]{2,1,0:T(1,128)}) custom-call(s32[2]{0:T(128)} %copy-done.57, bf16[4,2,256,1152]{3,2,1,0:T(8,128)(2,1)} %all-to-all-done.raw_ref, f32[2,1024,384]{2,1,0:T(8,128)} %get-tuple-element.233.cos_ref, f32[2,1024,384]{2,1,0:T(8,128)} %get-tuple-element.234.sin_ref, ...), custom_call_target="tpu_custom_call" | custom-call | flops 503316480 | bytes 503316 | tf_op jit(solution)/shard_map/self_backward/pallas_call | solution.py:260
  918.3 35.4 %collective-permute-done.55.refs_2_ = bf16[4,256,768]{2,1,0:T(8,128)(2,1)S(1)} collective-permute-done((bf16[4,256,768]{2,1,0:T(8,128)(2,1)}, bf16[4,256,768]{2,1,0:T(8,128)(2,1)S(1)}, u32[]{:S(2)}, u32[]{:S(2)}) %collective-permute-start.55) | collective-permute-done | bytes 1572896 | tf_op jit(solution)/shard_map/ppermute | solution.py:832
  953.8 22.4 %collective-permute-done.53.refs_5_.refs_6_ = bf16[4,352,384]{2,1,0:T(8,128)(2,1)S(1)} collective-permute-done((bf16[4,352,384]{2,1,0:T(8,128)(2,1)}, bf16[4,352,384]{2,1,0:T(8,128)(2,1)S(1)}, u32[]{:S(2)}, u32[]{:S(2)}) %collective-permute-start.53) | collective-permute-done | bytes 1081376 | tf_op jit(solution)/shard_map/ppermute | solution.py:832
  976.2 29.5 %all-to-all-done.3 = bf16[4,2,256,1152]{3,2,1,0:T(8,128)(2,1)} async-done(((bf16[4,2,256,1152]{3,2,1,0:T(8,128)(2,1)}), bf16[4,2,256,1152]{3,2,1,0:T(8,128)(2,1)}, u32[]{:S(2)}, u32[]{:S(2)}) %all-to-all-start.3) | async-done | bytes 4718624 | tf_op jit(solution)/shard_map/all_to_all | solution.py:1031
  1045.5 20.6 %to_features.11 = (bf16[2,512,704]{2,1,0:T(8,128)(2,1)}, f32[2,2,704]{2,1,0:T(2,128)}, f32[2,1,704]{2,1,0:T(1,128)}, f32[2,1,704]{2,1,0:T(1,128)}) custom-call(bf16[4,512,1152]{2,1,0:T(8,128)(2,1)} %bitcast.61.refs_1_.refs_0_, bf16[4,704,640]{2,1,0:T(8,128)(2,1)} %join_rows.16.refs_0_.refs_1_, bf16[4,704,640]{2,1,0:T(8,128)(2,1)} %collective-permute-done.19.refs_1_.refs_2_, ...), custom_call_target="tpu_custom_call" | custom-call | flops 415236096 | bytes 415236 | tf_op jit(solution)/shard_map/to_features/pallas_call | solution.py:401
  1094.3 24.8 %collective-permute-done.62.refs_5_.refs_6_ = bf16[4,352,384]{2,1,0:T(8,128)(2,1)S(1)} collective-permute-done((bf16[4,352,384]{2,1,0:T(8,128)(2,1)S(1)}, bf16[4,352,384]{2,1,0:T(8,128)(2,1)S(1)}, u32[]{:S(2)}, u32[]{:S(2)}) %collective-permute-start.62) | collective-permute-done | bytes 1081376 | tf_op jit(solution)/shard_map/ppermute | solution.py:832
  1119.1 14.3 %collective-permute-done.60.refs_2_ = bf16[4,352,768]{2,1,0:T(8,128)(2,1)} collective-permute-done((bf16[4,352,768]{2,1,0:T(8,128)(2,1)}, bf16[4,352,768]{2,1,0:T(8,128)(2,1)}, u32[]{:S(2)}, u32[]{:S(2)}) %collective-permute-start.60) | collective-permute-done | bytes 2162720 | tf_op jit(solution)/shard_map/ppermute | solution.py:832
  1153.0 16.4 %collective-permute-done.65.refs_2_ = bf16[4,352,384]{2,1,0:T(8,128)(2,1)S(1)} collective-permute-done((bf16[4,352,384]{2,1,0:T(8,128)(2,1)}, bf16[4,352,384]{2,1,0:T(8,128)(2,1)S(1)}, u32[]{:S(2)}, u32[]{:S(2)}) %collective-permute-start.65) | collective-permute-done | bytes 1081376 | tf_op jit(solution)/shard_map/ppermute | solution.py:832
  1181.1 13.4 %collective-permute-done.63.refs_3_ = bf16[4,176,768]{2,1,0:T(8,128)(2,1)} collective-permute-done((bf16[4,176,768]{2,1,0:T(8,128)(2,1)}, bf16[4,176,768]{2,1,0:T(8,128)(2,1)}, u32[]{:S(2)}, u32[]{:S(2)}) %collective-permute-start.63) | collective-permute-done | bytes 1081376 | tf_op jit(solution)/shard_map/ppermute | solution.py:832
  1227.4 12.3 to_inputs.1
  (566 shorter events, 515.3 us)
Async XLA Ops:
  9.1 93.7 %all-gather.21.cloned.1.call-start = ((), (), s32[]{:S(2)}) async-start(), calls=%async_computation.19 | async-start | bytes 2027520 | tf_op jit(solution)/shard_map/all_gather | solution.py:1017
  41.4 132.2 %all-gather.17.cloned.1.call-start = ((), (), s32[]{:S(2)}) async-start(), calls=%async_computation.17 | async-start | bytes 2027520 | tf_op jit(solution)/shard_map/all_gather | solution.py:1017
  91.9 83.6 %all-gather.19.cloned.1.call-start = ((), (), s32[]{:S(2)}) async-start(), calls=%async_computation.18 | async-start | bytes 2703360 | tf_op jit(solution)/shard_map/all_gather | solution.py:1017
  92.5 130.4 %all-gather.23.cloned.1.call-start = ((), (), s32[]{:S(2)}) async-start(), calls=%async_computation.20 | async-start | bytes 2703360 | tf_op jit(solution)/shard_map/all_gather | solution.py:1017
  222.9 138.7 %all-to-all-start = ((bf16[4,2,256,1152]{3,2,1,0:T(8,128)(2,1)}), bf16[4,2,256,1152]{3,2,1,0:T(8,128)(2,1)}, u32[]{:S(2)}, u32[]{:S(2)}) async-start(bf16[4,2,256,1152]{3,2,1,0:T(8,128)(2,1)} %bitcast.164), calls=%async_computation | async-start | bytes 9437184 | tf_op jit(solution)/shard_map/all_to_all | solution.py:1031
  227.9 172.1 %all-gather.27.cloned.1.call-start = ((), (), s32[]{:S(2)}) async-start(), calls=%async_computation.22 | async-start | bytes 1351680 | tf_op jit(solution)/shard_map/all_gather | solution.py:1017
  286.9 113.2 %collective-permute-start.28 = (bf16[4,704,768]{2,1,0:T(8,128)(2,1)}, bf16[4,704,768]{2,1,0:T(8,128)(2,1)}, u32[]{:S(2)}, u32[]{:S(2)}) collective-permute-start(bf16[4,704,768]{2,1,0:T(8,128)(2,1)} %join_rows.20.refs_1_.refs_0_), channel_id=1, source_target_pairs={{0,4},{4,0},{8,12},{12,8},{16,20},{20,16},{24,28},{28,24},{1,5},{5... | collective-permute-start | bytes 12976136 | tf_op jit(solution)/shard_map/ppermute | solution.py:832
  288.4 54.6 %collective-permute-start.33 = (bf16[4,176,1536]{2,1,0:T(8,128)(2,1)}, bf16[4,176,1536]{2,1,0:T(8,128)(2,1)}, u32[]{:S(2)}, u32[]{:S(2)}) collective-permute-start(bf16[4,176,1536]{2,1,0:T(8,128)(2,1)} %bitcast.181), channel_id=1, source_target_pairs={{0,16},{4,20},{8,24},{12,28},{16,0},{20,4},{24,8},{28,12},{1,17},{... | collective-permute-start | bytes 6488072 | tf_op jit(solution)/shard_map/ppermute | solution.py:832
  290.8 109.2 %all-gather.25.cloned.1.call-start = ((), (), s32[]{:S(2)}) async-start(), calls=%async_computation.21 | async-start | bytes 1966080 | tf_op jit(solution)/shard_map/all_gather | solution.py:1017
  302.6 97.4 %collective-permute-start.29 = (bf16[4,704,384]{2,1,0:T(8,128)(2,1)}, bf16[4,704,384]{2,1,0:T(8,128)(2,1)}, u32[]{:S(2)}, u32[]{:S(2)}) collective-permute-start(bf16[4,704,384]{2,1,0:T(8,128)(2,1)} %join_rows.21.refs_1_.refs_0_), channel_id=1, source_target_pairs={{0,4},{4,0},{8,12},{12,8},{16,20},{20,16},{24,28},{28,24},{1,5},{5... | collective-permute-start | bytes 6488072 | tf_op jit(solution)/shard_map/ppermute | solution.py:832
  341.5 118.1 %collective-permute-start.32 = (bf16[4,352,1536]{2,1,0:T(8,128)(2,1)}, bf16[4,352,1536]{2,1,0:T(8,128)(2,1)}, u32[]{:S(2)}, u32[]{:S(2)}) collective-permute-start(bf16[4,352,1536]{2,1,0:T(8,128)(2,1)} %join_rows.22.refs_0_.refs_1_), channel_id=1, source_target_pairs={{0,16},{4,20},{8,24},{12,28},{16,0},{20,4},{24,8},{28,12},{1,17},{... | collective-permute-start | bytes 12976136 | tf_op jit(solution)/shard_map/ppermute | solution.py:832
  347.8 112.6 %collective-permute-start.34 = (bf16[4,352,1536]{2,1,0:T(8,128)(2,1)}, bf16[4,352,1536]{2,1,0:T(8,128)(2,1)}, u32[]{:S(2)}, u32[]{:S(2)}) collective-permute-start(bf16[4,352,1536]{2,1,0:T(8,128)(2,1)} %join_rows.23.refs_0_.refs_2_), channel_id=1, source_target_pairs={{0,8},{4,12},{8,0},{12,4},{16,24},{20,28},{24,16},{28,20},{1,9},{5... | collective-permute-start | bytes 12976136 | tf_op jit(solution)/shard_map/ppermute | solution.py:832
  400.0 60.4 %all-to-all-start.1 = ((bf16[4,2,256,384]{3,2,1,0:T(8,128)(2,1)}), bf16[4,2,256,384]{3,2,1,0:T(8,128)(2,1)S(1)}, u32[]{:S(2)}, u32[]{:S(2)}) async-start(bf16[4,2,256,384]{3,2,1,0:T(8,128)(2,1)} %get-tuple-element.242), calls=%async_computation.1 | async-start | bytes 3145728 | tf_op jit(solution)/shard_map/all_to_all | solution.py:1031
  403.6 491.6 %reduce-scatter.7.cloned.1.call-start = ((), (), s32[]{:S(2)}) async-start(), calls=%async_computation.10 | async-start | bytes 2703360 | tf_op jit(solution)/shard_map/reduce_scatter | solution.py:1187
  468.2 103.1 %collective-permute-start.37 = (bf16[4,704,1536]{2,1,0:T(8,128)(2,1)}, bf16[4,704,1536]{2,1,0:T(8,128)(2,1)}, u32[]{:S(2)}, u32[]{:S(2)}) collective-permute-start(bf16[4,704,1536]{2,1,0:T(8,128)(2,1)} %join_rows.26.n1_ref), channel_id=1, source_target_pairs={{0,4},{4,0},{8,12},{12,8},{16,20},{20,16},{24,28},{28,24},{1,5},{5... | collective-permute-start | bytes 25952264 | tf_op jit(solution)/shard_map/ppermute | solution.py:832
  475.4 96.0 %collective-permute-start.38 = (bf16[4,704,1536]{2,1,0:T(8,128)(2,1)}, bf16[4,704,1536]{2,1,0:T(8,128)(2,1)}, u32[]{:S(2)}, u32[]{:S(2)}) collective-permute-start(bf16[4,704,1536]{2,1,0:T(8,128)(2,1)} %join_rows.27.n2_ref), channel_id=1, source_target_pairs={{0,4},{4,0},{8,12},{12,8},{16,20},{20,16},{24,28},{28,24},{1,5},{5... | collective-permute-start | bytes 25952264 | tf_op jit(solution)/shard_map/ppermute | solution.py:832
  597.4 50.7 %collective-permute-start.39 = (bf16[4,704,768]{2,1,0:T(8,128)(2,1)}, bf16[4,704,768]{2,1,0:T(8,128)(2,1)}, u32[]{:S(2)}, u32[]{:S(2)}) collective-permute-start(bf16[4,704,768]{2,1,0:T(8,128)(2,1)} %get-tuple-element.277), channel_id=1, source_target_pairs={{0,4},{4,0},{8,12},{12,8},{16,20},{20,16},{24,28},{28,24},{1,5},{5... | collective-permute-start | bytes 12976136 | tf_op jit(solution)/shard_map/ppermute | solution.py:832
  659.9 106.1 %collective-permute-start.45 = (bf16[4,704,768]{2,1,0:T(8,128)(2,1)}, bf16[4,704,768]{2,1,0:T(8,128)(2,1)}, u32[]{:S(2)}, u32[]{:S(2)}) collective-permute-start(bf16[4,704,768]{2,1,0:T(8,128)(2,1)} %get-tuple-element.298), channel_id=1, source_target_pairs={{0,4},{4,0},{8,12},{12,8},{16,20},{20,16},{24,28},{28,24},{1,5},{5... | collective-permute-start | bytes 12976136 | tf_op jit(solution)/shard_map/ppermute | solution.py:832
  689.6 76.4 %collective-permute-start.46 = (bf16[4,704,768]{2,1,0:T(8,128)(2,1)}, bf16[4,704,768]{2,1,0:T(8,128)(2,1)}, u32[]{:S(2)}, u32[]{:S(2)}) collective-permute-start(bf16[4,704,768]{2,1,0:T(8,128)(2,1)} %get-tuple-element.299), channel_id=1, source_target_pairs={{0,4},{4,0},{8,12},{12,8},{16,20},{20,16},{24,28},{28,24},{1,5},{5... | collective-permute-start | bytes 12976136 | tf_op jit(solution)/shard_map/ppermute | solution.py:832
  778.9 51.2 %all-to-all-start.2 = ((bf16[4,2,256,384]{3,2,1,0:T(8,128)(2,1)}), bf16[4,2,256,384]{3,2,1,0:T(8,128)(2,1)S(1)}, u32[]{:S(2)}, u32[]{:S(2)}) async-start(bf16[4,2,256,384]{3,2,1,0:T(8,128)(2,1)} %bitcast.174), calls=%async_computation.2 | async-start | bytes 3145728 | tf_op jit(solution)/shard_map/all_to_all | solution.py:1031
  783.6 111.6 %reduce-scatter.9.cloned.1.call-start = ((), (), s32[]{:S(2)}) async-start(), calls=%async_computation.11 | async-start | bytes 1966080 | tf_op jit(solution)/shard_map/reduce_scatter | solution.py:1187
  830.2 71.5 %collective-permute-start.51 = (bf16[4,704,1152]{2,1,0:T(8,128)(2,1)}, bf16[4,704,1152]{2,1,0:T(8,128)(2,1)}, u32[]{:S(2)}, u32[]{:S(2)}) collective-permute-start(bf16[4,704,1152]{2,1,0:T(8,128)(2,1)} %get-tuple-element.334), channel_id=1, source_target_pairs={{0,4},{4,0},{8,12},{12,8},{16,20},{20,16},{24,28},{28,24},{1,5},{5... | collective-permute-start | bytes 19464200 | tf_op jit(solution)/shard_map/ppermute | solution.py:832
  836.0 59.2 %collective-permute-start.49 = (bf16[4,176,768]{2,1,0:T(8,128)(2,1)}, bf16[4,176,768]{2,1,0:T(8,128)(2,1)S(1)}, u32[]{:S(2)}, u32[]{:S(2)}) collective-permute-start(bf16[4,176,768]{2,1,0:T(8,128)(2,1)} %get-tuple-element.330), channel_id=1, source_target_pairs={{0,8},{4,12},{8,0},{12,4},{16,24},{20,28},{24,16},{28,20},{1,9},{5... | collective-permute-start | bytes 3244040 | tf_op jit(solution)/shard_map/ppermute | solution.py:832
  837.3 58.0 %collective-permute-start.50 = (bf16[4,176,768]{2,1,0:T(8,128)(2,1)}, bf16[4,176,768]{2,1,0:T(8,128)(2,1)S(1)}, u32[]{:S(2)}, u32[]{:S(2)}) collective-permute-start(bf16[4,176,768]{2,1,0:T(8,128)(2,1)} %get-tuple-element.331), channel_id=1, source_target_pairs={{0,16},{4,20},{8,24},{12,28},{16,0},{20,4},{24,8},{28,12},{1,17},{... | collective-permute-start | bytes 3244040 | tf_op jit(solution)/shard_map/ppermute | solution.py:832
  896.6 109.1 %all-to-all-start.3 = ((bf16[4,2,256,1152]{3,2,1,0:T(8,128)(2,1)}), bf16[4,2,256,1152]{3,2,1,0:T(8,128)(2,1)}, u32[]{:S(2)}, u32[]{:S(2)}) async-start(bf16[4,2,256,1152]{3,2,1,0:T(8,128)(2,1)} %get-tuple-element.332), calls=%async_computation.5 | async-start | bytes 9437184 | tf_op jit(solution)/shard_map/all_to_all | solution.py:1031
  901.5 312.7 %reduce-scatter.17.cloned.1.call-start = ((), (), s32[]{:S(2)}) async-start(), calls=%async_computation.15 | async-start | bytes 2703360 | tf_op jit(solution)/shard_map/reduce_scatter | solution.py:1187
  906.7 69.5 %collective-permute-start.52 = (bf16[4,352,768]{2,1,0:T(8,128)(2,1)}, bf16[4,352,768]{2,1,0:T(8,128)(2,1)}, u32[]{:S(2)}, u32[]{:S(2)}) collective-permute-start(bf16[4,352,768]{2,1,0:T(8,128)(2,1)} %get-tuple-element.335), channel_id=1, source_target_pairs={{0,16},{4,20},{8,24},{12,28},{16,0},{20,4},{24,8},{28,12},{1,17},{... | collective-permute-start | bytes 6488072 | tf_op jit(solution)/shard_map/ppermute | solution.py:832
  917.1 59.1 %collective-permute-start.53 = (bf16[4,352,384]{2,1,0:T(8,128)(2,1)}, bf16[4,352,384]{2,1,0:T(8,128)(2,1)S(1)}, u32[]{:S(2)}, u32[]{:S(2)}) collective-permute-start(bf16[4,352,384]{2,1,0:T(8,128)(2,1)} %get-tuple-element.336), channel_id=1, source_target_pairs={{0,8},{4,12},{8,0},{12,4},{16,24},{20,28},{24,16},{28,20},{1,9},{5... | collective-permute-start | bytes 3244040 | tf_op jit(solution)/shard_map/ppermute | solution.py:832
  1025.9 228.2 %reduce-scatter.15.cloned.1.call-start = ((), (), s32[]{:S(2)}) async-start(), calls=%async_computation.14 | async-start | bytes 983040 | tf_op jit(solution)/shard_map/reduce_scatter | solution.py:1187
  1079.5 58.4 %collective-permute-start.61 = (bf16[4,704,768]{2,1,0:T(8,128)(2,1)}, bf16[4,704,768]{2,1,0:T(8,128)(2,1)}, u32[]{:S(2)}, u32[]{:S(2)}) collective-permute-start(bf16[4,704,768]{2,1,0:T(8,128)(2,1)} %get-tuple-element.358), channel_id=1, source_target_pairs={{0,4},{4,0},{8,12},{12,8},{16,20},{20,16},{24,28},{28,24},{1,5},{5... | collective-permute-start | bytes 12976136 | tf_op jit(solution)/shard_map/ppermute | solution.py:832
  1083.6 172.4 %reduce-scatter.13.cloned.1.call-start = ((), (), s32[]{:S(2)}) async-start(), calls=%async_computation.13 | async-start | bytes 2027520 | tf_op jit(solution)/shard_map/reduce_scatter | solution.py:1187
  1093.0 171.7 %reduce-scatter.11.cloned.1.call-start = ((), (), s32[]{:S(2)}) async-start(), calls=%async_computation.12 | async-start | bytes 3379200 | tf_op jit(solution)/shard_map/reduce_scatter | solution.py:1187
  (136 other events, 2776.6 us)
Sparse Core Ops, SparseCore 0:
  10.2 31.1 all-gather.14
  43.6 37.5 all-gather.20
  92.0 35.8 all-gather.16
  129.3 46.0 all-gather.18
  176.9 45.9 all-gather.22
  291.0 43.7 all-gather.26
  336.9 38.5 all-gather.24
  753.3 56.2 reduce-scatter.6
  830.3 34.2 reduce-scatter.8
  1026.0 47.1 reduce-scatter.16
  1083.7 21.8 reduce-scatter.14
  1107.8 35.4 reduce-scatter.12
  1212.2 52.4 reduce-scatter.10

commit v13 on v11

--- a/solution.py
+++ b/solution.py
@@ -1056,7 +1056,9 @@
     advance(qkv_m)
     cross_z = jnp.concatenate([pad_heads(side, local) for side in (w_out1.T, w_query2, w_out2.T)], 1)
     cross_z = spread(pin(cross_z, *skip_m))
-    fc1_z = spread(pin(w_fc1, *skip_m))
+    text_z = jnp.pad(pad_heads(w_text_kv.reshape(text_rows, -1), local), ((0, max(0, strip - text_rows)), (0, 0)))
+    text_z = spread(pin(text_z, *skip_m))
+    fc1_z = spread(pin(w_fc1, *qkv_m))
     join(skip_m)
     skip_w = [mover.weight() for mover in skip_m]
 
@@ -1122,55 +1124,51 @@
     hold(qkv_m, pre_attn)
     join(qkv_m)
     fc2_z = spread(pin(w_fc2.T, *after_qkv))
-    pre_attn, cross_z, fc1_z = tie(pre_attn, cross_z, fc1_z)
+    pre_attn, cross_z, text_z = tie(pre_attn, cross_z, text_z)
+    text_m = Gather(cube, text_z[:, :text_rows], 0, True)
+    hold([text_m], *after_qkv)
+    text_m.move()
     cross_m = fetch(cross_z, 2 * lanes, True)
     hold(cross_m, *after_qkv)
     advance(cross_m)
     qkv_w = [mover.weight() for mover in qkv_m]
     projected = to_lanes(pre_attn, qkv_w)
-    projected = bind(projected, *cross_m)
-    projected, fc2_z = tie(projected, fc2_z)
+    projected = bind(projected, text_m, *cross_m)
+    projected, fc1_z = tie(projected, fc1_z)
+    while cross_m[0].todo:
+        advance(cross_m + [text_m])
     fc_m = [Gather(cube, fc1_z, 0, True), Gather(cube, fc2_z, 1, True)]
+    arrived = [mover.pieces[-1] for mover in cross_m + [text_m]]
+    hold(fc_m, *arrived)
     advance(fc_m)
     raw = exchange(projected.reshape(parts, micros, slots, 3 * lanes))
-    cross_m[0].pieces[0], d_mlp, turn, text_turn = tie(cross_m[0].pieces[0], d_mlp, turn, text_turn)
-    arrived = fc_m[0].pieces + fc_m[1].pieces
     text_own = jnp.dot(text.reshape(-1, features), text_turn, preferred_element_type=F32).astype(BF)
     text_own = jnp.pad(
         text_own.reshape(micros, text_slots, features), ((0, 0), (0, text_strip - text_slots), (0, 0))
     ).reshape(micros * text_strip, features)
-    text_z = jnp.pad(pad_heads(w_text_kv.reshape(text_rows, -1), local), ((0, max(0, strip - text_rows)), (0, 0)))
     while fc_m[0].todo:
         advance(fc_m)
-    text_z = spread(pin(text_z, *arrived))
     text_all = spread(pin(text_own, *arrived))
-    while cross_m[0].todo:
-        advance(cross_m)
-    join(cross_m)
+    fc_m[0].pieces[0], d_mlp, turn, text_turn = tie(fc_m[0].pieces[0], d_mlp, turn, text_turn)
+    join(cross_m + [text_m])
     first_w, out2_w = [mover.weight() for mover in cross_m]
+    text_w = text_m.weight()
     out1_w, query2_w = (Lanes(first_w.near, first_w.far, lanes, index) for index in range(2))
     attended, turned_q, turned_k, norms = self_forward(raw, counts, cosine, sine, gain_q, gain_k)
-    attended = bind(attended, *fc_m)
-    attended, text_all, text_z, first_w.far, out2_w.far = tie(attended, text_all, text_z, first_w.far, out2_w.far)
+    attended, first_w.far, out2_w.far, text_w.far = tie(attended, first_w.far, out2_w.far, text_w.far)
     out1_w.far = query2_w.far = first_w.far
-    text_m = Gather(cube, text_z[:, :text_rows], 0, True)
-    text_m.move()
     attended = exchange(attended).reshape(parts, rows, lanes)
-    join(fc_m)
-    attended = bind(attended, text_m, *fc_m)
-    while text_m.todo:
-        text_m.move()
     text_all = text_all.reshape(-1, features)
     text_all = jnp.stack([text_all[:, : features // 2], text_all[:, features // 2 :]])
+    text_kv = to_lanes(text_all, [text_w]).reshape(parts, parts, micros, text_strip, 2 * lanes)
+    attended, text_kv = tie(attended, text_kv)
     stream1, pre_cross = to_features(
         attended, [out1_w], [stream, g_cross], [wide_shape, low_shape], next_norm
     )
+    hold(fc_m, pre_cross)
+    join(fc_m)
     fc1_w, fc2_w = [mover.weight() for mover in fc_m]
-    hold([text_m], pre_cross)
-    text_m.join()
-    text_w = text_m.weight()
     query2 = to_lanes(pre_cross, [query2_w]).reshape(parts, micros, slots, lanes)
-    text_kv = to_lanes(text_all, [text_w]).reshape(parts, parts, micros, text_strip, 2 * lanes)
     crossed = cross_forward(query2, text_kv, lengths, text_slots).reshape(parts, rows, lanes)
     stream2, pre_mlp = to_features(
         crossed, [out2_w], [stream1, g_mlp], [wide_shape, low_shape], next_norm
@@ -1238,7 +1236,7 @@
     cross_t = list(cross_t)
     d_heads, d_words, text_t[1], cross_t[1] = tie(d_heads, d_words, text_t[1], cross_t[1])
     d_words = settle([d_words])
-    text_s = scatter(cube, text_t, (lanes, 0, 0), (lanes, 1, 1))
+    text_s = scatter(cube, text_t, (2 * lanes, 0, 1))
     cross_s = scatter(cube, cross_t, (2 * lanes, 0, 0), (lanes, 2, 1))
     d_heads = bind(d_heads, *fc1_s)
     pack(fc1_s)
@@ -1301,10 +1299,8 @@
     send(skip_s)
     total_qkv = list(results(qkv_s))
     total_qkv[0] = bind(total_qkv[0], *skip_s)
-    total_skip = list(results(skip_s))
-    total_skip[0], term_cross, term_text = tie(total_skip[0], term_cross, term_text)
-    term_qkv = settle(total_qkv + total_skip)
-    term_qkv, term_skip = term_qkv[:, : 3 * lanes], term_qkv[:, 3 * lanes :]
+    last = settle(total_qkv + list(results(skip_s)))
+    term_qkv, term_skip = last[:, : 3 * lanes], last[:, 3 * lanes :]
     d_joined = to_inputs(d_base, skip_w, kept)
     result = (
         jnp.dot(result[0], turn[:, :middle].T, preferred_element_type=F32)

time: 1340 us -> 1290 us (0.963)
  waiting for transfers between devices: 493 us -> 435 us
    ppermute x81 -> x79, waiting for transfers between devices: 420 us -> 382 us  [swap(): return lax.ppermute(value, axis, pairs)]
    all_to_all x4, starting transfers between devices: 17.9 us -> 43.1 us  [exchange(): return lax.all_to_all(value, 'sp', split_axis=0, concat_axis=0, tiled=True)]
    ppermute x81 -> x79, starting transfers between devices: 95.7 us -> 83.3 us  [swap(): return lax.ppermute(value, axis, pairs)]
  transfers between devices with their start and end apart: 98 -> 96, of which waited for: 44 -> 43; matrix products, arithmetic and copies ran while one was open for 9% -> 9% of each run, Pallas kernels for 39% -> 41%
where the time goes in v13:
time: 1290 us; the launch traced here: 1280 us
  Pallas kernels  566 us (44%)
  waiting for transfers between devices  435 us (34%)
  starting transfers between devices  127 us (10%)
  local copies, waits for them, and re-layouts  58.7 us (5%)
  other arithmetic  58.4 us (5%)
  matrix products  17.5 us (1%)
  between operations  15.8 us (1%)
    ppermute x79, waiting for transfers between devices, swap(): return lax.ppermute(value, axis, pairs)  382 us
    pallas_call x18, Pallas kernels, sum_rows(): pl.pallas_call(kernel, name=name, grid=(parts,), in_specs=[spec(*rest) fo...  85 us
    ppermute x79, starting transfers between devices, swap(): return lax.ppermute(value, axis, pairs)  83.3 us
    pallas_call x6, Pallas kernels, to_features(): pl.pallas_call(kernel, name=name, grid=(parts,), in_specs=[pl.BlockSpec((...  78.6 us
    pallas_call x14, Pallas kernels, join_rows(): pl.pallas_call(kernel, name=name, grid=(parts,), in_specs=[spec(block) fo...  64.2 us
    pallas_call x2, Pallas kernels, mlp_backward(): pl.pallas_call(kernel, name='mlp_backward', grid=(parts, steps), in_specs...  54 us
    pallas_call x1, Pallas kernels, self_backward(): pl.pallas_call(kernel, name='self_backward', grid_spec=pltpu.PrefetchScal...  51.6 us
    pallas_call x2, Pallas kernels, mlp_forward(): pl.pallas_call(kernel, name='mlp_forward', grid=(parts, steps), in_specs=...  51.6 us
  transfers between devices with their start and end apart: 96, of which 43 were waited for; matrix products, arithmetic and copies ran while one was open for 9% of the time, Pallas kernels for 41%

profile of v13, /device:TPU:0, one launch (start us, length us, event | category | flops | bytes accessed | tf_op | source)
XLA Modules:
  0.0 1279.0 jit_solution(12266580065347141290)
XLA Ops:
  17.2 13.9 %negate_select_fusion = (f32[2,1024,384]{2,1,0:T(8,128)}, f32[2,1024,384]{2,1,0:T(8,128)}) fusion(f32[384]{0:T(512)S(1)} %fusion.51, s32[2,1024]{1,0:T(2,128)S(1)} %and_select_fusion.2, s32[2,1024]{1,0:T(2,128)S(1)} %and_select_fusion.3, pred[384]{0:T(512)(128)(4,1)S(1)} %get-tuple-element.470, pred[384]{0:T(512)(128)(4,1)S(1)} %get-tuple-element.471), kind=kLoop, calls=%fused_computation.4 | loop fusion | flops 3932160 | bytes 6310144 | tf_op jit(solution)/shard_map/jit(_where)/select_n | solution.py:41
  62.5 22.0 %collective-permute-done.9 = f32[4,2,176]{2,1,0:T(2,128)S(1)} collective-permute-done((f32[4,2,176]{2,1,0:T(2,128)S(1)}, f32[4,2,176]{2,1,0:T(2,128)S(1)}, u32[]{:S(2)}, u32[]{:S(2)}) %collective-permute-start.9) | collective-permute-done | bytes 5664 | tf_op jit(solution)/shard_map/ppermute | solution.py:832
  114.7 15.8 %collective-permute-done.16.refs_1_ = bf16[4,176,640]{2,1,0:T(8,128)(2,1)} collective-permute-done((bf16[4,176,640]{2,1,0:T(8,128)(2,1)S(1)}, bf16[4,176,640]{2,1,0:T(8,128)(2,1)}, u32[]{:S(2)}, u32[]{:S(2)}) %collective-permute-start.16) | collective-permute-done | bytes 901152 | tf_op jit(solution)/shard_map/ppermute | solution.py:832
  132.1 17.8 %collective-permute-done.21.refs_2_ = bf16[4,176,512]{2,1,0:T(8,128)(2,1)} collective-permute-done((bf16[4,176,512]{2,1,0:T(8,128)(2,1)S(1)}, bf16[4,176,512]{2,1,0:T(8,128)(2,1)}, u32[]{:S(2)}, u32[]{:S(2)}) %collective-permute-start.21) | collective-permute-done | bytes 720928 | tf_op jit(solution)/shard_map/ppermute | solution.py:832
  151.9 14.7 %to_features.6 = (f32[2,512,704]{2,1,0:T(8,128)}, f32[2,512,704]{2,1,0:T(8,128)}, bf16[2,512,704]{2,1,0:T(8,128)(2,1)}) custom-call(bf16[4,512,768]{2,1,0:T(8,128)(2,1)} %side_by_side.1.refs_0_.refs_1_, bf16[4,704,384]{2,1,0:T(8,128)(2,1)} %join_rows.14.refs_1_.refs_0_, bf16[4,704,384]{2,1,0:T(8,128)(2,1)} %collective-permute-done.11.refs_2_.refs_1_, ...), custom_call_target="tpu_custom_call" | custom-call | flops 276824064 | bytes 276824 | tf_op jit(solution)/shard_map/to_features/pallas_call | solution.py:401
  190.9 13.0 %to_lanes.5 = bf16[4,512,1152]{2,1,0:T(8,128)(2,1)} custom-call(bf16[2,512,704]{2,1,0:T(8,128)(2,1)} %get-tuple-element.220.x_ref.refs_0_, bf16[4,704,640]{2,1,0:T(8,128)(2,1)} %join_rows.16.refs_0_.refs_1_, bf16[4,704,640]{2,1,0:T(8,128)(2,1)} %collective-permute-done.19.refs_1_.refs_2_, bf16[4,704,512]{2,1,0:T(8,128)(2,1)} %join_rows.17.refs_2_.refs_3_, ...), custom_call_target="tpu_custom_call" | custom-call | flops 415236096 | bytes 415236 | tf_op jit(solution)/shard_map/to_lanes/pallas_call | solution.py:330
  204.4 25.6 %collective-permute-done.24.refs_1_ = bf16[4,128,768]{2,1,0:T(8,128)(2,1)} collective-permute-done((bf16[4,128,768]{2,1,0:T(8,128)(2,1)S(1)}, bf16[4,128,768]{2,1,0:T(8,128)(2,1)}, u32[]{:S(2)}, u32[]{:S(2)}) %collective-permute-start.24) | collective-permute-done | bytes 786464 | tf_op jit(solution)/shard_map/ppermute | solution.py:832
  249.2 40.5 %collective-permute-done.27.refs_2_.refs_3_ = bf16[4,352,768]{2,1,0:T(8,128)(2,1)S(1)} collective-permute-done((bf16[4,352,768]{2,1,0:T(8,128)(2,1)}, bf16[4,352,768]{2,1,0:T(8,128)(2,1)S(1)}, u32[]{:S(2)}, u32[]{:S(2)}) %collective-permute-start.27) | collective-permute-done | bytes 2162720 | tf_op jit(solution)/shard_map/ppermute | solution.py:832
  295.8 26.3 %collective-permute-done.31.refs_2_.refs_3_ = bf16[4,256,768]{2,1,0:T(8,128)(2,1)} collective-permute-done((bf16[4,256,768]{2,1,0:T(8,128)(2,1)}, bf16[4,256,768]{2,1,0:T(8,128)(2,1)}, u32[]{:S(2)}, u32[]{:S(2)}) %collective-permute-start.31) | collective-permute-done | bytes 1572896 | tf_op jit(solution)/shard_map/ppermute | solution.py:832
  332.3 37.9 %collective-permute-done.33.refs_1_ = bf16[4,176,1536]{2,1,0:T(8,128)(2,1)} collective-permute-done((bf16[4,176,1536]{2,1,0:T(8,128)(2,1)}, bf16[4,176,1536]{2,1,0:T(8,128)(2,1)}, u32[]{:S(2)}, u32[]{:S(2)}) %collective-permute-start.33) | collective-permute-done | bytes 2162720 | tf_op jit(solution)/shard_map/ppermute | solution.py:832
  397.9 34.8 %self_forward.1 = (bf16[4,2,256,384]{3,2,1,0:T(8,128)(2,1)}, bf16[2,1024,384]{2,1,0:T(8,128)(2,1)}, bf16[2,1024,384]{2,1,0:T(8,128)(2,1)}, f32[2,4,1024]{2,1,0:T(4,128)}) custom-call(s32[2]{0:T(128)} %copy-done.59, bf16[4,2,256,1152]{3,2,1,0:T(8,128)(2,1)} %all-to-all-done.raw_ref, f32[2,1024,384]{2,1,0:T(8,128)} %get-tuple-element.240.cos_ref, ...), custom_call_target="tpu_custom_call" | custom-call | flops 201326592 | bytes 201326 | tf_op jit(solution)/shard_map/self_forward/pallas_call | solution.py:150
  432.8 29.6 %all-to-all-start.1 = ((bf16[4,2,256,384]{3,2,1,0:T(8,128)(2,1)}), bf16[4,2,256,384]{3,2,1,0:T(8,128)(2,1)S(1)}, u32[]{:S(2)}, u32[]{:S(2)}) async-start(bf16[4,2,256,384]{3,2,1,0:T(8,128)(2,1)} %get-tuple-element.249), calls=%async_computation.1 | async-start | bytes 3145728 | tf_op jit(solution)/shard_map/all_to_all | solution.py:1031
  485.9 13.8 %all-to-all-done.1 = bf16[4,2,256,384]{3,2,1,0:T(8,128)(2,1)S(1)} async-done(((bf16[4,2,256,384]{3,2,1,0:T(8,128)(2,1)}), bf16[4,2,256,384]{3,2,1,0:T(8,128)(2,1)S(1)}, u32[]{:S(2)}, u32[]{:S(2)}) %all-to-all-start.1) | async-done | bytes 1572896 | tf_op jit(solution)/shard_map/all_to_all | solution.py:1031
  500.9 10.5 to_features.7
  535.1 19.1 %cross_forward.1 = bf16[4,2,256,384]{3,2,1,0:T(8,128)(2,1)} custom-call(s32[2,2]{1,0:T(2,128)} %bitcast.213, bf16[4,2,256,384]{3,2,1,0:T(8,128)(2,1)} %bitcast.167, bf16[4,4,2,96,768]{4,3,2,1,0:T(8,128)(2,1)} %bitcast.158), custom_call_target="tpu_custom_call" | custom-call | flops 75497472 | bytes 75497 | tf_op jit(solution)/shard_map/cross_forward/pallas_call | solution.py:738
  564.6 25.9 %mlp_forward.2 = (f32[4,512,768]{2,1,0:T(8,128)}, bf16[4,512,768]{2,1,0:T(8,128)(2,1)}, f32[2,512,704]{2,1,0:T(8,128)}, bf16[4,704,768]{2,1,0:T(8,128)(2,1)}, bf16[4,704,768]{2,1,0:T(8,128)(2,1)}) custom-call(bf16[2,512,704]{2,1,0:T(8,128)(2,1)} %get-tuple-element.259.x_ref, bf16[2,512,704]{2,1,0:T(8,128)(2,1)} %fusion.65.g_ref, ...), custom_call_target="tpu_custom_call" | custom-call | flops 830472192 | bytes 830472 | tf_op jit(solution)/shard_map/mlp_forward/pallas_call | solution.py:609
  591.0 25.7 %mlp_forward.3 = (f32[4,512,768]{2,1,0:T(8,128)}, bf16[4,512,768]{2,1,0:T(8,128)(2,1)}, bf16[2,512,704]{2,1,0:T(8,128)(2,1)}, bf16[4,704,768]{2,1,0:T(8,128)(2,1)}, bf16[4,704,768]{2,1,0:T(8,128)(2,1)}) custom-call(bf16[2,512,704]{2,1,0:T(8,128)(2,1)} %get-tuple-element.259.x_ref, bf16[2,512,704]{2,1,0:T(8,128)(2,1)} %fusion.65.g_ref, ...), custom_call_target="tpu_custom_call" | custom-call | flops 830472192 | bytes 830472 | tf_op jit(solution)/shard_map/mlp_forward/pallas_call | solution.py:609
  616.8 24.3 %mlp_backward.2 = (bf16[4,704,768]{2,1,0:T(8,128)(2,1)}, bf16[4,704,768]{2,1,0:T(8,128)(2,1)}, f32[2,512,704]{2,1,0:T(8,128)}) custom-call(bf16[2,512,704]{2,1,0:T(8,128)(2,1)} %fusion.65.g_ref, bf16[2,512,704]{2,1,0:T(8,128)(2,1)} %get-tuple-element.259.x_ref, f32[4,512,768]{2,1,0:T(8,128)} %get-tuple-element.278.hid_ref, ...), custom_call_target="tpu_custom_call" | custom-call | flops 830472192 | bytes 830472 | tf_op jit(solution)/shard_map/mlp_backward/pallas_call | solution.py:681
  656.8 29.8 %mlp_backward.3 = (bf16[4,704,768]{2,1,0:T(8,128)(2,1)}, bf16[4,704,768]{2,1,0:T(8,128)(2,1)}, f32[2,512,704]{2,1,0:T(8,128)}, bf16[2,512,704]{2,1,0:T(8,128)(2,1)}, f32[2,1,704]{2,1,0:T(1,128)}) custom-call(bf16[2,512,704]{2,1,0:T(8,128)(2,1)} %fusion.65.g_ref, bf16[2,512,704]{2,1,0:T(8,128)(2,1)} %get-tuple-element.259.x_ref, ...), custom_call_target="tpu_custom_call" | custom-call | flops 830472192 | bytes 830472 | tf_op jit(solution)/shard_map/mlp_backward/pallas_call | solution.py:681
  687.1 12.8 %collective-permute-done.41.refs_2_ = bf16[4,352,768]{2,1,0:T(8,128)(2,1)S(1)} collective-permute-done((bf16[4,352,768]{2,1,0:T(8,128)(2,1)}, bf16[4,352,768]{2,1,0:T(8,128)(2,1)S(1)}, u32[]{:S(2)}, u32[]{:S(2)}) %collective-permute-start.41) | collective-permute-done | bytes 2162720 | tf_op jit(solution)/shard_map/ppermute | solution.py:832
  715.4 22.5 %cross_backward.1 = (bf16[4,2,256,384]{3,2,1,0:T(8,128)(2,1)}, bf16[4,4,2,96,768]{4,3,2,1,0:T(8,128)(2,1)}) custom-call(s32[2,2]{1,0:T(2,128)} %bitcast.214, bf16[4,2,256,384]{3,2,1,0:T(8,128)(2,1)} %bitcast.168, bf16[4,4,2,96,768]{4,3,2,1,0:T(8,128)(2,1)} %bitcast.159, bf16[4,2,256,384]{3,2,1,0:T(8,128)(2,1)} %bitcast.171), custom_call_target="tpu_custom_call" | custom-call | flops 188743680 | bytes 188743 | tf_op jit(solution)/shard_map/cross_backward/pallas_call | solution.py:787
  748.6 13.0 %to_features.9 = (f32[2,512,704]{2,1,0:T(8,128)}, bf16[2,512,704]{2,1,0:T(8,128)(2,1)}, f32[2,1,704]{2,1,0:T(1,128)}) custom-call(bf16[4,512,384]{2,1,0:T(8,128)(2,1)} %bitcast.169, bf16[4,704,768]{2,1,0:T(8,128)(2,1)} %join_rows.19.refs_1_.refs_0_, bf16[4,704,768]{2,1,0:T(8,128)(2,1)} %collective-permute-done.28.refs_2_.refs_1_, ...), custom_call_target="tpu_custom_call" | custom-call | flops 138412032 | bytes 138412 | tf_op jit(solution)/shard_map/to_features/pallas_call | solution.py:401
  799.2 15.3 %terms_of.5 = (bf16[4,704,1152]{2,1,0:T(8,128)(2,1)}, bf16[4,704,1152]{2,1,0:T(8,128)(2,1)}) custom-call(bf16[2,512,704]{2,1,0:T(8,128)(2,1)} %get-tuple-element.311.x_ref.refs_0_, bf16[2,512,704]{2,1,0:T(8,128)(2,1)} %get-tuple-element.316.x_ref.refs_1_, bf16[2,512,704]{2,1,0:T(8,128)(2,1)} %get-tuple-element.290.x_ref.refs_2_, ...), custom_call_target="tpu_custom_call" | custom-call | flops 415236096 | bytes 415236 | tf_op jit(solution)/shard_map/terms_of/pallas_call | solution.py:445
  833.6 51.6 %self_backward.1 = (bf16[4,2,256,1152]{3,2,1,0:T(8,128)(2,1)}, f32[2,1,384]{2,1,0:T(1,128)}, f32[2,1,384]{2,1,0:T(1,128)}) custom-call(s32[2]{0:T(128)} %copy-done.59, bf16[4,2,256,1152]{3,2,1,0:T(8,128)(2,1)} %all-to-all-done.raw_ref, f32[2,1024,384]{2,1,0:T(8,128)} %get-tuple-element.240.cos_ref, f32[2,1024,384]{2,1,0:T(8,128)} %get-tuple-element.241.sin_ref, ...), custom_call_target="tpu_custom_call" | custom-call | flops 503316480 | bytes 503316 | tf_op jit(solution)/shard_map/self_backward/pallas_call | solution.py:260
  912.2 35.4 %collective-permute-done.55.refs_2_ = bf16[4,256,768]{2,1,0:T(8,128)(2,1)S(1)} collective-permute-done((bf16[4,256,768]{2,1,0:T(8,128)(2,1)}, bf16[4,256,768]{2,1,0:T(8,128)(2,1)S(1)}, u32[]{:S(2)}, u32[]{:S(2)}) %collective-permute-start.55) | collective-permute-done | bytes 1572896 | tf_op jit(solution)/shard_map/ppermute | solution.py:832
  947.6 22.6 %collective-permute-done.53.refs_5_.refs_6_ = bf16[4,352,384]{2,1,0:T(8,128)(2,1)S(1)} collective-permute-done((bf16[4,352,384]{2,1,0:T(8,128)(2,1)}, bf16[4,352,384]{2,1,0:T(8,128)(2,1)S(1)}, u32[]{:S(2)}, u32[]{:S(2)}) %collective-permute-start.53) | collective-permute-done | bytes 1081376 | tf_op jit(solution)/shard_map/ppermute | solution.py:832
  970.2 26.1 %all-to-all-done.3 = bf16[4,2,256,1152]{3,2,1,0:T(8,128)(2,1)} async-done(((bf16[4,2,256,1152]{3,2,1,0:T(8,128)(2,1)}), bf16[4,2,256,1152]{3,2,1,0:T(8,128)(2,1)}, u32[]{:S(2)}, u32[]{:S(2)}) %all-to-all-start.3) | async-done | bytes 4718624 | tf_op jit(solution)/shard_map/all_to_all | solution.py:1031
  996.3 11.6 terms_of.6
  1043.0 20.5 %to_features.11 = (bf16[2,512,704]{2,1,0:T(8,128)(2,1)}, f32[2,2,704]{2,1,0:T(2,128)}, f32[2,1,704]{2,1,0:T(1,128)}, f32[2,1,704]{2,1,0:T(1,128)}) custom-call(bf16[4,512,1152]{2,1,0:T(8,128)(2,1)} %bitcast.59.refs_1_.refs_0_, bf16[4,704,640]{2,1,0:T(8,128)(2,1)} %join_rows.16.refs_0_.refs_1_, bf16[4,704,640]{2,1,0:T(8,128)(2,1)} %collective-permute-done.19.refs_1_.refs_2_, ...), custom_call_target="tpu_custom_call" | custom-call | flops 415236096 | bytes 415236 | tf_op jit(solution)/shard_map/to_features/pallas_call | solution.py:401
  1063.5 43.6 %collective-permute-done.58.refs_7_ = bf16[4,176,384]{2,1,0:T(8,128)(2,1)S(1)} collective-permute-done((bf16[4,176,384]{2,1,0:T(8,128)(2,1)}, bf16[4,176,384]{2,1,0:T(8,128)(2,1)S(1)}, u32[]{:S(2)}, u32[]{:S(2)}) %collective-permute-start.58) | collective-permute-done | bytes 540704 | tf_op jit(solution)/shard_map/ppermute | solution.py:832
  1147.2 28.5 %collective-permute-done.63.refs_7_ = bf16[4,176,384]{2,1,0:T(8,128)(2,1)S(1)} collective-permute-done((bf16[4,176,384]{2,1,0:T(8,128)(2,1)}, bf16[4,176,384]{2,1,0:T(8,128)(2,1)S(1)}, u32[]{:S(2)}, u32[]{:S(2)}) %collective-permute-start.63) | collective-permute-done | bytes 540704 | tf_op jit(solution)/shard_map/ppermute | solution.py:832
  1242.4 12.4 to_inputs.1
  (558 shorter events, 506.0 us)
Async XLA Ops:
  9.1 98.1 %all-gather.21.cloned.1.call-start = ((), (), s32[]{:S(2)}) async-start(), calls=%async_computation.19 | async-start | bytes 2027520 | tf_op jit(solution)/shard_map/all_gather | solution.py:1017
  41.4 143.9 %all-gather.19.cloned.1.call-start = ((), (), s32[]{:S(2)}) async-start(), calls=%async_computation.18 | async-start | bytes 1351680 | tf_op jit(solution)/shard_map/all_gather | solution.py:1017
  91.0 94.3 %all-gather.17.cloned.1.call-start = ((), (), s32[]{:S(2)}) async-start(), calls=%async_computation.17 | async-start | bytes 2027520 | tf_op jit(solution)/shard_map/all_gather | solution.py:1017
  106.3 123.7 %all-gather.23.cloned.1.call-start = ((), (), s32[]{:S(2)}) async-start(), calls=%async_computation.20 | async-start | bytes 2703360 | tf_op jit(solution)/shard_map/all_gather | solution.py:1017
  111.4 55.3 %collective-permute-start.17 = (bf16[4,176,640]{2,1,0:T(8,128)(2,1)S(1)}, bf16[4,176,640]{2,1,0:T(8,128)(2,1)}, u32[]{:S(2)}, u32[]{:S(2)}) collective-permute-start(bf16[4,176,640]{2,1,0:T(8,128)(2,1)S(1)} %slice.425.refs_0_), channel_id=1, source_target_pairs={{0,16},{4,20},{8,24},{12,28},{16,0},{20,4},{24,8},{28,12},{1,17},{... | collective-permute-start | bytes 2703368 | tf_op jit(solution)/shard_map/ppermute | solution.py:832
  230.0 167.9 %all-to-all-start = ((bf16[4,2,256,1152]{3,2,1,0:T(8,128)(2,1)}), bf16[4,2,256,1152]{3,2,1,0:T(8,128)(2,1)}, u32[]{:S(2)}, u32[]{:S(2)}) async-start(bf16[4,2,256,1152]{3,2,1,0:T(8,128)(2,1)} %bitcast.162), calls=%async_computation | async-start | bytes 9437184 | tf_op jit(solution)/shard_map/all_to_all | solution.py:1031
  235.0 87.7 %all-gather.27.cloned.1.call-start = ((), (), s32[]{:S(2)}) async-start(), calls=%async_computation.22 | async-start | bytes 2703360 | tf_op jit(solution)/shard_map/all_gather | solution.py:1017
  235.6 238.1 %all-gather.25.cloned.1.call-start = ((), (), s32[]{:S(2)}) async-start(), calls=%async_computation.21 | async-start | bytes 1966080 | tf_op jit(solution)/shard_map/all_gather | solution.py:1017
  243.6 78.5 %collective-permute-start.31 = (bf16[4,256,768]{2,1,0:T(8,128)(2,1)}, bf16[4,256,768]{2,1,0:T(8,128)(2,1)}, u32[]{:S(2)}, u32[]{:S(2)}) collective-permute-start(bf16[4,256,768]{2,1,0:T(8,128)(2,1)} %join_rows.22.refs_0_.refs_1_), channel_id=1, source_target_pairs={{0,16},{4,20},{8,24},{12,28},{16,0},{20,4},{24,8},{28,12},{1,17},{... | collective-permute-start | bytes 4718600 | tf_op jit(solution)/shard_map/ppermute | solution.py:832
  295.8 137.0 %collective-permute-start.28 = (bf16[4,704,768]{2,1,0:T(8,128)(2,1)}, bf16[4,704,768]{2,1,0:T(8,128)(2,1)}, u32[]{:S(2)}, u32[]{:S(2)}) collective-permute-start(bf16[4,704,768]{2,1,0:T(8,128)(2,1)} %join_rows.19.refs_1_.refs_0_), channel_id=1, source_target_pairs={{0,4},{4,0},{8,12},{12,8},{16,20},{20,16},{24,28},{28,24},{1,5},{5... | collective-permute-start | bytes 12976136 | tf_op jit(solution)/shard_map/ppermute | solution.py:832
  327.9 104.9 %collective-permute-start.32 = (bf16[4,512,768]{2,1,0:T(8,128)(2,1)}, bf16[4,512,768]{2,1,0:T(8,128)(2,1)}, u32[]{:S(2)}, u32[]{:S(2)}) collective-permute-start(bf16[4,512,768]{2,1,0:T(8,128)(2,1)} %join_rows.23.refs_0_.refs_1_), channel_id=1, source_target_pairs={{0,4},{4,0},{8,12},{12,8},{16,20},{20,16},{24,28},{28,24},{1,5},{5... | collective-permute-start | bytes 9437192 | tf_op jit(solution)/shard_map/ppermute | solution.py:832
  331.8 101.0 %collective-permute-start.30 = (bf16[4,704,384]{2,1,0:T(8,128)(2,1)}, bf16[4,704,384]{2,1,0:T(8,128)(2,1)}, u32[]{:S(2)}, u32[]{:S(2)}) collective-permute-start(bf16[4,704,384]{2,1,0:T(8,128)(2,1)} %join_rows.21.refs_1_.refs_0_), channel_id=1, source_target_pairs={{0,4},{4,0},{8,12},{12,8},{16,20},{20,16},{24,28},{28,24},{1,5},{5... | collective-permute-start | bytes 6488072 | tf_op jit(solution)/shard_map/ppermute | solution.py:832
  374.9 136.5 %collective-permute-start.34 = (bf16[4,352,1536]{2,1,0:T(8,128)(2,1)}, bf16[4,352,1536]{2,1,0:T(8,128)(2,1)}, u32[]{:S(2)}, u32[]{:S(2)}) collective-permute-start(bf16[4,352,1536]{2,1,0:T(8,128)(2,1)} %join_rows.24.refs_0_.refs_1_), channel_id=1, source_target_pairs={{0,16},{4,20},{8,24},{12,28},{16,0},{20,4},{24,8},{28,12},{1,17},{... | collective-permute-start | bytes 12976136 | tf_op jit(solution)/shard_map/ppermute | solution.py:832
  381.6 137.9 %collective-permute-start.37 = (bf16[4,352,1536]{2,1,0:T(8,128)(2,1)}, bf16[4,352,1536]{2,1,0:T(8,128)(2,1)}, u32[]{:S(2)}, u32[]{:S(2)}) collective-permute-start(bf16[4,352,1536]{2,1,0:T(8,128)(2,1)} %join_rows.26.refs_0_.refs_2_), channel_id=1, source_target_pairs={{0,8},{4,12},{8,0},{12,4},{16,24},{20,28},{24,16},{28,20},{1,9},{5... | collective-permute-start | bytes 12976136 | tf_op jit(solution)/shard_map/ppermute | solution.py:832
  432.8 66.9 %all-to-all-start.1 = ((bf16[4,2,256,384]{3,2,1,0:T(8,128)(2,1)}), bf16[4,2,256,384]{3,2,1,0:T(8,128)(2,1)S(1)}, u32[]{:S(2)}, u32[]{:S(2)}) async-start(bf16[4,2,256,384]{3,2,1,0:T(8,128)(2,1)} %get-tuple-element.249), calls=%async_computation.1 | async-start | bytes 3145728 | tf_op jit(solution)/shard_map/all_to_all | solution.py:1031
  462.4 422.8 %reduce-scatter.7.cloned.1.call-start = ((), (), s32[]{:S(2)}) async-start(), calls=%async_computation.10 | async-start | bytes 2703360 | tf_op jit(solution)/shard_map/reduce_scatter | solution.py:1185
  656.7 104.8 %collective-permute-start.45 = (bf16[4,704,768]{2,1,0:T(8,128)(2,1)}, bf16[4,704,768]{2,1,0:T(8,128)(2,1)}, u32[]{:S(2)}, u32[]{:S(2)}) collective-permute-start(bf16[4,704,768]{2,1,0:T(8,128)(2,1)} %get-tuple-element.302), channel_id=1, source_target_pairs={{0,4},{4,0},{8,12},{12,8},{16,20},{20,16},{24,28},{28,24},{1,5},{5... | collective-permute-start | bytes 12976136 | tf_op jit(solution)/shard_map/ppermute | solution.py:832
  686.5 75.1 %collective-permute-start.46 = (bf16[4,704,768]{2,1,0:T(8,128)(2,1)}, bf16[4,704,768]{2,1,0:T(8,128)(2,1)}, u32[]{:S(2)}, u32[]{:S(2)}) collective-permute-start(bf16[4,704,768]{2,1,0:T(8,128)(2,1)} %get-tuple-element.303), channel_id=1, source_target_pairs={{0,4},{4,0},{8,12},{12,8},{16,20},{20,16},{24,28},{28,24},{1,5},{5... | collective-permute-start | bytes 12976136 | tf_op jit(solution)/shard_map/ppermute | solution.py:832
  778.1 107.2 %reduce-scatter.9.cloned.1.call-start = ((), (), s32[]{:S(2)}) async-start(), calls=%async_computation.11 | async-start | bytes 1966080 | tf_op jit(solution)/shard_map/reduce_scatter | solution.py:1185
  824.9 75.5 %collective-permute-start.51 = (bf16[4,704,1152]{2,1,0:T(8,128)(2,1)}, bf16[4,704,1152]{2,1,0:T(8,128)(2,1)}, u32[]{:S(2)}, u32[]{:S(2)}) collective-permute-start(bf16[4,704,1152]{2,1,0:T(8,128)(2,1)} %get-tuple-element.338), channel_id=1, source_target_pairs={{0,4},{4,0},{8,12},{12,8},{16,20},{20,16},{24,28},{28,24},{1,5},{5... | collective-permute-start | bytes 19464200 | tf_op jit(solution)/shard_map/ppermute | solution.py:832
  886.6 109.7 %all-to-all-start.3 = ((bf16[4,2,256,1152]{3,2,1,0:T(8,128)(2,1)}), bf16[4,2,256,1152]{3,2,1,0:T(8,128)(2,1)}, u32[]{:S(2)}, u32[]{:S(2)}) async-start(bf16[4,2,256,1152]{3,2,1,0:T(8,128)(2,1)} %get-tuple-element.336), calls=%async_computation.5 | async-start | bytes 9437184 | tf_op jit(solution)/shard_map/all_to_all | solution.py:1031
  891.5 340.7 %reduce-scatter.17.cloned.1.call-start = ((), (), s32[]{:S(2)}) async-start(), calls=%async_computation.15 | async-start | bytes 2703360 | tf_op jit(solution)/shard_map/reduce_scatter | solution.py:1185
  905.5 64.8 %collective-permute-start.52 = (bf16[4,352,768]{2,1,0:T(8,128)(2,1)}, bf16[4,352,768]{2,1,0:T(8,128)(2,1)}, u32[]{:S(2)}, u32[]{:S(2)}) collective-permute-start(bf16[4,352,768]{2,1,0:T(8,128)(2,1)} %get-tuple-element.339), channel_id=1, source_target_pairs={{0,16},{4,20},{8,24},{12,28},{16,0},{20,4},{24,8},{28,12},{1,17},{... | collective-permute-start | bytes 6488072 | tf_op jit(solution)/shard_map/ppermute | solution.py:832
  910.7 59.5 %collective-permute-start.53 = (bf16[4,352,384]{2,1,0:T(8,128)(2,1)}, bf16[4,352,384]{2,1,0:T(8,128)(2,1)S(1)}, u32[]{:S(2)}, u32[]{:S(2)}) collective-permute-start(bf16[4,352,384]{2,1,0:T(8,128)(2,1)} %get-tuple-element.340), channel_id=1, source_target_pairs={{0,8},{4,12},{8,0},{12,4},{16,24},{20,28},{24,16},{28,20},{1,9},{5... | collective-permute-start | bytes 3244040 | tf_op jit(solution)/shard_map/ppermute | solution.py:832
  1017.3 243.1 %reduce-scatter.15.cloned.1.call-start = ((), (), s32[]{:S(2)}) async-start(), calls=%async_computation.14 | async-start | bytes 983040 | tf_op jit(solution)/shard_map/reduce_scatter | solution.py:1185
  1024.5 92.5 %collective-permute-start.60 = (bf16[4,352,768]{2,1,0:T(8,128)(2,1)}, bf16[4,352,768]{2,1,0:T(8,128)(2,1)}, u32[]{:S(2)}, u32[]{:S(2)}) collective-permute-start(bf16[4,352,768]{2,1,0:T(8,128)(2,1)} %get-tuple-element.358), channel_id=1, source_target_pairs={{0,16},{4,20},{8,24},{12,28},{16,0},{20,4},{24,8},{28,12},{1,17},{... | collective-permute-start | bytes 6488072 | tf_op jit(solution)/shard_map/ppermute | solution.py:832
  1035.3 71.9 %collective-permute-start.57 = (bf16[4,176,768]{2,1,0:T(8,128)(2,1)}, bf16[4,176,768]{2,1,0:T(8,128)(2,1)S(1)}, u32[]{:S(2)}, u32[]{:S(2)}) collective-permute-start(bf16[4,176,768]{2,1,0:T(8,128)(2,1)} %get-tuple-element.354), channel_id=1, source_target_pairs={{0,8},{4,12},{8,0},{12,4},{16,24},{20,28},{24,16},{28,20},{1,9},{5... | collective-permute-start | bytes 3244040 | tf_op jit(solution)/shard_map/ppermute | solution.py:832
  1036.7 80.2 %collective-permute-start.61 = (bf16[4,352,384]{2,1,0:T(8,128)(2,1)}, bf16[4,352,384]{2,1,0:T(8,128)(2,1)S(1)}, u32[]{:S(2)}, u32[]{:S(2)}) collective-permute-start(bf16[4,352,384]{2,1,0:T(8,128)(2,1)} %get-tuple-element.359), channel_id=1, source_target_pairs={{0,8},{4,12},{8,0},{12,4},{16,24},{20,28},{24,16},{28,20},{1,9},{5... | collective-permute-start | bytes 3244040 | tf_op jit(solution)/shard_map/ppermute | solution.py:832
  1041.0 66.2 %collective-permute-start.59 = (bf16[4,128,768]{2,1,0:T(8,128)(2,1)}, bf16[4,128,768]{2,1,0:T(8,128)(2,1)S(1)}, u32[]{:S(2)}, u32[]{:S(2)}) collective-permute-start(bf16[4,128,768]{2,1,0:T(8,128)(2,1)} %sum_rows.27), channel_id=1, source_target_pairs={{0,16},{4,20},{8,24},{12,28},{16,0},{20,4},{24,8},{28,12},{1,17},{... | collective-permute-start | bytes 2359304 | tf_op jit(solution)/shard_map/ppermute | solution.py:832
  1041.0 66.2 %collective-permute-start.58 = (bf16[4,176,384]{2,1,0:T(8,128)(2,1)}, bf16[4,176,384]{2,1,0:T(8,128)(2,1)S(1)}, u32[]{:S(2)}, u32[]{:S(2)}) collective-permute-start(bf16[4,176,384]{2,1,0:T(8,128)(2,1)} %get-tuple-element.355), channel_id=1, source_target_pairs={{0,16},{4,20},{8,24},{12,28},{16,0},{20,4},{24,8},{28,12},{1,17},{... | collective-permute-start | bytes 1622024 | tf_op jit(solution)/shard_map/ppermute | solution.py:832
  1126.0 136.3 %reduce-scatter.13.cloned.1.call-start = ((), (), s32[]{:S(2)}) async-start(), calls=%async_computation.13 | async-start | bytes 2027520 | tf_op jit(solution)/shard_map/reduce_scatter | solution.py:1185
  1127.4 139.3 %reduce-scatter.11.cloned.1.call-start = ((), (), s32[]{:S(2)}) async-start(), calls=%async_computation.12 | async-start | bytes 3379200 | tf_op jit(solution)/shard_map/reduce_scatter | solution.py:1185
  (132 other events, 2897.7 us)
Sparse Core Ops, SparseCore 0:
  10.2 31.1 all-gather.14
  42.9 37.9 all-gather.20
  91.1 27.5 all-gather.18
  120.1 37.3 all-gather.16
  172.7 45.6 all-gather.22
  237.1 80.0 all-gather.26
  398.0 62.1 all-gather.24
  748.7 55.4 reduce-scatter.6
  825.0 34.2 reduce-scatter.8
  1017.5 48.5 reduce-scatter.16
  1126.1 22.4 reduce-scatter.14
  1150.7 35.4 reduce-scatter.12
  1210.0 53.7 reduce-scatter.10

commit v14 on v12

--- a/solution.py
+++ b/solution.py
@@ -1129,7 +1129,9 @@
     qkv_w = [mover.weight() for mover in qkv_m]
     projected = to_lanes(pre_attn, qkv_w)
     projected = bind(projected, *cross_m)
-    projected, fc2_z = tie(projected, fc2_z)
+    text_z = jnp.pad(pad_heads(w_text_kv.reshape(text_rows, -1), local), ((0, max(0, strip - text_rows)), (0, 0)))
+    projected, fc2_z, text_z = tie(projected, fc2_z, text_z)
+    text_z = spread(text_z)
     while cross_m[0].todo:
         advance(cross_m)
     fc_m = [Gather(cube, fc1_z, 0, True), Gather(cube, fc2_z, 1, True)]
@@ -1137,40 +1139,37 @@
     advance(fc_m)
     raw = exchange(projected.reshape(parts, micros, slots, 3 * lanes))
     arrived = [mover.pieces[-1] for mover in cross_m]
+    text_m = Gather(cube, text_z[:, :text_rows], 0, True)
+    hold([text_m], *arrived)
+    while text_m.todo:
+        text_m.move()
     text_own = jnp.dot(text.reshape(-1, features), text_turn, preferred_element_type=F32).astype(BF)
     text_own = jnp.pad(
         text_own.reshape(micros, text_slots, features), ((0, 0), (0, text_strip - text_slots), (0, 0))
     ).reshape(micros * text_strip, features)
-    text_z = jnp.pad(pad_heads(w_text_kv.reshape(text_rows, -1), local), ((0, max(0, strip - text_rows)), (0, 0)))
     while fc_m[0].todo:
         advance(fc_m)
-    text_z = spread(pin(text_z, *arrived))
     text_all = spread(pin(text_own, *arrived))
     fc_m[0].pieces[0], d_mlp, turn, text_turn = tie(fc_m[0].pieces[0], d_mlp, turn, text_turn)
-    join(cross_m)
+    join(cross_m + [text_m])
     first_w, out2_w = [mover.weight() for mover in cross_m]
+    text_w = text_m.weight()
     out1_w, query2_w = (Lanes(first_w.near, first_w.far, lanes, index) for index in range(2))
     attended, turned_q, turned_k, norms = self_forward(raw, counts, cosine, sine, gain_q, gain_k)
-    attended, text_all, text_z, first_w.far, out2_w.far = tie(attended, text_all, text_z, first_w.far, out2_w.far)
+    attended, first_w.far, out2_w.far, text_w.far = tie(attended, first_w.far, out2_w.far, text_w.far)
     out1_w.far = query2_w.far = first_w.far
-    text_m = Gather(cube, text_z[:, :text_rows], 0, True)
-    text_m.move()
     attended = exchange(attended).reshape(parts, rows, lanes)
-    attended = bind(attended, text_m, *fc_m)
-    while text_m.todo:
-        text_m.move()
-    join(fc_m)
     text_all = text_all.reshape(-1, features)
     text_all = jnp.stack([text_all[:, : features // 2], text_all[:, features // 2 :]])
+    text_kv = to_lanes(text_all, [text_w]).reshape(parts, parts, micros, text_strip, 2 * lanes)
+    attended, text_kv = tie(attended, text_kv)
     stream1, pre_cross = to_features(
         attended, [out1_w], [stream, g_cross], [wide_shape, low_shape], next_norm
     )
+    hold(fc_m, pre_cross)
+    join(fc_m)
     fc1_w, fc2_w = [mover.weight() for mover in fc_m]
-    hold([text_m], pre_cross)
-    text_m.join()
-    text_w = text_m.weight()
     query2 = to_lanes(pre_cross, [query2_w]).reshape(parts, micros, slots, lanes)
-    text_kv = to_lanes(text_all, [text_w]).reshape(parts, parts, micros, text_strip, 2 * lanes)
     crossed = cross_forward(query2, text_kv, lengths, text_slots).reshape(parts, rows, lanes)
     stream2, pre_mlp = to_features(
         crossed, [out2_w], [stream1, g_mlp], [wide_shape, low_shape], next_norm

time: 1290 us -> 1270 us (0.984)
  waiting for transfers between devices: 461 us -> 444 us
  starting transfers between devices: 95.3 us -> 110 us
    ppermute x79, waiting for transfers between devices: 385 us -> 328 us  [swap(): return lax.ppermute(value, axis, pairs)]
    all_gather x7, waiting for transfers between devices: 24.1 us -> 67.8 us  [spread(): return lax.all_gather(shard, 'sp', axis=0, tiled=False)]
    ppermute x79, starting transfers between devices: 76.5 us -> 91.9 us  [swap(): return lax.ppermute(value, axis, pairs)]
  transfers between devices with their start and end apart: 96 -> 96, of which waited for: 45 -> 47; matrix products, arithmetic and copies ran while one was open for 9% -> 9% of each run, Pallas kernels for 41% -> 41%
where the time goes in v14:
time: 1270 us; the launch traced here: 1260 us
  Pallas kernels  567 us (45%)
  waiting for transfers between devices  444 us (35%)
  starting transfers between devices  110 us (9%)
  other arithmetic  59.9 us (5%)
  local copies, waits for them, and re-layouts  54.7 us (4%)
  between operations  15.9 us (1%)
  matrix products  13.1 us (1%)
    ppermute x79, waiting for transfers between devices, swap(): return lax.ppermute(value, axis, pairs)  328 us
    ppermute x79, starting transfers between devices, swap(): return lax.ppermute(value, axis, pairs)  91.9 us
    pallas_call x18, Pallas kernels, sum_rows(): pl.pallas_call(kernel, name=name, grid=(parts,), in_specs=[spec(*rest) fo...  85.1 us
    pallas_call x6, Pallas kernels, to_features(): pl.pallas_call(kernel, name=name, grid=(parts,), in_specs=[pl.BlockSpec((...  78.7 us
    all_gather x7, waiting for transfers between devices, spread(): return lax.all_gather(shard, 'sp', axis=0, tiled=False)  67.8 us
    pallas_call x14, Pallas kernels, join_rows(): pl.pallas_call(kernel, name=name, grid=(parts,), in_specs=[spec(block) fo...  64.3 us
    pallas_call x2, Pallas kernels, mlp_backward(): pl.pallas_call(kernel, name='mlp_backward', grid=(parts, steps), in_specs...  54 us
    pallas_call x1, Pallas kernels, self_backward(): pl.pallas_call(kernel, name='self_backward', grid_spec=pltpu.PrefetchScal...  51.6 us
  transfers between devices with their start and end apart: 96, of which 47 were waited for; matrix products, arithmetic and copies ran while one was open for 9% of the time, Pallas kernels for 41%

profile of v14, /device:TPU:0, one launch (start us, length us, event | category | flops | bytes accessed | tf_op | source)
XLA Modules:
  0.0 1264.6 jit_solution(2772184883622069847)
XLA Ops:
  17.2 13.9 %negate_select_fusion = (f32[2,1024,384]{2,1,0:T(8,128)}, f32[2,1024,384]{2,1,0:T(8,128)}) fusion(f32[384]{0:T(512)S(1)} %fusion.51, s32[2,1024]{1,0:T(2,128)S(1)} %and_select_fusion.2, s32[2,1024]{1,0:T(2,128)S(1)} %and_select_fusion.3, pred[384]{0:T(512)(128)(4,1)S(1)} %get-tuple-element.454, pred[384]{0:T(512)(128)(4,1)S(1)} %get-tuple-element.455), kind=kLoop, calls=%fused_computation.4 | loop fusion | flops 3932160 | bytes 6310144 | tf_op jit(solution)/shard_map/jit(_where)/select_n | solution.py:41
  72.3 18.4 %collective-permute-done.10 = f32[4,2,176]{2,1,0:T(2,128)S(1)} collective-permute-done((f32[4,2,176]{2,1,0:T(2,128)S(1)}, f32[4,2,176]{2,1,0:T(2,128)S(1)}, u32[]{:S(2)}, u32[]{:S(2)}) %collective-permute-start.10) | collective-permute-done | bytes 5664 | tf_op jit(solution)/shard_map/ppermute | solution.py:832
  108.5 16.7 %collective-permute-done.16.refs_1_ = bf16[4,176,640]{2,1,0:T(8,128)(2,1)} collective-permute-done((bf16[4,176,640]{2,1,0:T(8,128)(2,1)S(1)}, bf16[4,176,640]{2,1,0:T(8,128)(2,1)}, u32[]{:S(2)}, u32[]{:S(2)}) %collective-permute-start.16) | collective-permute-done | bytes 901152 | tf_op jit(solution)/shard_map/ppermute | solution.py:832
  126.4 17.3 %collective-permute-done.21.refs_2_ = bf16[4,176,512]{2,1,0:T(8,128)(2,1)} collective-permute-done((bf16[4,176,512]{2,1,0:T(8,128)(2,1)S(1)}, bf16[4,176,512]{2,1,0:T(8,128)(2,1)}, u32[]{:S(2)}, u32[]{:S(2)}) %collective-permute-start.21) | collective-permute-done | bytes 720928 | tf_op jit(solution)/shard_map/ppermute | solution.py:832
  145.7 14.7 %to_features.6 = (f32[2,512,704]{2,1,0:T(8,128)}, f32[2,512,704]{2,1,0:T(8,128)}, bf16[2,512,704]{2,1,0:T(8,128)(2,1)}) custom-call(bf16[4,512,768]{2,1,0:T(8,128)(2,1)} %side_by_side.1.refs_0_.refs_1_, bf16[4,704,384]{2,1,0:T(8,128)(2,1)} %join_rows.14.refs_1_.refs_0_, bf16[4,704,384]{2,1,0:T(8,128)(2,1)} %collective-permute-done.11.refs_2_.refs_1_, ...), custom_call_target="tpu_custom_call" | custom-call | flops 276824064 | bytes 276824 | tf_op jit(solution)/shard_map/to_features/pallas_call | solution.py:401
  184.6 13.3 %to_lanes.5 = bf16[4,512,1152]{2,1,0:T(8,128)(2,1)} custom-call(bf16[2,512,704]{2,1,0:T(8,128)(2,1)} %get-tuple-element.212.x_ref.refs_0_, bf16[4,704,640]{2,1,0:T(8,128)(2,1)} %join_rows.16.refs_0_.refs_1_, bf16[4,704,640]{2,1,0:T(8,128)(2,1)} %collective-permute-done.19.refs_1_.refs_2_, bf16[4,704,512]{2,1,0:T(8,128)(2,1)} %join_rows.17.refs_2_.refs_3_, ...), custom_call_target="tpu_custom_call" | custom-call | flops 415236096 | bytes 415236 | tf_op jit(solution)/shard_map/to_lanes/pallas_call | solution.py:330
  211.4 14.1 %all-gather.23.cloned.1.call-done = bf16[704,1536]{1,0:T(8,128)(2,1)} async-done(((bf16[176,1536]{1,0:T(8,128)(2,1)}), bf16[704,1536]{1,0:T(8,128)(2,1)}) %all-gather.23.cloned.1.call-update) | async-done | bytes 2162704 | tf_op jit(solution)/shard_map/all_gather | solution.py:1017
  236.3 51.4 %all-gather.25.cloned.1.call-done = bf16[704,768]{1,0:T(8,128)(2,1)} async-done(((bf16[176,768]{1,0:T(8,128)(2,1)}), bf16[704,768]{1,0:T(8,128)(2,1)}) %all-gather.25.cloned.1.call-update) | async-done | bytes 1081360 | tf_op jit(solution)/shard_map/all_gather | solution.py:1017
  290.4 18.0 %collective-permute-done.30.refs_1_ = bf16[4,128,768]{2,1,0:T(8,128)(2,1)S(1)} collective-permute-done((bf16[4,128,768]{2,1,0:T(8,128)(2,1)S(1)}, bf16[4,128,768]{2,1,0:T(8,128)(2,1)S(1)}, u32[]{:S(2)}, u32[]{:S(2)}) %collective-permute-start.30) | collective-permute-done | bytes 786464 | tf_op jit(solution)/shard_map/ppermute | solution.py:832
  321.4 29.2 %collective-permute-done.31.refs_2_.refs_3_ = bf16[4,256,768]{2,1,0:T(8,128)(2,1)S(1)} collective-permute-done((bf16[4,256,768]{2,1,0:T(8,128)(2,1)}, bf16[4,256,768]{2,1,0:T(8,128)(2,1)S(1)}, u32[]{:S(2)}, u32[]{:S(2)}) %collective-permute-start.31) | collective-permute-done | bytes 1572896 | tf_op jit(solution)/shard_map/ppermute | solution.py:832
  374.4 22.6 %collective-permute-done.36.refs_1_ = bf16[4,176,1536]{2,1,0:T(8,128)(2,1)} collective-permute-done((bf16[4,176,1536]{2,1,0:T(8,128)(2,1)}, bf16[4,176,1536]{2,1,0:T(8,128)(2,1)}, u32[]{:S(2)}, u32[]{:S(2)}) %collective-permute-start.36) | collective-permute-done | bytes 2162720 | tf_op jit(solution)/shard_map/ppermute | solution.py:832
  418.6 34.8 %self_forward.1 = (bf16[4,2,256,384]{3,2,1,0:T(8,128)(2,1)}, bf16[2,1024,384]{2,1,0:T(8,128)(2,1)}, bf16[2,1024,384]{2,1,0:T(8,128)(2,1)}, f32[2,4,1024]{2,1,0:T(4,128)}) custom-call(s32[2]{0:T(128)} %copy-done.53, bf16[4,2,256,1152]{3,2,1,0:T(8,128)(2,1)} %all-to-all-done.raw_ref, f32[2,1024,384]{2,1,0:T(8,128)} %get-tuple-element.230.cos_ref, ...), custom_call_target="tpu_custom_call" | custom-call | flops 201326592 | bytes 201326 | tf_op jit(solution)/shard_map/self_forward/pallas_call | solution.py:150
  480.6 12.8 %all-to-all-done.1 = bf16[4,2,256,384]{3,2,1,0:T(8,128)(2,1)S(1)} async-done(((bf16[4,2,256,384]{3,2,1,0:T(8,128)(2,1)}), bf16[4,2,256,384]{3,2,1,0:T(8,128)(2,1)S(1)}, u32[]{:S(2)}, u32[]{:S(2)}) %all-to-all-start.1) | async-done | bytes 1572896 | tf_op jit(solution)/shard_map/all_to_all | solution.py:1031
  529.7 19.1 %cross_forward.1 = bf16[4,2,256,384]{3,2,1,0:T(8,128)(2,1)} custom-call(s32[2,2]{1,0:T(2,128)} %bitcast.213, bf16[4,2,256,384]{3,2,1,0:T(8,128)(2,1)} %bitcast.167, bf16[4,4,2,96,768]{4,3,2,1,0:T(8,128)(2,1)} %bitcast.158), custom_call_target="tpu_custom_call" | custom-call | flops 75497472 | bytes 75497 | tf_op jit(solution)/shard_map/cross_forward/pallas_call | solution.py:738
  559.2 25.9 %mlp_forward.2 = (f32[4,512,768]{2,1,0:T(8,128)}, bf16[4,512,768]{2,1,0:T(8,128)(2,1)}, f32[2,512,704]{2,1,0:T(8,128)}, bf16[4,704,768]{2,1,0:T(8,128)(2,1)}, bf16[4,704,768]{2,1,0:T(8,128)(2,1)}) custom-call(bf16[2,512,704]{2,1,0:T(8,128)(2,1)} %get-tuple-element.249.x_ref, bf16[2,512,704]{2,1,0:T(8,128)(2,1)} %fusion.65.g_ref, ...), custom_call_target="tpu_custom_call" | custom-call | flops 830472192 | bytes 830472 | tf_op jit(solution)/shard_map/mlp_forward/pallas_call | solution.py:609
  585.6 25.6 %mlp_forward.3 = (f32[4,512,768]{2,1,0:T(8,128)}, bf16[4,512,768]{2,1,0:T(8,128)(2,1)}, bf16[2,512,704]{2,1,0:T(8,128)(2,1)}, bf16[4,704,768]{2,1,0:T(8,128)(2,1)}, bf16[4,704,768]{2,1,0:T(8,128)(2,1)}) custom-call(bf16[2,512,704]{2,1,0:T(8,128)(2,1)} %get-tuple-element.249.x_ref, bf16[2,512,704]{2,1,0:T(8,128)(2,1)} %fusion.65.g_ref, ...), custom_call_target="tpu_custom_call" | custom-call | flops 830472192 | bytes 830472 | tf_op jit(solution)/shard_map/mlp_forward/pallas_call | solution.py:609
  611.4 24.3 %mlp_backward.2 = (bf16[4,704,768]{2,1,0:T(8,128)(2,1)}, bf16[4,704,768]{2,1,0:T(8,128)(2,1)}, f32[2,512,704]{2,1,0:T(8,128)}) custom-call(bf16[2,512,704]{2,1,0:T(8,128)(2,1)} %fusion.65.g_ref, bf16[2,512,704]{2,1,0:T(8,128)(2,1)} %get-tuple-element.249.x_ref, f32[4,512,768]{2,1,0:T(8,128)} %get-tuple-element.268.hid_ref, ...), custom_call_target="tpu_custom_call" | custom-call | flops 830472192 | bytes 830472 | tf_op jit(solution)/shard_map/mlp_backward/pallas_call | solution.py:681
  649.2 29.8 %mlp_backward.3 = (bf16[4,704,768]{2,1,0:T(8,128)(2,1)}, bf16[4,704,768]{2,1,0:T(8,128)(2,1)}, f32[2,512,704]{2,1,0:T(8,128)}, bf16[2,512,704]{2,1,0:T(8,128)(2,1)}, f32[2,1,704]{2,1,0:T(1,128)}) custom-call(bf16[2,512,704]{2,1,0:T(8,128)(2,1)} %fusion.65.g_ref, bf16[2,512,704]{2,1,0:T(8,128)(2,1)} %get-tuple-element.249.x_ref, ...), custom_call_target="tpu_custom_call" | custom-call | flops 830472192 | bytes 830472 | tf_op jit(solution)/shard_map/mlp_backward/pallas_call | solution.py:681
  708.1 22.6 %cross_backward.1 = (bf16[4,2,256,384]{3,2,1,0:T(8,128)(2,1)}, bf16[4,4,2,96,768]{4,3,2,1,0:T(8,128)(2,1)}) custom-call(s32[2,2]{1,0:T(2,128)} %bitcast.214, bf16[4,2,256,384]{3,2,1,0:T(8,128)(2,1)} %bitcast.168, bf16[4,4,2,96,768]{4,3,2,1,0:T(8,128)(2,1)} %bitcast.159, bf16[4,2,256,384]{3,2,1,0:T(8,128)(2,1)} %bitcast.171), custom_call_target="tpu_custom_call" | custom-call | flops 188743680 | bytes 188743 | tf_op jit(solution)/shard_map/cross_backward/pallas_call | solution.py:787
  742.0 13.0 %to_features.9 = (f32[2,512,704]{2,1,0:T(8,128)}, bf16[2,512,704]{2,1,0:T(8,128)(2,1)}, f32[2,1,704]{2,1,0:T(1,128)}) custom-call(bf16[4,512,384]{2,1,0:T(8,128)(2,1)} %bitcast.169, bf16[4,704,768]{2,1,0:T(8,128)(2,1)} %join_rows.19.refs_1_.refs_0_, bf16[4,704,768]{2,1,0:T(8,128)(2,1)} %collective-permute-done.27.refs_2_.refs_1_, ...), custom_call_target="tpu_custom_call" | custom-call | flops 138412032 | bytes 138412 | tf_op jit(solution)/shard_map/to_features/pallas_call | solution.py:401
  791.3 15.3 %terms_of.5 = (bf16[4,704,1152]{2,1,0:T(8,128)(2,1)}, bf16[4,704,1152]{2,1,0:T(8,128)(2,1)}) custom-call(bf16[2,512,704]{2,1,0:T(8,128)(2,1)} %get-tuple-element.301.x_ref.refs_0_, bf16[2,512,704]{2,1,0:T(8,128)(2,1)} %get-tuple-element.306.x_ref.refs_1_, bf16[2,512,704]{2,1,0:T(8,128)(2,1)} %get-tuple-element.280.x_ref.refs_2_, ...), custom_call_target="tpu_custom_call" | custom-call | flops 415236096 | bytes 415236 | tf_op jit(solution)/shard_map/terms_of/pallas_call | solution.py:445
  826.7 51.6 %self_backward.1 = (bf16[4,2,256,1152]{3,2,1,0:T(8,128)(2,1)}, f32[2,1,384]{2,1,0:T(1,128)}, f32[2,1,384]{2,1,0:T(1,128)}) custom-call(s32[2]{0:T(128)} %copy-done.53, bf16[4,2,256,1152]{3,2,1,0:T(8,128)(2,1)} %all-to-all-done.raw_ref, f32[2,1024,384]{2,1,0:T(8,128)} %get-tuple-element.230.cos_ref, f32[2,1024,384]{2,1,0:T(8,128)} %get-tuple-element.231.sin_ref, ...), custom_call_target="tpu_custom_call" | custom-call | flops 503316480 | bytes 503316 | tf_op jit(solution)/shard_map/self_backward/pallas_call | solution.py:260
  884.7 12.8 %collective-permute-start.54 = (bf16[4,512,768]{2,1,0:T(8,128)(2,1)}, bf16[4,512,768]{2,1,0:T(8,128)(2,1)}, u32[]{:S(2)}, u32[]{:S(2)}) collective-permute-start(bf16[4,512,768]{2,1,0:T(8,128)(2,1)} %get-tuple-element.332), channel_id=1, source_target_pairs={{0,4},{4,0},{8,12},{12,8},{16,20},{20,16},{24,28},{28,24},{1,5},{5... | collective-permute-start | bytes 9437192 | tf_op jit(solution)/shard_map/ppermute | solution.py:832
  910.7 35.4 %collective-permute-done.55.refs_2_ = bf16[4,256,768]{2,1,0:T(8,128)(2,1)S(1)} collective-permute-done((bf16[4,256,768]{2,1,0:T(8,128)(2,1)}, bf16[4,256,768]{2,1,0:T(8,128)(2,1)S(1)}, u32[]{:S(2)}, u32[]{:S(2)}) %collective-permute-start.55) | collective-permute-done | bytes 1572896 | tf_op jit(solution)/shard_map/ppermute | solution.py:832
  946.0 22.7 %collective-permute-done.53.refs_5_.refs_6_ = bf16[4,352,384]{2,1,0:T(8,128)(2,1)S(1)} collective-permute-done((bf16[4,352,384]{2,1,0:T(8,128)(2,1)}, bf16[4,352,384]{2,1,0:T(8,128)(2,1)S(1)}, u32[]{:S(2)}, u32[]{:S(2)}) %collective-permute-start.53) | collective-permute-done | bytes 1081376 | tf_op jit(solution)/shard_map/ppermute | solution.py:832
  968.7 20.7 %all-to-all-done.3 = bf16[4,2,256,1152]{3,2,1,0:T(8,128)(2,1)} async-done(((bf16[4,2,256,1152]{3,2,1,0:T(8,128)(2,1)}), bf16[4,2,256,1152]{3,2,1,0:T(8,128)(2,1)}, u32[]{:S(2)}, u32[]{:S(2)}) %all-to-all-start.3) | async-done | bytes 4718624 | tf_op jit(solution)/shard_map/all_to_all | solution.py:1031
  1033.5 20.5 %to_features.11 = (bf16[2,512,704]{2,1,0:T(8,128)(2,1)}, f32[2,2,704]{2,1,0:T(2,128)}, f32[2,1,704]{2,1,0:T(1,128)}, f32[2,1,704]{2,1,0:T(1,128)}) custom-call(bf16[4,512,1152]{2,1,0:T(8,128)(2,1)} %bitcast.59.refs_1_.refs_0_, bf16[4,704,640]{2,1,0:T(8,128)(2,1)} %join_rows.16.refs_0_.refs_1_, bf16[4,704,640]{2,1,0:T(8,128)(2,1)} %collective-permute-done.19.refs_1_.refs_2_, ...), custom_call_target="tpu_custom_call" | custom-call | flops 415236096 | bytes 415236 | tf_op jit(solution)/shard_map/to_features/pallas_call | solution.py:401
  1080.4 25.1 %collective-permute-done.62.refs_5_.refs_6_ = bf16[4,352,384]{2,1,0:T(8,128)(2,1)S(1)} collective-permute-done((bf16[4,352,384]{2,1,0:T(8,128)(2,1)S(1)}, bf16[4,352,384]{2,1,0:T(8,128)(2,1)S(1)}, u32[]{:S(2)}, u32[]{:S(2)}) %collective-permute-start.62) | collective-permute-done | bytes 1081376 | tf_op jit(solution)/shard_map/ppermute | solution.py:832
  1105.5 15.7 %collective-permute-done.60.refs_2_ = bf16[4,352,768]{2,1,0:T(8,128)(2,1)} collective-permute-done((bf16[4,352,768]{2,1,0:T(8,128)(2,1)}, bf16[4,352,768]{2,1,0:T(8,128)(2,1)}, u32[]{:S(2)}, u32[]{:S(2)}) %collective-permute-start.60) | collective-permute-done | bytes 2162720 | tf_op jit(solution)/shard_map/ppermute | solution.py:832
  1140.8 16.4 %collective-permute-done.65.refs_2_ = bf16[4,352,384]{2,1,0:T(8,128)(2,1)S(1)} collective-permute-done((bf16[4,352,384]{2,1,0:T(8,128)(2,1)}, bf16[4,352,384]{2,1,0:T(8,128)(2,1)S(1)}, u32[]{:S(2)}, u32[]{:S(2)}) %collective-permute-start.65) | collective-permute-done | bytes 1081376 | tf_op jit(solution)/shard_map/ppermute | solution.py:832
  1168.9 12.0 collective-permute-done.63.refs_3_
  1214.3 12.4 to_inputs.1
  (552 shorter events, 550.6 us)
Async XLA Ops:
  9.1 92.7 %all-gather.21.cloned.1.call-start = ((), (), s32[]{:S(2)}) async-start(), calls=%async_computation.19 | async-start | bytes 2027520 | tf_op jit(solution)/shard_map/all_gather | solution.py:1017
  41.4 137.7 %all-gather.17.cloned.1.call-start = ((), (), s32[]{:S(2)}) async-start(), calls=%async_computation.17 | async-start | bytes 2027520 | tf_op jit(solution)/shard_map/all_gather | solution.py:1017
  91.9 87.2 %all-gather.19.cloned.1.call-start = ((), (), s32[]{:S(2)}) async-start(), calls=%async_computation.18 | async-start | bytes 2703360 | tf_op jit(solution)/shard_map/all_gather | solution.py:1017
  100.5 125.0 %all-gather.23.cloned.1.call-start = ((), (), s32[]{:S(2)}) async-start(), calls=%async_computation.20 | async-start | bytes 2703360 | tf_op jit(solution)/shard_map/all_gather | solution.py:1017
  105.1 55.3 %collective-permute-start.17 = (bf16[4,176,640]{2,1,0:T(8,128)(2,1)S(1)}, bf16[4,176,640]{2,1,0:T(8,128)(2,1)}, u32[]{:S(2)}, u32[]{:S(2)}) collective-permute-start(bf16[4,176,640]{2,1,0:T(8,128)(2,1)S(1)} %slice.425.refs_0_), channel_id=1, source_target_pairs={{0,16},{4,20},{8,24},{12,28},{16,0},{20,4},{24,8},{28,12},{1,17},{... | collective-permute-start | bytes 2703368 | tf_op jit(solution)/shard_map/ppermute | solution.py:832
  179.0 108.6 %all-gather.25.cloned.1.call-start = ((), (), s32[]{:S(2)}) async-start(), calls=%async_computation.21 | async-start | bytes 1351680 | tf_op jit(solution)/shard_map/all_gather | solution.py:1017
  210.8 78.1 %collective-permute-start.26 = (bf16[4,352,768]{2,1,0:T(8,128)(2,1)}, bf16[4,352,768]{2,1,0:T(8,128)(2,1)}, u32[]{:S(2)}, u32[]{:S(2)}) collective-permute-start(bf16[4,352,768]{2,1,0:T(8,128)(2,1)} %join_rows.18.refs_0_.refs_1_), channel_id=1, source_target_pairs={{0,16},{4,20},{8,24},{12,28},{16,0},{20,4},{24,8},{28,12},{1,17},{... | collective-permute-start | bytes 6488072 | tf_op jit(solution)/shard_map/ppermute | solution.py:832
  226.3 192.3 %all-to-all-start = ((bf16[4,2,256,1152]{3,2,1,0:T(8,128)(2,1)}), bf16[4,2,256,1152]{3,2,1,0:T(8,128)(2,1)}, u32[]{:S(2)}, u32[]{:S(2)}) async-start(bf16[4,2,256,1152]{3,2,1,0:T(8,128)(2,1)} %bitcast.162), calls=%async_computation | async-start | bytes 9437184 | tf_op jit(solution)/shard_map/all_to_all | solution.py:1031
  231.3 237.1 %all-gather.27.cloned.1.call-start = ((), (), s32[]{:S(2)}) async-start(), calls=%async_computation.22 | async-start | bytes 1966080 | tf_op jit(solution)/shard_map/all_gather | solution.py:1017
  234.8 54.1 %collective-permute-start.28 = (bf16[4,352,384]{2,1,0:T(8,128)(2,1)}, bf16[4,352,384]{2,1,0:T(8,128)(2,1)S(1)}, u32[]{:S(2)}, u32[]{:S(2)}) collective-permute-start(bf16[4,352,384]{2,1,0:T(8,128)(2,1)} %join_rows.20.refs_0_.refs_2_), channel_id=1, source_target_pairs={{0,8},{4,12},{8,0},{12,4},{16,24},{20,28},{24,16},{28,20},{1,9},{5... | collective-permute-start | bytes 3244040 | tf_op jit(solution)/shard_map/ppermute | solution.py:832
  319.3 134.1 %collective-permute-start.27 = (bf16[4,704,768]{2,1,0:T(8,128)(2,1)}, bf16[4,704,768]{2,1,0:T(8,128)(2,1)}, u32[]{:S(2)}, u32[]{:S(2)}) collective-permute-start(bf16[4,704,768]{2,1,0:T(8,128)(2,1)} %join_rows.19.refs_1_.refs_0_), channel_id=1, source_target_pairs={{0,4},{4,0},{8,12},{12,8},{16,20},{20,16},{24,28},{28,24},{1,5},{5... | collective-permute-start | bytes 12976136 | tf_op jit(solution)/shard_map/ppermute | solution.py:832
  320.8 76.2 %collective-permute-start.36 = (bf16[4,176,1536]{2,1,0:T(8,128)(2,1)}, bf16[4,176,1536]{2,1,0:T(8,128)(2,1)}, u32[]{:S(2)}, u32[]{:S(2)}) collective-permute-start(bf16[4,176,1536]{2,1,0:T(8,128)(2,1)} %bitcast.179), channel_id=1, source_target_pairs={{0,16},{4,20},{8,24},{12,28},{16,0},{20,4},{24,8},{28,12},{1,17},{... | collective-permute-start | bytes 6488072 | tf_op jit(solution)/shard_map/ppermute | solution.py:832
  356.0 97.4 %collective-permute-start.32 = (bf16[4,512,768]{2,1,0:T(8,128)(2,1)}, bf16[4,512,768]{2,1,0:T(8,128)(2,1)}, u32[]{:S(2)}, u32[]{:S(2)}) collective-permute-start(bf16[4,512,768]{2,1,0:T(8,128)(2,1)} %join_rows.23.refs_0_.refs_1_), channel_id=1, source_target_pairs={{0,4},{4,0},{8,12},{12,8},{16,20},{20,16},{24,28},{28,24},{1,5},{5... | collective-permute-start | bytes 9437192 | tf_op jit(solution)/shard_map/ppermute | solution.py:832
  359.9 93.5 %collective-permute-start.29 = (bf16[4,704,384]{2,1,0:T(8,128)(2,1)}, bf16[4,704,384]{2,1,0:T(8,128)(2,1)}, u32[]{:S(2)}, u32[]{:S(2)}) collective-permute-start(bf16[4,704,384]{2,1,0:T(8,128)(2,1)} %join_rows.21.refs_1_.refs_0_), channel_id=1, source_target_pairs={{0,4},{4,0},{8,12},{12,8},{16,20},{20,16},{24,28},{28,24},{1,5},{5... | collective-permute-start | bytes 6488072 | tf_op jit(solution)/shard_map/ppermute | solution.py:832
  373.8 131.3 %collective-permute-start.34 = (bf16[4,352,1536]{2,1,0:T(8,128)(2,1)}, bf16[4,352,1536]{2,1,0:T(8,128)(2,1)}, u32[]{:S(2)}, u32[]{:S(2)}) collective-permute-start(bf16[4,352,1536]{2,1,0:T(8,128)(2,1)} %join_rows.24.refs_0_.refs_1_), channel_id=1, source_target_pairs={{0,16},{4,20},{8,24},{12,28},{16,0},{20,4},{24,8},{28,12},{1,17},{... | collective-permute-start | bytes 12976136 | tf_op jit(solution)/shard_map/ppermute | solution.py:832
  401.8 112.3 %collective-permute-start.37 = (bf16[4,352,1536]{2,1,0:T(8,128)(2,1)}, bf16[4,352,1536]{2,1,0:T(8,128)(2,1)}, u32[]{:S(2)}, u32[]{:S(2)}) collective-permute-start(bf16[4,352,1536]{2,1,0:T(8,128)(2,1)} %join_rows.26.refs_0_.refs_2_), channel_id=1, source_target_pairs={{0,8},{4,12},{8,0},{12,4},{16,24},{20,28},{24,16},{28,20},{1,9},{5... | collective-permute-start | bytes 12976136 | tf_op jit(solution)/shard_map/ppermute | solution.py:832
  457.0 421.3 %reduce-scatter.7.cloned.1.call-start = ((), (), s32[]{:S(2)}) async-start(), calls=%async_computation.10 | async-start | bytes 2703360 | tf_op jit(solution)/shard_map/reduce_scatter | solution.py:1186
  585.1 50.5 %collective-permute-start.39 = (bf16[4,704,768]{2,1,0:T(8,128)(2,1)}, bf16[4,704,768]{2,1,0:T(8,128)(2,1)}, u32[]{:S(2)}, u32[]{:S(2)}) collective-permute-start(bf16[4,704,768]{2,1,0:T(8,128)(2,1)} %get-tuple-element.271), channel_id=1, source_target_pairs={{0,4},{4,0},{8,12},{12,8},{16,20},{20,16},{24,28},{28,24},{1,5},{5... | collective-permute-start | bytes 12976136 | tf_op jit(solution)/shard_map/ppermute | solution.py:832
  649.2 105.8 %collective-permute-start.45 = (bf16[4,704,768]{2,1,0:T(8,128)(2,1)}, bf16[4,704,768]{2,1,0:T(8,128)(2,1)}, u32[]{:S(2)}, u32[]{:S(2)}) collective-permute-start(bf16[4,704,768]{2,1,0:T(8,128)(2,1)} %get-tuple-element.292), channel_id=1, source_target_pairs={{0,4},{4,0},{8,12},{12,8},{16,20},{20,16},{24,28},{28,24},{1,5},{5... | collective-permute-start | bytes 12976136 | tf_op jit(solution)/shard_map/ppermute | solution.py:832
  679.0 76.1 %collective-permute-start.46 = (bf16[4,704,768]{2,1,0:T(8,128)(2,1)}, bf16[4,704,768]{2,1,0:T(8,128)(2,1)}, u32[]{:S(2)}, u32[]{:S(2)}) collective-permute-start(bf16[4,704,768]{2,1,0:T(8,128)(2,1)} %get-tuple-element.293), channel_id=1, source_target_pairs={{0,4},{4,0},{8,12},{12,8},{16,20},{20,16},{24,28},{28,24},{1,5},{5... | collective-permute-start | bytes 12976136 | tf_op jit(solution)/shard_map/ppermute | solution.py:832
  771.6 106.8 %reduce-scatter.9.cloned.1.call-start = ((), (), s32[]{:S(2)}) async-start(), calls=%async_computation.11 | async-start | bytes 1966080 | tf_op jit(solution)/shard_map/reduce_scatter | solution.py:1186
  817.1 80.4 %collective-permute-start.51 = (bf16[4,704,1152]{2,1,0:T(8,128)(2,1)}, bf16[4,704,1152]{2,1,0:T(8,128)(2,1)}, u32[]{:S(2)}, u32[]{:S(2)}) collective-permute-start(bf16[4,704,1152]{2,1,0:T(8,128)(2,1)} %get-tuple-element.328), channel_id=1, source_target_pairs={{0,4},{4,0},{8,12},{12,8},{16,20},{20,16},{24,28},{28,24},{1,5},{5... | collective-permute-start | bytes 19464200 | tf_op jit(solution)/shard_map/ppermute | solution.py:832
  824.5 53.8 %collective-permute-start.49 = (bf16[4,176,768]{2,1,0:T(8,128)(2,1)}, bf16[4,176,768]{2,1,0:T(8,128)(2,1)S(1)}, u32[]{:S(2)}, u32[]{:S(2)}) collective-permute-start(bf16[4,176,768]{2,1,0:T(8,128)(2,1)} %get-tuple-element.324), channel_id=1, source_target_pairs={{0,8},{4,12},{8,0},{12,4},{16,24},{20,28},{24,16},{28,20},{1,9},{5... | collective-permute-start | bytes 3244040 | tf_op jit(solution)/shard_map/ppermute | solution.py:832
  825.7 52.7 %collective-permute-start.50 = (bf16[4,176,768]{2,1,0:T(8,128)(2,1)}, bf16[4,176,768]{2,1,0:T(8,128)(2,1)S(1)}, u32[]{:S(2)}, u32[]{:S(2)}) collective-permute-start(bf16[4,176,768]{2,1,0:T(8,128)(2,1)} %get-tuple-element.325), channel_id=1, source_target_pairs={{0,16},{4,20},{8,24},{12,28},{16,0},{20,4},{24,8},{28,12},{1,17},{... | collective-permute-start | bytes 3244040 | tf_op jit(solution)/shard_map/ppermute | solution.py:832
  879.7 109.7 %all-to-all-start.3 = ((bf16[4,2,256,1152]{3,2,1,0:T(8,128)(2,1)}), bf16[4,2,256,1152]{3,2,1,0:T(8,128)(2,1)}, u32[]{:S(2)}, u32[]{:S(2)}) async-start(bf16[4,2,256,1152]{3,2,1,0:T(8,128)(2,1)} %get-tuple-element.326), calls=%async_computation.5 | async-start | bytes 9437184 | tf_op jit(solution)/shard_map/all_to_all | solution.py:1031
  884.6 316.0 %reduce-scatter.17.cloned.1.call-start = ((), (), s32[]{:S(2)}) async-start(), calls=%async_computation.15 | async-start | bytes 2703360 | tf_op jit(solution)/shard_map/reduce_scatter | solution.py:1186
  902.5 66.2 %collective-permute-start.52 = (bf16[4,352,768]{2,1,0:T(8,128)(2,1)}, bf16[4,352,768]{2,1,0:T(8,128)(2,1)}, u32[]{:S(2)}, u32[]{:S(2)}) collective-permute-start(bf16[4,352,768]{2,1,0:T(8,128)(2,1)} %get-tuple-element.329), channel_id=1, source_target_pairs={{0,16},{4,20},{8,24},{12,28},{16,0},{20,4},{24,8},{28,12},{1,17},{... | collective-permute-start | bytes 6488072 | tf_op jit(solution)/shard_map/ppermute | solution.py:832
  910.7 58.1 %collective-permute-start.53 = (bf16[4,352,384]{2,1,0:T(8,128)(2,1)}, bf16[4,352,384]{2,1,0:T(8,128)(2,1)S(1)}, u32[]{:S(2)}, u32[]{:S(2)}) collective-permute-start(bf16[4,352,384]{2,1,0:T(8,128)(2,1)} %get-tuple-element.330), channel_id=1, source_target_pairs={{0,8},{4,12},{8,0},{12,4},{16,24},{20,28},{24,16},{28,20},{1,9},{5... | collective-permute-start | bytes 3244040 | tf_op jit(solution)/shard_map/ppermute | solution.py:832
  1010.5 231.4 %reduce-scatter.15.cloned.1.call-start = ((), (), s32[]{:S(2)}) async-start(), calls=%async_computation.14 | async-start | bytes 983040 | tf_op jit(solution)/shard_map/reduce_scatter | solution.py:1186
  1067.3 58.5 %collective-permute-start.61 = (bf16[4,704,768]{2,1,0:T(8,128)(2,1)}, bf16[4,704,768]{2,1,0:T(8,128)(2,1)}, u32[]{:S(2)}, u32[]{:S(2)}) collective-permute-start(bf16[4,704,768]{2,1,0:T(8,128)(2,1)} %get-tuple-element.352), channel_id=1, source_target_pairs={{0,4},{4,0},{8,12},{12,8},{16,20},{20,16},{24,28},{28,24},{1,5},{5... | collective-permute-start | bytes 12976136 | tf_op jit(solution)/shard_map/ppermute | solution.py:832
  1071.4 172.4 %reduce-scatter.13.cloned.1.call-start = ((), (), s32[]{:S(2)}) async-start(), calls=%async_computation.13 | async-start | bytes 2027520 | tf_op jit(solution)/shard_map/reduce_scatter | solution.py:1186
  1079.3 173.0 %reduce-scatter.11.cloned.1.call-start = ((), (), s32[]{:S(2)}) async-start(), calls=%async_computation.12 | async-start | bytes 3379200 | tf_op jit(solution)/shard_map/reduce_scatter | solution.py:1186
  (129 other events, 2818.1 us)
Sparse Core Ops, SparseCore 0:
  10.2 31.1 all-gather.14
  43.5 37.6 all-gather.20
  92.0 35.8 all-gather.16
  129.3 46.0 all-gather.18
  179.2 46.2 all-gather.22
  227.4 60.1 all-gather.24
  418.7 34.5 all-gather.26
  742.1 53.6 reduce-scatter.6
  817.2 34.2 reduce-scatter.8
  1010.6 49.3 reduce-scatter.16
  1071.5 20.8 reduce-scatter.14
  1094.5 35.4 reduce-scatter.12
  1198.6 53.6 reduce-scatter.10
